TPU v7x, 32 devices: a whole 2x2x4 slice. The times are simulated.
32 devices in a mesh: dp: 8 (over y, x, core), seq: 4 (over z).
Axes of the slice: x: 2, y: 2, z: 4, core: 2. Of those that a mesh axis runs over, the one named last changes fastest.
Arguments:
- tokens: bfloat16 [8192, 1152], P(('dp', 'seq')), may hold values from -6 to 6
- modulation: bfloat16 [32, 6912], P('dp'), may hold values from -4 to 4
- image_ids: int32 [8192], P('dp'), may hold values from 0 to 3, as said below
- w_qkv: bfloat16 [1152, 3456], replicated, may hold values from -0.1875 to 0.1875
- w_out: bfloat16 [1152, 1152], replicated, may hold values from -3 to 3
- w_fc1: bfloat16 [1152, 4608], replicated, may hold values from -0.1875 to 0.1875
- w_fc2: bfloat16 [4608, 1152], replicated, may hold values from -0.09375 to 0.09375
- w_proj1: bfloat16 [1152, 2048], replicated, may hold values from -0.1875 to 0.1875
- w_proj2: bfloat16 [2048, 2048], replicated, may hold values from -0.125 to 0.125
- w_proj3: bfloat16 [2048, 768], replicated, may hold values from -0.125 to 0.125
- dino: bfloat16 [8192, 768], P(('dp', 'seq')), may hold values from -6 to 6
- cotangent: bfloat16 [8192, 1152], P(('dp', 'seq')), may hold values from -6 to 6
Outputs:
- block_out: bfloat16 [8192, 1152], P(('dp', 'seq'))
- grad_tokens: bfloat16 [8192, 1152], P(('dp', 'seq'))
- grad_modulation: float32 [32, 6912], P('dp', 'seq')
- grad_qkv: float32 [1152, 3456], P('dp', 'seq')
- grad_out: float32 [1152, 1152], P('dp', 'seq')
- grad_fc1: float32 [1152, 4608], P('dp', 'seq')
- grad_fc2: float32 [4608, 1152], P('dp', 'seq')
- grad_proj1: float32 [1152, 2048], P('dp', 'seq')
- grad_proj2: float32 [2048, 2048], P('dp', 'seq')
- grad_proj3: float32 [2048, 768], P('dp', 'seq')
Inputs may be any that keep to these rules, and one draw needn't show every extreme that they name: `image_ids`: each aligned run of 1024 tokens is either one image, all its tokens with id 4 * r, or four images of 256 tokens in order with ids 4 * r to 4 * r + 3, where r (0 to 0) is the run's place within its group; the groups of 1024 tokens lie one to an index of dp.
All inputs are finite; a program needn't handle non-finite values.
Results may differ from a plain program's by a relative error of at most 0.022.
Values may be sent and summed in bfloat16 or wider, within the bound.
No kernel may reach another device: no remote copies, remote signals or barrier semaphores. Data moves between devices by JAX's collectives and lax.ppermute only.
A program may use at most 320 MiB of HBM per device.

v0:
```python
import jax
import jax.numpy as jnp
from jax import lax
from jax.sharding import PartitionSpec as P

H = 16
HD = 72
LEN = 1024


EPS_NORM = 1e-06
HIGH = lax.Precision.HIGHEST


def matmul(left, right):
    return jnp.dot(left, right, preferred_element_type=jnp.float32)


def times_trans(left, right):
    return lax.dot_general(
        left, right, (((1,), (1,)), ((), ())), preferred_element_type=jnp.float32
    )


def trans_times(left, right, precision=None):
    return lax.dot_general(
        left,
        right,
        (((0,), (0,)), ((), ())),
        precision=precision,
        preferred_element_type=jnp.float32,
    )


def normalize(v):
    centre = v - jnp.mean(v, axis=-1, keepdims=True)
    return centre * lax.rsqrt(jnp.mean(centre * centre, axis=-1, keepdims=True) + EPS_NORM)


def row_scores(queries, keys, ids_row):
    raw = jnp.einsum("qhd,khd->hqk", queries, keys, preferred_element_type=jnp.float32) * HD ** (
        -0.5
    )
    same = ids_row[:, None] == ids_row[None, :]
    return (raw, same)


def attend_forward(block):
    queries, keys, values, ids_row = block
    raw, same = row_scores(queries, keys, ids_row)
    masked = jnp.where(same[None], raw, -1e30)
    top = jnp.max(masked, axis=-1, keepdims=True)
    expo = jnp.exp(masked - top)
    total = jnp.sum(expo, axis=-1, keepdims=True)
    probs = (expo / total).astype(jnp.bfloat16)
    outputs = jnp.einsum("hqk,khd->qhd", probs, values, preferred_element_type=jnp.float32)
    return (outputs, (top + jnp.log(total))[..., 0])


def attend_backward(block):
    queries, keys, values, ids_row, logsum, grads_out = block
    raw, same = row_scores(queries, keys, ids_row)
    probs = jnp.where(same[None], jnp.exp(raw - logsum[..., None]), 0.0)
    dprob = jnp.einsum("qhd,khd->hqk", grads_out, values, preferred_element_type=jnp.float32)
    delta = jnp.sum(probs * dprob, axis=-1, keepdims=True)
    dscore = (probs * (dprob - delta)).astype(jnp.bfloat16)
    dquery = jnp.einsum("hqk,khd->qhd", dscore, keys, preferred_element_type=jnp.float32) * HD ** (
        -0.5
    )
    dkey = jnp.einsum("hqk,qhd->khd", dscore, queries, preferred_element_type=jnp.float32) * HD ** (
        -0.5
    )
    dvalue = jnp.einsum(
        "hqk,qhd->khd", probs.astype(jnp.bfloat16), grads_out, preferred_element_type=jnp.float32
    )
    return jnp.stack([dquery, dkey, dvalue], axis=1).astype(jnp.bfloat16)


def shards(
    tokens,
    modulation,
    image_ids,
    w_qkv,
    w_out,
    w_fc1,
    w_fc2,
    w_proj1,
    w_proj2,
    w_proj3,
    dino,
    cotangent,
):
    n_seq = lax.axis_size("seq")
    rank = lax.axis_index("seq")
    tok_dev = tokens.shape[0]
    width = tokens.shape[1]
    group_tok = image_ids.shape[0]
    rows = group_tok // LEN
    heads_local = H // n_seq
    local_width = heads_local * HD
    slots = modulation.shape[0]
    ids_tok = lax.dynamic_slice_in_dim(image_ids, rank * tok_dev, tok_dev)
    onehot = (ids_tok[:, None] == jnp.arange(slots, dtype=jnp.int32)[None, :]).astype(jnp.float32)
    mods = jnp.dot(
        onehot, modulation.astype(jnp.float32), precision=HIGH, preferred_element_type=jnp.float32
    )
    shift1 = mods[:, 0:width]
    scale1 = mods[:, width : 2 * width]
    gate1 = mods[:, 2 * width : 3 * width]
    shift2 = mods[:, 3 * width : 4 * width]
    scale2 = mods[:, 4 * width : 5 * width]
    gate2 = mods[:, 5 * width : 6 * width]
    inputs = tokens.astype(jnp.float32)
    normed1, norm_pull1 = jax.vjp(normalize, inputs)
    first = (normed1 * (1.0 + scale1) + shift1).astype(jnp.bfloat16)
    qkv = matmul(first, w_qkv).astype(jnp.bfloat16).reshape(tok_dev, 3, width)
    by_heads = lax.all_to_all(qkv, "seq", split_axis=2, concat_axis=0, tiled=True)
    split = by_heads.reshape(rows, LEN, 3, heads_local, HD)
    queries = split[:, :, 0]
    keys = split[:, :, 1]
    values = split[:, :, 2]
    ids_rows = image_ids.reshape(rows, LEN)
    attended, logsum = lax.map(attend_forward, (queries, keys, values, ids_rows))
    heads_out = attended.reshape(group_tok, local_width).astype(jnp.bfloat16)
    attn_in = lax.all_to_all(heads_out, "seq", split_axis=0, concat_axis=1, tiled=True)
    attn = matmul(attn_in, w_out)
    hidden1 = inputs + gate1 * attn
    normed2, norm_pull2 = jax.vjp(normalize, hidden1)
    second = (normed2 * (1.0 + scale2) + shift2).astype(jnp.bfloat16)
    upper = matmul(second, w_fc1)
    gelu_out, gelu_pull = jax.vjp(lambda v: jax.nn.gelu(v, approximate=True), upper)
    active = gelu_out.astype(jnp.bfloat16)
    mlp = matmul(active, w_fc2)
    out_y = hidden1 + gate2 * mlp
    rounded = out_y.astype(jnp.bfloat16)
    proj_r1 = matmul(rounded, w_proj1)
    silu1, silu_pull1 = jax.vjp(jax.nn.silu, proj_r1)
    proj_a1 = silu1.astype(jnp.bfloat16)
    proj_r2 = matmul(proj_a1, w_proj2)
    silu2, silu_pull2 = jax.vjp(jax.nn.silu, proj_r2)
    proj_a2 = silu2.astype(jnp.bfloat16)
    latent = matmul(proj_a2, w_proj3)
    targets = dino.astype(jnp.float32)
    inv_z = lax.rsqrt(jnp.sum(latent * latent, axis=-1, keepdims=True) + EPS_NORM)
    inv_t = lax.rsqrt(jnp.sum(targets * targets, axis=-1, keepdims=True) + EPS_NORM)
    cosine = jnp.sum(latent * targets, axis=-1, keepdims=True) * inv_z * inv_t
    dlatent = (-0.5 * (targets * (inv_z * inv_t) - cosine * inv_z * inv_z * latent)).astype(
        jnp.bfloat16
    )
    dr2 = silu_pull2(times_trans(dlatent, w_proj3))[0].astype(jnp.bfloat16)
    dr1 = silu_pull1(times_trans(dr2, w_proj2))[0].astype(jnp.bfloat16)
    dy = cotangent.astype(jnp.float32) + times_trans(dr1, w_proj1)
    dmlp = (gate2 * dy).astype(jnp.bfloat16)
    dupper = gelu_pull(times_trans(dmlp, w_fc2))[0].astype(jnp.bfloat16)
    dsecond = times_trans(dupper, w_fc1)
    dhidden1 = dy + norm_pull2(dsecond * (1.0 + scale2))[0]
    dattn = (gate1 * dhidden1).astype(jnp.bfloat16)
    dheads_in = times_trans(dattn, w_out).astype(jnp.bfloat16)
    dheads = lax.all_to_all(dheads_in, "seq", split_axis=1, concat_axis=0, tiled=True)
    dheads_rows = dheads.reshape(rows, LEN, heads_local, HD)
    dsplit = lax.map(attend_backward, (queries, keys, values, ids_rows, logsum, dheads_rows))
    dqkv_heads = dsplit.reshape(group_tok, 3, local_width)
    dqkv = lax.all_to_all(dqkv_heads, "seq", split_axis=0, concat_axis=2, tiled=True).reshape(
        tok_dev, 3 * width
    )
    dfirst = times_trans(dqkv, w_qkv)
    grad_inputs = (dhidden1 + norm_pull1(dfirst * (1.0 + scale1))[0]).astype(jnp.bfloat16)
    dmods = jnp.concatenate(
        [dfirst, dfirst * normed1, dhidden1 * attn, dsecond, dsecond * normed2, dy * mlp], axis=1
    )
    dmod_local = trans_times(onehot, dmods, HIGH)
    qkv_cols = 3 * width
    fc1_cols = w_fc1.shape[1]
    proj1_cols = w_proj1.shape[1]
    proj2_cols = w_proj2.shape[1]
    model_share = lax.psum_scatter(
        jnp.concatenate(
            [
                trans_times(first, dqkv),
                trans_times(attn_in, dattn),
                trans_times(second, dupper),
                trans_times(rounded, dr1),
            ],
            axis=1,
        ).astype(jnp.bfloat16),
        "dp",
        scatter_dimension=0,
        tiled=True,
    ).astype(jnp.float32)
    hidden_share = lax.psum_scatter(
        trans_times(active, dmlp).astype(jnp.bfloat16), "dp", scatter_dimension=0, tiled=True
    )
    projector_share = lax.psum_scatter(
        jnp.concatenate([trans_times(proj_a1, dr2), trans_times(proj_a2, dlatent)], axis=1).astype(
            jnp.bfloat16
        ),
        "dp",
        scatter_dimension=0,
        tiled=True,
    ).astype(jnp.float32)
    edge2 = qkv_cols + width
    edge3 = edge2 + fc1_cols
    summed = (
        lax.psum_scatter(
            model_share[:, 0:qkv_cols].astype(jnp.bfloat16), "seq", scatter_dimension=1, tiled=True
        ).astype(jnp.float32),
        lax.psum_scatter(
            model_share[:, qkv_cols:edge2].astype(jnp.bfloat16),
            "seq",
            scatter_dimension=1,
            tiled=True,
        ).astype(jnp.float32),
        lax.psum_scatter(
            model_share[:, edge2:edge3].astype(jnp.bfloat16), "seq", scatter_dimension=1, tiled=True
        ).astype(jnp.float32),
        lax.psum_scatter(hidden_share, "seq", scatter_dimension=1, tiled=True).astype(jnp.float32),
        lax.psum_scatter(
            model_share[:, edge3 : edge3 + proj1_cols].astype(jnp.bfloat16),
            "seq",
            scatter_dimension=1,
            tiled=True,
        ).astype(jnp.float32),
        lax.psum_scatter(
            projector_share[:, 0:proj2_cols].astype(jnp.bfloat16),
            "seq",
            scatter_dimension=1,
            tiled=True,
        ).astype(jnp.float32),
        lax.psum_scatter(
            projector_share[:, proj2_cols:].astype(jnp.bfloat16),
            "seq",
            scatter_dimension=1,
            tiled=True,
        ).astype(jnp.float32),
        lax.psum_scatter(
            dmod_local.astype(jnp.bfloat16), "seq", scatter_dimension=1, tiled=True
        ).astype(jnp.float32),
    )
    return (
        rounded,
        grad_inputs,
        summed[7],
        summed[0],
        summed[1],
        summed[2],
        summed[3],
        summed[4],
        summed[5],
        summed[6],
    )


def solution(mesh):
    in_specs = (
        P(("dp", "seq"), None),
        P("dp", None),
        P("dp"),
        P(),
        P(),
        P(),
        P(),
        P(),
        P(),
        P(),
        P(("dp", "seq"), None),
        P(("dp", "seq"), None),
    )
    out_specs = (
        P(("dp", "seq"), None),
        P(("dp", "seq"), None),
        P("dp", "seq"),
        P("dp", "seq"),
        P("dp", "seq"),
        P("dp", "seq"),
        P("dp", "seq"),
        P("dp", "seq"),
        P("dp", "seq"),
        P("dp", "seq"),
    )
    return jax.shard_map(shards, mesh=mesh, in_specs=in_specs, out_specs=out_specs, check_vma=False)
```

profile of v0, /device:TPU:0, one launch (start us, length us, event | category | flops | bytes accessed | tf_op | source)
XLA Modules:
  0.0 871.5 jit_solution(11449413185523003648)
XLA Ops:
  18.2 3.8 convolution_convert_fusion.7
  22.0 3.8 copy.56
  25.8 10.4 %copy.57 = bf16[256,3,1152]{0,1,2:T(4,128)(2,1)} copy(bf16[256,3,1152]{0,2,1:T(8,128)(2,1)} %bitcast.106) | data formatting | bytes 3538944 | tf_op jit(solution)/shard_map/reshape | solution.py:116
  36.2 6.5 all-to-all-start
  44.6 52.0 %all-to-all-done = bf16[256,3,1152]{0,1,2:T(4,128)(2,1)} async-done(((bf16[256,3,1152]{0,1,2:T(4,128)(2,1)}), bf16[256,3,1152]{0,1,2:T(4,128)(2,1)}, u32[]{:S(2)}, u32[]{:S(2)}) %all-to-all-start) | async-done | bytes 1769504 | tf_op jit(solution)/shard_map/all_to_all | solution.py:117
  101.1 4.2 reshape.183
  105.3 5.0 select_reduce_fusion
  110.3 3.7 fusion
  116.0 6.8 fusion.31
  126.3 17.8 %all_to_all.62 = bf16[4,256,288]{1,2,0:T(8,128)(2,1)S(1)} all-to-all(bf16[4,256,288]{1,2,0:T(8,128)(2,1)S(1)} %copy.61), channel_id=1, replica_groups=mesh['dp'=8,'seq'=4] {'seq'}, dimensions={0} | all-to-all | bytes 1179648 | tf_op jit(solution)/shard_map/all_to_all | solution.py:125
  144.1 4.6 fusion.62
  151.9 9.4 %fusion.63 = f32[256,4608]{1,0:T(8,128)} fusion(bf16[256,1152]{1,0:T(8,128)(2,1)S(1)} %fusion.37, bf16[1152,4608]{1,0:T(8,128)(2,1)} %param.17), kind=kOutput, calls=%fused_computation.132 | convolution fusion | flops 2717908992 | bytes 15925248 | tf_op jit(solution)/shard_map/dot_general | solution.py:16
  161.4 7.6 add_convert_fusion.1
  179.9 15.7 %pad_maximum_fusion.1 = bf16[2048,2816]{0,1:T(8,128)(2,1)} fusion(bf16[2048,768]{0,1:T(8,128)(2,1)S(1)} %convolution_convert_fusion.8, bf16[2048,2048]{0,1:T(8,128)(2,1)S(1)} %convolution_convert_fusion.5), kind=kLoop, calls=%fused_computation.11 | loop fusion | flops 23068672 | bytes 23068672 | tf_op jit(solution)/shard_map/concatenate | solution.py:194
  196.8 7.3 fusion.18
  204.0 6.1 multiply_convert_fusion.5
  210.2 9.5 %fusion.12 = bf16[256,4608]{1,0:T(8,128)(2,1)S(1)} fusion(f32[256,4608]{1,0:T(8,128)} %fusion.63, bf16[256,1152]{1,0:T(8,128)(2,1)S(1)} %get-tuple-element.119, bf16[4608,1152]{1,0:T(8,128)(2,1)} %param.18), kind=kOutput, calls=%fused_computation.29 | convolution fusion | flops 2741501952 | bytes 18284544 | tf_op jit(solution)/shard_map/dot_general | solution.py:20
  219.7 9.5 %multiply_reduce_fusion.1 = (f32[256]{0:T(256)S(1)}, f32[256,1152]{1,0:T(8,128)S(1)}) fusion(f32[256,1152]{1,0:T(8,128)S(1)} %copy-done.6, f32[256]{0:T(256)S(1)} %broadcast_multiply_fusion, f32[256,6912]{1,0:T(8,128)} %copy-done.4, bf16[256,4608]{1,0:T(8,128)(2,1)S(1)} %fusion.12, bf16[1152,4608]{1,0:T(8,128)(2,1)} %param.17), kind=kOutput, calls=%fused_computation.84 | convolution fusion | flops 2719383296 | bytes 16517120 | tf_op jit(solution)/shard_map/dot_general | solution.py:20
  232.9 6.7 convolution_convert_fusion
  239.7 3.1 multiply_convert_fusion.4
  246.9 3.9 all-to-all-start.2
  250.8 15.4 %all-to-all-done.2 = bf16[256,4,288]{0,2,1:T(8,128)(2,1)S(1)} async-done(((bf16[256,4,288]{0,2,1:T(8,128)(2,1)}), bf16[256,4,288]{0,2,1:T(8,128)(2,1)S(1)}, u32[]{:S(2)}, u32[]{:S(2)}) %all-to-all-start.2) | async-done | bytes 589856 | tf_op jit(solution)/shard_map/all_to_all | solution.py:159
  269.1 12.7 %multiply_reduce_fusion = (f32[4,1024]{1,0:T(4,128)S(1)}, f32[4,1024,1024]{1,2,0:T(8,128)}) fusion(f32[4,1024,1024]{1,2,0:T(8,128)} %copy-done.2, f32[4,1024]{1,0:T(4,128)S(1)} %log_add_fusion, pred[1024,1024]{0,1:T(8,128)(4,1)S(1)} %copy-done.8, bf16[1024,4,72]{0,2,1:T(8,128)(2,1)S(1)} %squeeze.39, bf16[1,1024,3,4,72]{1,4,3,2,0:T(8,128)(2,1)} %reshape.183), kind=kOutput, calls=%fused_computation.4 | convolution fusion | flops 624947200 | bytes 35815424 | tf_op jit(solution)/shard_map/while/body/eval_jaxpr/qhd,khd->hqk/dot_general | solution.py:64
  281.8 13.1 %multiply_convert_fusion = bf16[4,1024,1024]{1,2,0:T(8,128)(2,1)S(1)} fusion(f32[4,1024,1024]{1,2,0:T(8,128)} %get-tuple-element.124, f32[4,1024,1024]{1,2,0:T(8,128)} %copy-done.2, f32[4,1024]{1,0:T(4,128)S(1)} %get-tuple-element.123, f32[4,1024]{1,0:T(4,128)S(1)} %log_add_fusion, pred[1024,1024]{0,1:T(8,128)(4,1)S(1)} %copy-done.8), kind=kLoop, calls=%fused_computation.3 | loop fusion | flops 25165824 | bytes 43024384 | tf_op jit(solution)/shard_map/while/body/eval_jaxpr/convert_element_type | solution.py:66
  295.0 3.3 fusion.26
  299.8 3.0 copy.67
  302.8 6.4 fusion.27
  312.2 10.4 %fusion.28 = bf16[4,72,1024]{2,1,0:T(8,128)(2,1)} fusion(bf16[1024,4,72]{0,2,1:T(8,128)(2,1)} %copy-done.31, f32[4,1024,1024]{1,2,0:T(8,128)} %copy-done.2, f32[4,1024]{1,0:T(4,128)S(1)} %log_add_fusion, pred[1024,1024]{0,1:T(8,128)(4,1)S(1)} %copy-done.8), kind=kOutput, calls=%fused_computation.64 | convolution fusion | flops 621051904 | bytes 19021824 | tf_op jit(solution)/shard_map/while/body/eval_jaxpr/hqk,qhd->khd/dot_general | solution.py:73
  322.6 4.8 copy.69
  327.4 8.9 %pad_maximum_fusion.2 = bf16[1024,3,288]{2,1,0:T(4,128)(2,1)} fusion(bf16[1024,1,288]{2,1,0:T(2,128)(2,1)} %copy.69, bf16[1024,1,288]{2,1,0:T(2,128)(2,1)} %copy.68, bf16[1024,1,288]{2,1,0:T(2,128)(2,1)S(1)} %copy-done.16), kind=kLoop, calls=%fused_computation.32 | loop fusion | flops 5308416 | bytes 3538944 | tf_op jit(solution)/shard_map/while/body/eval_jaxpr/stack | solution.py:76
  336.3 4.8 all-to-all-start.3
  343.7 5.3 copy.72
  349.0 5.0 convolution_convert_fusion.6
  354.0 5.6 convolution_convert_fusion.1
  359.6 52.5 %all-to-all-done.3 = bf16[1024,3,288]{2,1,0:T(4,128)(2,1)} async-done(((bf16[1024,3,288]{2,1,0:T(4,128)(2,1)}), bf16[1024,3,288]{2,1,0:T(4,128)(2,1)}, u32[]{:S(2)}, u32[]{:S(2)}) %all-to-all-start.3) | async-done | bytes 1769504 | tf_op jit(solution)/shard_map/all_to_all | solution.py:163
  412.1 4.4 copy.71
  416.5 7.0 convolution_convert_fusion.2
  423.5 18.2 %pad_maximum_fusion = bf16[1152,11264]{1,0:T(8,128)(2,1)} fusion(bf16[1152,2048]{1,0:T(8,128)(2,1)} %convolution_convert_fusion.6, bf16[1152,4608]{1,0:T(8,128)(2,1)} %convolution_convert_fusion.1, bf16[1152,1152]{1,0:T(8,128)(2,1)} %copy.72, bf16[1152,3456]{1,0:T(8,128)(2,1)} %convolution_convert_fusion.2), kind=kLoop, calls=%fused_computation | loop fusion | flops 103809024 | bytes 51904512 | tf_op jit(solution)/shard_map/concatenate | solution.py:177
  442.7 7.1 constant_dynamic-update-slice_fusion.1
  466.6 135.4 %reduce-scatter.22.cloned.1.call-done = bf16[144,11264]{1,0:T(8,128)(2,1)} async-done(((bf16[1152,11264]{1,0:T(8,128)(2,1)}), bf16[144,11264]{1,0:T(8,128)(2,1)}) %reduce-scatter.22.cloned.1.call-update) | async-done | bytes 3244048 | tf_op jit(solution)/shard_map/reduce_scatter | solution.py:176
  610.5 32.1 %reduce-scatter.34.cloned.1.call-done = bf16[1728,4]{1,0:T(8,128)(2,1)} async-done(((bf16[6912,4]{1,0:T(8,128)(2,1)}), bf16[1728,4]{1,0:T(8,128)(2,1)}) %reduce-scatter.34.cloned.1.call-update) | async-done | bytes 13840
  644.4 20.7 %reduce-scatter.32.cloned.1.call-done = bf16[256,192]{0,1:T(8,128)(2,1)} async-done(((bf16[256,768]{0,1:T(8,128)(2,1)}), bf16[256,192]{0,1:T(8,128)(2,1)}) %reduce-scatter.32.cloned.1.call-update) | async-done | bytes 98320 | tf_op jit(solution)/shard_map/reduce_scatter | solution.py:229
  666.7 32.7 %reduce-scatter.42.cloned.1.call-done = bf16[288,576]{1,0:T(8,128)(2,1)} async-done(((bf16[1152,576]{1,0:T(8,128)(2,1)}), bf16[288,576]{1,0:T(8,128)(2,1)}) %reduce-scatter.42.cloned.1.call-update) | async-done | bytes 331792
  703.5 24.3 %reduce-scatter.30.cloned.1.call-done = bf16[256,512]{0,1:T(8,128)(2,1)} async-done(((bf16[256,2048]{0,1:T(8,128)(2,1)}), bf16[256,512]{0,1:T(8,128)(2,1)}) %reduce-scatter.30.cloned.1.call-update) | async-done | bytes 262160 | tf_op jit(solution)/shard_map/reduce_scatter | solution.py:223
  729.7 21.7 %reduce-scatter.38.cloned.1.call-done = bf16[288,144]{1,0:T(8,128)(2,1)} async-done(((bf16[1152,144]{1,0:T(8,128)(2,1)}), bf16[288,144]{1,0:T(8,128)(2,1)}) %reduce-scatter.38.cloned.1.call-update) | async-done | bytes 82960
  753.1 20.9 %reduce-scatter.26.cloned.1.call-done = bf16[144,512]{1,0:T(8,128)(2,1)} async-done(((bf16[144,2048]{1,0:T(8,128)(2,1)}), bf16[144,512]{1,0:T(8,128)(2,1)}) %reduce-scatter.26.cloned.1.call-update) | async-done | bytes 147472 | tf_op jit(solution)/shard_map/reduce_scatter | solution.py:217
  775.7 37.2 %reduce-scatter.36.cloned.1.call-done = bf16[864,144]{1,0:T(8,128)(2,1)} async-done(((bf16[3456,144]{1,0:T(8,128)(2,1)}), bf16[864,144]{1,0:T(8,128)(2,1)}) %reduce-scatter.36.cloned.1.call-update) | async-done | bytes 248848
  814.9 47.6 %reduce-scatter.40.cloned.1.call-done = bf16[1152,144]{1,0:T(8,128)(2,1)} async-done(((bf16[4608,144]{1,0:T(8,128)(2,1)}), bf16[1152,144]{1,0:T(8,128)(2,1)}) %reduce-scatter.40.cloned.1.call-update) | async-done | bytes 331792
  (214 shorter events, 99.2 us)
Async XLA Ops:
  7.2 165.9 %copy-start = (bf16[2048,768]{1,0:T(8,128)(2,1)S(1)}, bf16[2048,768]{1,0:T(8,128)(2,1)}, u32[]{:S(2)}) copy-start(bf16[2048,768]{1,0:T(8,128)(2,1)} %param.21) | copy-start | bytes 9437188
  8.6 5.4 copy-start.40
  11.9 5.1 copy-start.9
  11.9 6.3 copy-start.46
  36.2 6.6 copy-start.39
  36.2 60.4 %all-to-all-start = ((bf16[256,3,1152]{0,1,2:T(4,128)(2,1)}), bf16[256,3,1152]{0,1,2:T(4,128)(2,1)}, u32[]{:S(2)}, u32[]{:S(2)}) async-start(bf16[256,3,1152]{0,1,2:T(4,128)(2,1)} %copy.57), calls=%async_computation | async-start | bytes 4718592 | tf_op jit(solution)/shard_map/all_to_all | solution.py:117
  42.7 417.9 %reduce-scatter.28.cloned.1.call-start = ((), (), s32[]{:S(2)}) async-start(), calls=%async_computation.18 | async-start | bytes 12976128 | tf_op jit(solution)/shard_map/reduce_scatter | solution.py:193
  105.3 5.0 copy-start.7
  110.2 5.8 copy-start.2
  144.1 17.2 %slice-start.4 = ((s8[10616832]{0:T(1024)(128)(4,1)}), s8[4194304]{0:T(1024)(128)(4,1)S(1)}, s32[]{:S(2)}) async-start(s8[10616832]{0:T(1024)(128)(4,1)} %bitcast.124), calls=%async_computation.30 | async-start | bytes 8388608
  148.7 12.7 %copy-start.5 = (f32[256,1152]{1,0:T(8,128)}, f32[256,1152]{1,0:T(8,128)S(1)}, u32[]{:S(2)}) copy-start(f32[256,1152]{1,0:T(8,128)S(1)} %get-tuple-element.105) | copy-start | bytes 3538948
  149.0 12.4 %slice-start.5 = ((s8[10616832]{0:T(1024)(128)(4,1)}), s8[4194304]{0:T(1024)(128)(4,1)S(1)}, s32[]{:S(2)}) async-start(s8[10616832]{0:T(1024)(128)(4,1)} %bitcast.124), calls=%async_computation.31 | async-start | bytes 8388608
  151.9 9.5 %slice-start.6 = ((s8[10616832]{0:T(1024)(128)(4,1)}), s8[2228224]{0:T(1024)(128)(4,1)S(1)}, s32[]{:S(2)}) async-start(s8[10616832]{0:T(1024)(128)(4,1)} %bitcast.124), calls=%async_computation.32 | async-start | bytes 4456448
  151.9 17.1 %slice-start.2 = ((s8[4718592]{0:T(1024)(128)(4,1)}), s8[4194304]{0:T(1024)(128)(4,1)S(1)}, s32[]{:S(2)}) async-start(s8[4718592]{0:T(1024)(128)(4,1)} %bitcast.111), calls=%async_computation.28 | async-start | bytes 8388608
  151.9 18.6 %slice-start.7 = ((s8[8388608]{0:T(1024)(128)(4,1)}), s8[4194304]{0:T(1024)(128)(4,1)S(1)}, s32[]{:S(2)}) async-start(s8[8388608]{0:T(1024)(128)(4,1)} %bitcast.126), calls=%async_computation.33 | async-start | bytes 8388608
  161.4 7.6 slice-start.3
  161.4 9.2 %slice-start.8 = ((s8[8388608]{0:T(1024)(128)(4,1)}), s8[4194304]{0:T(1024)(128)(4,1)S(1)}, s32[]{:S(2)}) async-start(s8[8388608]{0:T(1024)(128)(4,1)} %bitcast.126), calls=%async_computation.34 | async-start | bytes 8388608
  170.6 6.6 copy-start.47
  195.6 8.5 copy-start.35
  195.6 267.0 %reduce-scatter.24.cloned.1.call-start = ((), (), s32[]{:S(2)}) async-start(), calls=%async_computation.16 | async-start | bytes 11943936 | tf_op jit(solution)/shard_map/reduce_scatter | solution.py:190
  204.0 6.1 copy-start.21
  210.1 29.6 %copy-start.11 = (f32[256,1152]{1,0:T(8,128)}, f32[256,1152]{1,0:T(8,128)S(1)}, u32[]{:S(2)}) copy-start(f32[256,1152]{1,0:T(8,128)S(1)} %get-tuple-element.120) | copy-start | bytes 3538948
  210.1 22.8 %slice-start.9 = ((s8[4718592]{0:T(1024)(128)(4,1)}), s8[4194304]{0:T(1024)(128)(4,1)S(1)}, s32[]{:S(2)}) async-start(s8[4718592]{0:T(1024)(128)(4,1)} %bitcast.128), calls=%async_computation.35 | async-start | bytes 8388608
  210.2 9.5 %copy-start.6 = (f32[256,1152]{1,0:T(8,128)S(1)}, f32[256,1152]{1,0:T(8,128)}, u32[]{:S(2)}) copy-start(f32[256,1152]{1,0:T(8,128)} %copy-done.5) | copy-start | bytes 3538948
  210.2 22.8 %slice-start.10 = ((s8[4718592]{0:T(1024)(128)(4,1)}), s8[524288]{0:T(1024)(128)(4,1)S(1)}, s32[]{:S(2)}) async-start(s8[4718592]{0:T(1024)(128)(4,1)} %bitcast.128), calls=%async_computation.36 | async-start | bytes 1048576
  219.7 9.5 %copy-start.27 = (bf16[256,4608]{1,0:T(8,128)(2,1)}, bf16[256,4608]{1,0:T(8,128)(2,1)S(1)}, u32[]{:S(2)}) copy-start(bf16[256,4608]{1,0:T(8,128)(2,1)S(1)} %fusion.12) | copy-start | bytes 7077892
  244.7 24.5 %copy-start.8 = (pred[1024,1024]{0,1:T(8,128)(4,1)S(1)}, pred[1024,1024]{0,1:T(8,128)(4,1)}, u32[]{:S(2)}) copy-start(pred[1024,1024]{0,1:T(8,128)(4,1)} %broadcast_compare_fusion) | copy-start | bytes 3145732
  246.9 19.3 %all-to-all-start.2 = ((bf16[256,4,288]{0,2,1:T(8,128)(2,1)}), bf16[256,4,288]{0,2,1:T(8,128)(2,1)S(1)}, u32[]{:S(2)}, u32[]{:S(2)}) async-start(bf16[256,4,288]{0,2,1:T(8,128)(2,1)} %bitcast.117), calls=%async_computation.2 | async-start | bytes 1179648 | tf_op jit(solution)/shard_map/all_to_all | solution.py:159
  269.1 12.7 %copy-start.31 = (bf16[1024,4,72]{0,2,1:T(8,128)(2,1)}, bf16[1024,4,72]{0,2,1:T(8,128)(2,1)S(1)}, u32[]{:S(2)}) copy-start(bf16[1024,4,72]{0,2,1:T(8,128)(2,1)S(1)} %squeeze.39) | copy-start | bytes 1769476
  295.0 4.9 copy-start.3
  336.3 75.8 %all-to-all-start.3 = ((bf16[1024,3,288]{2,1,0:T(4,128)(2,1)}), bf16[1024,3,288]{2,1,0:T(4,128)(2,1)}, u32[]{:S(2)}, u32[]{:S(2)}) async-start(bf16[1024,3,288]{2,1,0:T(4,128)(2,1)} %pad_maximum_fusion.2), calls=%async_computation.3 | async-start | bytes 6291456 | tf_op jit(solution)/shard_map/all_to_all | solution.py:163
  341.1 260.9 %reduce-scatter.22.cloned.1.call-start = ((), (), s32[]{:S(2)}) async-start(), calls=%async_computation.15 | async-start | bytes 29196288 | tf_op jit(solution)/shard_map/reduce_scatter | solution.py:176
  343.7 5.3 copy-start.22
  349.0 5.1 copy-start.26
  349.0 5.1 copy-start.28
  416.5 7.0 copy-start.15
  441.7 8.2 copy-start.45
  441.7 8.2 copy-start.43
  441.7 200.9 %reduce-scatter.34.cloned.1.call-start = ((), (), s32[]{:S(2)}) async-start(), calls=%async_computation.21 | async-start | bytes 2211840
  460.5 204.7 %reduce-scatter.32.cloned.1.call-start = ((), (), s32[]{:S(2)}) async-start(), calls=%async_computation.20 | async-start | bytes 491520 | tf_op jit(solution)/shard_map/reduce_scatter | solution.py:229
  460.5 4.9 copy-start.32
  462.5 236.9 %reduce-scatter.42.cloned.1.call-start = ((), (), s32[]{:S(2)}) async-start(), calls=%async_computation.25 | async-start | bytes 1843200
  465.4 262.4 %reduce-scatter.30.cloned.1.call-start = ((), (), s32[]{:S(2)}) async-start(), calls=%async_computation.19 | async-start | bytes 1310720 | tf_op jit(solution)/shard_map/reduce_scatter | solution.py:223
  466.6 284.8 %reduce-scatter.38.cloned.1.call-start = ((), (), s32[]{:S(2)}) async-start(), calls=%async_computation.23 | async-start | bytes 737280
  604.2 169.8 %reduce-scatter.26.cloned.1.call-start = ((), (), s32[]{:S(2)}) async-start(), calls=%async_computation.17 | async-start | bytes 737280 | tf_op jit(solution)/shard_map/reduce_scatter | solution.py:217
  606.2 206.7 %reduce-scatter.36.cloned.1.call-start = ((), (), s32[]{:S(2)}) async-start(), calls=%async_computation.22 | async-start | bytes 2211840
  608.0 254.5 %reduce-scatter.40.cloned.1.call-start = ((), (), s32[]{:S(2)}) async-start(), calls=%async_computation.24 | async-start | bytes 2949120
  699.4 165.3 %copy-start.1 = (bf16[2048,768]{1,0:T(8,128)(2,1)S(1)}, bf16[2048,768]{1,0:T(8,128)(2,1)}, u32[]{:S(2)}) copy-start(bf16[2048,768]{1,0:T(8,128)(2,1)} %param.21) | copy-start | bytes 9437188
  (27 other events, 64.1 us)
Sparse Core Ops, SparseCore 0:
  195.7 85.8 reduce-scatter.27
  285.1 82.1 reduce-scatter.23
  441.8 160.1 reduce-scatter.21
  604.2 38.3 reduce-scatter.33
  645.4 19.7 reduce-scatter.31
  667.3 32.0 reduce-scatter.41
  701.8 26.0 reduce-scatter.29
  730.7 20.6 reduce-scatter.37
  753.7 20.2 reduce-scatter.25
  776.2 36.6 reduce-scatter.35
  815.3 47.1 reduce-scatter.39
where the time goes:
time: 880 us; the launch traced here: 871 us
  waiting for transfers between devices  493 us (56%)
  matrix products  153 us (17%)
  local copies, waits for them, and re-layouts  94.4 us (11%)
  other arithmetic  82.8 us (9%)
  blocking collectives  17.8 us (2%)
  starting transfers between devices  15.9 us (2%)
  between operations  15 us (2%)
    unnamed x16, waiting for transfers between devices  171 us
    reduce_scatter x1, waiting for transfers between devices, shards(): lax.psum_scatter(jnp.concatenate([trans_times(first, dqkv), trans_times(a...  135 us
    all_to_all x1, waiting for transfers between devices, shards(): lax.all_to_all(dqkv_heads, 'seq', split_axis=0, concat_axis=2, tiled=True)  52.5 us
    all_to_all x1, waiting for transfers between devices, shards(): lax.all_to_all(qkv, 'seq', split_axis=2, concat_axis=0, tiled=True)  52 us
    dot_general x7, matrix products, times_trans(): lax.dot_general(left, right, (((1,), (1,)), ((), ())), preferred_element_...  42.6 us
    unnamed x131, local copies, waits for them, and re-layouts  35.5 us
    dot_general x8, matrix products, trans_times(): lax.dot_general(left, right, (((0,), (0,)), ((), ())), precision=precisio...  33.1 us
    dot_general x7, matrix products, matmul(): return jnp.dot(left, right, preferred_element_type=jnp.float32)  30.7 us
  transfers between devices with their start and end apart: 14, of which 12 were waited for; matrix products, arithmetic and copies ran while one was open for 24% of the time, Pallas kernels for 0%

commit v1 on v0

v1 whole, which is shorter than its diff:
```python
import functools

import jax
import jax.numpy as jnp
from jax import lax
from jax.experimental import pallas as pl
from jax.experimental.pallas import tpu as pltpu
from jax.sharding import PartitionSpec as P

H = 16
HD = 72
HP = 80
LEN = 1024
EPS_NORM = 1e-06
SCALE = HD ** (-0.5)
EXP2_SCALE = SCALE * 1.4426950408889634
GELU_A = 0.7978845608028654
GELU_B = 0.044715
BF = jnp.bfloat16
F32 = jnp.float32
ANY = pl.BlockSpec(memory_space=pl.ANY)
VMEM = pl.BlockSpec(memory_space=pltpu.VMEM)
SMEM = pl.BlockSpec(memory_space=pltpu.SMEM)
ROOM = 60 << 20


def matmul(left, right):
    return jnp.dot(left, right, preferred_element_type=F32)


def times_trans(left, right):
    return lax.dot_general(left, right, (((1,), (1,)), ((), ())), preferred_element_type=F32)


def trans_times(left, right):
    return lax.dot_general(left, right, (((0,), (0,)), ((), ())), preferred_element_type=F32)


def row_mean(v):
    return jnp.mean(v, axis=-1, keepdims=True)


def normalize(v):
    centre = v - row_mean(v)
    inv = lax.rsqrt(row_mean(centre * centre) + EPS_NORM)
    return centre * inv, inv


def norm_back(e, normed, inv):
    return (e - row_mean(e) - normed * row_mean(e * normed)) * inv


def col_sum(v):
    return jnp.sum(v, axis=0, keepdims=True)


def sigmoid(v):
    return 1.0 / (1.0 + jnp.exp(-v))


def shape(dims, kind=BF):
    return jax.ShapeDtypeStruct(dims, kind)


def params(**more):
    return pltpu.CompilerParams(vmem_limit_bytes=ROOM, **more)


def enter_kernel(slot_ref, tokens_ref, mod_ref, mods_ref, out_ref):
    width = tokens_ref.shape[1]
    table = mod_ref[...].astype(F32)
    mine = lax.broadcasted_iota(jnp.int32, table.shape, 0) == slot_ref[0]
    mods = col_sum(jnp.where(mine, table, 0.0))
    mods_ref[...] = jnp.zeros_like(mods_ref)
    for i in range(6):
        mods_ref[i : i + 1, :] = mods[:, i * width : (i + 1) * width]
    normed, _ = normalize(tokens_ref[...].astype(F32))
    first = normed * (1.0 + mods[:, width : 2 * width]) + mods[:, 0:width]
    out_ref[...] = jnp.transpose(first.astype(BF))


def enter(slot, tokens, modulation):
    tok, width = tokens.shape
    return pl.pallas_call(
        enter_kernel,
        out_shape=(shape((8, width), F32), shape((width, tok))),
        in_specs=[SMEM, VMEM, VMEM],
        out_specs=(VMEM, VMEM),
        compiler_params=params(),
        name="enter",
    )(slot, tokens, modulation)


def attend_forward_kernel(size, heads, tile, diagonal, one_ref, *refs):
    pieces = refs[: 2 * size - 1]
    w_ref, idk_ref, idq_ref, x_ref, o_ref, qkv_ref, lse_ref, k_ref, o_all_ref = refs[2 * size - 1 :]
    tok = pieces[0].shape[1]
    total = x_ref.shape[1]
    x_ref[:, 0:tok] = pieces[0][...]
    for d in range(1, size):
        x_ref[:, d * tok : (d + 1) * tok] = pieces[2 * d - 1][...] + pieces[2 * d][...]

    def project(i, carry):
        at = pl.ds(pl.multiple_of(i * tile, tile), tile)
        qkv_ref[:, at] = matmul(w_ref[...], x_ref[:, at]).astype(BF)
        return carry

    lax.fori_loop(0, total // tile, project, 0)

    def head_step(head, carry):
        q_at = pl.ds(pl.multiple_of(head * HP, HP), HP)
        k_at = pl.ds(pl.multiple_of((heads + head) * HP, HP), HP)
        v_at = pl.ds(pl.multiple_of((2 * heads + head) * HP, HP), HP)
        o_at = pl.ds(pl.multiple_of(head * HD, 8), HD)
        k_ref[...] = jnp.transpose(qkv_ref[k_at, :])

        def block(at, keys, masked):
            s = matmul(k_ref[keys, :], qkv_ref[q_at, at]) * EXP2_SCALE
            if masked:
                s = jnp.where(idk_ref[...] == idq_ref[:, at], s, -1e30)
            top = jnp.max(s, axis=0, keepdims=True)
            e = jnp.exp2(s - top)
            tot = col_sum(e)
            o = matmul(qkv_ref[v_at, keys], e.astype(BF)) * (1.0 / tot)
            o_all_ref[o_at, at] = o[0:HD, :]
            lse_ref[pl.ds(head, 1), at] = top + jnp.log2(tot)

        def full(masked):
            def step(i, inner):
                block(pl.ds(pl.multiple_of(i * tile, tile), tile), pl.ds(0, total), masked)
                return inner

            lax.fori_loop(0, total // tile, step, 0)

        @pl.when(one_ref[0] == 1)
        def _():
            full(False)

        @pl.when(one_ref[0] == 0)
        def _():
            if diagonal:

                def step(i, inner):
                    at = pl.ds(pl.multiple_of(i * tile, tile), tile)
                    block(at, at, False)
                    return inner

                lax.fori_loop(0, total // tile, step, 0)
            else:
                full(True)

        return carry

    lax.fori_loop(0, heads, head_step, 0)
    for d in range(size):
        o_ref[d] = o_all_ref[:, d * tok : (d + 1) * tok].astype(BF)


def attend_forward(one, pieces, w, idk, idq, heads, tile, diagonal):
    width, tok = pieces[0].shape
    size = (len(pieces) + 1) // 2
    total = size * tok
    return pl.pallas_call(
        functools.partial(attend_forward_kernel, size, heads, tile, diagonal),
        out_shape=(
            shape((width, total)),
            shape((size, heads * HD, tok)),
            shape((3 * heads * HP, total)),
            shape((heads, total), F32),
        ),
        in_specs=[SMEM] + [VMEM] * (len(pieces) + 3),
        out_specs=(VMEM,) * 4,
        scratch_shapes=[pltpu.VMEM((total, HP), BF), pltpu.VMEM((heads * HD, total), F32)],
        compiler_params=params(),
        name="attend_forward",
    )(one, *pieces, w, idk, idq)


def attend_backward_kernel(size, heads, tile, diagonal, one_ref, *refs):
    do_refs = refs[:size]
    qkv_ref, o_ref, lse_ref, w_ref, idk_ref, idq_ref = refs[size : size + 6]
    dqkv_ref, dx_ref, k_ref, v_ref, do_ref, dk_ref, dv_ref, acc_ref, delta_ref = refs[size + 6 :]
    tok = do_refs[0].shape[1]
    total = qkv_ref.shape[1]
    local = heads * HD
    for d in range(size):
        at = slice(d * tok, (d + 1) * tok)
        do = do_refs[d][...].astype(F32)
        do_ref[0:local, at] = do
        do_ref[local : local + HP - HD, at] = jnp.zeros((HP - HD, tok), F32)
        prod = do * o_ref[d].astype(F32)
        for head in range(heads):
            delta_ref[head : head + 1, at] = col_sum(prod[head * HD : (head + 1) * HD, :])

    def head_step(head, carry):
        q_at = pl.ds(pl.multiple_of(head * HP, HP), HP)
        k_at = pl.ds(pl.multiple_of((heads + head) * HP, HP), HP)
        v_at = pl.ds(pl.multiple_of((2 * heads + head) * HP, HP), HP)
        o_at = pl.ds(pl.multiple_of(head * HD, 8), HP)
        k_ref[...] = jnp.transpose(qkv_ref[k_at, :])
        v_ref[...] = jnp.transpose(qkv_ref[v_at, :])

        def out_at(part):
            return pl.ds(pl.multiple_of(part * local + head * HD, 8), HD)

        def block(at, keys, masked, fresh):
            q = qkv_ref[q_at, at]
            do = do_ref[o_at, at].astype(BF)
            p = jnp.exp2(matmul(k_ref[keys, :], q) * EXP2_SCALE - lse_ref[pl.ds(head, 1), at])
            if masked:
                p = jnp.where(idk_ref[...] == idq_ref[:, at], p, 0.0)
            ds = (p * (matmul(v_ref[keys, :], do) - delta_ref[pl.ds(head, 1), at])).astype(BF)
            dv = times_trans(do, p.astype(BF))
            dk = times_trans(q, ds)
            if fresh:
                dv_ref[:, keys] = dv
                dk_ref[:, keys] = dk
            else:
                dv_ref[:, keys] += dv
                dk_ref[:, keys] += dk
            dq = matmul(qkv_ref[k_at, keys], ds) * SCALE
            acc_ref[out_at(0), at] = dq[0:HD, :]

        def full(masked):
            dk_ref[...] = jnp.zeros_like(dk_ref)
            dv_ref[...] = jnp.zeros_like(dv_ref)

            def step(i, inner):
                block(pl.ds(pl.multiple_of(i * tile, tile), tile), pl.ds(0, total), masked, False)
                return inner

            lax.fori_loop(0, total // tile, step, 0)

        @pl.when(one_ref[0] == 1)
        def _():
            full(False)

        @pl.when(one_ref[0] == 0)
        def _():
            if diagonal:

                def step(i, inner):
                    at = pl.ds(pl.multiple_of(i * tile, tile), tile)
                    block(at, at, False, True)
                    return inner

                lax.fori_loop(0, total // tile, step, 0)
            else:
                full(True)

        acc_ref[out_at(1), :] = dk_ref[0:HD, :] * SCALE
        acc_ref[out_at(2), :] = dv_ref[0:HD, :]
        return carry

    lax.fori_loop(0, heads, head_step, 0)
    dqkv_ref[...] = acc_ref[...].astype(BF)
    for d in range(size):
        dx_ref[d] = trans_times(dqkv_ref[:, d * tok : (d + 1) * tok], w_ref[...]).astype(BF)


def attend_backward(one, dos, qkv, o, lse, w, idk, idq, heads, tile, diagonal):
    size = len(dos)
    local, tok = dos[0].shape
    total = size * tok
    width = w.shape[1]
    return pl.pallas_call(
        functools.partial(attend_backward_kernel, size, heads, tile, diagonal),
        out_shape=(shape((3 * local, total)), shape((size, tok, width))),
        in_specs=[SMEM] + [VMEM] * (size + 6),
        out_specs=(VMEM, VMEM),
        scratch_shapes=[
            pltpu.VMEM((total, HP), BF),
            pltpu.VMEM((total, HP), BF),
            pltpu.VMEM((local + HP - HD, total), F32),
            pltpu.VMEM((HP, total), F32),
            pltpu.VMEM((HP, total), F32),
            pltpu.VMEM((3 * local, total), F32),
            pltpu.VMEM((heads, total), F32),
        ],
        compiler_params=params(),
        name="attend_backward",
    )(one, *dos, qkv, o, lse, w, idk, idq)


STEP = 512


def fetch_rows(rank, size, w_ref, held_ref, sems):
    local = w_ref.shape[0] // size
    copies = []
    for d in range(size):
        block = lax.rem(rank - d + size, size)
        copies.append(
            pltpu.make_async_copy(
                w_ref.at[pl.ds(pl.multiple_of(block * local, local), local), :],
                held_ref.at[pl.ds(d * local, local), :],
                sems.at[d],
            )
        )
    return copies


def middle_kernel(size, rank_ref, *refs):
    o_refs = refs[:size]
    (tokens_ref, mods_ref, dino_ref, cot_ref, wo_any, w1_any, w2_any, p1_any, p2_any, p3_any) = refs[size : size + 10]
    (out_ref, b_ref, g_ref, y_ref, a1_ref, a2_ref, gp_ref, dz_ref, dr2_ref, dr1_ref,
     dmlp_ref, dy_ref, normed_ref, inv_ref, attn_ref, gate_ref) = refs[size + 10 : size + 26]
    (wo_ref, w1_ref, w2_ref, p1_ref, p2_ref, p3_ref, act_ref, o_ref, wo_sem, w1_sem, sems) = refs[size + 26 :]
    local, tok = o_refs[0].shape
    hidden = w1_any.shape[1]
    steps = hidden // STEP
    slots = w1_ref.shape[0]
    wo_copies = fetch_rows(rank_ref[0], size, wo_any, wo_ref, wo_sem)
    for copy in wo_copies:
        copy.start()

    def w1_copy(i):
        at = pl.ds(pl.multiple_of(i * STEP, STEP), STEP)
        slot = lax.rem(i, slots)
        return pltpu.make_async_copy(w1_any.at[:, at], w1_ref.at[slot], w1_sem.at[slot])

    for i in range(slots):
        w1_copy(i).start()
    w2_copy = pltpu.make_async_copy(w2_any, w2_ref, sems.at[0])
    p1_copy = pltpu.make_async_copy(p1_any, p1_ref, sems.at[1])
    p2_copy = pltpu.make_async_copy(p2_any, p2_ref, sems.at[2])
    p3_copy = pltpu.make_async_copy(p3_any, p3_ref, sems.at[3])
    for copy in (w2_copy, p1_copy, p2_copy, p3_copy):
        copy.start()

    gate1, shift2, scale2, gate2 = [mods_ref[i : i + 1, :] for i in (2, 3, 4, 5)]
    for d in range(size):
        o_ref[d * local : (d + 1) * local, :] = o_refs[d][...]
    for copy in wo_copies:
        copy.wait()
    attn = trans_times(o_ref[...], wo_ref[...])
    attn_ref[...] = attn
    h1 = tokens_ref[...].astype(F32) + gate1 * attn
    normed, inv = normalize(h1)
    normed_ref[...] = normed
    inv_ref[...] = inv
    b = (normed * (1.0 + scale2) + shift2).astype(BF)
    b_ref[...] = jnp.transpose(b)

    def up(i, carry):
        at = pl.ds(pl.multiple_of(i * STEP, STEP), STEP)
        w1_copy(i).wait()
        u = matmul(b, w1_ref[lax.rem(i, slots)])

        @pl.when(i + slots < steps)
        def _():
            w1_copy(i + slots).start()

        sq = u * u
        t = jnp.tanh(u * (GELU_A + (GELU_A * GELU_B) * sq))
        half = 0.5 * (1.0 + t)
        g = (u * half).astype(BF)
        gp_ref[:, at] = (half + u * (1.0 - t * t) * (0.5 * GELU_A + (1.5 * GELU_A * GELU_B) * sq)).astype(BF)
        act_ref[:, at] = g
        g_ref[at, :] = jnp.transpose(g)
        return carry

    lax.fori_loop(0, steps, up, 0)
    w2_copy.wait()
    mlp = matmul(act_ref[...], w2_ref[...])
    y = (h1 + gate2 * mlp).astype(BF)
    out_ref[...] = y
    y_ref[...] = jnp.transpose(y)
    wide = p1_ref.shape[1]

    def project(source, w_ref, held, out_t_ref, slope_ref):
        def step(i, carry):
            at = pl.ds(pl.multiple_of(i * STEP, STEP), STEP)
            r = matmul(source, w_ref[:, at])
            sig = sigmoid(r)
            act = (r * sig).astype(BF)
            act_ref[:, pl.ds(pl.multiple_of(held + i * STEP, STEP), STEP)] = act
            out_t_ref[at, :] = jnp.transpose(act)
            slope_ref[:, at] = (sig * (1.0 + r * (1.0 - sig))).astype(BF)
            return carry

        lax.fori_loop(0, wide // STEP, step, 0)
        return act_ref[:, held : held + wide]

    def project_back(source, w_ref, slope_ref):
        def step(i, carry):
            at = pl.ds(pl.multiple_of(i * STEP, STEP), STEP)
            slope_ref[:, at] = (times_trans(source, w_ref[at, :]) * slope_ref[:, at].astype(F32)).astype(BF)
            return carry

        lax.fori_loop(0, wide // STEP, step, 0)
        return slope_ref[...]

    p1_copy.wait()
    a1 = project(y, p1_ref, 0, a1_ref, dr1_ref)
    p2_copy.wait()
    a2 = project(a1, p2_ref, wide, a2_ref, dr2_ref)
    p3_copy.wait()
    z = matmul(a2, p3_ref[...])
    t = dino_ref[...].astype(F32)
    nz = lax.rsqrt(jnp.sum(z * z, axis=-1, keepdims=True) + EPS_NORM)
    nt = lax.rsqrt(jnp.sum(t * t, axis=-1, keepdims=True) + EPS_NORM)
    cosine = jnp.sum(z * t, axis=-1, keepdims=True) * nz * nt
    dz = (-0.5 * (t * (nz * nt) - (cosine * nz * nz) * z)).astype(BF)
    dz_ref[...] = dz
    dr2 = project_back(dz, p3_ref, dr2_ref)
    dr1 = project_back(dr2, p2_ref, dr1_ref)
    dy = cot_ref[...].astype(F32) + times_trans(dr1, p1_ref[...])
    dy_ref[...] = dy
    dmlp_ref[...] = (gate2 * dy).astype(BF)
    gate_ref[...] = col_sum(dy * mlp)


def middle(rank, os, tokens, mods, dino, cot, wo, w1, w2, p1, p2, p3):
    size = len(os)
    tok, width = tokens.shape
    hidden, wide, narrow = w1.shape[1], p1.shape[1], p3.shape[1]
    return pl.pallas_call(
        functools.partial(middle_kernel, size),
        out_shape=(
            shape((tok, width)), shape((width, tok)), shape((hidden, tok)), shape((width, tok)),
            shape((wide, tok)), shape((wide, tok)), shape((tok, hidden)), shape((tok, narrow)),
            shape((tok, wide)), shape((tok, wide)), shape((tok, width)), shape((tok, width), F32),
            shape((tok, width), F32), shape((tok, 1), F32), shape((tok, width), F32), shape((1, width), F32),
        ),
        in_specs=[SMEM] + [VMEM] * (size + 4) + [ANY] * 6,
        out_specs=(VMEM,) * 16,
        scratch_shapes=[pltpu.VMEM(dims, BF) for dims in (wo.shape, (4, width, STEP), w2.shape, p1.shape, p2.shape, p3.shape)]
        + [
            pltpu.VMEM((tok, hidden), BF),
            pltpu.VMEM((width, tok), BF),
            pltpu.SemaphoreType.DMA((size,)),
            pltpu.SemaphoreType.DMA((4,)),
            pltpu.SemaphoreType.DMA((4,)),
        ],
        compiler_params=params(),
        name="middle",
    )(rank, *os, tokens, mods, dino, cot, wo, w1, w2, p1, p2, p3)


def descend_kernel(size, rank_ref, *refs):
    (dmlp_ref, gp_ref, dy_ref, normed_ref, inv_ref, attn_ref, mods_ref, w2_any, w1_any, wo_any) = refs[:10]
    (du_ref, dh1_ref, dattn_ref, do_ref, sums_ref) = refs[10:15]
    (w2_ref, w1_ref, wo_ref, w2_sem, w1_sem, wo_sem) = refs[15:]
    hidden = w1_ref.shape[1]
    local = do_ref.shape[1]
    steps = hidden // STEP

    def w2_copy(i):
        at = pl.ds(pl.multiple_of(i * STEP, STEP), STEP)
        return pltpu.make_async_copy(w2_any.at[at, :], w2_ref.at[at, :], w2_sem.at[i])

    for i in range(steps):
        w2_copy(i).start()
    w1_copy = pltpu.make_async_copy(w1_any, w1_ref, w1_sem.at[0])
    w1_copy.start()
    wo_copies = fetch_rows(rank_ref[0], size, wo_any, wo_ref, wo_sem)
    for copy in wo_copies:
        copy.start()
    dmlp = dmlp_ref[...]

    def down(i, carry):
        at = pl.ds(pl.multiple_of(i * STEP, STEP), STEP)
        w2_copy(i).wait()
        du_ref[:, at] = (times_trans(dmlp, w2_ref[at, :]) * gp_ref[:, at].astype(F32)).astype(BF)
        return carry

    lax.fori_loop(0, steps, down, 0)
    w1_copy.wait()
    db = times_trans(du_ref[...], w1_ref[...])
    gate1, scale2 = mods_ref[2:3, :], mods_ref[4:5, :]
    normed = normed_ref[...]
    dh1 = dy_ref[...] + norm_back(db * (1.0 + scale2), normed, inv_ref[...])
    dh1_ref[...] = dh1
    dattn = (gate1 * dh1).astype(BF)
    dattn_ref[...] = dattn
    sums_ref[...] = jnp.zeros_like(sums_ref)
    sums_ref[0:1, :] = col_sum(dh1 * attn_ref[...])
    sums_ref[1:2, :] = col_sum(db)
    sums_ref[2:3, :] = col_sum(db * normed)
    for copy in wo_copies:
        copy.wait()
    for d in range(size):
        do_ref[d] = times_trans(wo_ref[d * local : (d + 1) * local, :], dattn).astype(BF)


def descend(rank, size, dmlp, gp, dy, normed, inv, attn, mods, w2, w1, wo):
    tok, width = dmlp.shape
    hidden = w1.shape[1]
    return pl.pallas_call(
        functools.partial(descend_kernel, size),
        out_shape=(
            shape((tok, hidden)), shape((tok, width), F32), shape((tok, width)),
            shape((size, width // size, tok)), shape((8, width), F32),
        ),
        in_specs=[SMEM] + [VMEM] * 7 + [ANY] * 3,
        out_specs=(VMEM,) * 5,
        scratch_shapes=[pltpu.VMEM(w.shape, BF) for w in (w2, w1, wo)]
        + [
            pltpu.SemaphoreType.DMA((hidden // STEP,)),
            pltpu.SemaphoreType.DMA((1,)),
            pltpu.SemaphoreType.DMA((size,)),
        ],
        compiler_params=params(),
        name="descend",
    )(rank, dmlp, gp, dy, normed, inv, attn, mods, w2, w1, wo)


def leave_kernel(part_ref, left_ref, right_ref, tokens_ref, dh1_ref, mods_ref, out_ref, sums_ref):
    da = part_ref[...].astype(F32) + left_ref[...].astype(F32) + right_ref[...].astype(F32)
    normed, inv = normalize(tokens_ref[...].astype(F32))
    out_ref[...] = (dh1_ref[...] + norm_back(da * (1.0 + mods_ref[1:2, :]), normed, inv)).astype(BF)
    sums_ref[...] = jnp.zeros_like(sums_ref)
    sums_ref[0:1, :] = col_sum(da)
    sums_ref[1:2, :] = col_sum(da * normed)


def leave(part, from_left, from_right, tokens, dh1, mods):
    return pl.pallas_call(
        leave_kernel,
        out_shape=(shape(tokens.shape), shape((8, tokens.shape[1]), F32)),
        in_specs=[VMEM] * 6,
        out_specs=(VMEM, VMEM),
        compiler_params=params(),
        name="leave",
    )(part, from_left, from_right, tokens, dh1, mods)


def weight_grad_kernel(count, flat, rows_ref, *refs):
    lefts, rights = refs[:count], refs[count : 2 * count]
    send_ref, keep_ref, held_ref = refs[2 * count :]
    half, rows, wide = send_ref.shape
    part = lefts[0].shape[1]

    @pl.when(pl.program_id(0) == 0)
    def _():
        for i in range(2 * half):
            at = pl.ds(pl.multiple_of(rows_ref[i], 16), rows)
            for j in range(count):
                held_ref[i * rows : (i + 1) * rows, j * part : (j + 1) * part] = lefts[j][at, :]

    dot = times_trans if flat else matmul
    for out_ref, base in ((send_ref, 0), (keep_ref, half * rows)):
        total = None
        for j in range(count):
            term = dot(held_ref[base : base + half * rows, j * part : (j + 1) * part], rights[j][...])
            total = term if total is None else total + term
        out_ref[...] = total.reshape(half, rows, wide).astype(BF)


def weight_grad(lefts, rights, row_starts, rows, step, flat=False):
    count = len(lefts)
    half = row_starts.shape[0] // 2
    part = lefts[0].shape[1]
    wide = rights[0].shape[0 if flat else 1]
    right_spec = (
        pl.BlockSpec((step, part), lambda i, b: (i, 0)) if flat else pl.BlockSpec((part, step), lambda i, b: (0, i))
    )
    out_spec = pl.BlockSpec((half, rows, step), lambda i, b: (0, 0, i))
    return pl.pallas_call(
        functools.partial(weight_grad_kernel, count, flat),
        out_shape=(shape((half, rows, wide)), shape((half, rows, wide))),
        grid_spec=pltpu.PrefetchScalarGridSpec(
            num_scalar_prefetch=1,
            grid=(wide // step,),
            in_specs=[pl.BlockSpec(a.shape, lambda i, b: (0, 0)) for a in lefts] + [right_spec] * count,
            out_specs=(out_spec, out_spec),
            scratch_shapes=[pltpu.VMEM((2 * half * rows, part * count), BF)],
        ),
        compiler_params=params(dimension_semantics=("arbitrary",)),
        name="weight_grad",
    )(row_starts, *lefts, *rights)


def flip(x, axis, size, bit):
    return lax.ppermute(x, axis, [(i, i ^ bit) for i in range(size)])


def add(a, b):
    return (a.astype(F32) + b.astype(F32)).astype(BF)


def after(x, *others):
    return lax.optimization_barrier((x,) + others)[0]


def masks_of(bits):
    out = []
    for i in range(2 ** len(bits)):
        mask = 0
        for spot, bit in enumerate(bits):
            if not (i >> (len(bits) - 1 - spot)) & 1:
                mask |= bit
        out.append(mask)
    return out


def halve(send, keep, axis, size, bits):
    for bit in bits[:-1]:
        got = flip(send, axis, size, bit)
        half = keep.shape[0] // 2
        send = add(keep[:half], got[:half])
        keep = add(keep[half:], got[half:])
    got = flip(send, axis, size, bits[-1])
    return add(keep, got)


def scatter_columns(share, rank, size):
    rows, cols = share.shape
    blocks = jnp.transpose(share.reshape(rows, size, cols // size), (1, 0, 2))
    bits = [1 << i for i in range(size.bit_length() - 1)]
    order = [lax.dynamic_slice_in_dim(blocks, rank ^ m, 1, 0) for m in masks_of(bits)]
    half = size // 2
    send = jnp.concatenate(order[:half], axis=0)
    keep = jnp.concatenate(order[half:], axis=0)
    return halve(send, keep, "seq", size, bits)[0]


def shards(
    tokens, modulation, image_ids, w_qkv, w_out, w_fc1, w_fc2, w_proj1, w_proj2, w_proj3, dino, cotangent,
):
    n_seq = lax.axis_size("seq")
    n_dp = lax.axis_size("dp")
    rank = lax.axis_index("seq")
    me = lax.axis_index("dp")
    tok_dev, width = tokens.shape
    group_tok = image_ids.shape[0]
    heads = H // n_seq
    local = heads * HD
    slots = modulation.shape[0]
    dp_bits = [1 << i for i in range(n_dp.bit_length() - 1)]
    rank_arg = rank.reshape(1).astype(jnp.int32)

    my_slot = lax.dynamic_slice_in_dim(image_ids, rank * tok_dev, 1)
    mods, first = enter(my_slot, tokens, modulation)

    right, left = [first], [first]
    for s in range(1, n_seq):
        right.append(lax.ppermute(right[-1], "seq", [(i, i + 1) for i in range(s - 1, n_seq - 1)]))
        left.append(lax.ppermute(left[-1], "seq", [(i, i - 1) for i in range(1, n_seq - s + 1)]))
    pieces = [first]
    for d in range(1, n_seq):
        pieces += [left[d], right[n_seq - d]]

    columns = [lax.dynamic_slice_in_dim(w_qkv, i * width + rank * local, local, 1) for i in range(3)]
    w_rows = jnp.transpose(jnp.concatenate(columns, axis=1))
    w_pad = jnp.pad(w_rows.reshape(3 * heads, HD, width), ((0, 0), (0, HP - HD), (0, 0))).reshape(3 * heads * HP, width)
    ids_rel = lax.dynamic_slice_in_dim(jnp.concatenate([image_ids, image_ids]), rank * tok_dev, group_tok)
    idk, idq = ids_rel[:, None], ids_rel[None, :]
    one = (image_ids[0] == image_ids[group_tok - 1]).astype(jnp.int32).reshape(1)
    tile = group_tok // 4
    diagonal = tok_dev % tile == 0

    first_all, heads_out, qkv, lse = attend_forward(one, pieces, w_pad, idk, idq, heads, tile, diagonal)

    attended = [heads_out[0]]
    for d in range(1, n_seq):
        attended.append(lax.ppermute(heads_out[d], "seq", [(i, (i + d) % n_seq) for i in range(n_seq)]))
    (rounded, second, active, rounded_t, proj_a1, proj_a2, gelu_slope, dlatent, dr2, dr1,
     dmlp, dy, normed2, inv2, attn, sum_gate2) = middle(
        rank_arg, attended, tokens, mods, dino, cotangent, w_out, w_fc1, w_fc2, w_proj1, w_proj2, w_proj3
    )

    fast = all(k % (16 * n_dp) == 0 for k in (width, w_fc2.shape[0], w_proj2.shape[0])) and n_dp > 2
    xy, yx = dp_bits[1:], dp_bits[:0:-1]

    def partial(lefts, rights, bits, starts, step):
        rows = lefts.shape[0] // n_dp
        pair = [flip(lefts, "dp", n_dp, 1), flip(rights, "dp", n_dp, 1)]
        return weight_grad([lefts, pair[0]], [rights, pair[1]], starts, rows, step)

    def starts_of(deep, bits):
        return (me ^ jnp.array(masks_of(bits), jnp.int32)) * (deep // n_dp)

    def finish(send, keep, bits):
        share = halve(send, keep, "dp", n_dp, bits)[0]
        return scatter_columns(share, rank, n_seq).astype(F32)

    if fast:
        deep = w_proj2.shape[0]
        p3 = partial(proj_a2, dlatent, xy, starts_of(deep, xy), 384)
        p2 = partial(proj_a1, dr2, yx, starts_of(deep, yx), 512)
        p1 = partial(rounded_t, dr1, xy, starts_of(width, xy), 512)
        dmlp = after(dmlp, p3[0], p2[0], p1[0])

    dupper, dhidden1, dattn, dheads, sums2 = descend(
        rank_arg, n_seq, dmlp, gelu_slope, dy, normed2, inv2, attn, mods, w_fc2, w_fc1, w_out
    )
    dheads_in = [dheads[0]]
    for d in range(1, n_seq):
        dheads_in.append(lax.ppermute(dheads[d], "seq", [(i, (i - d) % n_seq) for i in range(n_seq)]))
    attn_t = jnp.concatenate(attended, axis=0)
    if fast:
        f2 = partial(active, dmlp, yx, starts_of(w_fc2.shape[0], yx), 384)
        f1 = partial(second, dupper, xy, starts_of(width, xy), 1152)
        rows = width // n_dp
        starts = starts_of(width, yx)
        owner = starts // local
        fo = partial(attn_t, dattn, yx, ((rank - owner) % n_seq) * local + starts % local, 384)
        dheads_in[0] = after(dheads_in[0], f2[0])
    dqkv, dfirst_part = attend_backward(one, dheads_in, qkv, heads_out, lse, w_rows, idk, idq, heads, tile, diagonal)

    from_left, from_right = None, None
    for s in range(1, n_seq):
        up = dfirst_part[n_seq - s] if from_left is None else add(dfirst_part[n_seq - s], from_left)
        down = dfirst_part[s] if from_right is None else add(dfirst_part[s], from_right)
        from_left = lax.ppermute(up, "seq", [(i, i + 1) for i in range(s)])
        from_right = lax.ppermute(down, "seq", [(i, i - 1) for i in range(n_seq - s, n_seq)])
    grad_inputs, sums1 = leave(dfirst_part[0], from_left, from_right, tokens, dhidden1, mods)

    dmods = jnp.concatenate(
        [sums1[0:2], sums2[0:3], sum_gate2], axis=0
    ).reshape(n_seq, 1, 6 * width // n_seq)
    grad_mods = jnp.zeros((slots, 6 * width // n_seq), F32)
    slot = jnp.arange(slots, dtype=jnp.int32)[:, None]
    for d in range(n_seq):
        mine = lax.dynamic_index_in_dim(dmods, (rank + d) % n_seq, keepdims=False)
        got = lax.ppermute(mine, "seq", [(i, (i + d) % n_seq) for i in range(n_seq)]) if d else mine
        whose = lax.dynamic_slice_in_dim(image_ids, ((rank - d) % n_seq) * tok_dev, 1)
        grad_mods = grad_mods + jnp.where(slot == whose, got, 0.0)

    if fast:
        rows = width // n_dp
        fq = weight_grad([first_all], [dqkv], starts_of(width, dp_bits), rows, 3 * local, flat=True)
        g_proj3 = finish(*p3, xy)
        g_proj2 = finish(*p2, yx)
        g_proj1 = finish(*p1, xy)
        g_fc2 = finish(*f2, yx)
        g_fc1 = finish(*f1, xy)
        g_out = finish(*fo, yx)
        g_heads = halve(*fq, "dp", n_dp, dp_bits)[0]
    else:

        def reduced(a, b):
            share = lax.psum_scatter(matmul(a, b).astype(BF), "dp", scatter_dimension=0, tiled=True)
            return lax.psum_scatter(share, "seq", scatter_dimension=1, tiled=True).astype(F32)

        g_proj3 = reduced(proj_a2, dlatent)
        g_proj2 = reduced(proj_a1, dr2)
        g_proj1 = reduced(rounded_t, dr1)
        g_fc2 = reduced(active, dmlp)
        g_fc1 = reduced(second, dupper)
        ordered = jnp.concatenate(
            [lax.dynamic_slice_in_dim(attn_t, ((rank - j) % n_seq) * local, local, 0) for j in range(n_seq)], axis=0
        )
        g_out = reduced(ordered, dattn)
        g_heads = lax.psum_scatter(
            times_trans(first_all, dqkv).astype(BF), "dp", scatter_dimension=0, tiled=True
        )

    units = [g_heads[:, i * local : (i + 1) * local] for i in range(3)]
    columns = [jnp.zeros(units[0].shape, F32) for _ in range(3)]
    for d in range(n_seq):
        target, source = (rank + d) % n_seq, (rank - d) % n_seq
        mine = jnp.zeros_like(units[0])
        for i in range(3):
            mine = jnp.where((n_seq * i + rank) // 3 == target, units[i], mine)
        got = lax.ppermute(mine, "seq", [(i, (i + d) % n_seq) for i in range(n_seq)]) if d else mine
        for i in range(3):
            unit = n_seq * i + source
            for at in range(3):
                here = (unit // 3 == rank) & (unit % 3 == at)
                columns[at] = jnp.where(here, got.astype(F32), columns[at])
    g_qkv = jnp.concatenate(columns, axis=1)

    return (rounded, grad_inputs, grad_mods, g_qkv, g_out, g_fc1, g_fc2, g_proj1, g_proj2, g_proj3)


def solution(mesh):
    tok = P(("dp", "seq"), None)
    in_specs = (tok, P("dp", None), P("dp")) + (P(),) * 7 + (tok, tok)
    out_specs = (tok, tok) + (P("dp", "seq"),) * 8
    return jax.shard_map(shards, mesh=mesh, in_specs=in_specs, out_specs=out_specs, check_vma=False)
```

time: 880 us -> 576 us (0.65)
  waiting for transfers between devices: 493 us -> 197 us
  Pallas kernels: 0 us -> 155 us
  matrix products: 153 us -> 0 us
  starting transfers between devices: 15.9 us -> 122 us
  local copies, waits for them, and re-layouts: 94.4 us -> 36.4 us
  other arithmetic: 82.8 us -> 54.4 us
  blocking collectives: 17.8 us -> 0 us
  between operations: 15 us -> 4.07 us
    reduce_scatter x6 -> x0, waiting for transfers between devices: 201 us -> none  [the longest x1 135 us: shards(): lax.psum_scatter(jnp.concatenate([trans_times(first, dqkv), trans_times(a...]
    ppermute x0 -> x63, waiting for transfers between devices: none -> 197 us  [the longest x39 136 us: flip(): return lax.ppermute(x, axis, [(i, i ^ bit) for i in range(size)])]
    unnamed x16 -> x0, waiting for transfers between devices: 171 us -> none
    pallas_call x0 -> x13, Pallas kernels: none -> 155 us  [the longest x7 45 us: weight_grad(): pl.pallas_call(functools.partial(weight_grad_kernel, count, flat), out_sh...]
    dot_general x29 -> x0, matrix products: 153 us -> none  [the longest x7 42.6 us: times_trans(): lax.dot_general(left, right, (((1,), (1,)), ((), ())), preferred_element_...]
    ppermute x0 -> x63, starting transfers between devices: none -> 122 us  [the longest x39 70.9 us: flip(): return lax.ppermute(x, axis, [(i, i ^ bit) for i in range(size)])]
    all_to_all x3 -> x0, waiting for transfers between devices: 120 us -> none  [the longest x1 52.5 us: shards(): lax.all_to_all(dqkv_heads, 'seq', split_axis=0, concat_axis=2, tiled=True)]
    concatenate x3 -> x10, other arithmetic: 34 us -> 3.12 us  [the longest x6 1.98 us: scatter_columns(): send = jnp.concatenate(order[:half], axis=0)]
  transfers between devices with their start and end apart: 14 -> 63, of which waited for: 12 -> 23; matrix products, arithmetic and copies ran while one was open for 24% -> 14% of each run, Pallas kernels for 0% -> 17%
where the time goes in v1:
time: 576 us; the launch traced here: 569 us
  waiting for transfers between devices  197 us (34%)
  Pallas kernels  155 us (27%)
  starting transfers between devices  122 us (21%)
  other arithmetic  54.4 us (9%)
  local copies, waits for them, and re-layouts  36.4 us (6%)
    ppermute x39, waiting for transfers between devices, flip(): return lax.ppermute(x, axis, [(i, i ^ bit) for i in range(size)])  136 us
    ppermute x39, starting transfers between devices, flip(): return lax.ppermute(x, axis, [(i, i ^ bit) for i in range(size)])  70.9 us
    pallas_call x7, Pallas kernels, weight_grad(): pl.pallas_call(functools.partial(weight_grad_kernel, count, flat), out_sh...  45 us
    pallas_call x1, Pallas kernels, middle(): pl.pallas_call(functools.partial(middle_kernel, size), out_shape=(shape((...  41.2 us
    convert_element_type x22, other arithmetic, add(): return (a.astype(F32) + b.astype(F32)).astype(BF)  33.4 us
    pallas_call x1, Pallas kernels, descend(): pl.pallas_call(functools.partial(descend_kernel, size), out_shape=(shape(...  31.9 us
    ppermute x3, waiting for transfers between devices, shards(): lax.ppermute(left[-1], 'seq', [(i, i - 1) for i in range(1, n_seq - s + 1)])  20.7 us
    pallas_call x1, Pallas kernels, attend_forward(): pl.pallas_call(functools.partial(attend_forward_kernel, size, heads, tile...  15.7 us
  transfers between devices with their start and end apart: 63, of which 23 were waited for; matrix products, arithmetic and copies ran while one was open for 14% of the time, Pallas kernels for 17%

profile of v1, /device:TPU:0, one launch (start us, length us, event | category | flops | bytes accessed | tf_op | source)
XLA Modules:
  0.0 568.6 jit_solution(7594669060102922409)
XLA Ops:
  2.3 3.1 enter.1
  5.4 5.0 collective-permute-start.1
  11.7 11.5 %collective-permute-done.1.refs_6_ = bf16[1152,256]{1,0:T(8,128)(2,1)S(1)} collective-permute-done((bf16[1152,256]{1,0:T(8,128)(2,1)}, bf16[1152,256]{1,0:T(8,128)(2,1)S(1)}, u32[]{:S(2)}, u32[]{:S(2)}) %collective-permute-start.1) | collective-permute-done | bytes 589856 | tf_op jit(solution)/shard_map/ppermute | solution.py:639
  24.7 2.5 collective-permute-done.refs_1_
  30.1 14.0 %collective-permute-done.4.refs_3_ = bf16[1152,256]{1,0:T(8,128)(2,1)} collective-permute-done((bf16[1152,256]{1,0:T(8,128)(2,1)S(1)}, bf16[1152,256]{1,0:T(8,128)(2,1)}, u32[]{:S(2)}, u32[]{:S(2)}) %collective-permute-start.4) | collective-permute-done | bytes 589856 | tf_op jit(solution)/shard_map/ppermute | solution.py:640
  45.4 3.5 constant_dynamic-slice_fusion.22
  55.5 4.1 collective-permute-done.5.refs_5_
  59.6 15.7 %attend_forward.1 = (bf16[1152,1024]{1,0:T(8,128)(2,1)}, bf16[4,288,256]{2,1,0:T(8,128)(2,1)}, bf16[960,1024]{1,0:T(8,128)(2,1)}, f32[4,1024]{1,0:T(4,128)}) custom-call(s32[1]{0:T(128)S(6)} %convert_element_type.600.one_ref, bf16[1152,256]{1,0:T(8,128)(2,1)} %get-tuple-element.57.refs_0_, bf16[1152,256]{1,0:T(8,128)(2,1)} %copy-done.33, ...), custom_call_target="tpu_custom_call" | custom-call | tf_op jit(solution)/shard_map/attend_forward/pallas_call | solution.py:163
  77.4 3.8 collective-permute-start.8
  81.2 3.4 collective-permute-done.6.refs_1_
  84.6 5.4 collective-permute-done.7.refs_2_
  90.7 41.2 %middle.1 = (bf16[256,1152]{1,0:T(8,128)(2,1)}, bf16[1152,256]{1,0:T(8,128)(2,1)}, bf16[4608,256]{1,0:T(8,128)(2,1)}, bf16[1152,256]{1,0:T(8,128)(2,1)}, bf16[20...) custom-call(s32[1]{0:T(128)} %bitcast.rank_ref, ...), custom_call_target="tpu_custom_call" | custom-call | tf_op jit(solution)/shard_map/middle/pallas_call | solution.py:418
  138.1 4.7 weight_grad.7
  146.2 5.7 weight_grad.9
  154.0 6.8 %weight_grad.8 = (bf16[2,256,2048]{2,1,0:T(8,128)(2,1)}, bf16[2,256,2048]{2,1,0:T(8,128)(2,1)}) custom-call(s32[4]{0:T(128)} %get-tuple-element.164.rows_ref, bf16[2048,256]{1,0:T(8,128)(2,1)} %get-tuple-element.65.refs_0_, bf16[2048,256]{1,0:T(8,128)(2,1)} %copy-done.13, bf16[256,2048]{1,0:T(8,128)(2,1)} %get-tuple-element.66.refs_2_, ...), custom_call_target="tpu_custom_call" | custom-call | tf_op jit(solution)/shard_map/weight_grad/pallas_call | solution.py:560
  160.8 31.9 %descend.1 = (bf16[256,4608]{1,0:T(8,128)(2,1)}, f32[256,1152]{1,0:T(8,128)}, bf16[256,1152]{1,0:T(8,128)(2,1)}, bf16[4,288,256]{2,1,0:T(8,128)(2,1)}, f32[8,1152]{1,0:T(8,128)}) custom-call(s32[1]{0:T(128)} %bitcast.rank_ref, bf16[256,1152]{1,0:T(8,128)(2,1)} %get-tuple-element.71.refs_0_.refs_2_, bf16[256,4608]{1,0:T(8,128)(2,1)} %get-tuple-element.72.refs_1_, ...), custom_call_target="tpu_custom_call" | custom-call | tf_op jit(solution)/shard_map/descend/pallas_call | solution.py:490
  204.9 4.9 weight_grad.12
  217.8 9.4 %collective-permute-done.37 = bf16[2,144,1152]{2,1,0:T(8,128)(2,1)} collective-permute-done((bf16[2,144,1152]{2,1,0:T(8,128)(2,1)}, bf16[2,144,1152]{2,1,0:T(8,128)(2,1)}, u32[]{:S(2)}, u32[]{:S(2)}) %collective-permute-start.37) | collective-permute-done | bytes 663584 | tf_op jit(solution)/shard_map/ppermute | solution.py:576
  230.2 8.7 %weight_grad.10 = (bf16[2,576,1152]{2,1,0:T(8,128)(2,1)}, bf16[2,576,1152]{2,1,0:T(8,128)(2,1)}) custom-call(s32[4]{0:T(128)} %get-tuple-element.163.rows_ref, bf16[4608,256]{1,0:T(8,128)(2,1)} %get-tuple-element.78.refs_0_, bf16[4608,256]{1,0:T(8,128)(2,1)} %collective-permute-done.15.refs_1_, bf16[256,1152]{1,0:T(8,128)(2,1)} %get-tuple-element.71.refs_0_.refs_2_, ...), custom_call_target="tpu_custom_call" | custom-call | tf_op jit(solution)/shard_map/weight_grad/pallas_call | solution.py:560
  242.3 14.4 %attend_backward.1 = (bf16[864,1024]{1,0:T(8,128)(2,1)}, bf16[4,256,1152]{2,1,0:T(8,128)(2,1)}) custom-call(s32[1]{0:T(128)S(6)} %convert_element_type.600.one_ref, bf16[288,256]{1,0:T(8,128)(2,1)} %get-tuple-element.80.refs_0_, bf16[288,256]{1,0:T(8,128)(2,1)} %collective-permute-done.17.refs_1_, bf16[288,256]{1,0:T(8,128)(2,1)} %collective-permute-done.18.refs_2_, ...), custom_call_target="tpu_custom_call" | custom-call | tf_op jit(solution)/shard_map/attend_backward/pallas_call | solution.py:266
  256.6 2.7 slice_bitcast_fusion.1
  259.3 6.4 %weight_grad.11 = (bf16[4,144,864]{2,1,0:T(8,128)(2,1)}, bf16[4,144,864]{2,1,0:T(8,128)(2,1)}) custom-call(s32[8]{0:T(128)} %xor_multiply_fusion.5.rows_ref, bf16[1152,1024]{1,0:T(8,128)(2,1)} %get-tuple-element.89.refs_0_, bf16[864,1024]{1,0:T(8,128)(2,1)} %get-tuple-element.90.refs_1_), custom_call_target="tpu_custom_call" | custom-call | tf_op jit(solution)/shard_map/weight_grad/pallas_call | solution.py:560
  265.7 6.2 %collective-permute-start.29 = (bf16[4,144,864]{2,1,0:T(8,128)(2,1)}, bf16[4,144,864]{2,1,0:T(8,128)(2,1)}, u32[]{:S(2)}, u32[]{:S(2)}) collective-permute-start(bf16[4,144,864]{2,1,0:T(8,128)(2,1)} %get-tuple-element.92), channel_id=1, source_target_pairs={{0,4},{4,0},{8,12},{12,8},{16,20},{20,16},{24,28},{28,24},{1,5},{5... | collective-permute-start | bytes 2985992 | tf_op jit(solution)/shard_map/ppermute | solution.py:576
  273.4 2.7 collective-permute-start.62
  283.0 5.4 collective-permute-done.39
  288.3 3.0 collective-permute-start.20
  296.9 7.1 %collective-permute-done.20 = bf16[256,1152]{1,0:T(8,128)(2,1)} collective-permute-done((bf16[256,1152]{1,0:T(8,128)(2,1)}, bf16[256,1152]{1,0:T(8,128)(2,1)}, u32[]{:S(2)}, u32[]{:S(2)}) %collective-permute-start.20) | collective-permute-done | bytes 589856 | tf_op jit(solution)/shard_map/ppermute | solution.py:707
  303.9 2.5 collective-permute-start.53
  309.7 4.7 collective-permute-start.21
  318.1 5.9 %collective-permute-done.21 = bf16[256,1152]{1,0:T(8,128)(2,1)S(1)} collective-permute-done((bf16[256,1152]{1,0:T(8,128)(2,1)S(1)}, bf16[256,1152]{1,0:T(8,128)(2,1)S(1)}, u32[]{:S(2)}, u32[]{:S(2)}) %collective-permute-start.21) | collective-permute-done | bytes 589856 | tf_op jit(solution)/shard_map/ppermute | solution.py:707
  327.9 7.0 %collective-permute-done.30 = bf16[2,144,864]{2,1,0:T(8,128)(2,1)S(1)} collective-permute-done((bf16[2,144,864]{2,1,0:T(8,128)(2,1)S(1)}, bf16[2,144,864]{2,1,0:T(8,128)(2,1)S(1)}, u32[]{:S(2)}, u32[]{:S(2)}) %collective-permute-start.30) | collective-permute-done | bytes 497696 | tf_op jit(solution)/shard_map/ppermute | solution.py:576
  334.9 7.6 %collective-permute-start.22 = (bf16[256,1152]{1,0:T(8,128)(2,1)}, bf16[256,1152]{1,0:T(8,128)(2,1)}, u32[]{:S(2)}, u32[]{:S(2)}) collective-permute-start(bf16[256,1152]{1,0:T(8,128)(2,1)} %get-tuple-element.110), channel_id=1, source_target_pairs={{0,1},{1,2},{2,3},{4,5},{5,6},{6,7},{8,9},{9,10},{10,11},{12,13},{... | collective-permute-start | bytes 1769480 | tf_op jit(solution)/shard_map/ppermute | solution.py:707
  345.5 2.6 add_convert_fusion.7
  348.1 2.8 collective-permute-start.54
  351.0 7.8 %weight_grad.13 = (bf16[2,144,4608]{2,1,0:T(8,128)(2,1)}, bf16[2,144,4608]{2,1,0:T(8,128)(2,1)}) custom-call(s32[4]{0:T(128)} %get-tuple-element.165.rows_ref, bf16[1152,256]{1,0:T(8,128)(2,1)} %get-tuple-element.96.refs_0_, bf16[1152,256]{1,0:T(8,128)(2,1)} %copy-done.34, bf16[256,4608]{1,0:T(8,128)(2,1)} %get-tuple-element.97.refs_2_, ...), custom_call_target="tpu_custom_call" | custom-call | tf_op jit(solution)/shard_map/weight_grad/pallas_call | solution.py:560
  358.8 26.3 %collective-permute-done.31 = bf16[1,144,864]{2,1,0:T(8,128)(2,1)S(1)} collective-permute-done((bf16[1,144,864]{2,1,0:T(8,128)(2,1)S(1)}, bf16[1,144,864]{2,1,0:T(8,128)(2,1)S(1)}, u32[]{:S(2)}, u32[]{:S(2)}) %collective-permute-start.31) | collective-permute-done | bytes 248864 | tf_op jit(solution)/shard_map/ppermute | solution.py:576
  388.3 4.0 leave.1
  414.6 48.6 %collective-permute-done.56 = bf16[1,256,2048]{2,1,0:T(8,128)(2,1)} collective-permute-done((bf16[1,256,2048]{2,1,0:T(8,128)(2,1)S(1)}, bf16[1,256,2048]{2,1,0:T(8,128)(2,1)}, u32[]{:S(2)}, u32[]{:S(2)}) %collective-permute-start.56) | collective-permute-done | bytes 1048608 | tf_op jit(solution)/shard_map/ppermute | solution.py:576
  469.5 2.7 add_convert_fusion.4
  473.0 3.0 constant_dynamic-slice_fusion.3
  479.4 14.4 %collective-permute-done.48 = bf16[1,576,1152]{2,1,0:T(8,128)(2,1)S(1)} collective-permute-done((bf16[1,576,1152]{2,1,0:T(8,128)(2,1)S(1)}, bf16[1,576,1152]{2,1,0:T(8,128)(2,1)S(1)}, u32[]{:S(2)}, u32[]{:S(2)}) %collective-permute-start.48) | collective-permute-done | bytes 1327136 | tf_op jit(solution)/shard_map/ppermute | solution.py:576
  500.3 3.3 add_convert_fusion.3
  503.6 2.7 reshape_squeeze.19
  506.3 2.7 constant_dynamic-slice_fusion.11
  512.5 11.3 %collective-permute-start.58 = (bf16[1,256,512]{2,1,0:T(8,128)(2,1)S(1)}, bf16[1,256,512]{2,1,0:T(8,128)(2,1)S(1)}, u32[]{:S(2)}, u32[]{:S(2)}) collective-permute-start(bf16[1,256,512]{2,1,0:T(8,128)(2,1)S(1)} %fusion.6), channel_id=1, source_target_pairs={{0,2},{1,3},{2,0},{3,1},{4,6},{5,7},{6,4},{7,5},{8,10},{9,11},{10,... | collective-permute-start | bytes 786440 | tf_op jit(solution)/shard_map/ppermute | solution.py:576
  524.9 7.8 %collective-permute-start.50 = (bf16[1,576,288]{1,2,0:T(8,128)(2,1)S(1)}, bf16[1,576,288]{1,2,0:T(8,128)(2,1)S(1)}, u32[]{:S(2)}, u32[]{:S(2)}) collective-permute-start(bf16[1,576,288]{1,2,0:T(8,128)(2,1)S(1)} %fusion.2), channel_id=1, source_target_pairs={{0,2},{1,3},{2,0},{3,1},{4,6},{5,7},{6,4},{7,5},{8,10},{9,11},{10,... | collective-permute-start | bytes 995336 | tf_op jit(solution)/shard_map/ppermute | solution.py:576
  534.4 11.6 %collective-permute-start.46 = (bf16[1,144,1152]{2,1,0:T(8,128)(2,1)S(1)}, bf16[1,144,1152]{2,1,0:T(8,128)(2,1)S(1)}, u32[]{:S(2)}, u32[]{:S(2)}) collective-permute-start(bf16[1,144,1152]{2,1,0:T(8,128)(2,1)S(1)} %fusion.4), channel_id=1, source_target_pairs={{0,2},{1,3},{2,0},{3,1},{4,6},{5,7},{6,4},{7,5},{8,10},{9,11},{10,... | collective-permute-start | bytes 995336 | tf_op jit(solution)/shard_map/ppermute | solution.py:576
  549.8 17.5 %collective-permute-done.46 = bf16[1,144,1152]{2,1,0:T(8,128)(2,1)S(1)} collective-permute-done((bf16[1,144,1152]{2,1,0:T(8,128)(2,1)S(1)}, bf16[1,144,1152]{2,1,0:T(8,128)(2,1)S(1)}, u32[]{:S(2)}, u32[]{:S(2)}) %collective-permute-start.46) | collective-permute-done | bytes 331808 | tf_op jit(solution)/shard_map/ppermute | solution.py:576
  (290 shorter events, 134.6 us)
Async XLA Ops:
  5.4 17.8 %collective-permute-start.1 = (bf16[1152,256]{1,0:T(8,128)(2,1)}, bf16[1152,256]{1,0:T(8,128)(2,1)S(1)}, u32[]{:S(2)}, u32[]{:S(2)}) collective-permute-start(bf16[1152,256]{1,0:T(8,128)(2,1)} %get-tuple-element.57.refs_0_), channel_id=1, source_target_pairs={{0,1},{1,2},{2,3},{4,5},{5,6},{6,7},{8,9},{9,10},{10,11},{12,13},{... | collective-permute-start | bytes 1769480 | tf_op jit(solution)/shard_map/ppermute | solution.py:639
  10.4 16.9 %collective-permute-start = (bf16[1152,256]{1,0:T(8,128)(2,1)}, bf16[1152,256]{1,0:T(8,128)(2,1)S(1)}, u32[]{:S(2)}, u32[]{:S(2)}) collective-permute-start(bf16[1152,256]{1,0:T(8,128)(2,1)} %get-tuple-element.57.refs_0_), channel_id=1, source_target_pairs={{1,0},{2,1},{3,2},{5,4},{6,5},{7,6},{9,8},{10,9},{11,10},{13,12},{... | collective-permute-start | bytes 1769480 | tf_op jit(solution)/shard_map/ppermute | solution.py:640
  27.3 16.8 %collective-permute-start.4 = (bf16[1152,256]{1,0:T(8,128)(2,1)S(1)}, bf16[1152,256]{1,0:T(8,128)(2,1)}, u32[]{:S(2)}, u32[]{:S(2)}) collective-permute-start(bf16[1152,256]{1,0:T(8,128)(2,1)S(1)} %collective-permute-done.refs_1_), channel_id=1, source_target_pairs={{1,0},{2,1},{5,4},{6,5},{9,8},{10,9},{13,12},{14,13},{17,16},{18,1... | collective-permute-start | bytes 1769480 | tf_op jit(solution)/shard_map/ppermute | solution.py:640
  28.6 26.9 %collective-permute-start.3 = (bf16[1152,256]{1,0:T(8,128)(2,1)}, bf16[1152,256]{1,0:T(8,128)(2,1)}, u32[]{:S(2)}, u32[]{:S(2)}) collective-permute-start(bf16[1152,256]{1,0:T(8,128)(2,1)} %collective-permute-done.2.refs_4_), channel_id=1, source_target_pairs={{2,3},{6,7},{10,11},{14,15},{18,19},{22,23},{26,27},{30,31}} | collective-permute-start | bytes 1769480 | tf_op jit(solution)/shard_map/ppermute | solution.py:639
  44.1 15.5 %collective-permute-start.5 = (bf16[1152,256]{1,0:T(8,128)(2,1)}, bf16[1152,256]{1,0:T(8,128)(2,1)}, u32[]{:S(2)}, u32[]{:S(2)}) collective-permute-start(bf16[1152,256]{1,0:T(8,128)(2,1)} %collective-permute-done.4.refs_3_), channel_id=1, source_target_pairs={{1,0},{5,4},{9,8},{13,12},{17,16},{21,20},{25,24},{29,28}} | collective-permute-start | bytes 1769480 | tf_op jit(solution)/shard_map/ppermute | solution.py:640
  77.1 12.9 %collective-permute-start.7 = (bf16[288,256]{1,0:T(8,128)(2,1)S(1)}, bf16[288,256]{1,0:T(8,128)(2,1)S(1)}, u32[]{:S(2)}, u32[]{:S(2)}) collective-permute-start(bf16[288,256]{1,0:T(8,128)(2,1)S(1)} %get-tuple-element.139), channel_id=1, source_target_pairs={{0,2},{1,3},{2,0},{3,1},{4,6},{5,7},{6,4},{7,5},{8,10},{9,11},{10,... | collective-permute-start | bytes 442376 | tf_op jit(solution)/shard_map/ppermute | solution.py:658
  77.4 12.6 %collective-permute-start.8 = (bf16[288,256]{1,0:T(8,128)(2,1)S(1)}, bf16[288,256]{1,0:T(8,128)(2,1)S(1)}, u32[]{:S(2)}, u32[]{:S(2)}) collective-permute-start(bf16[288,256]{1,0:T(8,128)(2,1)S(1)} %get-tuple-element.138), channel_id=1, source_target_pairs={{0,3},{1,0},{2,1},{3,2},{4,7},{5,4},{6,5},{7,6},{8,11},{9,8},{10,9... | collective-permute-start | bytes 442376 | tf_op jit(solution)/shard_map/ppermute | solution.py:658
  134.0 11.5 %collective-permute-start.14 = (bf16[256,2048]{1,0:T(8,128)(2,1)}, bf16[256,2048]{1,0:T(8,128)(2,1)}, u32[]{:S(2)}, u32[]{:S(2)}) collective-permute-start(bf16[256,2048]{1,0:T(8,128)(2,1)} %get-tuple-element.69.refs_2_), channel_id=1, source_target_pairs={{0,4},{4,0},{8,12},{12,8},{16,20},{20,16},{24,28},{28,24},{1,5},{5... | collective-permute-start | bytes 3145736 | tf_op jit(solution)/shard_map/ppermute | solution.py:576
  134.4 18.3 %collective-permute-start.11 = (bf16[2048,256]{1,0:T(8,128)(2,1)}, bf16[2048,256]{1,0:T(8,128)(2,1)S(1)}, u32[]{:S(2)}, u32[]{:S(2)}) collective-permute-start(bf16[2048,256]{1,0:T(8,128)(2,1)} %get-tuple-element.65.refs_0_), channel_id=1, source_target_pairs={{0,4},{4,0},{8,12},{12,8},{16,20},{20,16},{24,28},{28,24},{1,5},{5... | collective-permute-start | bytes 3145736 | tf_op jit(solution)/shard_map/ppermute | solution.py:576
  134.5 18.3 %collective-permute-start.12 = (bf16[256,2048]{1,0:T(8,128)(2,1)}, bf16[256,2048]{1,0:T(8,128)(2,1)S(1)}, u32[]{:S(2)}, u32[]{:S(2)}) collective-permute-start(bf16[256,2048]{1,0:T(8,128)(2,1)} %get-tuple-element.66.refs_2_), channel_id=1, source_target_pairs={{0,4},{4,0},{8,12},{12,8},{16,20},{20,16},{24,28},{28,24},{1,5},{5... | collective-permute-start | bytes 3145736 | tf_op jit(solution)/shard_map/ppermute | solution.py:576
  142.9 50.2 %collective-permute-start.59 = (bf16[2,256,768]{2,1,0:T(8,128)(2,1)}, bf16[2,256,768]{2,1,0:T(8,128)(2,1)}, u32[]{:S(2)}, u32[]{:S(2)}) collective-permute-start(bf16[2,256,768]{2,1,0:T(8,128)(2,1)} %get-tuple-element.64), channel_id=1, source_target_pairs={{0,8},{4,12},{8,0},{12,4},{16,24},{20,28},{24,16},{28,20},{1,9},{5... | collective-permute-start | bytes 2359304 | tf_op jit(solution)/shard_map/ppermute | solution.py:576
  145.4 84.8 %collective-permute-start.15 = (bf16[4608,256]{1,0:T(8,128)(2,1)}, bf16[4608,256]{1,0:T(8,128)(2,1)}, u32[]{:S(2)}, u32[]{:S(2)}) collective-permute-start(bf16[4608,256]{1,0:T(8,128)(2,1)} %get-tuple-element.78.refs_0_), channel_id=1, source_target_pairs={{0,4},{4,0},{8,12},{12,8},{16,20},{20,16},{24,28},{28,24},{1,5},{5... | collective-permute-start | bytes 7077896 | tf_op jit(solution)/shard_map/ppermute | solution.py:576
  151.9 61.9 %collective-permute-start.51 = (bf16[2,144,2048]{2,1,0:T(8,128)(2,1)}, bf16[2,144,2048]{2,1,0:T(8,128)(2,1)}, u32[]{:S(2)}, u32[]{:S(2)}) collective-permute-start(bf16[2,144,2048]{2,1,0:T(8,128)(2,1)} %get-tuple-element.70), channel_id=1, source_target_pairs={{0,8},{4,12},{8,0},{12,4},{16,24},{20,28},{24,16},{28,20},{1,9},{5... | collective-permute-start | bytes 3538952 | tf_op jit(solution)/shard_map/ppermute | solution.py:576
  152.7 49.6 %collective-permute-start.35 = (bf16[1152,256]{1,0:T(8,128)(2,1)S(1)}, bf16[1152,256]{1,0:T(8,128)(2,1)}, u32[]{:S(2)}, u32[]{:S(2)}) collective-permute-start(bf16[1152,256]{1,0:T(8,128)(2,1)S(1)} %pad_maximum_fusion.3.refs_0_), channel_id=1, source_target_pairs={{0,4},{4,0},{8,12},{12,8},{16,20},{20,16},{24,28},{28,24},{1,5},{5... | collective-permute-start | bytes 1769480 | tf_op jit(solution)/shard_map/ppermute | solution.py:576
  192.8 9.6 %collective-permute-start.36 = (bf16[256,1152]{1,0:T(8,128)(2,1)}, bf16[256,1152]{1,0:T(8,128)(2,1)S(1)}, u32[]{:S(2)}, u32[]{:S(2)}) collective-permute-start(bf16[256,1152]{1,0:T(8,128)(2,1)} %get-tuple-element.93.refs_2_), channel_id=1, source_target_pairs={{0,4},{4,0},{8,12},{12,8},{16,20},{20,16},{24,28},{28,24},{1,5},{5... | collective-permute-start | bytes 1769480 | tf_op jit(solution)/shard_map/ppermute | solution.py:576
  195.0 14.9 %collective-permute-start.60 = (bf16[1,256,768]{2,1,0:T(8,128)(2,1)}, bf16[1,256,768]{2,1,0:T(8,128)(2,1)S(1)}, u32[]{:S(2)}, u32[]{:S(2)}) collective-permute-start(bf16[1,256,768]{2,1,0:T(8,128)(2,1)} %add_convert_fusion.17), channel_id=1, source_target_pairs={{0,16},{4,20},{8,24},{12,28},{16,0},{20,4},{24,8},{28,12},{1,17},{... | collective-permute-start | bytes 1179656 | tf_op jit(solution)/shard_map/ppermute | solution.py:576
  202.3 26.6 %collective-permute-start.16 = (bf16[256,1152]{1,0:T(8,128)(2,1)S(1)}, bf16[256,1152]{1,0:T(8,128)(2,1)}, u32[]{:S(2)}, u32[]{:S(2)}) collective-permute-start(bf16[256,1152]{1,0:T(8,128)(2,1)S(1)} %copy-done.6), channel_id=1, source_target_pairs={{0,4},{4,0},{8,12},{12,8},{16,20},{20,16},{24,28},{28,24},{1,5},{5... | collective-permute-start | bytes 1769480 | tf_op jit(solution)/shard_map/ppermute | solution.py:576
  202.4 36.6 %collective-permute-start.17 = (bf16[288,256]{1,0:T(8,128)(2,1)}, bf16[288,256]{1,0:T(8,128)(2,1)}, u32[]{:S(2)}, u32[]{:S(2)}) collective-permute-start(bf16[288,256]{1,0:T(8,128)(2,1)} %get-tuple-element.136), channel_id=1, source_target_pairs={{0,3},{1,0},{2,1},{3,2},{4,7},{5,4},{6,5},{7,6},{8,11},{9,8},{10,9... | collective-permute-start | bytes 442376 | tf_op jit(solution)/shard_map/ppermute | solution.py:691
  209.8 17.4 %collective-permute-start.37 = (bf16[2,144,1152]{2,1,0:T(8,128)(2,1)}, bf16[2,144,1152]{2,1,0:T(8,128)(2,1)}, u32[]{:S(2)}, u32[]{:S(2)}) collective-permute-start(bf16[2,144,1152]{2,1,0:T(8,128)(2,1)} %get-tuple-element.95), channel_id=1, source_target_pairs={{0,16},{4,20},{8,24},{12,28},{16,0},{20,4},{24,8},{28,12},{1,17},{... | collective-permute-start | bytes 1990664 | tf_op jit(solution)/shard_map/ppermute | solution.py:576
  213.8 26.2 %collective-permute-start.18 = (bf16[288,256]{1,0:T(8,128)(2,1)}, bf16[288,256]{1,0:T(8,128)(2,1)}, u32[]{:S(2)}, u32[]{:S(2)}) collective-permute-start(bf16[288,256]{1,0:T(8,128)(2,1)} %get-tuple-element.135), channel_id=1, source_target_pairs={{0,2},{1,3},{2,0},{3,1},{4,6},{5,7},{6,4},{7,5},{8,10},{9,11},{10,... | collective-permute-start | bytes 442376 | tf_op jit(solution)/shard_map/ppermute | solution.py:691
  227.2 13.6 %collective-permute-start.19 = (bf16[288,256]{1,0:T(8,128)(2,1)}, bf16[288,256]{1,0:T(8,128)(2,1)S(1)}, u32[]{:S(2)}, u32[]{:S(2)}) collective-permute-start(bf16[288,256]{1,0:T(8,128)(2,1)} %get-tuple-element.134), channel_id=1, source_target_pairs={{0,1},{1,2},{2,3},{3,0},{4,5},{5,6},{6,7},{7,4},{8,9},{9,10},{10,1... | collective-permute-start | bytes 442376 | tf_op jit(solution)/shard_map/ppermute | solution.py:691
  228.9 114.9 %collective-permute-start.55 = (bf16[2,256,2048]{2,1,0:T(8,128)(2,1)}, bf16[2,256,2048]{2,1,0:T(8,128)(2,1)}, u32[]{:S(2)}, u32[]{:S(2)}) collective-permute-start(bf16[2,256,2048]{2,1,0:T(8,128)(2,1)} %get-tuple-element.67), channel_id=1, source_target_pairs={{0,16},{4,20},{8,24},{12,28},{16,0},{20,4},{24,8},{28,12},{1,17},{... | collective-permute-start | bytes 6291464 | tf_op jit(solution)/shard_map/ppermute | solution.py:576
  230.2 117.9 %collective-permute-start.42 = (bf16[256,4608]{1,0:T(8,128)(2,1)S(1)}, bf16[256,4608]{1,0:T(8,128)(2,1)}, u32[]{:S(2)}, u32[]{:S(2)}) collective-permute-start(bf16[256,4608]{1,0:T(8,128)(2,1)S(1)} %copy-done.4), channel_id=1, source_target_pairs={{0,4},{4,0},{8,12},{12,8},{16,20},{20,16},{24,28},{28,24},{1,5},{5... | collective-permute-start | bytes 7077896 | tf_op jit(solution)/shard_map/ppermute | solution.py:576
  238.9 26.8 %collective-permute-start.61 = (bf16[2,256,192]{1,2,0:T(8,128)(2,1)S(1)}, bf16[2,256,192]{1,2,0:T(8,128)(2,1)S(1)}, u32[]{:S(2)}, u32[]{:S(2)}) collective-permute-start(bf16[2,256,192]{1,2,0:T(8,128)(2,1)S(1)} %pad_maximum_fusion.8), channel_id=1, source_target_pairs={{0,1},{1,0},{2,3},{3,2},{4,5},{5,4},{6,7},{7,6},{8,9},{9,8},{10,11... | collective-permute-start | bytes 589832 | tf_op jit(solution)/shard_map/ppermute | solution.py:576
  239.9 52.1 %collective-permute-start.52 = (bf16[1,144,2048]{2,1,0:T(8,128)(2,1)}, bf16[1,144,2048]{2,1,0:T(8,128)(2,1)}, u32[]{:S(2)}, u32[]{:S(2)}) collective-permute-start(bf16[1,144,2048]{2,1,0:T(8,128)(2,1)} %add_convert_fusion.10), channel_id=1, source_target_pairs={{0,16},{4,20},{8,24},{12,28},{16,0},{20,4},{24,8},{28,12},{1,17},{... | collective-permute-start | bytes 1769480 | tf_op jit(solution)/shard_map/ppermute | solution.py:576
  240.8 31.9 %collective-permute-start.38 = (bf16[1,144,1152]{2,1,0:T(8,128)(2,1)S(1)}, bf16[1,144,1152]{2,1,0:T(8,128)(2,1)S(1)}, u32[]{:S(2)}, u32[]{:S(2)}) collective-permute-start(bf16[1,144,1152]{2,1,0:T(8,128)(2,1)S(1)} %add_convert_fusion.22), channel_id=1, source_target_pairs={{0,8},{4,12},{8,0},{12,4},{16,24},{20,28},{24,16},{28,20},{1,9},{5... | collective-permute-start | bytes 995336 | tf_op jit(solution)/shard_map/ppermute | solution.py:576
  265.7 50.8 %collective-permute-start.29 = (bf16[4,144,864]{2,1,0:T(8,128)(2,1)}, bf16[4,144,864]{2,1,0:T(8,128)(2,1)}, u32[]{:S(2)}, u32[]{:S(2)}) collective-permute-start(bf16[4,144,864]{2,1,0:T(8,128)(2,1)} %get-tuple-element.92), channel_id=1, source_target_pairs={{0,4},{4,0},{8,12},{12,8},{16,20},{20,16},{24,28},{28,24},{1,5},{5... | collective-permute-start | bytes 2985992 | tf_op jit(solution)/shard_map/ppermute | solution.py:576
  288.3 15.6 %collective-permute-start.20 = (bf16[256,1152]{1,0:T(8,128)(2,1)}, bf16[256,1152]{1,0:T(8,128)(2,1)}, u32[]{:S(2)}, u32[]{:S(2)}) collective-permute-start(bf16[256,1152]{1,0:T(8,128)(2,1)} %get-tuple-element.114), channel_id=1, source_target_pairs={{0,1},{4,5},{8,9},{12,13},{16,17},{20,21},{24,25},{28,29}} | collective-permute-start | bytes 1769480 | tf_op jit(solution)/shard_map/ppermute | solution.py:707
  292.0 11.9 %collective-permute-start.23 = (bf16[256,1152]{1,0:T(8,128)(2,1)}, bf16[256,1152]{1,0:T(8,128)(2,1)}, u32[]{:S(2)}, u32[]{:S(2)}) collective-permute-start(bf16[256,1152]{1,0:T(8,128)(2,1)} %get-tuple-element.113), channel_id=1, source_target_pairs={{3,2},{7,6},{11,10},{15,14},{19,18},{23,22},{27,26},{31,30}} | collective-permute-start | bytes 1769480 | tf_op jit(solution)/shard_map/ppermute | solution.py:708
  303.9 10.5 %collective-permute-start.53 = (bf16[2,144,512]{2,1,0:T(8,128)(2,1)S(1)}, bf16[2,144,512]{2,1,0:T(8,128)(2,1)S(1)}, u32[]{:S(2)}, u32[]{:S(2)}) collective-permute-start(bf16[2,144,512]{2,1,0:T(8,128)(2,1)S(1)} %pad_maximum_fusion.6), channel_id=1, source_target_pairs={{0,1},{1,0},{2,3},{3,2},{4,5},{5,4},{6,7},{7,6},{8,9},{9,8},{10,11... | collective-permute-start | bytes 884744 | tf_op jit(solution)/shard_map/ppermute | solution.py:576
  309.7 14.3 %collective-permute-start.21 = (bf16[256,1152]{1,0:T(8,128)(2,1)S(1)}, bf16[256,1152]{1,0:T(8,128)(2,1)S(1)}, u32[]{:S(2)}, u32[]{:S(2)}) collective-permute-start(bf16[256,1152]{1,0:T(8,128)(2,1)S(1)} %get-tuple-element.112), channel_id=1, source_target_pairs={{0,1},{1,2},{4,5},{5,6},{8,9},{9,10},{12,13},{13,14},{16,17},{17,1... | collective-permute-start | bytes 1769480 | tf_op jit(solution)/shard_map/ppermute | solution.py:707
  314.4 11.4 %collective-permute-start.24 = (bf16[256,1152]{1,0:T(8,128)(2,1)S(1)}, bf16[256,1152]{1,0:T(8,128)(2,1)S(1)}, u32[]{:S(2)}, u32[]{:S(2)}) collective-permute-start(bf16[256,1152]{1,0:T(8,128)(2,1)S(1)} %get-tuple-element.111), channel_id=1, source_target_pairs={{2,1},{3,2},{6,5},{7,6},{10,9},{11,10},{14,13},{15,14},{18,17},{19... | collective-permute-start | bytes 1769480 | tf_op jit(solution)/shard_map/ppermute | solution.py:708
  316.6 26.0 %collective-permute-start.41 = (bf16[1152,256]{1,0:T(8,128)(2,1)S(1)}, bf16[1152,256]{1,0:T(8,128)(2,1)S(1)}, u32[]{:S(2)}, u32[]{:S(2)}) collective-permute-start(bf16[1152,256]{1,0:T(8,128)(2,1)S(1)} %copy-done.31), channel_id=1, source_target_pairs={{0,4},{4,0},{8,12},{12,8},{16,20},{20,16},{24,28},{28,24},{1,5},{5... | collective-permute-start | bytes 1769480 | tf_op jit(solution)/shard_map/ppermute | solution.py:576
  324.0 142.4 %collective-permute-start.47 = (bf16[2,576,1152]{2,1,0:T(8,128)(2,1)}, bf16[2,576,1152]{2,1,0:T(8,128)(2,1)}, u32[]{:S(2)}, u32[]{:S(2)}) collective-permute-start(bf16[2,576,1152]{2,1,0:T(8,128)(2,1)} %get-tuple-element.79), channel_id=1, source_target_pairs={{0,16},{4,20},{8,24},{12,28},{16,0},{20,4},{24,8},{28,12},{1,17},{... | collective-permute-start | bytes 7962632 | tf_op jit(solution)/shard_map/ppermute | solution.py:576
  334.9 53.3 %collective-permute-start.22 = (bf16[256,1152]{1,0:T(8,128)(2,1)}, bf16[256,1152]{1,0:T(8,128)(2,1)}, u32[]{:S(2)}, u32[]{:S(2)}) collective-permute-start(bf16[256,1152]{1,0:T(8,128)(2,1)} %get-tuple-element.110), channel_id=1, source_target_pairs={{0,1},{1,2},{2,3},{4,5},{5,6},{6,7},{8,9},{9,10},{10,11},{12,13},{... | collective-permute-start | bytes 1769480 | tf_op jit(solution)/shard_map/ppermute | solution.py:707
  342.6 45.7 %collective-permute-start.25 = (bf16[256,1152]{1,0:T(8,128)(2,1)}, bf16[256,1152]{1,0:T(8,128)(2,1)}, u32[]{:S(2)}, u32[]{:S(2)}) collective-permute-start(bf16[256,1152]{1,0:T(8,128)(2,1)} %get-tuple-element.109), channel_id=1, source_target_pairs={{1,0},{2,1},{3,2},{5,4},{6,5},{7,6},{9,8},{10,9},{11,10},{13,12},{... | collective-permute-start | bytes 1769480 | tf_op jit(solution)/shard_map/ppermute | solution.py:708
  343.9 41.2 %collective-permute-start.31 = (bf16[1,144,864]{2,1,0:T(8,128)(2,1)S(1)}, bf16[1,144,864]{2,1,0:T(8,128)(2,1)S(1)}, u32[]{:S(2)}, u32[]{:S(2)}) collective-permute-start(bf16[1,144,864]{2,1,0:T(8,128)(2,1)S(1)} %add_convert_fusion.26), channel_id=1, source_target_pairs={{0,16},{4,20},{8,24},{12,28},{16,0},{20,4},{24,8},{28,12},{1,17},{... | collective-permute-start | bytes 746504 | tf_op jit(solution)/shard_map/ppermute | solution.py:576
  348.1 49.8 %collective-permute-start.54 = (bf16[1,144,512]{2,1,0:T(8,128)(2,1)}, bf16[1,144,512]{2,1,0:T(8,128)(2,1)S(1)}, u32[]{:S(2)}, u32[]{:S(2)}) collective-permute-start(bf16[1,144,512]{2,1,0:T(8,128)(2,1)} %fusion.12), channel_id=1, source_target_pairs={{0,2},{1,3},{2,0},{3,1},{4,6},{5,7},{6,4},{7,5},{8,10},{9,11},{10,... | collective-permute-start | bytes 442376 | tf_op jit(solution)/shard_map/ppermute | solution.py:576
  385.8 83.7 %collective-permute-start.43 = (bf16[2,144,4608]{2,1,0:T(8,128)(2,1)}, bf16[2,144,4608]{2,1,0:T(8,128)(2,1)}, u32[]{:S(2)}, u32[]{:S(2)}) collective-permute-start(bf16[2,144,4608]{2,1,0:T(8,128)(2,1)} %get-tuple-element.99), channel_id=1, source_target_pairs={{0,8},{4,12},{8,0},{12,4},{16,24},{20,28},{24,16},{28,20},{1,9},{5... | collective-permute-start | bytes 7962632 | tf_op jit(solution)/shard_map/ppermute | solution.py:576
  398.0 65.2 %collective-permute-start.56 = (bf16[1,256,2048]{2,1,0:T(8,128)(2,1)S(1)}, bf16[1,256,2048]{2,1,0:T(8,128)(2,1)}, u32[]{:S(2)}, u32[]{:S(2)}) collective-permute-start(bf16[1,256,2048]{2,1,0:T(8,128)(2,1)S(1)} %copy-done.12), channel_id=1, source_target_pairs={{0,8},{4,12},{8,0},{12,4},{16,24},{20,28},{24,16},{28,20},{1,9},{5... | collective-permute-start | bytes 3145736 | tf_op jit(solution)/shard_map/ppermute | solution.py:576
  468.6 25.3 %collective-permute-start.48 = (bf16[1,576,1152]{2,1,0:T(8,128)(2,1)S(1)}, bf16[1,576,1152]{2,1,0:T(8,128)(2,1)S(1)}, u32[]{:S(2)}, u32[]{:S(2)}) collective-permute-start(bf16[1,576,1152]{2,1,0:T(8,128)(2,1)S(1)} %add_convert_fusion.1), channel_id=1, source_target_pairs={{0,8},{4,12},{8,0},{12,4},{16,24},{20,28},{24,16},{28,20},{1,9},{5... | collective-permute-start | bytes 3981320 | tf_op jit(solution)/shard_map/ppermute | solution.py:576
  472.2 28.1 %collective-permute-start.44 = (bf16[1,144,4608]{2,1,0:T(8,128)(2,1)}, bf16[1,144,4608]{2,1,0:T(8,128)(2,1)}, u32[]{:S(2)}, u32[]{:S(2)}) collective-permute-start(bf16[1,144,4608]{2,1,0:T(8,128)(2,1)} %add_convert_fusion.4), channel_id=1, source_target_pairs={{0,16},{4,20},{8,24},{12,28},{16,0},{20,4},{24,8},{28,12},{1,17},{... | collective-permute-start | bytes 3981320 | tf_op jit(solution)/shard_map/ppermute | solution.py:576
  476.9 34.5 %collective-permute-start.57 = (bf16[2,256,512]{2,1,0:T(8,128)(2,1)}, bf16[2,256,512]{2,1,0:T(8,128)(2,1)}, u32[]{:S(2)}, u32[]{:S(2)}) collective-permute-start(bf16[2,256,512]{2,1,0:T(8,128)(2,1)} %pad_maximum_fusion.4), channel_id=1, source_target_pairs={{0,1},{1,0},{2,3},{3,2},{4,5},{5,4},{6,7},{7,6},{8,9},{9,8},{10,11... | collective-permute-start | bytes 1572872 | tf_op jit(solution)/shard_map/ppermute | solution.py:576
  497.9 26.0 %collective-permute-start.49 = (bf16[2,576,288]{1,2,0:T(8,128)(2,1)}, bf16[2,576,288]{1,2,0:T(8,128)(2,1)}, u32[]{:S(2)}, u32[]{:S(2)}) collective-permute-start(bf16[2,576,288]{1,2,0:T(8,128)(2,1)} %pad_maximum_fusion.1), channel_id=1, source_target_pairs={{0,1},{1,0},{2,3},{3,2},{4,5},{5,4},{6,7},{7,6},{8,9},{9,8},{10,11... | collective-permute-start | bytes 1990664 | tf_op jit(solution)/shard_map/ppermute | solution.py:576
  509.3 25.1 %collective-permute-start.45 = (bf16[2,144,1152]{2,1,0:T(8,128)(2,1)S(1)}, bf16[2,144,1152]{2,1,0:T(8,128)(2,1)S(1)}, u32[]{:S(2)}, u32[]{:S(2)}) collective-permute-start(bf16[2,144,1152]{2,1,0:T(8,128)(2,1)S(1)} %pad_maximum_fusion.2), channel_id=1, source_target_pairs={{0,1},{1,0},{2,3},{3,2},{4,5},{5,4},{6,7},{7,6},{8,9},{9,8},{10,11... | collective-permute-start | bytes 1990664 | tf_op jit(solution)/shard_map/ppermute | solution.py:576
  512.5 33.5 %collective-permute-start.58 = (bf16[1,256,512]{2,1,0:T(8,128)(2,1)S(1)}, bf16[1,256,512]{2,1,0:T(8,128)(2,1)S(1)}, u32[]{:S(2)}, u32[]{:S(2)}) collective-permute-start(bf16[1,256,512]{2,1,0:T(8,128)(2,1)S(1)} %fusion.6), channel_id=1, source_target_pairs={{0,2},{1,3},{2,0},{3,1},{4,6},{5,7},{6,4},{7,5},{8,10},{9,11},{10,... | collective-permute-start | bytes 786440 | tf_op jit(solution)/shard_map/ppermute | solution.py:576
  524.9 23.0 %collective-permute-start.50 = (bf16[1,576,288]{1,2,0:T(8,128)(2,1)S(1)}, bf16[1,576,288]{1,2,0:T(8,128)(2,1)S(1)}, u32[]{:S(2)}, u32[]{:S(2)}) collective-permute-start(bf16[1,576,288]{1,2,0:T(8,128)(2,1)S(1)} %fusion.2), channel_id=1, source_target_pairs={{0,2},{1,3},{2,0},{3,1},{4,6},{5,7},{6,4},{7,5},{8,10},{9,11},{10,... | collective-permute-start | bytes 995336 | tf_op jit(solution)/shard_map/ppermute | solution.py:576
  534.4 32.9 %collective-permute-start.46 = (bf16[1,144,1152]{2,1,0:T(8,128)(2,1)S(1)}, bf16[1,144,1152]{2,1,0:T(8,128)(2,1)S(1)}, u32[]{:S(2)}, u32[]{:S(2)}) collective-permute-start(bf16[1,144,1152]{2,1,0:T(8,128)(2,1)S(1)} %fusion.4), channel_id=1, source_target_pairs={{0,2},{1,3},{2,0},{3,1},{4,6},{5,7},{6,4},{7,5},{8,10},{9,11},{10,... | collective-permute-start | bytes 995336 | tf_op jit(solution)/shard_map/ppermute | solution.py:576
  (73 other events, 718.5 us)

commit v2 on v1

--- a/solution.py
+++ b/solution.py
@@ -62,6 +62,10 @@
     return jax.ShapeDtypeStruct(dims, kind)
 
 
+def price(us):
+    return pl.CostEstimate(flops=0, transcendentals=0, bytes_accessed=int(us * 3.0e6))
+
+
 def params(**more):
     return pltpu.CompilerParams(vmem_limit_bytes=ROOM, **more)
 
@@ -87,11 +91,12 @@
         in_specs=[SMEM, VMEM, VMEM],
         out_specs=(VMEM, VMEM),
         compiler_params=params(),
+        cost_estimate=price(3),
         name="enter",
     )(slot, tokens, modulation)
 
 
-def attend_forward_kernel(size, heads, tile, diagonal, one_ref, *refs):
+def attend_forward_kernel(size, heads, tile, diagonal, one_ref, rank_ref, *refs):
     pieces = refs[: 2 * size - 1]
     w_ref, idk_ref, idq_ref, x_ref, o_ref, qkv_ref, lse_ref, k_ref, o_all_ref = refs[2 * size - 1 :]
     tok = pieces[0].shape[1]
@@ -153,10 +158,10 @@
 
     lax.fori_loop(0, heads, head_step, 0)
     for d in range(size):
-        o_ref[d] = o_all_ref[:, d * tok : (d + 1) * tok].astype(BF)
-
-
-def attend_forward(one, pieces, w, idk, idq, heads, tile, diagonal):
+        o_ref[lax.rem(rank_ref[0] + d, size)] = o_all_ref[:, d * tok : (d + 1) * tok].astype(BF)
+
+
+def attend_forward(one, rank, pieces, w, idk, idq, heads, tile, diagonal):
     width, tok = pieces[0].shape
     size = (len(pieces) + 1) // 2
     total = size * tok
@@ -168,27 +173,28 @@
             shape((3 * heads * HP, total)),
             shape((heads, total), F32),
         ),
-        in_specs=[SMEM] + [VMEM] * (len(pieces) + 3),
+        in_specs=[SMEM, SMEM] + [VMEM] * (len(pieces) + 3),
         out_specs=(VMEM,) * 4,
         scratch_shapes=[pltpu.VMEM((total, HP), BF), pltpu.VMEM((heads * HD, total), F32)],
         compiler_params=params(),
+        cost_estimate=price(23),
         name="attend_forward",
-    )(one, *pieces, w, idk, idq)
-
-
-def attend_backward_kernel(size, heads, tile, diagonal, one_ref, *refs):
-    do_refs = refs[:size]
-    qkv_ref, o_ref, lse_ref, w_ref, idk_ref, idq_ref = refs[size : size + 6]
-    dqkv_ref, dx_ref, k_ref, v_ref, do_ref, dk_ref, dv_ref, acc_ref, delta_ref = refs[size + 6 :]
-    tok = do_refs[0].shape[1]
+    )(one, rank, *pieces, w, idk, idq)
+
+
+def attend_backward_kernel(size, heads, tile, diagonal, one_ref, rank_ref, *refs):
+    dos_ref, qkv_ref, o_ref, lse_ref, w_ref, idk_ref, idq_ref = refs[:7]
+    dqkv_ref, dx_ref, k_ref, v_ref, do_ref, dk_ref, dv_ref, acc_ref, delta_ref = refs[7:]
+    tok = dos_ref.shape[2]
     total = qkv_ref.shape[1]
     local = heads * HD
     for d in range(size):
         at = slice(d * tok, (d + 1) * tok)
-        do = do_refs[d][...].astype(F32)
+        owner = lax.rem(rank_ref[0] + d, size)
+        do = dos_ref[owner].astype(F32)
         do_ref[0:local, at] = do
         do_ref[local : local + HP - HD, at] = jnp.zeros((HP - HD, tok), F32)
-        prod = do * o_ref[d].astype(F32)
+        prod = do * o_ref[owner].astype(F32)
         for head in range(heads):
             delta_ref[head : head + 1, at] = col_sum(prod[head * HD : (head + 1) * HD, :])
 
@@ -255,18 +261,17 @@
     lax.fori_loop(0, heads, head_step, 0)
     dqkv_ref[...] = acc_ref[...].astype(BF)
     for d in range(size):
-        dx_ref[d] = trans_times(dqkv_ref[:, d * tok : (d + 1) * tok], w_ref[...]).astype(BF)
-
-
-def attend_backward(one, dos, qkv, o, lse, w, idk, idq, heads, tile, diagonal):
-    size = len(dos)
-    local, tok = dos[0].shape
+        dx_ref[lax.rem(rank_ref[0] + d, size)] = trans_times(dqkv_ref[:, d * tok : (d + 1) * tok], w_ref[...]).astype(BF)
+
+
+def attend_backward(one, rank, dos, qkv, o, lse, w, idk, idq, heads, tile, diagonal):
+    size, local, tok = dos.shape
     total = size * tok
     width = w.shape[1]
     return pl.pallas_call(
         functools.partial(attend_backward_kernel, size, heads, tile, diagonal),
         out_shape=(shape((3 * local, total)), shape((size, tok, width))),
-        in_specs=[SMEM] + [VMEM] * (size + 6),
+        in_specs=[SMEM, SMEM] + [VMEM] * 7,
         out_specs=(VMEM, VMEM),
         scratch_shapes=[
             pltpu.VMEM((total, HP), BF),
@@ -278,41 +283,33 @@
             pltpu.VMEM((heads, total), F32),
         ],
         compiler_params=params(),
+        cost_estimate=price(23),
         name="attend_backward",
-    )(one, *dos, qkv, o, lse, w, idk, idq)
+    )(one, rank, dos, qkv, o, lse, w, idk, idq)
 
 
 STEP = 512
 
 
-def fetch_rows(rank, size, w_ref, held_ref, sems):
-    local = w_ref.shape[0] // size
-    copies = []
-    for d in range(size):
-        block = lax.rem(rank - d + size, size)
-        copies.append(
-            pltpu.make_async_copy(
-                w_ref.at[pl.ds(pl.multiple_of(block * local, local), local), :],
-                held_ref.at[pl.ds(d * local, local), :],
-                sems.at[d],
-            )
-        )
-    return copies
-
-
-def middle_kernel(size, rank_ref, *refs):
-    o_refs = refs[:size]
-    (tokens_ref, mods_ref, dino_ref, cot_ref, wo_any, w1_any, w2_any, p1_any, p2_any, p3_any) = refs[size : size + 10]
-    (out_ref, b_ref, g_ref, y_ref, a1_ref, a2_ref, gp_ref, dz_ref, dr2_ref, dr1_ref,
-     dmlp_ref, dy_ref, normed_ref, inv_ref, attn_ref, gate_ref) = refs[size + 10 : size + 26]
-    (wo_ref, w1_ref, w2_ref, p1_ref, p2_ref, p3_ref, act_ref, o_ref, wo_sem, w1_sem, sems) = refs[size + 26 :]
-    local, tok = o_refs[0].shape
+def middle_kernel(*refs):
+    (o_refs, tokens_ref, mods_ref, dino_ref, cot_ref, wo_any, w1_any, w2_any, p1_any, p2_any, p3_any) = refs[:11]
+    (out_ref, left1_ref, left2_ref, right1_ref, gp_ref, dmlp_ref, dy_ref, normed_ref, inv_ref, attn_ref,
+     gate_ref) = refs[11:22]
+    (wo_ref, w1_ref, w2_ref, p1_ref, p2_ref, p3_ref, act_ref, w1_sem, sems) = refs[22:]
+    size, local, tok = o_refs.shape
+    width = size * local
     hidden = w1_any.shape[1]
+    wide, narrow = p3_ref.shape
     steps = hidden // STEP
     slots = w1_ref.shape[0]
-    wo_copies = fetch_rows(rank_ref[0], size, wo_any, wo_ref, wo_sem)
-    for copy in wo_copies:
-        copy.start()
+    a2_ref, a1_ref = left1_ref.at[0:wide, :], left1_ref.at[wide : 2 * wide, :]
+    y_ref = left1_ref.at[2 * wide :, :]
+    g_ref, b_ref = left2_ref.at[0:hidden, :], left2_ref.at[hidden : hidden + width, :]
+    o_ref = left2_ref.at[hidden + width :, :]
+    dr2_ref, dr1_ref = right1_ref.at[:, 0:wide], right1_ref.at[:, wide : 2 * wide]
+    dz_ref = right1_ref.at[:, 2 * wide :]
+    wo_copy = pltpu.make_async_copy(wo_any, wo_ref, sems.at[4])
+    wo_copy.start()
 
     def w1_copy(i):
         at = pl.ds(pl.multiple_of(i * STEP, STEP), STEP)
@@ -330,9 +327,8 @@
 
     gate1, shift2, scale2, gate2 = [mods_ref[i : i + 1, :] for i in (2, 3, 4, 5)]
     for d in range(size):
-        o_ref[d * local : (d + 1) * local, :] = o_refs[d][...]
-    for copy in wo_copies:
-        copy.wait()
+        o_ref[d * local : (d + 1) * local, :] = o_refs[d]
+    wo_copy.wait()
     attn = trans_times(o_ref[...], wo_ref[...])
     attn_ref[...] = attn
     h1 = tokens_ref[...].astype(F32) + gate1 * attn
@@ -366,8 +362,6 @@
     y = (h1 + gate2 * mlp).astype(BF)
     out_ref[...] = y
     y_ref[...] = jnp.transpose(y)
-    wide = p1_ref.shape[1]
-
     def project(source, w_ref, held, out_t_ref, slope_ref):
         def step(i, carry):
             at = pl.ds(pl.multiple_of(i * STEP, STEP), STEP)
@@ -411,38 +405,35 @@
     gate_ref[...] = col_sum(dy * mlp)
 
 
-def middle(rank, os, tokens, mods, dino, cot, wo, w1, w2, p1, p2, p3):
-    size = len(os)
+def middle(os, tokens, mods, dino, cot, wo, w1, w2, p1, p2, p3):
     tok, width = tokens.shape
     hidden, wide, narrow = w1.shape[1], p1.shape[1], p3.shape[1]
     return pl.pallas_call(
-        functools.partial(middle_kernel, size),
+        middle_kernel,
         out_shape=(
-            shape((tok, width)), shape((width, tok)), shape((hidden, tok)), shape((width, tok)),
-            shape((wide, tok)), shape((wide, tok)), shape((tok, hidden)), shape((tok, narrow)),
-            shape((tok, wide)), shape((tok, wide)), shape((tok, width)), shape((tok, width), F32),
+            shape((tok, width)), shape((2 * wide + width, tok)), shape((hidden + 2 * width, tok)),
+            shape((tok, 2 * wide + narrow)), shape((tok, hidden)), shape((tok, width)), shape((tok, width), F32),
             shape((tok, width), F32), shape((tok, 1), F32), shape((tok, width), F32), shape((1, width), F32),
         ),
-        in_specs=[SMEM] + [VMEM] * (size + 4) + [ANY] * 6,
-        out_specs=(VMEM,) * 16,
-        scratch_shapes=[pltpu.VMEM(dims, BF) for dims in (wo.shape, (4, width, STEP), w2.shape, p1.shape, p2.shape, p3.shape)]
-        + [
-            pltpu.VMEM((tok, hidden), BF),
-            pltpu.VMEM((width, tok), BF),
-            pltpu.SemaphoreType.DMA((size,)),
-            pltpu.SemaphoreType.DMA((4,)),
-            pltpu.SemaphoreType.DMA((4,)),
-        ],
+        in_specs=[VMEM] * 5 + [ANY] * 6,
+        out_specs=(VMEM,) * 11,
+        scratch_shapes=[
+            pltpu.VMEM(dims, BF)
+            for dims in (wo.shape, (4, width, STEP), w2.shape, p1.shape, p2.shape, p3.shape, (tok, hidden))
+        ]
+        + [pltpu.SemaphoreType.DMA((4,)), pltpu.SemaphoreType.DMA((5,))],
         compiler_params=params(),
+        cost_estimate=price(41),
         name="middle",
-    )(rank, *os, tokens, mods, dino, cot, wo, w1, w2, p1, p2, p3)
-
-
-def descend_kernel(size, rank_ref, *refs):
+    )(os, tokens, mods, dino, cot, wo, w1, w2, p1, p2, p3)
+
+
+def descend_kernel(size, *refs):
     (dmlp_ref, gp_ref, dy_ref, normed_ref, inv_ref, attn_ref, mods_ref, w2_any, w1_any, wo_any) = refs[:10]
-    (du_ref, dh1_ref, dattn_ref, do_ref, sums_ref) = refs[10:15]
-    (w2_ref, w1_ref, wo_ref, w2_sem, w1_sem, wo_sem) = refs[15:]
+    (right2_ref, dh1_ref, do_ref, sums_ref) = refs[10:14]
+    (w2_ref, w1_ref, wo_ref, w2_sem, w1_sem, wo_sem) = refs[14:]
     hidden = w1_ref.shape[1]
+    du_ref, dattn_ref = right2_ref.at[:, 0:hidden], right2_ref.at[:, hidden:]
     local = do_ref.shape[1]
     steps = hidden // STEP
 
@@ -454,9 +445,8 @@
         w2_copy(i).start()
     w1_copy = pltpu.make_async_copy(w1_any, w1_ref, w1_sem.at[0])
     w1_copy.start()
-    wo_copies = fetch_rows(rank_ref[0], size, wo_any, wo_ref, wo_sem)
-    for copy in wo_copies:
-        copy.start()
+    wo_copy = pltpu.make_async_copy(wo_any, wo_ref, wo_sem.at[0])
+    wo_copy.start()
     dmlp = dmlp_ref[...]
 
     def down(i, carry):
@@ -478,36 +468,38 @@
     sums_ref[0:1, :] = col_sum(dh1 * attn_ref[...])
     sums_ref[1:2, :] = col_sum(db)
     sums_ref[2:3, :] = col_sum(db * normed)
-    for copy in wo_copies:
-        copy.wait()
+    wo_copy.wait()
     for d in range(size):
         do_ref[d] = times_trans(wo_ref[d * local : (d + 1) * local, :], dattn).astype(BF)
 
 
-def descend(rank, size, dmlp, gp, dy, normed, inv, attn, mods, w2, w1, wo):
+def descend(size, dmlp, gp, dy, normed, inv, attn, mods, w2, w1, wo):
     tok, width = dmlp.shape
     hidden = w1.shape[1]
     return pl.pallas_call(
         functools.partial(descend_kernel, size),
         out_shape=(
-            shape((tok, hidden)), shape((tok, width), F32), shape((tok, width)),
+            shape((tok, hidden + width)), shape((tok, width), F32),
             shape((size, width // size, tok)), shape((8, width), F32),
         ),
-        in_specs=[SMEM] + [VMEM] * 7 + [ANY] * 3,
-        out_specs=(VMEM,) * 5,
+        in_specs=[VMEM] * 7 + [ANY] * 3,
+        out_specs=(VMEM,) * 4,
         scratch_shapes=[pltpu.VMEM(w.shape, BF) for w in (w2, w1, wo)]
         + [
             pltpu.SemaphoreType.DMA((hidden // STEP,)),
             pltpu.SemaphoreType.DMA((1,)),
-            pltpu.SemaphoreType.DMA((size,)),
+            pltpu.SemaphoreType.DMA((1,)),
         ],
         compiler_params=params(),
+        cost_estimate=price(20),
         name="descend",
-    )(rank, dmlp, gp, dy, normed, inv, attn, mods, w2, w1, wo)
-
-
-def leave_kernel(part_ref, left_ref, right_ref, tokens_ref, dh1_ref, mods_ref, out_ref, sums_ref):
-    da = part_ref[...].astype(F32) + left_ref[...].astype(F32) + right_ref[...].astype(F32)
+    )(dmlp, gp, dy, normed, inv, attn, mods, w2, w1, wo)
+
+
+def leave_kernel(parts_ref, tokens_ref, dh1_ref, mods_ref, out_ref, sums_ref):
+    da = parts_ref[0].astype(F32)
+    for i in range(1, parts_ref.shape[0]):
+        da = da + parts_ref[i].astype(F32)
     normed, inv = normalize(tokens_ref[...].astype(F32))
     out_ref[...] = (dh1_ref[...] + norm_back(da * (1.0 + mods_ref[1:2, :]), normed, inv)).astype(BF)
     sums_ref[...] = jnp.zeros_like(sums_ref)
@@ -515,61 +507,89 @@
     sums_ref[1:2, :] = col_sum(da * normed)
 
 
-def leave(part, from_left, from_right, tokens, dh1, mods):
+def leave(parts, tokens, dh1, mods):
     return pl.pallas_call(
         leave_kernel,
         out_shape=(shape(tokens.shape), shape((8, tokens.shape[1]), F32)),
-        in_specs=[VMEM] * 6,
+        in_specs=[VMEM] * 4,
         out_specs=(VMEM, VMEM),
         compiler_params=params(),
+        cost_estimate=price(4.5),
         name="leave",
-    )(part, from_left, from_right, tokens, dh1, mods)
-
-
-def weight_grad_kernel(count, flat, rows_ref, *refs):
-    lefts, rights = refs[:count], refs[count : 2 * count]
-    send_ref, keep_ref, held_ref = refs[2 * count :]
-    half, rows, wide = send_ref.shape
+    )(parts, tokens, dh1, mods)
+
+
+def weight_grad_kernel(count, flat, rows, rows_ref, *refs):
+    lefts = refs[:count]
+    rights = refs[count : count * (1 + len(rows))]
+    send_ref, keep_ref, held_ref, sem = refs[count * (1 + len(rows)) :]
+    half, height, wide = send_ref.shape
     part = lefts[0].shape[1]
+    copies, held_at, held = [], [], 0
+    for job, deep in enumerate(rows):
+        held_at.append(held)
+        for i in range(2 * half):
+            at = pl.ds(pl.multiple_of(rows_ref[job * 2 * half + i], 16), deep)
+            for j in range(count):
+                copies.append(
+                    pltpu.make_async_copy(
+                        lefts[j].at[at, :],
+                        held_ref.at[held : held + deep, j * part : (j + 1) * part],
+                        sem.at[len(copies)],
+                    )
+                )
+            held += deep
 
     @pl.when(pl.program_id(0) == 0)
     def _():
-        for i in range(2 * half):
-            at = pl.ds(pl.multiple_of(rows_ref[i], 16), rows)
+        for copy in copies:
+            copy.start()
+        for copy in copies:
+            copy.wait()
+
+    dot = times_trans if flat else matmul
+    for job, deep in enumerate(rows):
+        top = sum(rows[:job])
+        for out_ref, base in ((send_ref, held_at[job]), (keep_ref, held_at[job] + half * deep)):
+            total = None
             for j in range(count):
-                held_ref[i * rows : (i + 1) * rows, j * part : (j + 1) * part] = lefts[j][at, :]
-
-    dot = times_trans if flat else matmul
-    for out_ref, base in ((send_ref, 0), (keep_ref, half * rows)):
-        total = None
-        for j in range(count):
-            term = dot(held_ref[base : base + half * rows, j * part : (j + 1) * part], rights[j][...])
-            total = term if total is None else total + term
-        out_ref[...] = total.reshape(half, rows, wide).astype(BF)
-
-
-def weight_grad(lefts, rights, row_starts, rows, step, flat=False):
+                term = dot(
+                    held_ref[base : base + half * deep, j * part : (j + 1) * part], rights[job * count + j][...]
+                )
+                total = term if total is None else total + term
+            out_ref[:, top : top + deep, :] = total.reshape(half, deep, wide).astype(BF)
+
+
+def weight_grad(lefts, rights, jobs, wide, step, flat=False):
     count = len(lefts)
-    half = row_starts.shape[0] // 2
+    half = jobs[0][0].shape[0] // 2
     part = lefts[0].shape[1]
-    wide = rights[0].shape[0 if flat else 1]
-    right_spec = (
-        pl.BlockSpec((step, part), lambda i, b: (i, 0)) if flat else pl.BlockSpec((part, step), lambda i, b: (0, i))
-    )
-    out_spec = pl.BlockSpec((half, rows, step), lambda i, b: (0, 0, i))
+    rows = tuple(job[1] for job in jobs)
+    height = sum(rows)
+
+    def right_spec(base):
+        if flat:
+            return pl.BlockSpec((step, part), lambda i, b: (i + base, 0))
+        return pl.BlockSpec((part, step), lambda i, b: (0, i + base))
+
+    out_spec = pl.BlockSpec((half, height, step), lambda i, b: (0, 0, i))
     return pl.pallas_call(
-        functools.partial(weight_grad_kernel, count, flat),
-        out_shape=(shape((half, rows, wide)), shape((half, rows, wide))),
+        functools.partial(weight_grad_kernel, count, flat, rows),
+        out_shape=(shape((half, height, wide)), shape((half, height, wide))),
         grid_spec=pltpu.PrefetchScalarGridSpec(
             num_scalar_prefetch=1,
             grid=(wide // step,),
-            in_specs=[pl.BlockSpec(a.shape, lambda i, b: (0, 0)) for a in lefts] + [right_spec] * count,
+            in_specs=[ANY] * count + [right_spec(job[2]) for job in jobs for _ in range(count)],
             out_specs=(out_spec, out_spec),
-            scratch_shapes=[pltpu.VMEM((2 * half * rows, part * count), BF)],
+            scratch_shapes=[
+                pltpu.VMEM((2 * half * height, part * count), BF),
+                pltpu.SemaphoreType.DMA((2 * half * count * len(rows),)),
+            ],
         ),
         compiler_params=params(dimension_semantics=("arbitrary",)),
+        cost_estimate=price(3.0 + 1.2e-6 * count * half * height * wide),
         name="weight_grad",
-    )(row_starts, *lefts, *rights)
+    )(jnp.concatenate([job[0] for job in jobs]), *lefts, *(list(rights) * len(jobs)))
 
 
 def flip(x, axis, size, bit):
@@ -595,25 +615,24 @@
     return out
 
 
-def halve(send, keep, axis, size, bits):
+def halve(send, keep, size, bits, swap):
     for bit in bits[:-1]:
-        got = flip(send, axis, size, bit)
+        got = swap(send, bit)
         half = keep.shape[0] // 2
         send = add(keep[:half], got[:half])
         keep = add(keep[half:], got[half:])
-    got = flip(send, axis, size, bits[-1])
-    return add(keep, got)
-
-
-def scatter_columns(share, rank, size):
+    got = swap(send, bits[-1])
+    return add(keep, got)[0]
+
+
+def exchange(blocks):
+    return lax.all_to_all(blocks, "seq", split_axis=0, concat_axis=0, tiled=True)
+
+
+def scatter_columns(share, size):
     rows, cols = share.shape
     blocks = jnp.transpose(share.reshape(rows, size, cols // size), (1, 0, 2))
-    bits = [1 << i for i in range(size.bit_length() - 1)]
-    order = [lax.dynamic_slice_in_dim(blocks, rank ^ m, 1, 0) for m in masks_of(bits)]
-    half = size // 2
-    send = jnp.concatenate(order[:half], axis=0)
-    keep = jnp.concatenate(order[half:], axis=0)
-    return halve(send, keep, "seq", size, bits)[0]
+    return jnp.sum(exchange(blocks).astype(F32), axis=0)
 
 
 def shards(
@@ -625,6 +644,7 @@
     me = lax.axis_index("dp")
     tok_dev, width = tokens.shape
     group_tok = image_ids.shape[0]
+    hidden, wide, narrow = w_fc1.shape[1], w_proj2.shape[0], w_proj3.shape[1]
     heads = H // n_seq
     local = heads * HD
     slots = modulation.shape[0]
@@ -651,117 +671,97 @@
     tile = group_tok // 4
     diagonal = tok_dev % tile == 0
 
-    first_all, heads_out, qkv, lse = attend_forward(one, pieces, w_pad, idk, idq, heads, tile, diagonal)
-
-    attended = [heads_out[0]]
-    for d in range(1, n_seq):
-        attended.append(lax.ppermute(heads_out[d], "seq", [(i, (i + d) % n_seq) for i in range(n_seq)]))
-    (rounded, second, active, rounded_t, proj_a1, proj_a2, gelu_slope, dlatent, dr2, dr1,
-     dmlp, dy, normed2, inv2, attn, sum_gate2) = middle(
-        rank_arg, attended, tokens, mods, dino, cotangent, w_out, w_fc1, w_fc2, w_proj1, w_proj2, w_proj3
+    first_all, heads_out, qkv, lse = attend_forward(
+        one, rank_arg, pieces, w_pad, idk, idq, heads, tile, diagonal
     )
-
-    fast = all(k % (16 * n_dp) == 0 for k in (width, w_fc2.shape[0], w_proj2.shape[0])) and n_dp > 2
+    attended = exchange(heads_out)
+    (rounded, left1, left2, right1, gelu_slope, dmlp, dy, normed2, inv2, attn, sum_gate2) = middle(
+        attended, tokens, mods, dino, cotangent, w_out, w_fc1, w_fc2, w_proj1, w_proj2, w_proj3
+    )
+
+    fast = all(k % (16 * n_dp) == 0 for k in (width, hidden, wide)) and n_dp > 2
     xy, yx = dp_bits[1:], dp_bits[:0:-1]
-
-    def partial(lefts, rights, bits, starts, step):
-        rows = lefts.shape[0] // n_dp
-        pair = [flip(lefts, "dp", n_dp, 1), flip(rights, "dp", n_dp, 1)]
-        return weight_grad([lefts, pair[0]], [rights, pair[1]], starts, rows, step)
-
-    def starts_of(deep, bits):
-        return (me ^ jnp.array(masks_of(bits), jnp.int32)) * (deep // n_dp)
-
-    def finish(send, keep, bits):
-        share = halve(send, keep, "dp", n_dp, bits)[0]
-        return scatter_columns(share, rank, n_seq).astype(F32)
+    swap = lambda x, bit: flip(x, "dp", n_dp, bit)
+
+    def starts(base, deep, bits):
+        return base + (me ^ jnp.array(masks_of(bits), jnp.int32)) * (deep // n_dp)
+
+    def job(base, deep, bits, column):
+        return (starts(base, deep, bits), deep // n_dp, column)
 
     if fast:
-        deep = w_proj2.shape[0]
-        p3 = partial(proj_a2, dlatent, xy, starts_of(deep, xy), 384)
-        p2 = partial(proj_a1, dr2, yx, starts_of(deep, yx), 512)
-        p1 = partial(rounded_t, dr1, xy, starts_of(width, xy), 512)
-        dmlp = after(dmlp, p3[0], p2[0], p1[0])
-
-    dupper, dhidden1, dattn, dheads, sums2 = descend(
-        rank_arg, n_seq, dmlp, gelu_slope, dy, normed2, inv2, attn, mods, w_fc2, w_fc1, w_out
+        lefts1, rights1 = [left1, swap(left1, 1)], [right1, swap(right1, 1)]
+        p21 = weight_grad(
+            lefts1, rights1, [job(wide, wide, xy, 0), job(2 * wide, width, xy, wide // STEP)], wide, STEP
+        )
+        rights1[0] = after(rights1[0], p21[0])
+        p3 = weight_grad(lefts1, rights1, [job(0, wide, yx, 2 * wide // 256)], narrow, 256)
+        lefts2 = [left2, swap(left2, 1)]
+        f2 = weight_grad(lefts2, [after(dmlp, p3[0]), swap(dmlp, 1)], [job(0, hidden, yx, 0)], width, 384)
+        dmlp = after(dmlp, f2[0])
+
+    right2, dhidden1, dheads, sums2 = descend(
+        n_seq, dmlp, gelu_slope, dy, normed2, inv2, attn, mods, w_fc2, w_fc1, w_out
     )
-    dheads_in = [dheads[0]]
-    for d in range(1, n_seq):
-        dheads_in.append(lax.ppermute(dheads[d], "seq", [(i, (i - d) % n_seq) for i in range(n_seq)]))
-    attn_t = jnp.concatenate(attended, axis=0)
+    dheads_in = exchange(dheads)
     if fast:
-        f2 = partial(active, dmlp, yx, starts_of(w_fc2.shape[0], yx), 384)
-        f1 = partial(second, dupper, xy, starts_of(width, xy), 1152)
-        rows = width // n_dp
-        starts = starts_of(width, yx)
-        owner = starts // local
-        fo = partial(attn_t, dattn, yx, ((rank - owner) % n_seq) * local + starts % local, 384)
-        dheads_in[0] = after(dheads_in[0], f2[0])
-    dqkv, dfirst_part = attend_backward(one, dheads_in, qkv, heads_out, lse, w_rows, idk, idq, heads, tile, diagonal)
-
-    from_left, from_right = None, None
-    for s in range(1, n_seq):
-        up = dfirst_part[n_seq - s] if from_left is None else add(dfirst_part[n_seq - s], from_left)
-        down = dfirst_part[s] if from_right is None else add(dfirst_part[s], from_right)
-        from_left = lax.ppermute(up, "seq", [(i, i + 1) for i in range(s)])
-        from_right = lax.ppermute(down, "seq", [(i, i - 1) for i in range(n_seq - s, n_seq)])
-    grad_inputs, sums1 = leave(dfirst_part[0], from_left, from_right, tokens, dhidden1, mods)
-
-    dmods = jnp.concatenate(
-        [sums1[0:2], sums2[0:3], sum_gate2], axis=0
-    ).reshape(n_seq, 1, 6 * width // n_seq)
-    grad_mods = jnp.zeros((slots, 6 * width // n_seq), F32)
-    slot = jnp.arange(slots, dtype=jnp.int32)[:, None]
-    for d in range(n_seq):
-        mine = lax.dynamic_index_in_dim(dmods, (rank + d) % n_seq, keepdims=False)
-        got = lax.ppermute(mine, "seq", [(i, (i + d) % n_seq) for i in range(n_seq)]) if d else mine
-        whose = lax.dynamic_slice_in_dim(image_ids, ((rank - d) % n_seq) * tok_dev, 1)
-        grad_mods = grad_mods + jnp.where(slot == whose, got, 0.0)
+        rights2 = [right2, swap(right2, 1)]
+        f1 = weight_grad(lefts2, rights2, [job(hidden, width, xy, 0)], hidden, 1152)
+        rights2[0] = after(rights2[0], f1[0])
+        fo = weight_grad(lefts2, rights2, [job(hidden + width, width, yx, hidden // 384)], width, 384)
+        dheads_in = after(dheads_in, fo[0])
+    dqkv, dfirst_parts = attend_backward(
+        one, rank_arg, dheads_in, qkv, heads_out, lse, w_rows, idk, idq, heads, tile, diagonal
+    )
+
+    grad_inputs, sums1 = leave(exchange(dfirst_parts), tokens, dhidden1, mods)
+
+    dmods = jnp.concatenate([sums1[0:2], sums2[0:3], sum_gate2], axis=0)
+    dmods = exchange(dmods.reshape(n_seq, 6 * width // n_seq))
+    slot = jnp.arange(slots, dtype=jnp.int32)[:, None, None]
+    whose = image_ids[::tok_dev]
+    grad_mods = jnp.sum(jnp.where(slot == whose[None, :, None], dmods[None], 0.0), axis=1)
 
     if fast:
         rows = width // n_dp
-        fq = weight_grad([first_all], [dqkv], starts_of(width, dp_bits), rows, 3 * local, flat=True)
-        g_proj3 = finish(*p3, xy)
-        g_proj2 = finish(*p2, yx)
-        g_proj1 = finish(*p1, xy)
-        g_fc2 = finish(*f2, yx)
-        g_fc1 = finish(*f1, xy)
-        g_out = finish(*fo, yx)
-        g_heads = halve(*fq, "dp", n_dp, dp_bits)[0]
+        fq = weight_grad([first_all], [dqkv], [job(0, width, dp_bits, 0)], 3 * local, 3 * local, flat=True)
+        g_p21 = scatter_columns(halve(*p21, n_dp, xy, swap), n_seq)
+        g_proj2, g_proj1 = g_p21[: wide // n_dp], g_p21[wide // n_dp :]
+        g_proj3 = scatter_columns(halve(*p3, n_dp, yx, swap), n_seq)
+        g_fc2 = scatter_columns(halve(*f2, n_dp, yx, swap), n_seq)
+        g_fc1 = scatter_columns(halve(*f1, n_dp, xy, swap), n_seq)
+        g_out = scatter_columns(halve(*fo, n_dp, yx, swap), n_seq)
+        g_heads = halve(*fq, n_dp, dp_bits, swap)
     else:
 
         def reduced(a, b):
             share = lax.psum_scatter(matmul(a, b).astype(BF), "dp", scatter_dimension=0, tiled=True)
             return lax.psum_scatter(share, "seq", scatter_dimension=1, tiled=True).astype(F32)
 
-        g_proj3 = reduced(proj_a2, dlatent)
-        g_proj2 = reduced(proj_a1, dr2)
-        g_proj1 = reduced(rounded_t, dr1)
-        g_fc2 = reduced(active, dmlp)
-        g_fc1 = reduced(second, dupper)
-        ordered = jnp.concatenate(
-            [lax.dynamic_slice_in_dim(attn_t, ((rank - j) % n_seq) * local, local, 0) for j in range(n_seq)], axis=0
-        )
-        g_out = reduced(ordered, dattn)
+        g_proj3 = reduced(left1[:wide], right1[:, 2 * wide :])
+        g_proj2 = reduced(left1[wide : 2 * wide], right1[:, :wide])
+        g_proj1 = reduced(left1[2 * wide :], right1[:, wide : 2 * wide])
+        g_fc2 = reduced(left2[:hidden], dmlp)
+        g_fc1 = reduced(left2[hidden : hidden + width], right2[:, :hidden])
+        g_out = reduced(left2[hidden + width :], right2[:, hidden:])
         g_heads = lax.psum_scatter(
             times_trans(first_all, dqkv).astype(BF), "dp", scatter_dimension=0, tiled=True
         )
 
     units = [g_heads[:, i * local : (i + 1) * local] for i in range(3)]
-    columns = [jnp.zeros(units[0].shape, F32) for _ in range(3)]
-    for d in range(n_seq):
-        target, source = (rank + d) % n_seq, (rank - d) % n_seq
+    outgoing = []
+    for target in range(n_seq):
         mine = jnp.zeros_like(units[0])
         for i in range(3):
             mine = jnp.where((n_seq * i + rank) // 3 == target, units[i], mine)
-        got = lax.ppermute(mine, "seq", [(i, (i + d) % n_seq) for i in range(n_seq)]) if d else mine
+        outgoing.append(mine)
+    incoming = exchange(jnp.stack(outgoing))
+    columns = [jnp.zeros(units[0].shape, BF) for _ in range(3)]
+    for source in range(n_seq):
         for i in range(3):
             unit = n_seq * i + source
-            for at in range(3):
-                here = (unit // 3 == rank) & (unit % 3 == at)
-                columns[at] = jnp.where(here, got.astype(F32), columns[at])
-    g_qkv = jnp.concatenate(columns, axis=1)
+            columns[unit % 3] = jnp.where(unit // 3 == rank, incoming[source], columns[unit % 3])
+    g_qkv = jnp.concatenate(columns, axis=1).astype(F32)
 
     return (rounded, grad_inputs, grad_mods, g_qkv, g_out, g_fc1, g_fc2, g_proj1, g_proj2, g_proj3)
 

time: 576 us -> 635 us (1.10)
  waiting for transfers between devices: 197 us -> 298 us
  starting transfers between devices: 122 us -> 62.5 us
  blocking collectives: 0 us -> 56.9 us
  Pallas kernels: 155 us -> 138 us
  other arithmetic: 54.4 us -> 39.7 us
  local copies, waits for them, and re-layouts: 36.4 us -> 29.2 us
    all_to_all x0 -> x8, waiting for transfers between devices: none -> 65.2 us  [exchange(): lax.all_to_all(blocks, 'seq', split_axis=0, concat_axis=0, tiled=True)]
    ppermute x39 -> x18, waiting for transfers between devices: 136 us -> 200 us  [flip(): return lax.ppermute(x, axis, [(i, i ^ bit) for i in range(size)])]
    all_to_all x0 -> x2, blocking collectives: none -> 56.9 us  [exchange(): lax.all_to_all(blocks, 'seq', split_axis=0, concat_axis=0, tiled=True)]
    ppermute x39 -> x18, starting transfers between devices: 70.9 us -> 20.7 us  [flip(): return lax.ppermute(x, axis, [(i, i ^ bit) for i in range(size)])]
    ppermute x18 -> x0, starting transfers between devices: 39.1 us -> none  [the longest x3 15.3 us: shards(): from_left = lax.ppermute(up, 'seq', [(i, i + 1) for i in range(s)])]
    all_to_all x0 -> x8, starting transfers between devices: none -> 30 us  [exchange(): lax.all_to_all(blocks, 'seq', split_axis=0, concat_axis=0, tiled=True)]
    ppermute x18 -> x0, waiting for transfers between devices: 28.1 us -> none  [the longest x3 13 us: shards(): from_left = lax.ppermute(up, 'seq', [(i, i + 1) for i in range(s)])]
    pallas_call x1, Pallas kernels: 31.9 us -> 16.9 us  [descend(): pl.pallas_call(functools.partial(descend_kernel, size), out_shape=(shape(...]
  transfers between devices with their start and end apart: 63 -> 32, of which waited for: 23 -> 17; matrix products, arithmetic and copies ran while one was open for 14% -> 10% of each run, Pallas kernels for 17% -> 9%
where the time goes in v2:
time: 635 us; the launch traced here: 627 us
  waiting for transfers between devices  298 us (47%)
  Pallas kernels  138 us (22%)
  starting transfers between devices  62.5 us (10%)
  blocking collectives  56.9 us (9%)
  other arithmetic  39.7 us (6%)
  local copies, waits for them, and re-layouts  29.2 us (5%)
    ppermute x18, waiting for transfers between devices, flip(): return lax.ppermute(x, axis, [(i, i ^ bit) for i in range(size)])  200 us
    all_to_all x8, waiting for transfers between devices, exchange(): lax.all_to_all(blocks, 'seq', split_axis=0, concat_axis=0, tiled=True)  65.2 us
    all_to_all x2, blocking collectives, exchange(): lax.all_to_all(blocks, 'seq', split_axis=0, concat_axis=0, tiled=True)  56.9 us
    pallas_call x6, Pallas kernels, weight_grad(): pl.pallas_call(functools.partial(weight_grad_kernel, count, flat, rows),...  45.6 us
    pallas_call x1, Pallas kernels, middle(): pl.pallas_call(middle_kernel, out_shape=(shape((tok, width)), shape((2 *...  37.9 us
    all_to_all x8, starting transfers between devices, exchange(): lax.all_to_all(blocks, 'seq', split_axis=0, concat_axis=0, tiled=True)  30 us
    convert_element_type x12, other arithmetic, add(): return (a.astype(F32) + b.astype(F32)).astype(BF)  24.4 us
    ppermute x18, starting transfers between devices, flip(): return lax.ppermute(x, axis, [(i, i ^ bit) for i in range(size)])  20.7 us
  transfers between devices with their start and end apart: 32, of which 17 were waited for; matrix products, arithmetic and copies ran while one was open for 10% of the time, Pallas kernels for 9%

profile of v2, /device:TPU:0, one launch (start us, length us, event | category | flops | bytes accessed | tf_op | source)
XLA Modules:
  0.0 626.5 jit_solution(2900563151954983104)
XLA Ops:
  2.0 3.1 enter.1
  5.1 5.0 collective-permute-start.1
  11.4 11.5 %collective-permute-done.1.refs_6_ = bf16[1152,256]{1,0:T(8,128)(2,1)S(1)} collective-permute-done((bf16[1152,256]{1,0:T(8,128)(2,1)}, bf16[1152,256]{1,0:T(8,128)(2,1)S(1)}, u32[]{:S(2)}, u32[]{:S(2)}) %collective-permute-start.1) | collective-permute-done | bytes 589856 | tf_op jit(solution)/shard_map/ppermute | solution.py:659
  24.4 2.6 collective-permute-done.refs_1_
  29.7 14.0 %collective-permute-done.4.refs_3_ = bf16[1152,256]{1,0:T(8,128)(2,1)} collective-permute-done((bf16[1152,256]{1,0:T(8,128)(2,1)S(1)}, bf16[1152,256]{1,0:T(8,128)(2,1)}, u32[]{:S(2)}, u32[]{:S(2)}) %collective-permute-start.4) | collective-permute-done | bytes 589856 | tf_op jit(solution)/shard_map/ppermute | solution.py:660
  45.1 3.5 constant_dynamic-slice_fusion.2
  55.2 4.0 collective-permute-done.5.refs_5_
  59.2 15.7 %attend_forward.1 = (bf16[1152,1024]{1,0:T(8,128)(2,1)}, bf16[4,288,256]{2,1,0:T(8,128)(2,1)}, bf16[960,1024]{1,0:T(8,128)(2,1)}, f32[4,1024]{1,0:T(4,128)}) custom-call(s32[1]{0:T(128)S(6)} %convert_element_type.204.one_ref, s32[1]{0:T(128)} %bitcast.rank_ref, bf16[1152,256]{1,0:T(8,128)(2,1)} %get-tuple-element.52.refs_0_, bf16[1152,256]{1,0:T(8,128)(2,1)} %copy-done.11, ...), custom_call_target="tpu_custom_call" | custom-call | bytes 69000000 | tf_op jit(solution)/shard_map/attend_forward/pallas_call | solution.py:168
  74.9 20.7 %all_to_all.55.refs_0_ = bf16[4,288,256]{2,1,0:T(8,128)(2,1)} all-to-all(bf16[4,288,256]{2,1,0:T(8,128)(2,1)} %get-tuple-element.53.refs_2_), channel_id=1, replica_groups=mesh['dp'=8,'seq'=4] {'seq'}, dimensions={0} | all-to-all | bytes 1179648 | tf_op jit(solution)/shard_map/all_to_all | solution.py:629
  95.6 37.9 %middle.1 = (bf16[256,1152]{1,0:T(8,128)(2,1)}, bf16[5248,256]{1,0:T(8,128)(2,1)}, bf16[6912,256]{1,0:T(8,128)(2,1)}, bf16[256,4864]{1,0:T(8,128)(2,1)}, bf16[25...) custom-call(bf16[4,288,256]{2,1,0:T(8,128)(2,1)} %all_to_all.55.refs, ...), custom_call_target="tpu_custom_call" | custom-call | bytes 123000000 | tf_op jit(solution)/shard_map/middle/pallas_call | solution.py:411
  136.7 11.3 %collective-permute-done.8.refs_3_.refs_5_ = bf16[256,4864]{1,0:T(8,128)(2,1)} collective-permute-done((bf16[256,4864]{1,0:T(8,128)(2,1)}, bf16[256,4864]{1,0:T(8,128)(2,1)}, u32[]{:S(2)}, u32[]{:S(2)}) %collective-permute-start.8) | collective-permute-done | bytes 2490400 | tf_op jit(solution)/shard_map/ppermute | solution.py:596
  148.0 9.4 %weight_grad.6 = (bf16[2,400,2048]{2,1,0:T(8,128)(2,1)}, bf16[2,400,2048]{2,1,0:T(8,128)(2,1)}) custom-call(s32[8]{0:T(128)} %pad_add_fusion.rows_ref, bf16[5248,256]{1,0:T(8,128)(2,1)} %get-tuple-element.58.refs_0_, bf16[5248,256]{1,0:T(8,128)(2,1)} %collective-permute-done.7.refs_1_, bf16[256,4864]{1,0:T(8,128)(2,1)} %get-tuple-element.61.refs_2_.refs_4_, ...), custom_call_target="tpu_custom_call" | custom-call | bytes 20796480 | tf_op jit(solution)/shard_map/weight_grad/pallas_call | solution.py:576
  157.4 5.9 weight_grad.7
  165.2 8.6 %weight_grad.8 = (bf16[2,576,1152]{2,1,0:T(8,128)(2,1)}, bf16[2,576,1152]{2,1,0:T(8,128)(2,1)}) custom-call(s32[4]{0:T(128)} %get-tuple-element.115.rows_ref, bf16[6912,256]{1,0:T(8,128)(2,1)} %get-tuple-element.57.refs_0_, bf16[6912,256]{1,0:T(8,128)(2,1)} %copy-done, bf16[256,1152]{1,0:T(8,128)(2,1)} %get-tuple-element.65.refs_2_.refs_0_, ...), custom_call_target="tpu_custom_call" | custom-call | bytes 18555148 | tf_op jit(solution)/shard_map/weight_grad/pallas_call | solution.py:576
  173.8 16.9 %descend.1 = (bf16[256,5760]{1,0:T(8,128)(2,1)}, f32[256,1152]{1,0:T(8,128)}, bf16[4,288,256]{2,1,0:T(8,128)(2,1)}, f32[8,1152]{1,0:T(8,128)}) custom-call(bf16[256,1152]{1,0:T(8,128)(2,1)} %get-tuple-element.65.refs_2_.refs_0_, bf16[256,4608]{1,0:T(8,128)(2,1)} %get-tuple-element.66.refs_1_, f32[256,1152]{1,0:T(8,128)} %get-tuple-element.67.refs_2_, ...), custom_call_target="tpu_custom_call" | custom-call | bytes 60000000 | tf_op jit(solution)/shard_map/descend/pallas_call | solution.py:479
  193.2 3.5 all-to-all-start.1
  196.7 71.3 %collective-permute-done.22 = bf16[2,256,768]{2,1,0:T(8,128)(2,1)} collective-permute-done((bf16[2,256,768]{2,1,0:T(8,128)(2,1)}, bf16[2,256,768]{2,1,0:T(8,128)(2,1)}, u32[]{:S(2)}, u32[]{:S(2)}) %collective-permute-start.22) | collective-permute-done | bytes 786464 | tf_op jit(solution)/shard_map/ppermute | solution.py:596
  269.9 3.3 collective-permute-start.23
  274.8 8.4 %weight_grad.9 = (bf16[2,144,4608]{2,1,0:T(8,128)(2,1)}, bf16[2,144,4608]{2,1,0:T(8,128)(2,1)}) custom-call(s32[4]{0:T(128)} %get-tuple-element.110.rows_ref, bf16[6912,256]{1,0:T(8,128)(2,1)} %get-tuple-element.57.refs_0_, bf16[6912,256]{1,0:T(8,128)(2,1)} %copy-done, bf16[256,5760]{1,0:T(8,128)(2,1)} %get-tuple-element.74.refs_2_, bf16[256,5760]{1,0:T(8,128)(2,1)} %copy-done.1), custom_call_target="tpu_custom_call" | custom-call | bytes 18555148 | tf_op jit(solution)/shard_map/weight_grad/pallas_call | solution.py:576
  283.2 5.8 weight_grad.10
  290.7 14.4 %attend_backward.1 = (bf16[864,1024]{1,0:T(8,128)(2,1)}, bf16[4,256,1152]{2,1,0:T(8,128)(2,1)}) custom-call(s32[1]{0:T(128)S(6)} %convert_element_type.204.one_ref, s32[1]{0:T(128)} %bitcast.rank_ref, bf16[4,288,256]{2,1,0:T(8,128)(2,1)} %copy-done.6, bf16[960,1024]{1,0:T(8,128)(2,1)} %get-tuple-element.77.refs_1_, ...), custom_call_target="tpu_custom_call" | custom-call | bytes 69000000 | tf_op jit(solution)/shard_map/attend_backward/pallas_call | solution.py:271
  305.1 7.5 %weight_grad.11 = (bf16[4,144,864]{2,1,0:T(8,128)(2,1)}, bf16[4,144,864]{2,1,0:T(8,128)(2,1)}) custom-call(s32[8]{0:T(128)} %xor_multiply_fusion.5.rows_ref, bf16[1152,1024]{1,0:T(8,128)(2,1)} %get-tuple-element.85.refs_0_, bf16[864,1024]{1,0:T(8,128)(2,1)} %get-tuple-element.86.refs_1_), custom_call_target="tpu_custom_call" | custom-call | bytes 10791590 | tf_op jit(solution)/shard_map/weight_grad/pallas_call | solution.py:576
  312.6 5.8 collective-permute-start.11
  321.6 4.5 all-to-all-start.9
  331.2 2.8 add_convert_fusion.4
  335.1 75.5 %collective-permute-done.12 = bf16[2,144,864]{2,1,0:T(8,128)(2,1)S(1)} collective-permute-done((bf16[2,144,864]{2,1,0:T(8,128)(2,1)S(1)}, bf16[2,144,864]{2,1,0:T(8,128)(2,1)S(1)}, u32[]{:S(2)}, u32[]{:S(2)}) %collective-permute-start.12) | collective-permute-done | bytes 497696 | tf_op jit(solution)/shard_map/ppermute | solution.py:596
  413.7 3.6 collective-permute-done.13
  418.4 3.5 all-to-all-start.5
  423.1 9.7 %all-to-all-done.5 = bf16[4,144,288]{2,1,0:T(8,128)(2,1)S(1)} async-done(((bf16[4,144,288]{2,1,0:T(8,128)(2,1)}), bf16[4,144,288]{2,1,0:T(8,128)(2,1)S(1)}, u32[]{:S(2)}, u32[]{:S(2)}) %all-to-all-start.5) | async-done | bytes 331808 | tf_op jit(solution)/shard_map/all_to_all | solution.py:629
  432.8 3.5 all-to-all-start.4
  436.3 2.1 collective-permute-done.19
  438.4 2.6 add_convert_fusion.3
  442.1 4.9 all-to-all-done.4
  447.0 36.2 %all_to_all.56 = bf16[4,576,288]{1,2,0:T(8,128)(2,1)} all-to-all(bf16[4,576,288]{1,2,0:T(8,128)(2,1)S(1)} %bitcast.45), channel_id=1, replica_groups=mesh['dp'=8,'seq'=4] {'seq'}, dimensions={0} | all-to-all | bytes 2654208 | tf_op jit(solution)/shard_map/all_to_all | solution.py:629
  483.2 3.6 all-to-all-start.2
  488.7 2.5 add_convert_fusion.1
  491.9 35.3 %collective-permute-done.21 = bf16[1,400,2048]{2,1,0:T(8,128)(2,1)S(1)} collective-permute-done((bf16[1,400,2048]{2,1,0:T(8,128)(2,1)S(1)}, bf16[1,400,2048]{2,1,0:T(8,128)(2,1)S(1)}, u32[]{:S(2)}, u32[]{:S(2)}) %collective-permute-start.21) | collective-permute-done | bytes 1638432 | tf_op jit(solution)/shard_map/ppermute | solution.py:596
  527.1 3.5 add_convert_fusion
  530.6 4.7 reshape_squeeze.18
  535.3 2.9 copy.69
  539.4 4.4 all-to-all-start.8
  545.1 3.1 add_convert_fusion.7
  548.9 4.1 leave.1
  554.5 27.3 %all-to-all-done.8 = bf16[4,400,512]{2,1,0:T(8,128)(2,1)} async-done(((bf16[4,400,512]{2,1,0:T(8,128)(2,1)}), bf16[4,400,512]{2,1,0:T(8,128)(2,1)}, u32[]{:S(2)}, u32[]{:S(2)}) %all-to-all-start.8) | async-done | bytes 1638432 | tf_op jit(solution)/shard_map/all_to_all | solution.py:629
  581.8 3.3 all-to-all-start.3
  585.0 2.6 add_convert_fusion.6
  590.6 3.8 all-to-all-start.6
  604.3 20.8 %all-to-all-done.6 = bf16[4,144,1152]{2,1,0:T(8,128)(2,1)S(1)} async-done(((bf16[4,144,1152]{2,1,0:T(8,128)(2,1)}), bf16[4,144,1152]{2,1,0:T(8,128)(2,1)S(1)}, u32[]{:S(2)}, u32[]{:S(2)}) %all-to-all-start.6) | async-done | bytes 1327136 | tf_op jit(solution)/shard_map/all_to_all | solution.py:629
  (124 shorter events, 63.0 us)
Async XLA Ops:
  5.1 17.8 %collective-permute-start.1 = (bf16[1152,256]{1,0:T(8,128)(2,1)}, bf16[1152,256]{1,0:T(8,128)(2,1)S(1)}, u32[]{:S(2)}, u32[]{:S(2)}) collective-permute-start(bf16[1152,256]{1,0:T(8,128)(2,1)} %get-tuple-element.52.refs_0_), channel_id=1, source_target_pairs={{0,1},{1,2},{2,3},{4,5},{5,6},{6,7},{8,9},{9,10},{10,11},{12,13},{... | collective-permute-start | bytes 1769480 | tf_op jit(solution)/shard_map/ppermute | solution.py:659
  10.1 16.9 %collective-permute-start = (bf16[1152,256]{1,0:T(8,128)(2,1)}, bf16[1152,256]{1,0:T(8,128)(2,1)S(1)}, u32[]{:S(2)}, u32[]{:S(2)}) collective-permute-start(bf16[1152,256]{1,0:T(8,128)(2,1)} %get-tuple-element.52.refs_0_), channel_id=1, source_target_pairs={{1,0},{2,1},{3,2},{5,4},{6,5},{7,6},{9,8},{10,9},{11,10},{13,12},{... | collective-permute-start | bytes 1769480 | tf_op jit(solution)/shard_map/ppermute | solution.py:660
  22.9 20.9 %copy-start.10 = (bf16[1152,256]{1,0:T(8,128)(2,1)}, bf16[1152,256]{1,0:T(8,128)(2,1)S(1)}, u32[]{:S(2)}) copy-start(bf16[1152,256]{1,0:T(8,128)(2,1)S(1)} %collective-permute-done.1.refs_6_) | copy-start | bytes 1769476
  22.9 5.3 collective-permute-start.2
  26.9 16.8 %copy-start.11 = (bf16[1152,256]{1,0:T(8,128)(2,1)}, bf16[1152,256]{1,0:T(8,128)(2,1)S(1)}, u32[]{:S(2)}) copy-start(bf16[1152,256]{1,0:T(8,128)(2,1)S(1)} %collective-permute-done.refs_1_) | copy-start | bytes 1769476
  27.0 16.8 %collective-permute-start.4 = (bf16[1152,256]{1,0:T(8,128)(2,1)S(1)}, bf16[1152,256]{1,0:T(8,128)(2,1)}, u32[]{:S(2)}, u32[]{:S(2)}) collective-permute-start(bf16[1152,256]{1,0:T(8,128)(2,1)S(1)} %collective-permute-done.refs_1_), channel_id=1, source_target_pairs={{1,0},{2,1},{5,4},{6,5},{9,8},{10,9},{13,12},{14,13},{17,16},{18,1... | collective-permute-start | bytes 1769480 | tf_op jit(solution)/shard_map/ppermute | solution.py:660
  28.3 27.0 %collective-permute-start.3 = (bf16[1152,256]{1,0:T(8,128)(2,1)}, bf16[1152,256]{1,0:T(8,128)(2,1)}, u32[]{:S(2)}, u32[]{:S(2)}) collective-permute-start(bf16[1152,256]{1,0:T(8,128)(2,1)} %collective-permute-done.2.refs_4_), channel_id=1, source_target_pairs={{2,3},{6,7},{10,11},{14,15},{18,19},{22,23},{26,27},{30,31}} | collective-permute-start | bytes 1769480 | tf_op jit(solution)/shard_map/ppermute | solution.py:659
  43.8 15.5 %collective-permute-start.5 = (bf16[1152,256]{1,0:T(8,128)(2,1)}, bf16[1152,256]{1,0:T(8,128)(2,1)}, u32[]{:S(2)}, u32[]{:S(2)}) collective-permute-start(bf16[1152,256]{1,0:T(8,128)(2,1)} %collective-permute-done.4.refs_3_), channel_id=1, source_target_pairs={{1,0},{5,4},{9,8},{13,12},{17,16},{21,20},{25,24},{29,28}} | collective-permute-start | bytes 1769480 | tf_op jit(solution)/shard_map/ppermute | solution.py:660
  48.6 2.4 copy-start.15
  51.0 2.6 copy-start.13
  95.6 39.4 %copy-start.18 = (s32[4]{0:T(128)S(1)}, s32[4]{0:T(128)}, u32[]{:S(2)}) copy-start(s32[4]{0:T(128)} %constant.92.clone) | copy-start | bytes 52
  95.6 40.5 %copy-start.17 = (s32[4]{0:T(128)S(1)}, s32[4]{0:T(128)}, u32[]{:S(2)}) copy-start(s32[4]{0:T(128)} %constant.93.clone) | copy-start | bytes 52
  133.5 29.8 %collective-permute-start.6 = (bf16[6912,256]{1,0:T(8,128)(2,1)}, bf16[6912,256]{1,0:T(8,128)(2,1)S(1)}, u32[]{:S(2)}, u32[]{:S(2)}) collective-permute-start(bf16[6912,256]{1,0:T(8,128)(2,1)} %get-tuple-element.57.refs_0_), channel_id=1, source_target_pairs={{0,4},{4,0},{8,12},{12,8},{16,20},{20,16},{24,28},{28,24},{1,5},{5... | collective-permute-start | bytes 10616840 | tf_op jit(solution)/shard_map/ppermute | solution.py:596
  134.4 13.6 %collective-permute-start.7 = (bf16[5248,256]{1,0:T(8,128)(2,1)}, bf16[5248,256]{1,0:T(8,128)(2,1)}, u32[]{:S(2)}, u32[]{:S(2)}) collective-permute-start(bf16[5248,256]{1,0:T(8,128)(2,1)} %get-tuple-element.58.refs_0_), channel_id=1, source_target_pairs={{0,4},{4,0},{8,12},{12,8},{16,20},{20,16},{24,28},{28,24},{1,5},{5... | collective-permute-start | bytes 8060936 | tf_op jit(solution)/shard_map/ppermute | solution.py:596
  134.5 13.5 %collective-permute-start.8 = (bf16[256,4864]{1,0:T(8,128)(2,1)}, bf16[256,4864]{1,0:T(8,128)(2,1)}, u32[]{:S(2)}, u32[]{:S(2)}) collective-permute-start(bf16[256,4864]{1,0:T(8,128)(2,1)} %get-tuple-element.61.refs_2_.refs_4_), channel_id=1, source_target_pairs={{0,4},{4,0},{8,12},{12,8},{16,20},{20,16},{24,28},{28,24},{1,5},{5... | collective-permute-start | bytes 7471112 | tf_op jit(solution)/shard_map/ppermute | solution.py:596
  134.9 28.4 %collective-permute-start.9 = (bf16[256,1152]{1,0:T(8,128)(2,1)}, bf16[256,1152]{1,0:T(8,128)(2,1)}, u32[]{:S(2)}, u32[]{:S(2)}) collective-permute-start(bf16[256,1152]{1,0:T(8,128)(2,1)} %get-tuple-element.65.refs_2_.refs_0_), channel_id=1, source_target_pairs={{0,4},{4,0},{8,12},{12,8},{16,20},{20,16},{24,28},{28,24},{1,5},{5... | collective-permute-start | bytes 1769480 | tf_op jit(solution)/shard_map/ppermute | solution.py:596
  190.7 82.4 %collective-permute-start.10 = (bf16[256,5760]{1,0:T(8,128)(2,1)}, bf16[256,5760]{1,0:T(8,128)(2,1)S(1)}, u32[]{:S(2)}, u32[]{:S(2)}) collective-permute-start(bf16[256,5760]{1,0:T(8,128)(2,1)} %get-tuple-element.74.refs_2_), channel_id=1, source_target_pairs={{0,4},{4,0},{8,12},{12,8},{16,20},{20,16},{24,28},{28,24},{1,5},{5... | collective-permute-start | bytes 8847368 | tf_op jit(solution)/shard_map/ppermute | solution.py:596
  191.1 140.0 %collective-permute-start.18 = (bf16[2,576,1152]{2,1,0:T(8,128)(2,1)}, bf16[2,576,1152]{2,1,0:T(8,128)(2,1)}, u32[]{:S(2)}, u32[]{:S(2)}) collective-permute-start(bf16[2,576,1152]{2,1,0:T(8,128)(2,1)} %get-tuple-element.64), channel_id=1, source_target_pairs={{0,16},{4,20},{8,24},{12,28},{16,0},{20,4},{24,8},{28,12},{1,17},{... | collective-permute-start | bytes 7962632 | tf_op jit(solution)/shard_map/ppermute | solution.py:596
  191.2 76.8 %collective-permute-start.22 = (bf16[2,256,768]{2,1,0:T(8,128)(2,1)}, bf16[2,256,768]{2,1,0:T(8,128)(2,1)}, u32[]{:S(2)}, u32[]{:S(2)}) collective-permute-start(bf16[2,256,768]{2,1,0:T(8,128)(2,1)} %get-tuple-element.62), channel_id=1, source_target_pairs={{0,16},{4,20},{8,24},{12,28},{16,0},{20,4},{24,8},{28,12},{1,17},{... | collective-permute-start | bytes 2359304 | tf_op jit(solution)/shard_map/ppermute | solution.py:596
  193.2 96.7 %all-to-all-start.1 = ((bf16[4,288,256]{2,1,0:T(8,128)(2,1)}), bf16[4,288,256]{2,1,0:T(8,128)(2,1)S(1)}, u32[]{:S(2)}, u32[]{:S(2)}) async-start(bf16[4,288,256]{2,1,0:T(8,128)(2,1)} %get-tuple-element.71), calls=%async_computation.1 | async-start | bytes 1179648 | tf_op jit(solution)/shard_map/all_to_all | solution.py:629
  269.9 49.5 %collective-permute-start.23 = (bf16[1,256,768]{2,1,0:T(8,128)(2,1)}, bf16[1,256,768]{2,1,0:T(8,128)(2,1)}, u32[]{:S(2)}, u32[]{:S(2)}) collective-permute-start(bf16[1,256,768]{2,1,0:T(8,128)(2,1)} %add_convert_fusion.12), channel_id=1, source_target_pairs={{0,8},{4,12},{8,0},{12,4},{16,24},{20,28},{24,16},{28,20},{1,9},{5... | collective-permute-start | bytes 1179656 | tf_op jit(solution)/shard_map/ppermute | solution.py:596
  283.2 6.1 copy-start.19
  289.0 37.1 %collective-permute-start.14 = (bf16[2,144,1152]{2,1,0:T(8,128)(2,1)}, bf16[2,144,1152]{2,1,0:T(8,128)(2,1)}, u32[]{:S(2)}, u32[]{:S(2)}) collective-permute-start(bf16[2,144,1152]{2,1,0:T(8,128)(2,1)} %get-tuple-element.75), channel_id=1, source_target_pairs={{0,16},{4,20},{8,24},{12,28},{16,0},{20,4},{24,8},{28,12},{1,17},{... | collective-permute-start | bytes 1990664 | tf_op jit(solution)/shard_map/ppermute | solution.py:596
  305.1 14.3 %copy-start.8 = (bf16[2,256,768]{2,1,0:T(8,128)(2,1)S(1)}, bf16[2,256,768]{2,1,0:T(8,128)(2,1)}, u32[]{:S(2)}) copy-start(bf16[2,256,768]{2,1,0:T(8,128)(2,1)} %get-tuple-element.93) | copy-start | bytes 2359300
  312.6 15.8 %collective-permute-start.11 = (bf16[4,144,864]{2,1,0:T(8,128)(2,1)}, bf16[4,144,864]{2,1,0:T(8,128)(2,1)}, u32[]{:S(2)}, u32[]{:S(2)}) collective-permute-start(bf16[4,144,864]{2,1,0:T(8,128)(2,1)} %get-tuple-element.88), channel_id=1, source_target_pairs={{0,4},{4,0},{8,12},{12,8},{16,20},{20,16},{24,28},{28,24},{1,5},{5... | collective-permute-start | bytes 2985992 | tf_op jit(solution)/shard_map/ppermute | solution.py:596
  318.5 170.2 %collective-permute-start.20 = (bf16[2,400,2048]{2,1,0:T(8,128)(2,1)}, bf16[2,400,2048]{2,1,0:T(8,128)(2,1)}, u32[]{:S(2)}, u32[]{:S(2)}) collective-permute-start(bf16[2,400,2048]{2,1,0:T(8,128)(2,1)} %get-tuple-element.60), channel_id=1, source_target_pairs={{0,8},{4,12},{8,0},{12,4},{16,24},{20,28},{24,16},{28,20},{1,9},{5... | collective-permute-start | bytes 9830408 | tf_op jit(solution)/shard_map/ppermute | solution.py:596
  320.7 10.5 %copy-start.5 = (bf16[2,576,1152]{2,1,0:T(8,128)(2,1)S(1)}, bf16[2,576,1152]{2,1,0:T(8,128)(2,1)}, u32[]{:S(2)}) copy-start(bf16[2,576,1152]{2,1,0:T(8,128)(2,1)} %get-tuple-element.91) | copy-start | bytes 7962628
  321.6 96.8 %all-to-all-start.9 = ((bf16[4,256,192]{1,2,0:T(8,128)(2,1)}), bf16[4,256,192]{1,2,0:T(8,128)(2,1)}, u32[]{:S(2)}, u32[]{:S(2)}) async-start(bf16[4,256,192]{1,2,0:T(8,128)(2,1)} %bitcast.20), calls=%async_computation.9 | async-start | bytes 786432 | tf_op jit(solution)/shard_map/all_to_all | solution.py:629
  327.3 83.5 %collective-permute-start.15 = (bf16[1,144,1152]{2,1,0:T(8,128)(2,1)S(1)}, bf16[1,144,1152]{2,1,0:T(8,128)(2,1)S(1)}, u32[]{:S(2)}, u32[]{:S(2)}) collective-permute-start(bf16[1,144,1152]{2,1,0:T(8,128)(2,1)S(1)} %add_convert_fusion.15), channel_id=1, source_target_pairs={{0,8},{4,12},{8,0},{12,4},{16,24},{20,28},{24,16},{28,20},{1,9},{5... | collective-permute-start | bytes 995336 | tf_op jit(solution)/shard_map/ppermute | solution.py:596
  330.2 81.2 %copy-start.9 = (bf16[2,144,1152]{2,1,0:T(8,128)(2,1)S(1)}, bf16[2,144,1152]{2,1,0:T(8,128)(2,1)}, u32[]{:S(2)}) copy-start(bf16[2,144,1152]{2,1,0:T(8,128)(2,1)} %get-tuple-element.89) | copy-start | bytes 1990660
  330.2 80.4 %collective-permute-start.12 = (bf16[2,144,864]{2,1,0:T(8,128)(2,1)S(1)}, bf16[2,144,864]{2,1,0:T(8,128)(2,1)S(1)}, u32[]{:S(2)}, u32[]{:S(2)}) collective-permute-start(bf16[2,144,864]{2,1,0:T(8,128)(2,1)S(1)} %get-tuple-element.98), channel_id=1, source_target_pairs={{0,8},{4,12},{8,0},{12,4},{16,24},{20,28},{24,16},{28,20},{1,9},{5... | collective-permute-start | bytes 1493000 | tf_op jit(solution)/shard_map/ppermute | solution.py:596
  334.0 104.4 %collective-permute-start.19 = (bf16[1,576,1152]{2,1,0:T(8,128)(2,1)}, bf16[1,576,1152]{2,1,0:T(8,128)(2,1)}, u32[]{:S(2)}, u32[]{:S(2)}) collective-permute-start(bf16[1,576,1152]{2,1,0:T(8,128)(2,1)} %add_convert_fusion.4), channel_id=1, source_target_pairs={{0,8},{4,12},{8,0},{12,4},{16,24},{20,28},{24,16},{28,20},{1,9},{5... | collective-permute-start | bytes 3981320 | tf_op jit(solution)/shard_map/ppermute | solution.py:596
  410.7 6.7 %collective-permute-start.13 = (bf16[1,144,864]{2,1,0:T(8,128)(2,1)S(1)}, bf16[1,144,864]{2,1,0:T(8,128)(2,1)S(1)}, u32[]{:S(2)}, u32[]{:S(2)}) collective-permute-start(bf16[1,144,864]{2,1,0:T(8,128)(2,1)S(1)} %add_convert_fusion.18), channel_id=1, source_target_pairs={{0,16},{4,20},{8,24},{12,28},{16,0},{20,4},{24,8},{28,12},{1,17},{... | collective-permute-start | bytes 746504 | tf_op jit(solution)/shard_map/ppermute | solution.py:596
  418.4 14.3 %all-to-all-start.5 = ((bf16[4,144,288]{2,1,0:T(8,128)(2,1)}), bf16[4,144,288]{2,1,0:T(8,128)(2,1)S(1)}, u32[]{:S(2)}, u32[]{:S(2)}) async-start(bf16[4,144,288]{2,1,0:T(8,128)(2,1)} %bitcast.40), calls=%async_computation.5 | async-start | bytes 884736 | tf_op jit(solution)/shard_map/all_to_all | solution.py:629
  432.8 5.6 copy-start.7
  432.8 14.2 %all-to-all-start.4 = ((bf16[4,144,288]{2,1,0:T(8,128)(2,1)}), bf16[4,144,288]{2,1,0:T(8,128)(2,1)S(1)}, u32[]{:S(2)}, u32[]{:S(2)}) async-start(bf16[4,144,288]{2,1,0:T(8,128)(2,1)} %pad_maximum_fusion.1), calls=%async_computation.4 | async-start | bytes 884736 | tf_op jit(solution)/shard_map/all_to_all | solution.py:629
  483.2 56.3 %all-to-all-start.2 = ((bf16[4,256,1152]{2,1,0:T(8,128)(2,1)}), bf16[4,256,1152]{2,1,0:T(8,128)(2,1)S(1)}, u32[]{:S(2)}, u32[]{:S(2)}) async-start(bf16[4,256,1152]{2,1,0:T(8,128)(2,1)} %get-tuple-element.79), calls=%async_computation.2 | async-start | bytes 4718592 | tf_op jit(solution)/shard_map/all_to_all | solution.py:629
  486.8 40.3 %copy-start.4 = (bf16[2,400,2048]{2,1,0:T(8,128)(2,1)S(1)}, bf16[2,400,2048]{2,1,0:T(8,128)(2,1)}, u32[]{:S(2)}) copy-start(bf16[2,400,2048]{2,1,0:T(8,128)(2,1)} %get-tuple-element.92) | copy-start | bytes 9830404
  486.8 58.3 %collective-permute-start.16 = (bf16[2,144,4608]{2,1,0:T(8,128)(2,1)}, bf16[2,144,4608]{2,1,0:T(8,128)(2,1)}, u32[]{:S(2)}, u32[]{:S(2)}) collective-permute-start(bf16[2,144,4608]{2,1,0:T(8,128)(2,1)} %get-tuple-element.73), channel_id=1, source_target_pairs={{0,8},{4,12},{8,0},{12,4},{16,24},{20,28},{24,16},{28,20},{1,9},{5... | collective-permute-start | bytes 7962632 | tf_op jit(solution)/shard_map/ppermute | solution.py:596
  491.2 35.9 %collective-permute-start.21 = (bf16[1,400,2048]{2,1,0:T(8,128)(2,1)S(1)}, bf16[1,400,2048]{2,1,0:T(8,128)(2,1)S(1)}, u32[]{:S(2)}, u32[]{:S(2)}) collective-permute-start(bf16[1,400,2048]{2,1,0:T(8,128)(2,1)S(1)} %add_convert_fusion.1), channel_id=1, source_target_pairs={{0,16},{4,20},{8,24},{12,28},{16,0},{20,4},{24,8},{28,12},{1,17},{... | collective-permute-start | bytes 4915208 | tf_op jit(solution)/shard_map/ppermute | solution.py:596
  539.4 8.8 %copy-start.2 = (bf16[4,256,1152]{2,1,0:T(8,128)(2,1)}, bf16[4,256,1152]{2,1,0:T(8,128)(2,1)S(1)}, u32[]{:S(2)}) copy-start(bf16[4,256,1152]{2,1,0:T(8,128)(2,1)S(1)} %all-to-all-done.2.parts_ref) | copy-start | bytes 7077892
  539.4 42.3 %all-to-all-start.8 = ((bf16[4,400,512]{2,1,0:T(8,128)(2,1)}), bf16[4,400,512]{2,1,0:T(8,128)(2,1)}, u32[]{:S(2)}, u32[]{:S(2)}) async-start(bf16[4,400,512]{2,1,0:T(8,128)(2,1)} %bitcast.44), calls=%async_computation.8 | async-start | bytes 3276800 | tf_op jit(solution)/shard_map/all_to_all | solution.py:629
  543.8 5.0 copy-start.14
  548.3 5.5 copy-start.16
  548.3 36.7 %collective-permute-start.17 = (bf16[1,144,4608]{2,1,0:T(8,128)(2,1)}, bf16[1,144,4608]{2,1,0:T(8,128)(2,1)}, u32[]{:S(2)}, u32[]{:S(2)}) collective-permute-start(bf16[1,144,4608]{2,1,0:T(8,128)(2,1)} %add_convert_fusion.7), channel_id=1, source_target_pairs={{0,16},{4,20},{8,24},{12,28},{16,0},{20,4},{24,8},{28,12},{1,17},{... | collective-permute-start | bytes 3981320 | tf_op jit(solution)/shard_map/ppermute | solution.py:596
  581.8 8.9 %all-to-all-start.3 = ((f32[4,1,1728]{2,1,0:T(1,128)}), f32[4,1,1728]{2,1,0:T(1,128)S(1)}, u32[]{:S(2)}, u32[]{:S(2)}) async-start(f32[4,1,1728]{2,1,0:T(1,128)} %all_to_all.44), calls=%async_computation.3 | async-start | bytes 57344 | tf_op jit(solution)/shard_map/all_to_all | solution.py:629
  590.6 8.4 %copy-start.3 = (bf16[4,576,288]{1,2,0:T(8,128)(2,1)S(1)}, bf16[4,576,288]{1,2,0:T(8,128)(2,1)}, u32[]{:S(2)}) copy-start(bf16[4,576,288]{1,2,0:T(8,128)(2,1)} %all_to_all.56) | copy-start | bytes 3981316
  590.6 34.4 %all-to-all-start.6 = ((bf16[4,144,1152]{2,1,0:T(8,128)(2,1)}), bf16[4,144,1152]{2,1,0:T(8,128)(2,1)S(1)}, u32[]{:S(2)}, u32[]{:S(2)}) async-start(bf16[4,144,1152]{2,1,0:T(8,128)(2,1)} %bitcast.39), calls=%async_computation.6 | async-start | bytes 2654208 | tf_op jit(solution)/shard_map/all_to_all | solution.py:629
  (4 other events, 5.1 us)

commit v3 on v2

--- a/solution.py
+++ b/solution.py
@@ -62,10 +62,6 @@
     return jax.ShapeDtypeStruct(dims, kind)
 
 
-def price(us):
-    return pl.CostEstimate(flops=0, transcendentals=0, bytes_accessed=int(us * 3.0e6))
-
-
 def params(**more):
     return pltpu.CompilerParams(vmem_limit_bytes=ROOM, **more)
 
@@ -91,7 +87,6 @@
         in_specs=[SMEM, VMEM, VMEM],
         out_specs=(VMEM, VMEM),
         compiler_params=params(),
-        cost_estimate=price(3),
         name="enter",
     )(slot, tokens, modulation)
 
@@ -177,7 +172,6 @@
         out_specs=(VMEM,) * 4,
         scratch_shapes=[pltpu.VMEM((total, HP), BF), pltpu.VMEM((heads * HD, total), F32)],
         compiler_params=params(),
-        cost_estimate=price(23),
         name="attend_forward",
     )(one, rank, *pieces, w, idk, idq)
 
@@ -283,7 +277,6 @@
             pltpu.VMEM((heads, total), F32),
         ],
         compiler_params=params(),
-        cost_estimate=price(23),
         name="attend_backward",
     )(one, rank, dos, qkv, o, lse, w, idk, idq)
 
@@ -423,7 +416,6 @@
         ]
         + [pltpu.SemaphoreType.DMA((4,)), pltpu.SemaphoreType.DMA((5,))],
         compiler_params=params(),
-        cost_estimate=price(41),
         name="middle",
     )(os, tokens, mods, dino, cot, wo, w1, w2, p1, p2, p3)
 
@@ -491,7 +483,6 @@
             pltpu.SemaphoreType.DMA((1,)),
         ],
         compiler_params=params(),
-        cost_estimate=price(20),
         name="descend",
     )(dmlp, gp, dy, normed, inv, attn, mods, w2, w1, wo)
 
@@ -514,22 +505,22 @@
         in_specs=[VMEM] * 4,
         out_specs=(VMEM, VMEM),
         compiler_params=params(),
-        cost_estimate=price(4.5),
         name="leave",
     )(parts, tokens, dh1, mods)
 
 
-def weight_grad_kernel(count, flat, rows, rows_ref, *refs):
+def weight_grad_kernel(count, flat, rows, packs, rows_ref, *refs):
     lefts = refs[:count]
     rights = refs[count : count * (1 + len(rows))]
-    send_ref, keep_ref, held_ref, sem = refs[count * (1 + len(rows)) :]
-    half, height, wide = send_ref.shape
+    outs = refs[count * (1 + len(rows)) : -2]
+    held_ref, sem = refs[-2:]
+    blocks = sum(packs)
     part = lefts[0].shape[1]
     copies, held_at, held = [], [], 0
     for job, deep in enumerate(rows):
         held_at.append(held)
-        for i in range(2 * half):
-            at = pl.ds(pl.multiple_of(rows_ref[job * 2 * half + i], 16), deep)
+        for i in range(blocks):
+            at = pl.ds(pl.multiple_of(rows_ref[job * blocks + i], 16), deep)
             for j in range(count):
                 copies.append(
                     pltpu.make_async_copy(
@@ -549,47 +540,86 @@
 
     dot = times_trans if flat else matmul
     for job, deep in enumerate(rows):
-        top = sum(rows[:job])
-        for out_ref, base in ((send_ref, held_at[job]), (keep_ref, held_at[job] + half * deep)):
+        base = held_at[job]
+        for spot, pack in enumerate(packs):
+            out_ref = outs[job * len(packs) + spot]
             total = None
             for j in range(count):
                 term = dot(
-                    held_ref[base : base + half * deep, j * part : (j + 1) * part], rights[job * count + j][...]
+                    held_ref[base : base + pack * deep, j * part : (j + 1) * part], rights[job * count + j][...]
                 )
                 total = term if total is None else total + term
-            out_ref[:, top : top + deep, :] = total.reshape(half, deep, wide).astype(BF)
-
-
-def weight_grad(lefts, rights, jobs, wide, step, flat=False):
+            out_ref[...] = total.reshape(out_ref.shape).astype(BF)
+            base += pack * deep
+
+
+def weight_grad(lefts, rights, jobs, packs, wide, step, flat=False):
     count = len(lefts)
-    half = jobs[0][0].shape[0] // 2
     part = lefts[0].shape[1]
     rows = tuple(job[1] for job in jobs)
-    height = sum(rows)
 
     def right_spec(base):
         if flat:
             return pl.BlockSpec((step, part), lambda i, b: (i + base, 0))
         return pl.BlockSpec((part, step), lambda i, b: (0, i + base))
 
-    out_spec = pl.BlockSpec((half, height, step), lambda i, b: (0, 0, i))
-    return pl.pallas_call(
-        functools.partial(weight_grad_kernel, count, flat, rows),
-        out_shape=(shape((half, height, wide)), shape((half, height, wide))),
+    outs = pl.pallas_call(
+        functools.partial(weight_grad_kernel, count, flat, rows, packs),
+        out_shape=tuple(shape((pack, deep, wide)) for deep in rows for pack in packs),
         grid_spec=pltpu.PrefetchScalarGridSpec(
             num_scalar_prefetch=1,
             grid=(wide // step,),
             in_specs=[ANY] * count + [right_spec(job[2]) for job in jobs for _ in range(count)],
-            out_specs=(out_spec, out_spec),
+            out_specs=tuple(
+                pl.BlockSpec((pack, deep, step), lambda i, b: (0, 0, i)) for deep in rows for pack in packs
+            ),
             scratch_shapes=[
-                pltpu.VMEM((2 * half * height, part * count), BF),
-                pltpu.SemaphoreType.DMA((2 * half * count * len(rows),)),
+                pltpu.VMEM((sum(packs) * sum(rows), part * count), BF),
+                pltpu.SemaphoreType.DMA((sum(packs) * count * len(rows),)),
             ],
         ),
         compiler_params=params(dimension_semantics=("arbitrary",)),
-        cost_estimate=price(3.0 + 1.2e-6 * count * half * height * wide),
         name="weight_grad",
     )(jnp.concatenate([job[0] for job in jobs]), *lefts, *(list(rights) * len(jobs)))
+    return [outs[i * len(packs) : (i + 1) * len(packs)] for i in range(len(jobs))]
+
+
+def split_kernel(rank_ref, keep_ref, got_ref, near_ref, far_ref, own_ref):
+    rows, cols = keep_ref.shape
+    size = near_ref.shape[0] * 2
+    block = cols // size
+    total = (keep_ref[...].astype(F32) + got_ref[...].astype(F32)).astype(BF)
+    for j in range(size):
+        piece = total[:, j * block : (j + 1) * block]
+        mask = j ^ rank_ref[0]
+
+        @pl.when(mask == 3)
+        def _():
+            near_ref[0] = piece
+
+        @pl.when(mask == 1)
+        def _():
+            near_ref[1] = piece
+
+        @pl.when(mask == 2)
+        def _():
+            far_ref[...] = piece
+
+        @pl.when(mask == 0)
+        def _():
+            own_ref[...] = piece
+
+
+def split(rank, keep, got):
+    rows, cols = keep.shape
+    return pl.pallas_call(
+        split_kernel,
+        out_shape=(shape((2, rows, cols // 4)), shape((rows, cols // 4)), shape((rows, cols // 4))),
+        in_specs=[SMEM, VMEM, VMEM],
+        out_specs=(VMEM,) * 3,
+        compiler_params=params(),
+        name="split",
+    )(rank, keep, got)
 
 
 def flip(x, axis, size, bit):
@@ -615,24 +645,13 @@
     return out
 
 
-def halve(send, keep, size, bits, swap):
-    for bit in bits[:-1]:
-        got = swap(send, bit)
-        half = keep.shape[0] // 2
-        send = add(keep[:half], got[:half])
-        keep = add(keep[half:], got[half:])
-    got = swap(send, bits[-1])
-    return add(keep, got)[0]
+def together(*values):
+    leaves, tree = jax.tree.flatten(values)
+    return jax.tree.unflatten(tree, lax.optimization_barrier(tuple(leaves)))
 
 
 def exchange(blocks):
     return lax.all_to_all(blocks, "seq", split_axis=0, concat_axis=0, tiled=True)
-
-
-def scatter_columns(share, size):
-    rows, cols = share.shape
-    blocks = jnp.transpose(share.reshape(rows, size, cols // size), (1, 0, 2))
-    return jnp.sum(exchange(blocks).astype(F32), axis=0)
 
 
 def shards(
@@ -679,60 +698,120 @@
         attended, tokens, mods, dino, cotangent, w_out, w_fc1, w_fc2, w_proj1, w_proj2, w_proj3
     )
 
-    fast = all(k % (16 * n_dp) == 0 for k in (width, hidden, wide)) and n_dp > 2
-    xy, yx = dp_bits[1:], dp_bits[:0:-1]
-    swap = lambda x, bit: flip(x, "dp", n_dp, bit)
-
-    def starts(base, deep, bits):
-        return base + (me ^ jnp.array(masks_of(bits), jnp.int32)) * (deep // n_dp)
-
-    def job(base, deep, bits, column):
-        return (starts(base, deep, bits), deep // n_dp, column)
+    fast = all(k % (16 * n_dp) == 0 for k in (width, hidden, wide)) and n_dp == 8 and n_seq == 4
+
+    def down(dmlp):
+        return descend(n_seq, dmlp, gelu_slope, dy, normed2, inv2, attn, mods, w_fc2, w_fc1, w_out)
+
+    def back(dos):
+        return attend_backward(
+            one, rank_arg, dos, qkv, heads_out, lse, w_rows, idk, idq, heads, tile, diagonal
+        )
 
     if fast:
-        lefts1, rights1 = [left1, swap(left1, 1)], [right1, swap(right1, 1)]
-        p21 = weight_grad(
-            lefts1, rights1, [job(wide, wide, xy, 0), job(2 * wide, width, xy, wide // STEP)], wide, STEP
-        )
-        rights1[0] = after(rights1[0], p21[0])
-        p3 = weight_grad(lefts1, rights1, [job(0, wide, yx, 2 * wide // 256)], narrow, 256)
-        lefts2 = [left2, swap(left2, 1)]
-        f2 = weight_grad(lefts2, [after(dmlp, p3[0]), swap(dmlp, 1)], [job(0, hidden, yx, 0)], width, 384)
-        dmlp = after(dmlp, f2[0])
-
-    right2, dhidden1, dheads, sums2 = descend(
-        n_seq, dmlp, gelu_slope, dy, normed2, inv2, attn, mods, w_fc2, w_fc1, w_out
-    )
-    dheads_in = exchange(dheads)
-    if fast:
-        rights2 = [right2, swap(right2, 1)]
-        f1 = weight_grad(lefts2, rights2, [job(hidden, width, xy, 0)], hidden, 1152)
-        rights2[0] = after(rights2[0], f1[0])
-        fo = weight_grad(lefts2, rights2, [job(hidden + width, width, yx, hidden // 384)], width, 384)
-        dheads_in = after(dheads_in, fo[0])
-    dqkv, dfirst_parts = attend_backward(
-        one, rank_arg, dheads_in, qkv, heads_out, lse, w_rows, idk, idq, heads, tile, diagonal
-    )
-
-    grad_inputs, sums1 = leave(exchange(dfirst_parts), tokens, dhidden1, mods)
-
-    dmods = jnp.concatenate([sums1[0:2], sums2[0:3], sum_gate2], axis=0)
-    dmods = exchange(dmods.reshape(n_seq, 6 * width // n_seq))
-    slot = jnp.arange(slots, dtype=jnp.int32)[:, None, None]
-    whose = image_ids[::tok_dev]
-    grad_mods = jnp.sum(jnp.where(slot == whose[None, :, None], dmods[None], 0.0), axis=1)
-
-    if fast:
-        rows = width // n_dp
-        fq = weight_grad([first_all], [dqkv], [job(0, width, dp_bits, 0)], 3 * local, 3 * local, flat=True)
-        g_p21 = scatter_columns(halve(*p21, n_dp, xy, swap), n_seq)
-        g_proj2, g_proj1 = g_p21[: wide // n_dp], g_p21[wide // n_dp :]
-        g_proj3 = scatter_columns(halve(*p3, n_dp, yx, swap), n_seq)
-        g_fc2 = scatter_columns(halve(*f2, n_dp, yx, swap), n_seq)
-        g_fc1 = scatter_columns(halve(*f1, n_dp, xy, swap), n_seq)
-        g_out = scatter_columns(halve(*fo, n_dp, yx, swap), n_seq)
-        g_heads = halve(*fq, n_dp, dp_bits, swap)
+        swap = lambda x, bit: flip(x, "dp", n_dp, bit)
+        core, x, y = dp_bits
+        near = lambda v: flip(v, "seq", n_seq, 1)
+        far = lambda v: flip(v, "seq", n_seq, 2)
+
+        def job(base, deep, bits, column):
+            starts = base + (me ^ jnp.array(masks_of(bits), jnp.int32)) * (deep // n_dp)
+            return (starts, deep // n_dp, column)
+
+        quarter = (1, 1, 1, 1)
+        lefts1, rights1 = [left1, swap(left1, core)], [right1, swap(right1, core)]
+        (p2, p1) = weight_grad(
+            lefts1, rights1, [job(wide, wide, (x, y), 0), job(2 * wide, width, (y, x), wide // STEP)],
+            quarter, wide, STEP,
+        )
+        left2_other, dmlp_other = swap(left2, core), swap(dmlp, core)
+        lefts1, rights1, p2, p1, left2_other, dmlp_other = together(
+            lefts1, rights1, p2, p1, left2_other, dmlp_other
+        )
+
+        p2a, p1a, p1b = swap(p2[0], x), swap(p1[0], y), swap(p1[1], y)
+        lefts2 = [left2, left2_other]
+        (f2,) = weight_grad(lefts2, [dmlp, dmlp_other], [job(0, hidden, (y, x), 0)], quarter, width, 384)
+        rights1 = together(rights1, f2)[0]
+        (p3,) = weight_grad(lefts1, rights1, [job(0, wide, (x, y), 2 * wide // 256)], quarter, narrow, 256)
+        p2a, p1a, p1b, f2, p3, p2, p1, dmlp = together(p2a, p1a, p1b, f2, p3, p2, p1, dmlp)
+
+        p2b, f2a = swap(p2[1], x), swap(f2[0], y)
+        right2, dhidden1, dheads, sums2 = down(dmlp)
+        p1s = add(p1[2], p1a)
+        p2b, f2a, right2, dhidden1, dheads, sums2, p1s, f2, p3, p2a = together(
+            p2b, f2a, right2, dhidden1, dheads, sums2, p1s, f2, p3, p2a
+        )
+
+        dheads_in = exchange(dheads)
+        rights2 = [right2, swap(right2, core)]
+        p1c, p3a, p3b, f2b = swap(p1s, x), swap(p3[0], x), swap(p3[1], x), swap(f2[1], y)
+        p2s, f2s = add(p2[2], p2a), add(f2[2], f2a)
+        (f1,) = weight_grad(lefts2, rights2, [job(hidden, width, (x, y), 0)], quarter, hidden, 1152)
+        rights2 = together(rights2, f1)[0]
+        (fo,) = weight_grad(
+            lefts2, rights2, [job(hidden + width, width, (y, x), hidden // 384)], quarter, width, 384
+        )
+        dheads_in, p1c, p3a, p3b, f2b, p2s, f2s, f1, fo, p3 = together(
+            dheads_in, p1c, p3a, p3b, f2b, p2s, f2s, f1, fo, p3
+        )
+
+        f2c, p2c = swap(f2s, x), swap(p2s, y)
+        dqkv, dfirst_parts = back(dheads_in)
+        p1n, p1f, p1o = split(rank_arg, add(p1[3], p1b)[0], p1c[0])
+        p3s = add(p3[2], p3a)
+        f2c, p2c, dqkv, dfirst_parts, p1n, p1f, p1o, p3s, f1, fo, p3b = together(
+            f2c, p2c, dqkv, dfirst_parts, p1n, p1f, p1o, p3s, f1, fo, p3b
+        )
+
+        dfirst_in = exchange(dfirst_parts)
+        f1a, foa, fob, p3c, p1z = swap(f1[0], x), swap(fo[0], y), swap(fo[1], y), swap(p3s, y), near(p1n)
+        (fq,) = weight_grad(
+            [first_all], [dqkv], [job(0, width, (core, y, x), 0)], (4, 2, 2), 3 * local, 3 * local, flat=True
+        )
+        fqa = swap(fq[0], core)
+        f2n, f2f, f2o = split(rank_arg, add(f2[3], f2b)[0], f2c[0])
+        p2n, p2f, p2o = split(rank_arg, add(p2[3], p2b)[0], p2c[0])
+        f1a, foa, fob, p3c, p1z, fq, fqa, f2n, p2n, f1, fo = together(
+            f1a, foa, fob, p3c, p1z, fq, fqa, f2n, p2n, f1, fo
+        )
+
+        fqs, fqk = add(fq[1], fqa[:2]), add(fq[2], fqa[2:])
+        f1b, f1s, p2z = swap(f1[1], x), add(f1[2], f1a), near(p2n)
+        fqb = swap(fqs, y)
+        fos = add(fo[2], foa)
+        p1y = far(add(p1f, p1z[0]))
+        p1o = add(p1o, p1z[1])
+        p3n, p3f, p3o = split(rank_arg, add(p3[3], p3b)[0], p3c[0])
+        f1b, f1s, p2z, fqb, fos, p1y, p1o, p3n, f2n, fqk, f1 = together(
+            f1b, f1s, p2z, fqb, fos, p1y, p1o, p3n, f2n, fqk, f1
+        )
+
+        f1c, foc, f2z = swap(f1s, y), swap(fos, x), near(f2n)
+        fqs, fqk = add(fqk[0], fqb[0]), add(fqk[1], fqb[1])
+        fqc = swap(fqs, x)
+        p2y = far(add(p2f, p2z[0]))
+        p2o = add(p2o, p2z[1])
+        g_proj1 = p1o.astype(F32) + p1y.astype(F32)
+        grad_inputs, sums1 = leave(dfirst_in, tokens, dhidden1, mods)
+        f1c, foc, f2z, fqk, fqc, p2y, p2o, p3n, sums1 = together(f1c, foc, f2z, fqk, fqc, p2y, p2o, p3n, sums1)
+
+        f1n, f1f, f1o = split(rank_arg, add(f1[3], f1b)[0], f1c[0])
+        fon, fof, foo = split(rank_arg, add(fo[3], fob)[0], foc[0])
+        f1z, f2y, p3z, foz = near(f1n), far(add(f2f, f2z[0])), near(p3n), near(fon)
+        f2o = add(f2o, f2z[1])
+        g_heads = add(fqk, fqc)
+        g_proj2 = p2o.astype(F32) + p2y.astype(F32)
+        f1z, f2y, p3z, foz, f1f, fof, f2o, f1o, foo = together(f1z, f2y, p3z, foz, f1f, fof, f2o, f1o, foo)
+
+        f1y, p3y, foy = far(add(f1f, f1z[0])), far(add(p3f, p3z[0])), far(add(fof, foz[0]))
+        g_fc2 = f2o.astype(F32) + f2y.astype(F32)
+        last = lambda own, z, far_got: own.astype(F32) + z[1].astype(F32) + far_got.astype(F32)
+        g_fc1, g_proj3, g_out = last(f1o, f1z, f1y), last(p3o, p3z, p3y), last(foo, foz, foy)
     else:
+        right2, dhidden1, dheads, sums2 = down(dmlp)
+        dqkv, dfirst_parts = back(exchange(dheads))
+        grad_inputs, sums1 = leave(exchange(dfirst_parts), tokens, dhidden1, mods)
 
         def reduced(a, b):
             share = lax.psum_scatter(matmul(a, b).astype(BF), "dp", scatter_dimension=0, tiled=True)
@@ -747,6 +826,12 @@
         g_heads = lax.psum_scatter(
             times_trans(first_all, dqkv).astype(BF), "dp", scatter_dimension=0, tiled=True
         )
+
+    dmods = jnp.concatenate([sums1[0:2], sums2[0:3], sum_gate2], axis=0)
+    dmods = exchange(dmods.reshape(n_seq, 6 * width // n_seq))
+    slot = jnp.arange(slots, dtype=jnp.int32)[:, None, None]
+    whose = image_ids[::tok_dev]
+    grad_mods = jnp.sum(jnp.where(slot == whose[None, :, None], dmods[None], 0.0), axis=1)
 
     units = [g_heads[:, i * local : (i + 1) * local] for i in range(3)]
     outgoing = []

time: 635 us -> 494 us (0.78)
  waiting for transfers between devices: 298 us -> 164 us
  blocking collectives: 56.9 us -> 15.7 us
  Pallas kernels: 138 us -> 168 us
  other arithmetic: 39.7 us -> 53.2 us
  local copies, waits for them, and re-layouts: 29.2 us -> 21.4 us
    ppermute x18 -> x38, waiting for transfers between devices: 200 us -> 122 us  [flip(): return lax.ppermute(x, axis, [(i, i ^ bit) for i in range(size)])]
    all_to_all x8 -> x4, waiting for transfers between devices: 65.2 us -> 9.24 us  [exchange(): lax.all_to_all(blocks, 'seq', split_axis=0, concat_axis=0, tiled=True)]
    all_to_all x2 -> x1, blocking collectives: 56.9 us -> 15.7 us  [exchange(): lax.all_to_all(blocks, 'seq', split_axis=0, concat_axis=0, tiled=True)]
    pallas_call x6 -> x12, Pallas kernels: 45.6 us -> 63.8 us  [the longest x6 45.4 us: weight_grad(): pl.pallas_call(functools.partial(weight_grad_kernel, count, flat, rows, p...]
    ppermute x18 -> x38, starting transfers between devices: 20.7 us -> 36.9 us  [flip(): return lax.ppermute(x, axis, [(i, i ^ bit) for i in range(size)])]
    all_to_all x8 -> x4, starting transfers between devices: 30 us -> 14.5 us  [exchange(): lax.all_to_all(blocks, 'seq', split_axis=0, concat_axis=0, tiled=True)]
    squeeze x1 -> x6, other arithmetic: 1.04 us -> 13 us  [the longest x1 3.09 us: shards(): f1n, f1f, f1o = split(rank_arg, add(f1[3], f1b)[0], f1c[0])]
    another operation x6 -> x0, local copies, waits for them, and re-layouts: 10.4 us -> none  [scatter_columns(): blocks = jnp.transpose(share.reshape(rows, size, cols // size), (1, 0, 2))]
  transfers between devices with their start and end apart: 32 -> 48, of which waited for: 17 -> 21; matrix products, arithmetic and copies ran while one was open for 10% -> 13% of each run, Pallas kernels for 9% -> 20%
where the time goes in v3:
time: 494 us; the launch traced here: 488 us
  Pallas kernels  168 us (34%)
  waiting for transfers between devices  164 us (33%)
  starting transfers between devices  63.2 us (13%)
  other arithmetic  53.2 us (11%)
  local copies, waits for them, and re-layouts  21.4 us (4%)
  blocking collectives  15.7 us (3%)
    ppermute x38, waiting for transfers between devices, flip(): return lax.ppermute(x, axis, [(i, i ^ bit) for i in range(size)])  122 us
    pallas_call x6, Pallas kernels, weight_grad(): pl.pallas_call(functools.partial(weight_grad_kernel, count, flat, rows, p...  45.4 us
    pallas_call x1, Pallas kernels, middle(): pl.pallas_call(middle_kernel, out_shape=(shape((tok, width)), shape((2 *...  37.9 us
    ppermute x38, starting transfers between devices, flip(): return lax.ppermute(x, axis, [(i, i ^ bit) for i in range(size)])  36.9 us
    convert_element_type x15, other arithmetic, add(): return (a.astype(F32) + b.astype(F32)).astype(BF)  26.5 us
    pallas_call x1, Pallas kernels, attend_backward(): pl.pallas_call(functools.partial(attend_backward_kernel, size, heads, til...  21.2 us
    pallas_call x1, Pallas kernels, attend_forward(): pl.pallas_call(functools.partial(attend_forward_kernel, size, heads, tile...  20.8 us
    ppermute x3, waiting for transfers between devices, shards(): lax.ppermute(left[-1], 'seq', [(i, i - 1) for i in range(1, n_seq - s + 1)])  20.6 us
  transfers between devices with their start and end apart: 48, of which 21 were waited for; matrix products, arithmetic and copies ran while one was open for 13% of the time, Pallas kernels for 20%

profile of v3, /device:TPU:0, one launch (start us, length us, event | category | flops | bytes accessed | tf_op | source)
XLA Modules:
  0.0 487.6 jit_solution(10241350906334313670)
XLA Ops:
  2.0 3.1 enter.1
  5.1 5.0 %collective-permute-start.1 = (bf16[1152,256]{1,0:T(8,128)(2,1)}, bf16[1152,256]{1,0:T(8,128)(2,1)S(1)}, u32[]{:S(2)}, u32[]{:S(2)}) collective-permute-start(bf16[1152,256]{1,0:T(8,128)(2,1)} %get-tuple-element.208.refs_0_), channel_id=1, source_target_pairs={{0,1},{1,2},{2,3},{4,5},{5,6},{6,7},{8,9},{9,10},{10,11},{12,13},{... | collective-permute-start | bytes 1769480 | tf_op jit(solution)/shard_map/ppermute | solution.py:678
  11.4 11.5 %collective-permute-done.1.refs_6_ = bf16[1152,256]{1,0:T(8,128)(2,1)S(1)} collective-permute-done((bf16[1152,256]{1,0:T(8,128)(2,1)}, bf16[1152,256]{1,0:T(8,128)(2,1)S(1)}, u32[]{:S(2)}, u32[]{:S(2)}) %collective-permute-start.1) | collective-permute-done | bytes 589856 | tf_op jit(solution)/shard_map/ppermute | solution.py:678
  24.4 2.6 collective-permute-done.refs_1_
  29.7 14.0 %collective-permute-done.4.refs_3_ = bf16[1152,256]{1,0:T(8,128)(2,1)} collective-permute-done((bf16[1152,256]{1,0:T(8,128)(2,1)S(1)}, bf16[1152,256]{1,0:T(8,128)(2,1)}, u32[]{:S(2)}, u32[]{:S(2)}) %collective-permute-start.4) | collective-permute-done | bytes 589856 | tf_op jit(solution)/shard_map/ppermute | solution.py:679
  45.0 3.5 constant_dynamic-slice_fusion.2
  55.2 4.1 collective-permute-done.5.refs_5_
  59.2 20.8 %attend_forward.1 = (bf16[1152,1024]{1,0:T(8,128)(2,1)}, bf16[4,288,256]{2,1,0:T(8,128)(2,1)}, bf16[960,1024]{1,0:T(8,128)(2,1)}, f32[4,1024]{1,0:T(4,128)}) custom-call(s32[1]{0:T(128)S(6)} %convert_element_type.334.one_ref, s32[1]{0:T(128)} %bitcast.rank_ref, bf16[1152,256]{1,0:T(8,128)(2,1)} %get-tuple-element.208.refs_0_, bf16[1152,256]{1,0:T(8,128)(2,1)} %copy-done.14, ...), custom_call_target="tpu_custom_call" | custom-call | tf_op jit(solution)/shard_map/attend_forward/pallas_call | solution.py:163
  80.0 15.7 %all_to_all.30.refs_0_ = bf16[4,288,256]{2,1,0:T(8,128)(2,1)} all-to-all(bf16[4,288,256]{2,1,0:T(8,128)(2,1)} %get-tuple-element.209.refs_2_), channel_id=1, replica_groups=mesh['dp'=8,'seq'=4] {'seq'}, dimensions={0} | all-to-all | bytes 1179648 | tf_op jit(solution)/shard_map/all_to_all | solution.py:654
  95.7 37.9 %middle.1 = (bf16[256,1152]{1,0:T(8,128)(2,1)}, bf16[5248,256]{1,0:T(8,128)(2,1)}, bf16[6912,256]{1,0:T(8,128)(2,1)}, bf16[256,4864]{1,0:T(8,128)(2,1)}, bf16[25...) custom-call(bf16[4,288,256]{2,1,0:T(8,128)(2,1)} %all_to_all.30.refs, ...), custom_call_target="tpu_custom_call" | custom-call | tf_op jit(solution)/shard_map/middle/pallas_call | solution.py:404
  136.0 11.7 %collective-permute-done.7.refs_3_.refs_5_ = bf16[256,4864]{1,0:T(8,128)(2,1)} collective-permute-done((bf16[256,4864]{1,0:T(8,128)(2,1)}, bf16[256,4864]{1,0:T(8,128)(2,1)}, u32[]{:S(2)}, u32[]{:S(2)}) %collective-permute-start.7) | collective-permute-done | bytes 2490400 | tf_op jit(solution)/shard_map/ppermute | solution.py:626
  147.7 9.0 %weight_grad.6 = (bf16[1,256,2048]{2,1,0:T(8,128)(2,1)}, bf16[1,256,2048]{2,1,0:T(8,128)(2,1)}, bf16[1,256,2048]{2,1,0:T(8,128)(2,1)}, bf16[1,256,2048]{2,1,0:T(...) custom-call(s32[8]{0:T(128)} %pad_add_fusion.rows_ref, ...), custom_call_target="tpu_custom_call" | custom-call | tf_op jit(solution)/shard_map/weight_grad/pallas_call | solution.py:566
  158.9 8.6 %weight_grad.7 = (bf16[1,576,1152]{2,1,0:T(8,128)(2,1)}, bf16[1,576,1152]{2,1,0:T(8,128)(2,1)}, bf16[1,576,1152]{2,1,0:T(8,128)(2,1)}, bf16[1,576,1152]{2,1,0:T(8,128)(2,1)}) custom-call(s32[4]{0:T(128)} %get-tuple-element.477.rows_ref, bf16[6912,256]{1,0:T(8,128)(2,1)} %get-tuple-element.222.refs_0_, bf16[6912,256]{1,0:T(8,128)(2,1)} %copy-done, ...), custom_call_target="tpu_custom_call" | custom-call | tf_op jit(solution)/shard_map/weight_grad/pallas_call | solution.py:566
  167.5 5.8 %weight_grad.8 = (bf16[1,256,768]{2,1,0:T(8,128)(2,1)}, bf16[1,256,768]{2,1,0:T(8,128)(2,1)}, bf16[1,256,768]{2,1,0:T(8,128)(2,1)}, bf16[1,256,768]{2,1,0:T(8,128)(2,1)}) custom-call(s32[4]{0:T(128)} %get-tuple-element.475.rows_ref, bf16[5248,256]{1,0:T(8,128)(2,1)} %get-tuple-element.233.refs_0_, bf16[5248,256]{1,0:T(8,128)(2,1)} %collective-permute-done.6.refs_1_, ...), custom_call_target="tpu_custom_call" | custom-call | tf_op jit(solution)/shard_map/weight_grad/pallas_call | solution.py:566
  173.4 11.8 %collective-permute-done.12 = bf16[1,144,2048]{2,1,0:T(8,128)(2,1)} collective-permute-done((bf16[1,144,2048]{2,1,0:T(8,128)(2,1)}, bf16[1,144,2048]{2,1,0:T(8,128)(2,1)}, u32[]{:S(2)}, u32[]{:S(2)}) %collective-permute-start.12) | collective-permute-done | bytes 589856 | tf_op jit(solution)/shard_map/ppermute | solution.py:626
  188.4 16.9 %descend.1 = (bf16[256,5760]{1,0:T(8,128)(2,1)}, f32[256,1152]{1,0:T(8,128)}, bf16[4,288,256]{2,1,0:T(8,128)(2,1)}, f32[8,1152]{1,0:T(8,128)}) custom-call(bf16[256,1152]{1,0:T(8,128)(2,1)} %get-tuple-element.250.refs_2_.refs_0_, bf16[256,4608]{1,0:T(8,128)(2,1)} %get-tuple-element.251.refs_1_, f32[256,1152]{1,0:T(8,128)} %get-tuple-element.252.refs_2_, ...), custom_call_target="tpu_custom_call" | custom-call | tf_op jit(solution)/shard_map/descend/pallas_call | solution.py:471
  207.4 3.4 collective-permute-done.13
  210.8 5.0 %collective-permute-done.14 = bf16[1,576,1152]{2,1,0:T(8,128)(2,1)S(1)} collective-permute-done((bf16[1,576,1152]{2,1,0:T(8,128)(2,1)}, bf16[1,576,1152]{2,1,0:T(8,128)(2,1)S(1)}, u32[]{:S(2)}, u32[]{:S(2)}) %collective-permute-start.14) | collective-permute-done | bytes 1327136 | tf_op jit(solution)/shard_map/ppermute | solution.py:626
  221.8 3.5 all-to-all-start.1
  225.3 3.2 add_convert_fusion.3
  228.5 2.6 add_convert_fusion.5
  232.7 8.5 %weight_grad.9 = (bf16[1,144,4608]{2,1,0:T(8,128)(2,1)}, bf16[1,144,4608]{2,1,0:T(8,128)(2,1)}, bf16[1,144,4608]{2,1,0:T(8,128)(2,1)}, bf16[1,144,4608]{2,1,0:T(8,128)(2,1)}) custom-call(s32[4]{0:T(128)} %get-tuple-element.473.rows_ref, bf16[6912,256]{1,0:T(8,128)(2,1)} %get-tuple-element.222.refs_0_, bf16[6912,256]{1,0:T(8,128)(2,1)} %copy-done, ...), custom_call_target="tpu_custom_call" | custom-call | tf_op jit(solution)/shard_map/weight_grad/pallas_call | solution.py:566
  241.3 5.7 %weight_grad.10 = (bf16[1,144,1152]{2,1,0:T(8,128)(2,1)}, bf16[1,144,1152]{2,1,0:T(8,128)(2,1)}, bf16[1,144,1152]{2,1,0:T(8,128)(2,1)}, bf16[1,144,1152]{2,1,0:T(8,128)(2,1)}) custom-call(s32[4]{0:T(128)} %get-tuple-element.478.rows_ref, bf16[6912,256]{1,0:T(8,128)(2,1)} %get-tuple-element.222.refs_0_, bf16[6912,256]{1,0:T(8,128)(2,1)} %copy-done, ...), custom_call_target="tpu_custom_call" | custom-call | tf_op jit(solution)/shard_map/weight_grad/pallas_call | solution.py:566
  247.0 4.0 collective-permute-done.17
  255.9 2.4 split.6
  258.3 21.2 %attend_backward.1 = (bf16[864,1024]{1,0:T(8,128)(2,1)}, bf16[4,256,1152]{2,1,0:T(8,128)(2,1)}) custom-call(s32[1]{0:T(128)S(6)} %convert_element_type.334.one_ref, s32[1]{0:T(128)} %bitcast.rank_ref, bf16[4,288,256]{2,1,0:T(8,128)(2,1)} %copy-done.3, bf16[960,1024]{1,0:T(8,128)(2,1)} %get-tuple-element.295.refs_1_, ...), custom_call_target="tpu_custom_call" | custom-call | tf_op jit(solution)/shard_map/attend_backward/pallas_call | solution.py:265
  281.6 7.7 %weight_grad.11 = (bf16[4,144,864]{2,1,0:T(8,128)(2,1)}, bf16[2,144,864]{2,1,0:T(8,128)(2,1)}, bf16[2,144,864]{2,1,0:T(8,128)(2,1)}) custom-call(s32[8]{0:T(128)} %xor_multiply_fusion.4.rows_ref, bf16[1152,1024]{1,0:T(8,128)(2,1)} %get-tuple-element.324.refs_0_, bf16[864,1024]{1,0:T(8,128)(2,1)} %get-tuple-element.325.refs_1_), custom_call_target="tpu_custom_call" | custom-call | tf_op jit(solution)/shard_map/weight_grad/pallas_call | solution.py:566
  295.3 4.7 collective-permute-done.26
  300.6 2.7 fusion.keep_ref
  303.3 3.6 all-to-all-start.2
  306.9 3.2 split.8
  310.1 4.5 split.7
  318.7 2.6 collective-permute-done.22
  329.2 2.8 add_convert_fusion.1
  335.5 2.3 split.9
  337.8 28.8 %collective-permute-done.31 = bf16[144,512]{1,0:T(8,128)(2,1)} collective-permute-done((bf16[144,512]{1,0:T(8,128)(2,1)}, bf16[144,512]{1,0:T(8,128)(2,1)}, u32[]{:S(2)}, u32[]{:S(2)}) %collective-permute-start.31) | collective-permute-done | bytes 147488 | tf_op jit(solution)/shard_map/ppermute | solution.py:626
  378.9 3.1 fusion.1.keep_ref
  385.1 4.1 leave.1
  389.2 7.8 %collective-permute-done.34 = bf16[2,576,288]{1,2,0:T(8,128)(2,1)} collective-permute-done((bf16[2,576,288]{1,2,0:T(8,128)(2,1)}, bf16[2,576,288]{1,2,0:T(8,128)(2,1)}, u32[]{:S(2)}, u32[]{:S(2)}) %collective-permute-start.34) | collective-permute-done | bytes 663584 | tf_op jit(solution)/shard_map/ppermute | solution.py:626
  397.0 8.4 %collective-permute-done.32 = bf16[1,144,4608]{2,1,0:T(8,128)(2,1)} collective-permute-done((bf16[1,144,4608]{2,1,0:T(8,128)(2,1)}, bf16[1,144,4608]{2,1,0:T(8,128)(2,1)}, u32[]{:S(2)}, u32[]{:S(2)}) %collective-permute-start.32) | collective-permute-done | bytes 1327136 | tf_op jit(solution)/shard_map/ppermute | solution.py:626
  405.4 2.3 split.11
  410.5 3.9 all-to-all-start.3
  420.1 3.5 all-to-all-start.4
  424.6 2.9 collective-permute-start.38
  427.4 3.6 split.10
  435.7 7.3 %all-to-all-done.4 = bf16[4,144,288]{2,1,0:T(8,128)(2,1)S(1)} async-done(((bf16[4,144,288]{2,1,0:T(8,128)(2,1)}), bf16[4,144,288]{2,1,0:T(8,128)(2,1)S(1)}, u32[]{:S(2)}, u32[]{:S(2)}) %all-to-all-start.4) | async-done | bytes 331808 | tf_op jit(solution)/shard_map/all_to_all | solution.py:654
  444.0 17.1 %collective-permute-done.39 = bf16[2,256,192]{2,1,0:T(8,128)(2,1)S(1)} collective-permute-done((bf16[2,256,192]{2,1,0:T(8,128)(2,1)S(1)}, bf16[2,256,192]{2,1,0:T(8,128)(2,1)S(1)}, u32[]{:S(2)}, u32[]{:S(2)}) %collective-permute-start.39) | collective-permute-done | bytes 196640 | tf_op jit(solution)/shard_map/ppermute | solution.py:626
  468.4 13.5 %collective-permute-done.41 = bf16[144,288]{1,0:T(8,128)(2,1)} collective-permute-done((bf16[144,288]{1,0:T(8,128)(2,1)}, bf16[144,288]{1,0:T(8,128)(2,1)}, u32[]{:S(2)}, u32[]{:S(2)}) %collective-permute-start.41) | collective-permute-done | bytes 82976 | tf_op jit(solution)/shard_map/ppermute | solution.py:626
  (209 shorter events, 103.0 us)
Async XLA Ops:
  5.1 17.8 %collective-permute-start.1 = (bf16[1152,256]{1,0:T(8,128)(2,1)}, bf16[1152,256]{1,0:T(8,128)(2,1)S(1)}, u32[]{:S(2)}, u32[]{:S(2)}) collective-permute-start(bf16[1152,256]{1,0:T(8,128)(2,1)} %get-tuple-element.208.refs_0_), channel_id=1, source_target_pairs={{0,1},{1,2},{2,3},{4,5},{5,6},{6,7},{8,9},{9,10},{10,11},{12,13},{... | collective-permute-start | bytes 1769480 | tf_op jit(solution)/shard_map/ppermute | solution.py:678
  10.1 16.9 %collective-permute-start = (bf16[1152,256]{1,0:T(8,128)(2,1)}, bf16[1152,256]{1,0:T(8,128)(2,1)S(1)}, u32[]{:S(2)}, u32[]{:S(2)}) collective-permute-start(bf16[1152,256]{1,0:T(8,128)(2,1)} %get-tuple-element.208.refs_0_), channel_id=1, source_target_pairs={{1,0},{2,1},{3,2},{5,4},{6,5},{7,6},{9,8},{10,9},{11,10},{13,12},{... | collective-permute-start | bytes 1769480 | tf_op jit(solution)/shard_map/ppermute | solution.py:679
  22.9 5.3 %collective-permute-start.2 = (bf16[1152,256]{1,0:T(8,128)(2,1)S(1)}, bf16[1152,256]{1,0:T(8,128)(2,1)}, u32[]{:S(2)}, u32[]{:S(2)}) collective-permute-start(bf16[1152,256]{1,0:T(8,128)(2,1)S(1)} %collective-permute-done.1.refs_6_), channel_id=1, source_target_pairs={{1,2},{2,3},{5,6},{6,7},{9,10},{10,11},{13,14},{14,15},{17,18},{18... | collective-permute-start | bytes 1769480 | tf_op jit(solution)/shard_map/ppermute | solution.py:678
  27.0 16.8 %collective-permute-start.4 = (bf16[1152,256]{1,0:T(8,128)(2,1)S(1)}, bf16[1152,256]{1,0:T(8,128)(2,1)}, u32[]{:S(2)}, u32[]{:S(2)}) collective-permute-start(bf16[1152,256]{1,0:T(8,128)(2,1)S(1)} %collective-permute-done.refs_1_), channel_id=1, source_target_pairs={{1,0},{2,1},{5,4},{6,5},{9,8},{10,9},{13,12},{14,13},{17,16},{18,1... | collective-permute-start | bytes 1769480 | tf_op jit(solution)/shard_map/ppermute | solution.py:679
  28.3 26.9 %collective-permute-start.3 = (bf16[1152,256]{1,0:T(8,128)(2,1)}, bf16[1152,256]{1,0:T(8,128)(2,1)}, u32[]{:S(2)}, u32[]{:S(2)}) collective-permute-start(bf16[1152,256]{1,0:T(8,128)(2,1)} %collective-permute-done.2.refs_4_), channel_id=1, source_target_pairs={{2,3},{6,7},{10,11},{14,15},{18,19},{22,23},{26,27},{30,31}} | collective-permute-start | bytes 1769480 | tf_op jit(solution)/shard_map/ppermute | solution.py:678
  43.8 15.5 %collective-permute-start.5 = (bf16[1152,256]{1,0:T(8,128)(2,1)}, bf16[1152,256]{1,0:T(8,128)(2,1)}, u32[]{:S(2)}, u32[]{:S(2)}) collective-permute-start(bf16[1152,256]{1,0:T(8,128)(2,1)} %collective-permute-done.4.refs_3_), channel_id=1, source_target_pairs={{1,0},{5,4},{9,8},{13,12},{17,16},{21,20},{25,24},{29,28}} | collective-permute-start | bytes 1769480 | tf_op jit(solution)/shard_map/ppermute | solution.py:679
  133.6 23.1 %collective-permute-start.8 = (bf16[6912,256]{1,0:T(8,128)(2,1)}, bf16[6912,256]{1,0:T(8,128)(2,1)S(1)}, u32[]{:S(2)}, u32[]{:S(2)}) collective-permute-start(bf16[6912,256]{1,0:T(8,128)(2,1)} %get-tuple-element.222.refs_0_), channel_id=1, source_target_pairs={{0,4},{4,0},{8,12},{12,8},{16,20},{20,16},{24,28},{28,24},{1,5},{5... | collective-permute-start | bytes 10616840 | tf_op jit(solution)/shard_map/ppermute | solution.py:626
  133.7 14.0 %collective-permute-start.6 = (bf16[5248,256]{1,0:T(8,128)(2,1)}, bf16[5248,256]{1,0:T(8,128)(2,1)}, u32[]{:S(2)}, u32[]{:S(2)}) collective-permute-start(bf16[5248,256]{1,0:T(8,128)(2,1)} %get-tuple-element.233.refs_0_), channel_id=1, source_target_pairs={{0,4},{4,0},{8,12},{12,8},{16,20},{20,16},{24,28},{28,24},{1,5},{5... | collective-permute-start | bytes 8060936 | tf_op jit(solution)/shard_map/ppermute | solution.py:626
  134.2 13.5 %collective-permute-start.7 = (bf16[256,4864]{1,0:T(8,128)(2,1)}, bf16[256,4864]{1,0:T(8,128)(2,1)}, u32[]{:S(2)}, u32[]{:S(2)}) collective-permute-start(bf16[256,4864]{1,0:T(8,128)(2,1)} %get-tuple-element.237.refs_2_.refs_4_), channel_id=1, source_target_pairs={{0,4},{4,0},{8,12},{12,8},{16,20},{20,16},{24,28},{28,24},{1,5},{5... | collective-permute-start | bytes 7471112 | tf_op jit(solution)/shard_map/ppermute | solution.py:626
  134.3 22.4 %collective-permute-start.9 = (bf16[256,1152]{1,0:T(8,128)(2,1)}, bf16[256,1152]{1,0:T(8,128)(2,1)}, u32[]{:S(2)}, u32[]{:S(2)}) collective-permute-start(bf16[256,1152]{1,0:T(8,128)(2,1)} %get-tuple-element.250.refs_2_.refs_0_), channel_id=1, source_target_pairs={{0,4},{4,0},{8,12},{12,8},{16,20},{20,16},{24,28},{28,24},{1,5},{5... | collective-permute-start | bytes 1769480 | tf_op jit(solution)/shard_map/ppermute | solution.py:626
  156.7 28.5 %collective-permute-start.10 = (bf16[1,256,2048]{2,1,0:T(8,128)(2,1)}, bf16[1,256,2048]{2,1,0:T(8,128)(2,1)}, u32[]{:S(2)}, u32[]{:S(2)}) collective-permute-start(bf16[1,256,2048]{2,1,0:T(8,128)(2,1)} %get-tuple-element.224), channel_id=1, source_target_pairs={{0,8},{4,12},{8,0},{12,4},{16,24},{20,28},{24,16},{28,20},{1,9},{5... | collective-permute-start | bytes 3145736 | tf_op jit(solution)/shard_map/ppermute | solution.py:626
  156.8 16.6 %collective-permute-start.11 = (bf16[1,144,2048]{2,1,0:T(8,128)(2,1)}, bf16[1,144,2048]{2,1,0:T(8,128)(2,1)}, u32[]{:S(2)}, u32[]{:S(2)}) collective-permute-start(bf16[1,144,2048]{2,1,0:T(8,128)(2,1)} %get-tuple-element.225), channel_id=1, source_target_pairs={{0,16},{4,20},{8,24},{12,28},{16,0},{20,4},{24,8},{28,12},{1,17},{... | collective-permute-start | bytes 1769480 | tf_op jit(solution)/shard_map/ppermute | solution.py:626
  158.4 26.8 %collective-permute-start.12 = (bf16[1,144,2048]{2,1,0:T(8,128)(2,1)}, bf16[1,144,2048]{2,1,0:T(8,128)(2,1)}, u32[]{:S(2)}, u32[]{:S(2)}) collective-permute-start(bf16[1,144,2048]{2,1,0:T(8,128)(2,1)} %get-tuple-element.226), channel_id=1, source_target_pairs={{0,16},{4,20},{8,24},{12,28},{16,0},{20,4},{24,8},{28,12},{1,17},{... | collective-permute-start | bytes 1769480 | tf_op jit(solution)/shard_map/ppermute | solution.py:626
  185.2 30.5 %collective-permute-start.14 = (bf16[1,576,1152]{2,1,0:T(8,128)(2,1)}, bf16[1,576,1152]{2,1,0:T(8,128)(2,1)S(1)}, u32[]{:S(2)}, u32[]{:S(2)}) collective-permute-start(bf16[1,576,1152]{2,1,0:T(8,128)(2,1)} %get-tuple-element.249), channel_id=1, source_target_pairs={{0,16},{4,20},{8,24},{12,28},{16,0},{20,4},{24,8},{28,12},{1,17},{... | collective-permute-start | bytes 3981320 | tf_op jit(solution)/shard_map/ppermute | solution.py:626
  186.7 24.1 %collective-permute-start.13 = (bf16[1,256,2048]{2,1,0:T(8,128)(2,1)S(1)}, bf16[1,256,2048]{2,1,0:T(8,128)(2,1)S(1)}, u32[]{:S(2)}, u32[]{:S(2)}) collective-permute-start(bf16[1,256,2048]{2,1,0:T(8,128)(2,1)S(1)} %copy-done.39), channel_id=1, source_target_pairs={{0,8},{4,12},{8,0},{12,4},{16,24},{20,28},{24,16},{28,20},{1,9},{5... | collective-permute-start | bytes 3145736 | tf_op jit(solution)/shard_map/ppermute | solution.py:626
  216.9 14.2 %collective-permute-start.19 = (bf16[256,5760]{1,0:T(8,128)(2,1)}, bf16[256,5760]{1,0:T(8,128)(2,1)S(1)}, u32[]{:S(2)}, u32[]{:S(2)}) collective-permute-start(bf16[256,5760]{1,0:T(8,128)(2,1)} %get-tuple-element.284.refs_2_), channel_id=1, source_target_pairs={{0,4},{4,0},{8,12},{12,8},{16,20},{20,16},{24,28},{28,24},{1,5},{5... | collective-permute-start | bytes 8847368 | tf_op jit(solution)/shard_map/ppermute | solution.py:626
  216.9 34.1 %collective-permute-start.18 = (bf16[1,576,1152]{2,1,0:T(8,128)(2,1)}, bf16[1,576,1152]{2,1,0:T(8,128)(2,1)}, u32[]{:S(2)}, u32[]{:S(2)}) collective-permute-start(bf16[1,576,1152]{2,1,0:T(8,128)(2,1)} %get-tuple-element.274), channel_id=1, source_target_pairs={{0,16},{4,20},{8,24},{12,28},{16,0},{20,4},{24,8},{28,12},{1,17},{... | collective-permute-start | bytes 3981320 | tf_op jit(solution)/shard_map/ppermute | solution.py:626
  218.4 32.6 %collective-permute-start.15 = (bf16[1,144,2048]{2,1,0:T(8,128)(2,1)}, bf16[1,144,2048]{2,1,0:T(8,128)(2,1)}, u32[]{:S(2)}, u32[]{:S(2)}) collective-permute-start(bf16[1,144,2048]{2,1,0:T(8,128)(2,1)} %add_convert_fusion.7), channel_id=1, source_target_pairs={{0,8},{4,12},{8,0},{12,4},{16,24},{20,28},{24,16},{28,20},{1,9},{5... | collective-permute-start | bytes 1769480 | tf_op jit(solution)/shard_map/ppermute | solution.py:626
  219.8 27.3 %collective-permute-start.16 = (bf16[1,256,768]{2,1,0:T(8,128)(2,1)}, bf16[1,256,768]{2,1,0:T(8,128)(2,1)}, u32[]{:S(2)}, u32[]{:S(2)}) collective-permute-start(bf16[1,256,768]{2,1,0:T(8,128)(2,1)} %get-tuple-element.272), channel_id=1, source_target_pairs={{0,8},{4,12},{8,0},{12,4},{16,24},{20,28},{24,16},{28,20},{1,9},{5... | collective-permute-start | bytes 1179656 | tf_op jit(solution)/shard_map/ppermute | solution.py:626
  220.4 30.6 %collective-permute-start.17 = (bf16[1,256,768]{2,1,0:T(8,128)(2,1)}, bf16[1,256,768]{2,1,0:T(8,128)(2,1)}, u32[]{:S(2)}, u32[]{:S(2)}) collective-permute-start(bf16[1,256,768]{2,1,0:T(8,128)(2,1)} %get-tuple-element.273), channel_id=1, source_target_pairs={{0,8},{4,12},{8,0},{12,4},{16,24},{20,28},{24,16},{28,20},{1,9},{5... | collective-permute-start | bytes 1179656 | tf_op jit(solution)/shard_map/ppermute | solution.py:626
  221.8 29.2 %all-to-all-start.1 = ((bf16[4,288,256]{2,1,0:T(8,128)(2,1)}), bf16[4,288,256]{2,1,0:T(8,128)(2,1)S(1)}, u32[]{:S(2)}, u32[]{:S(2)}) async-start(bf16[4,288,256]{2,1,0:T(8,128)(2,1)} %get-tuple-element.270), calls=%async_computation.1 | async-start | bytes 1179648 | tf_op jit(solution)/shard_map/all_to_all | solution.py:654
  251.1 30.5 %collective-permute-start.20 = (bf16[1,576,1152]{2,1,0:T(8,128)(2,1)S(1)}, bf16[1,576,1152]{2,1,0:T(8,128)(2,1)S(1)}, u32[]{:S(2)}, u32[]{:S(2)}) collective-permute-start(bf16[1,576,1152]{2,1,0:T(8,128)(2,1)S(1)} %copy-done.7), channel_id=1, source_target_pairs={{0,8},{4,12},{8,0},{12,4},{16,24},{20,28},{24,16},{28,20},{1,9},{5... | collective-permute-start | bytes 3981320 | tf_op jit(solution)/shard_map/ppermute | solution.py:626
  252.5 28.9 %collective-permute-start.21 = (bf16[1,256,2048]{2,1,0:T(8,128)(2,1)}, bf16[1,256,2048]{2,1,0:T(8,128)(2,1)}, u32[]{:S(2)}, u32[]{:S(2)}) collective-permute-start(bf16[1,256,2048]{2,1,0:T(8,128)(2,1)} %add_convert_fusion.5), channel_id=1, source_target_pairs={{0,16},{4,20},{8,24},{12,28},{16,0},{20,4},{24,8},{28,12},{1,17},{... | collective-permute-start | bytes 3145736 | tf_op jit(solution)/shard_map/ppermute | solution.py:626
  289.4 29.4 %collective-permute-start.27 = (bf16[4,144,864]{2,1,0:T(8,128)(2,1)}, bf16[4,144,864]{2,1,0:T(8,128)(2,1)}, u32[]{:S(2)}, u32[]{:S(2)}) collective-permute-start(bf16[4,144,864]{2,1,0:T(8,128)(2,1)} %get-tuple-element.326), channel_id=1, source_target_pairs={{0,4},{4,0},{8,12},{12,8},{16,20},{20,16},{24,28},{28,24},{1,5},{5... | collective-permute-start | bytes 2985992 | tf_op jit(solution)/shard_map/ppermute | solution.py:626
  289.4 31.9 %collective-permute-start.22 = (bf16[1,144,4608]{2,1,0:T(8,128)(2,1)}, bf16[1,144,4608]{2,1,0:T(8,128)(2,1)}, u32[]{:S(2)}, u32[]{:S(2)}) collective-permute-start(bf16[1,144,4608]{2,1,0:T(8,128)(2,1)} %get-tuple-element.319), channel_id=1, source_target_pairs={{0,8},{4,12},{8,0},{12,4},{16,24},{20,28},{24,16},{28,20},{1,9},{5... | collective-permute-start | bytes 3981320 | tf_op jit(solution)/shard_map/ppermute | solution.py:626
  290.9 9.2 %collective-permute-start.26 = (bf16[2,144,512]{2,1,0:T(8,128)(2,1)S(1)}, bf16[2,144,512]{2,1,0:T(8,128)(2,1)}, u32[]{:S(2)}, u32[]{:S(2)}) collective-permute-start(bf16[2,144,512]{2,1,0:T(8,128)(2,1)S(1)} %copy-done.40), channel_id=1, source_target_pairs={{0,1},{1,0},{2,3},{3,2},{4,5},{5,4},{6,7},{7,6},{8,9},{9,8},{10,11... | collective-permute-start | bytes 884744 | tf_op jit(solution)/shard_map/ppermute | solution.py:626
  293.3 25.4 %collective-permute-start.25 = (bf16[1,256,768]{2,1,0:T(8,128)(2,1)}, bf16[1,256,768]{2,1,0:T(8,128)(2,1)}, u32[]{:S(2)}, u32[]{:S(2)}) collective-permute-start(bf16[1,256,768]{2,1,0:T(8,128)(2,1)} %add_convert_fusion.11), channel_id=1, source_target_pairs={{0,16},{4,20},{8,24},{12,28},{16,0},{20,4},{24,8},{28,12},{1,17},{... | collective-permute-start | bytes 1179656 | tf_op jit(solution)/shard_map/ppermute | solution.py:626
  293.8 22.7 %collective-permute-start.23 = (bf16[1,144,1152]{2,1,0:T(8,128)(2,1)}, bf16[1,144,1152]{2,1,0:T(8,128)(2,1)}, u32[]{:S(2)}, u32[]{:S(2)}) collective-permute-start(bf16[1,144,1152]{2,1,0:T(8,128)(2,1)} %get-tuple-element.320), channel_id=1, source_target_pairs={{0,16},{4,20},{8,24},{12,28},{16,0},{20,4},{24,8},{28,12},{1,17},{... | collective-permute-start | bytes 995336 | tf_op jit(solution)/shard_map/ppermute | solution.py:626
  300.1 18.7 %collective-permute-start.24 = (bf16[1,144,1152]{2,1,0:T(8,128)(2,1)}, bf16[1,144,1152]{2,1,0:T(8,128)(2,1)}, u32[]{:S(2)}, u32[]{:S(2)}) collective-permute-start(bf16[1,144,1152]{2,1,0:T(8,128)(2,1)} %get-tuple-element.321), channel_id=1, source_target_pairs={{0,16},{4,20},{8,24},{12,28},{16,0},{20,4},{24,8},{28,12},{1,17},{... | collective-permute-start | bytes 995336 | tf_op jit(solution)/shard_map/ppermute | solution.py:626
  303.3 80.4 %all-to-all-start.2 = ((bf16[4,256,1152]{2,1,0:T(8,128)(2,1)}), bf16[4,256,1152]{2,1,0:T(8,128)(2,1)S(1)}, u32[]{:S(2)}, u32[]{:S(2)}) async-start(bf16[4,256,1152]{2,1,0:T(8,128)(2,1)} %get-tuple-element.316), calls=%async_computation.2 | async-start | bytes 4718592 | tf_op jit(solution)/shard_map/all_to_all | solution.py:654
  323.2 43.5 %collective-permute-start.31 = (bf16[144,512]{1,0:T(8,128)(2,1)}, bf16[144,512]{1,0:T(8,128)(2,1)}, u32[]{:S(2)}, u32[]{:S(2)}) collective-permute-start(bf16[144,512]{1,0:T(8,128)(2,1)} %get-tuple-element.463), channel_id=1, source_target_pairs={{0,2},{1,3},{2,0},{3,1},{4,6},{5,7},{6,4},{7,5},{8,10},{9,11},{10,... | collective-permute-start | bytes 442376 | tf_op jit(solution)/shard_map/ppermute | solution.py:626
  325.6 41.0 %collective-permute-start.30 = (bf16[2,144,864]{2,1,0:T(8,128)(2,1)}, bf16[2,144,864]{2,1,0:T(8,128)(2,1)S(1)}, u32[]{:S(2)}, u32[]{:S(2)}) collective-permute-start(bf16[2,144,864]{2,1,0:T(8,128)(2,1)} %get-tuple-element.454), channel_id=1, source_target_pairs={{0,16},{4,20},{8,24},{12,28},{16,0},{20,4},{24,8},{28,12},{1,17},{... | collective-permute-start | bytes 1493000 | tf_op jit(solution)/shard_map/ppermute | solution.py:626
  327.0 39.7 %collective-permute-start.28 = (bf16[1,144,4608]{2,1,0:T(8,128)(2,1)}, bf16[1,144,4608]{2,1,0:T(8,128)(2,1)}, u32[]{:S(2)}, u32[]{:S(2)}) collective-permute-start(bf16[1,144,4608]{2,1,0:T(8,128)(2,1)} %get-tuple-element.342), channel_id=1, source_target_pairs={{0,8},{4,12},{8,0},{12,4},{16,24},{20,28},{24,16},{28,20},{1,9},{5... | collective-permute-start | bytes 3981320 | tf_op jit(solution)/shard_map/ppermute | solution.py:626
  327.5 39.1 %collective-permute-start.29 = (bf16[2,256,512]{2,1,0:T(8,128)(2,1)}, bf16[2,256,512]{2,1,0:T(8,128)(2,1)S(1)}, u32[]{:S(2)}, u32[]{:S(2)}) collective-permute-start(bf16[2,256,512]{2,1,0:T(8,128)(2,1)} %get-tuple-element.345), channel_id=1, source_target_pairs={{0,1},{1,0},{2,3},{3,2},{4,5},{5,4},{6,7},{7,6},{8,9},{9,8},{10,11... | collective-permute-start | bytes 1572872 | tf_op jit(solution)/shard_map/ppermute | solution.py:626
  369.3 19.9 %collective-permute-start.36 = (bf16[256,512]{1,0:T(8,128)(2,1)}, bf16[256,512]{1,0:T(8,128)(2,1)}, u32[]{:S(2)}, u32[]{:S(2)}) collective-permute-start(bf16[256,512]{1,0:T(8,128)(2,1)} %get-tuple-element.458), channel_id=1, source_target_pairs={{0,2},{1,3},{2,0},{3,1},{4,6},{5,7},{6,4},{7,5},{8,10},{9,11},{10,... | collective-permute-start | bytes 786440 | tf_op jit(solution)/shard_map/ppermute | solution.py:626
  371.2 18.0 %collective-permute-start.35 = (bf16[144,864]{1,0:T(8,128)(2,1)}, bf16[144,864]{1,0:T(8,128)(2,1)}, u32[]{:S(2)}, u32[]{:S(2)}) collective-permute-start(bf16[144,864]{1,0:T(8,128)(2,1)} %get-tuple-element.451), channel_id=1, source_target_pairs={{0,8},{4,12},{8,0},{12,4},{16,24},{20,28},{24,16},{28,20},{1,9},{5... | collective-permute-start | bytes 746504 | tf_op jit(solution)/shard_map/ppermute | solution.py:626
  374.9 22.1 %collective-permute-start.34 = (bf16[2,576,288]{1,2,0:T(8,128)(2,1)}, bf16[2,576,288]{1,2,0:T(8,128)(2,1)}, u32[]{:S(2)}, u32[]{:S(2)}) collective-permute-start(bf16[2,576,288]{1,2,0:T(8,128)(2,1)} %copy.57), channel_id=1, source_target_pairs={{0,1},{1,0},{2,3},{3,2},{4,5},{5,4},{6,7},{7,6},{8,9},{9,8},{10,11... | collective-permute-start | bytes 1990664 | tf_op jit(solution)/shard_map/ppermute | solution.py:626
  376.9 28.5 %collective-permute-start.32 = (bf16[1,144,4608]{2,1,0:T(8,128)(2,1)}, bf16[1,144,4608]{2,1,0:T(8,128)(2,1)}, u32[]{:S(2)}, u32[]{:S(2)}) collective-permute-start(bf16[1,144,4608]{2,1,0:T(8,128)(2,1)} %add_convert_fusion.1), channel_id=1, source_target_pairs={{0,16},{4,20},{8,24},{12,28},{16,0},{20,4},{24,8},{28,12},{1,17},{... | collective-permute-start | bytes 3981320 | tf_op jit(solution)/shard_map/ppermute | solution.py:626
  377.5 11.6 %collective-permute-start.33 = (bf16[1,144,1152]{2,1,0:T(8,128)(2,1)}, bf16[1,144,1152]{2,1,0:T(8,128)(2,1)S(1)}, u32[]{:S(2)}, u32[]{:S(2)}) collective-permute-start(bf16[1,144,1152]{2,1,0:T(8,128)(2,1)} %add_convert_fusion.13), channel_id=1, source_target_pairs={{0,8},{4,12},{8,0},{12,4},{16,24},{20,28},{24,16},{28,20},{1,9},{5... | collective-permute-start | bytes 995336 | tf_op jit(solution)/shard_map/ppermute | solution.py:626
  407.7 36.2 %collective-permute-start.40 = (bf16[2,144,288]{2,1,0:T(8,128)(2,1)}, bf16[2,144,288]{2,1,0:T(8,128)(2,1)}, u32[]{:S(2)}, u32[]{:S(2)}) collective-permute-start(bf16[2,144,288]{2,1,0:T(8,128)(2,1)} %get-tuple-element.385), channel_id=1, source_target_pairs={{0,1},{1,0},{2,3},{3,2},{4,5},{5,4},{6,7},{7,6},{8,9},{9,8},{10,11... | collective-permute-start | bytes 497672 | tf_op jit(solution)/shard_map/ppermute | solution.py:626
  410.5 9.6 %all-to-all-start.3 = ((f32[4,1,1728]{2,1,0:T(1,128)}), f32[4,1,1728]{2,1,0:T(1,128)S(1)}, u32[]{:S(2)}, u32[]{:S(2)}) async-start(f32[4,1,1728]{2,1,0:T(1,128)} %all_to_all.24), calls=%async_computation.3 | async-start | bytes 57344 | tf_op jit(solution)/shard_map/all_to_all | solution.py:654
  420.1 22.9 %all-to-all-start.4 = ((bf16[4,144,288]{2,1,0:T(8,128)(2,1)}), bf16[4,144,288]{2,1,0:T(8,128)(2,1)S(1)}, u32[]{:S(2)}, u32[]{:S(2)}) async-start(bf16[4,144,288]{2,1,0:T(8,128)(2,1)} %pad_maximum_fusion.1), calls=%async_computation.4 | async-start | bytes 884736 | tf_op jit(solution)/shard_map/all_to_all | solution.py:654
  424.6 36.4 %collective-permute-start.38 = (bf16[576,288]{1,0:T(8,128)(2,1)}, bf16[576,288]{1,0:T(8,128)(2,1)S(1)}, u32[]{:S(2)}, u32[]{:S(2)}) collective-permute-start(bf16[576,288]{1,0:T(8,128)(2,1)} %get-tuple-element.456), channel_id=1, source_target_pairs={{0,2},{1,3},{2,0},{3,1},{4,6},{5,7},{6,4},{7,5},{8,10},{9,11},{10,... | collective-permute-start | bytes 995336 | tf_op jit(solution)/shard_map/ppermute | solution.py:626
  431.0 30.0 %collective-permute-start.37 = (bf16[2,144,1152]{2,1,0:T(8,128)(2,1)}, bf16[2,144,1152]{2,1,0:T(8,128)(2,1)S(1)}, u32[]{:S(2)}, u32[]{:S(2)}) collective-permute-start(bf16[2,144,1152]{2,1,0:T(8,128)(2,1)} %get-tuple-element.378), channel_id=1, source_target_pairs={{0,1},{1,0},{2,3},{3,2},{4,5},{5,4},{6,7},{7,6},{8,9},{9,8},{10,11... | collective-permute-start | bytes 1990664 | tf_op jit(solution)/shard_map/ppermute | solution.py:626
  432.5 28.5 %collective-permute-start.39 = (bf16[2,256,192]{2,1,0:T(8,128)(2,1)S(1)}, bf16[2,256,192]{2,1,0:T(8,128)(2,1)S(1)}, u32[]{:S(2)}, u32[]{:S(2)}) collective-permute-start(bf16[2,256,192]{2,1,0:T(8,128)(2,1)S(1)} %copy-done.41), channel_id=1, source_target_pairs={{0,1},{1,0},{2,3},{3,2},{4,5},{5,4},{6,7},{7,6},{8,9},{9,8},{10,11... | collective-permute-start | bytes 589832 | tf_op jit(solution)/shard_map/ppermute | solution.py:626
  461.7 21.9 %collective-permute-start.43 = (bf16[256,192]{1,0:T(8,128)(2,1)}, bf16[256,192]{1,0:T(8,128)(2,1)}, u32[]{:S(2)}, u32[]{:S(2)}) collective-permute-start(bf16[256,192]{1,0:T(8,128)(2,1)} %fusion.14), channel_id=1, source_target_pairs={{0,2},{1,3},{2,0},{3,1},{4,6},{5,7},{6,4},{7,5},{8,10},{9,11},{10,... | collective-permute-start | bytes 294920 | tf_op jit(solution)/shard_map/ppermute | solution.py:626
  464.1 17.8 %collective-permute-start.41 = (bf16[144,288]{1,0:T(8,128)(2,1)}, bf16[144,288]{1,0:T(8,128)(2,1)}, u32[]{:S(2)}, u32[]{:S(2)}) collective-permute-start(bf16[144,288]{1,0:T(8,128)(2,1)} %fusion.18), channel_id=1, source_target_pairs={{0,2},{1,3},{2,0},{3,1},{4,6},{5,7},{6,4},{7,5},{8,10},{9,11},{10,... | collective-permute-start | bytes 248840 | tf_op jit(solution)/shard_map/ppermute | solution.py:626
  467.6 18.7 %collective-permute-start.42 = (bf16[144,1152]{1,0:T(8,128)(2,1)S(1)}, bf16[144,1152]{1,0:T(8,128)(2,1)S(1)}, u32[]{:S(2)}, u32[]{:S(2)}) collective-permute-start(bf16[144,1152]{1,0:T(8,128)(2,1)S(1)} %fusion.5), channel_id=1, source_target_pairs={{0,2},{1,3},{2,0},{3,1},{4,6},{5,7},{6,4},{7,5},{8,10},{9,11},{10,... | collective-permute-start | bytes 995336 | tf_op jit(solution)/shard_map/ppermute | solution.py:626
  (43 other events, 567.2 us)

commit v4 on v3

--- a/solution.py
+++ b/solution.py
@@ -255,7 +255,7 @@
     lax.fori_loop(0, heads, head_step, 0)
     dqkv_ref[...] = acc_ref[...].astype(BF)
     for d in range(size):
-        dx_ref[lax.rem(rank_ref[0] + d, size)] = trans_times(dqkv_ref[:, d * tok : (d + 1) * tok], w_ref[...]).astype(BF)
+        dx_ref[d] = trans_times(dqkv_ref[:, d * tok : (d + 1) * tok], w_ref[...]).astype(BF)
 
 
 def attend_backward(one, rank, dos, qkv, o, lse, w, idk, idq, heads, tile, diagonal):
@@ -286,21 +286,19 @@
 
 def middle_kernel(*refs):
     (o_refs, tokens_ref, mods_ref, dino_ref, cot_ref, wo_any, w1_any, w2_any, p1_any, p2_any, p3_any) = refs[:11]
-    (out_ref, left1_ref, left2_ref, right1_ref, gp_ref, dmlp_ref, dy_ref, normed_ref, inv_ref, attn_ref,
-     gate_ref) = refs[11:22]
-    (wo_ref, w1_ref, w2_ref, p1_ref, p2_ref, p3_ref, act_ref, w1_sem, sems) = refs[22:]
+    (out_ref, a1_ref, dr2_ref, left1_ref, right1_ref, left2_ref, gp_ref, dmlp_ref, dy_ref, normed_ref, inv_ref, attn_ref,
+     gate_ref) = refs[11:24]
+    (wo_ref, w1_ref, w2_ref, p1_ref, p2_ref, p3_ref, act_ref, w1_sem, sems) = refs[24:]
     size, local, tok = o_refs.shape
     width = size * local
     hidden = w1_any.shape[1]
     wide, narrow = p3_ref.shape
     steps = hidden // STEP
     slots = w1_ref.shape[0]
-    a2_ref, a1_ref = left1_ref.at[0:wide, :], left1_ref.at[wide : 2 * wide, :]
-    y_ref = left1_ref.at[2 * wide :, :]
+    a2_ref, y_ref = left1_ref.at[0:wide, :], left1_ref.at[wide:, :]
     g_ref, b_ref = left2_ref.at[0:hidden, :], left2_ref.at[hidden : hidden + width, :]
     o_ref = left2_ref.at[hidden + width :, :]
-    dr2_ref, dr1_ref = right1_ref.at[:, 0:wide], right1_ref.at[:, wide : 2 * wide]
-    dz_ref = right1_ref.at[:, 2 * wide :]
+    dr1_ref, dz_ref = right1_ref.at[:, 0:wide], right1_ref.at[:, wide:]
     wo_copy = pltpu.make_async_copy(wo_any, wo_ref, sems.at[4])
     wo_copy.start()
 
@@ -404,12 +402,12 @@
     return pl.pallas_call(
         middle_kernel,
         out_shape=(
-            shape((tok, width)), shape((2 * wide + width, tok)), shape((hidden + 2 * width, tok)),
-            shape((tok, 2 * wide + narrow)), shape((tok, hidden)), shape((tok, width)), shape((tok, width), F32),
+            shape((tok, width)), shape((wide, tok)), shape((tok, wide)), shape((wide + width, tok)),
+            shape((tok, wide + narrow)), shape((hidden + 2 * width, tok)), shape((tok, hidden)), shape((tok, width)), shape((tok, width), F32),
             shape((tok, width), F32), shape((tok, 1), F32), shape((tok, width), F32), shape((1, width), F32),
         ),
         in_specs=[VMEM] * 5 + [ANY] * 6,
-        out_specs=(VMEM,) * 11,
+        out_specs=(VMEM,) * 13,
         scratch_shapes=[
             pltpu.VMEM(dims, BF)
             for dims in (wo.shape, (4, width, STEP), w2.shape, p1.shape, p2.shape, p3.shape, (tok, hidden))
@@ -487,10 +485,8 @@
     )(dmlp, gp, dy, normed, inv, attn, mods, w2, w1, wo)
 
 
-def leave_kernel(parts_ref, tokens_ref, dh1_ref, mods_ref, out_ref, sums_ref):
-    da = parts_ref[0].astype(F32)
-    for i in range(1, parts_ref.shape[0]):
-        da = da + parts_ref[i].astype(F32)
+def leave_kernel(part_ref, left_ref, right_ref, tokens_ref, dh1_ref, mods_ref, out_ref, sums_ref):
+    da = part_ref[...].astype(F32) + left_ref[...].astype(F32) + right_ref[...].astype(F32)
     normed, inv = normalize(tokens_ref[...].astype(F32))
     out_ref[...] = (dh1_ref[...] + norm_back(da * (1.0 + mods_ref[1:2, :]), normed, inv)).astype(BF)
     sums_ref[...] = jnp.zeros_like(sums_ref)
@@ -498,15 +494,15 @@
     sums_ref[1:2, :] = col_sum(da * normed)
 
 
-def leave(parts, tokens, dh1, mods):
+def leave(part, from_left, from_right, tokens, dh1, mods):
     return pl.pallas_call(
         leave_kernel,
         out_shape=(shape(tokens.shape), shape((8, tokens.shape[1]), F32)),
-        in_specs=[VMEM] * 4,
+        in_specs=[VMEM] * 6,
         out_specs=(VMEM, VMEM),
         compiler_params=params(),
         name="leave",
-    )(parts, tokens, dh1, mods)
+    )(part, from_left, from_right, tokens, dh1, mods)
 
 
 def weight_grad_kernel(count, flat, rows, packs, rows_ref, *refs):
@@ -584,13 +580,84 @@
     return [outs[i * len(packs) : (i + 1) * len(packs)] for i in range(len(jobs))]
 
 
-def split_kernel(rank_ref, keep_ref, got_ref, near_ref, far_ref, own_ref):
-    rows, cols = keep_ref.shape
-    size = near_ref.shape[0] * 2
-    block = cols // size
-    total = (keep_ref[...].astype(F32) + got_ref[...].astype(F32)).astype(BF)
+def weight_grad_seq_kernel(count, rows, order_ref, *refs):
+    lefts, rights = refs[:count], refs[count : 2 * count]
+    near_ref, far_ref, own_ref, held_ref, sem = refs[2 * count :]
+    blocks = held_ref.shape[0] // rows
+    part = lefts[0].shape[1]
+    step = pl.program_id(0)
+    copies = [
+        pltpu.make_async_copy(
+            lefts[j].at[pl.ds(pl.multiple_of(order_ref[4 + i], 16), rows), :],
+            held_ref.at[i * rows : (i + 1) * rows, j * part : (j + 1) * part],
+            sem.at[i * count + j],
+        )
+        for i in range(blocks)
+        for j in range(count)
+    ]
+
+    @pl.when(step == 0)
+    def _():
+        for copy in copies:
+            copy.start()
+        for copy in copies:
+            copy.wait()
+
+    total = None
+    for j in range(count):
+        term = matmul(held_ref[:, j * part : (j + 1) * part], rights[j][...])
+        total = term if total is None else total + term
+    total = total.astype(BF)
+
+    @pl.when(step < 2)
+    def _():
+        near_ref[0] = total
+
+    @pl.when(step == 2)
+    def _():
+        far_ref[...] = total
+
+    @pl.when(step == 3)
+    def _():
+        own_ref[...] = total
+
+
+def weight_grad_seq(lefts, rights, row_starts, rows, columns, step):
+    count = len(lefts)
+    part = lefts[0].shape[1]
+    blocks = row_starts.shape[0]
+    return pl.pallas_call(
+        functools.partial(weight_grad_seq_kernel, count, rows),
+        out_shape=(shape((2, blocks * rows, step)), shape((blocks * rows, step)), shape((blocks * rows, step))),
+        grid_spec=pltpu.PrefetchScalarGridSpec(
+            num_scalar_prefetch=1,
+            grid=(4,),
+            in_specs=[ANY] * count + [pl.BlockSpec((part, step), lambda i, b: (0, b[i]))] * count,
+            out_specs=(
+                pl.BlockSpec((1, blocks * rows, step), lambda i, b: (jnp.minimum(i, 1), 0, 0)),
+                pl.BlockSpec((blocks * rows, step), lambda i, b: (0, 0)),
+                pl.BlockSpec((blocks * rows, step), lambda i, b: (0, 0)),
+            ),
+            scratch_shapes=[
+                pltpu.VMEM((blocks * rows, part * count), BF),
+                pltpu.SemaphoreType.DMA((blocks * count,)),
+            ],
+        ),
+        compiler_params=params(dimension_semantics=("arbitrary",)),
+        name="weight_grad_seq",
+    )(jnp.concatenate([columns, row_starts]), *lefts, *rights)
+
+
+def split_kernel(turned, rank_ref, keep_ref, got1_ref, got2_ref, near_ref, far_ref, own_ref):
+    total = keep_ref[0].astype(F32) + got1_ref[got1_ref.shape[0] - 1].astype(F32) + got2_ref[0].astype(F32)
+    total = total.astype(BF)
+    if turned:
+        total = jnp.transpose(total)
+    size = 4
+    block = total.shape[0 if turned else 1] // size
     for j in range(size):
-        piece = total[:, j * block : (j + 1) * block]
+        at = slice(j * block, (j + 1) * block)
+        piece = total[at, :] if turned else total[:, at]
         mask = j ^ rank_ref[0]
 
         @pl.when(mask == 3)
@@ -610,16 +677,17 @@
             own_ref[...] = piece
 
 
-def split(rank, keep, got):
-    rows, cols = keep.shape
+def split(rank, keep, got1, got2, turned=False):
+    rows, cols = keep.shape[1:]
+    dims = (cols // 4, rows) if turned else (rows, cols // 4)
     return pl.pallas_call(
-        split_kernel,
-        out_shape=(shape((2, rows, cols // 4)), shape((rows, cols // 4)), shape((rows, cols // 4))),
-        in_specs=[SMEM, VMEM, VMEM],
+        functools.partial(split_kernel, turned),
+        out_shape=(shape((2,) + dims), shape(dims), shape(dims)),
+        in_specs=[SMEM, VMEM, VMEM, VMEM],
         out_specs=(VMEM,) * 3,
         compiler_params=params(),
         name="split",
-    )(rank, keep, got)
+    )(rank, keep, got1, got2)
 
 
 def flip(x, axis, size, bit):
@@ -628,10 +696,6 @@
 
 def add(a, b):
     return (a.astype(F32) + b.astype(F32)).astype(BF)
-
-
-def after(x, *others):
-    return lax.optimization_barrier((x,) + others)[0]
 
 
 def masks_of(bits):
@@ -643,6 +707,10 @@
                 mask |= bit
         out.append(mask)
     return out
+
+
+def after(x, *others):
+    return together(x, *others)[0]
 
 
 def together(*values):
@@ -694,7 +762,7 @@
         one, rank_arg, pieces, w_pad, idk, idq, heads, tile, diagonal
     )
     attended = exchange(heads_out)
-    (rounded, left1, left2, right1, gelu_slope, dmlp, dy, normed2, inv2, attn, sum_gate2) = middle(
+    (rounded, act1, dr2, left1, right1, left2, gelu_slope, dmlp, dy, normed2, inv2, attn, sum_gate2) = middle(
         attended, tokens, mods, dino, cotangent, w_out, w_fc1, w_fc2, w_proj1, w_proj2, w_proj3
     )
 
@@ -718,108 +786,123 @@
             starts = base + (me ^ jnp.array(masks_of(bits), jnp.int32)) * (deep // n_dp)
             return (starts, deep // n_dp, column)
 
+        def right(v, step):
+            return lax.ppermute(v, "seq", [(i, i + 1) for i in range(step)])
+
+        def left(v, step):
+            return lax.ppermute(v, "seq", [(i, i - 1) for i in range(n_seq - step, n_seq)])
+
+        def row_starts(base, deep, bits):
+            return base + (me ^ jnp.array(masks_of(bits), jnp.int32)) * (deep // n_dp)
+
         quarter = (1, 1, 1, 1)
+        act1_other, dr2_other = swap(act1, core), swap(dr2, core)
+        lefts2, dmlps = [left2, swap(left2, core)], [dmlp, swap(dmlp, core)]
+        (p2,) = weight_grad([act1, act1_other], [dr2, dr2_other], [job(0, wide, (x, y), 0)], quarter, wide, STEP)
+        p2, lefts2, dmlps, left1, right1 = together(p2, lefts2, dmlps, left1, right1)
+
+        p2a = swap(p2[0], x)
+        p2b = swap(after(p2[1], p2a), x)
+        (f2,) = weight_grad(lefts2, dmlps, [job(0, hidden, (y, x), 0)], quarter, width, 384)
+        f2a = swap(f2[0], y)
         lefts1, rights1 = [left1, swap(left1, core)], [right1, swap(right1, core)]
-        (p2, p1) = weight_grad(
-            lefts1, rights1, [job(wide, wide, (x, y), 0), job(2 * wide, width, (y, x), wide // STEP)],
-            quarter, wide, STEP,
+        p1n, p1f, p1o = weight_grad_seq(
+            lefts1, after(rights1, f2), row_starts(wide, width, (y, x)), width // n_dp,
+            rank ^ jnp.array(masks_of((1, 2)), jnp.int32), wide // n_seq,
         )
-        left2_other, dmlp_other = swap(left2, core), swap(dmlp, core)
-        lefts1, rights1, p2, p1, left2_other, dmlp_other = together(
-            lefts1, rights1, p2, p1, left2_other, dmlp_other
+        p1z = near(p1n)
+        (p3,) = weight_grad(
+            lefts1, after(rights1, p1n), [job(0, wide, (y, x), wide // 256)], (2, 1, 1), narrow, 256
         )
-
-        p2a, p1a, p1b = swap(p2[0], x), swap(p1[0], y), swap(p1[1], y)
-        lefts2 = [left2, left2_other]
-        (f2,) = weight_grad(lefts2, [dmlp, dmlp_other], [job(0, hidden, (y, x), 0)], quarter, width, 384)
-        rights1 = together(rights1, f2)[0]
-        (p3,) = weight_grad(lefts1, rights1, [job(0, wide, (x, y), 2 * wide // 256)], quarter, narrow, 256)
-        p2a, p1a, p1b, f2, p3, p2, p1, dmlp = together(p2a, p1a, p1b, f2, p3, p2, p1, dmlp)
-
-        p2b, f2a = swap(p2[1], x), swap(f2[0], y)
-        right2, dhidden1, dheads, sums2 = down(dmlp)
-        p1s = add(p1[2], p1a)
-        p2b, f2a, right2, dhidden1, dheads, sums2, p1s, f2, p3, p2a = together(
-            p2b, f2a, right2, dhidden1, dheads, sums2, p1s, f2, p3, p2a
+        p3a = swap(p3[0], y)
+        right2, dhidden1, dheads, sums2 = down(after(dmlp, p3, p2a))
+        p2, f2, p2a, p2b, f2a, p1f, p1o, p1z, p3, p3a, right2, dhidden1, dheads, sums2, lefts2 = together(
+            p2, f2, p2a, p2b, f2a, p1f, p1o, p1z, p3, p3a, right2, dhidden1, dheads, sums2, lefts2
         )
 
+        f2c, f2b = swap(add(f2[2], f2a), x), swap(f2[1], y)
         dheads_in = exchange(dheads)
         rights2 = [right2, swap(right2, core)]
-        p1c, p3a, p3b, f2b = swap(p1s, x), swap(p3[0], x), swap(p3[1], x), swap(f2[1], y)
-        p2s, f2s = add(p2[2], p2a), add(f2[2], f2a)
         (f1,) = weight_grad(lefts2, rights2, [job(hidden, width, (x, y), 0)], quarter, hidden, 1152)
-        rights2 = together(rights2, f1)[0]
         (fo,) = weight_grad(
-            lefts2, rights2, [job(hidden + width, width, (y, x), hidden // 384)], quarter, width, 384
+            lefts2, after(rights2, f1), [job(hidden + width, width, (y, x), hidden // 384)], (2, 1, 1), width, 384
         )
-        dheads_in, p1c, p3a, p3b, f2b, p2s, f2s, f1, fo, p3 = together(
-            dheads_in, p1c, p3a, p3b, f2b, p2s, f2s, f1, fo, p3
-        )
-
-        f2c, p2c = swap(f2s, x), swap(p2s, y)
-        dqkv, dfirst_parts = back(dheads_in)
-        p1n, p1f, p1o = split(rank_arg, add(p1[3], p1b)[0], p1c[0])
-        p3s = add(p3[2], p3a)
-        f2c, p2c, dqkv, dfirst_parts, p1n, p1f, p1o, p3s, f1, fo, p3b = together(
-            f2c, p2c, dqkv, dfirst_parts, p1n, p1f, p1o, p3s, f1, fo, p3b
-        )
-
-        dfirst_in = exchange(dfirst_parts)
-        f1a, foa, fob, p3c, p1z = swap(f1[0], x), swap(fo[0], y), swap(fo[1], y), swap(p3s, y), near(p1n)
+        p2s, p1f, p1o = add(p2[2], p2a), add(p1f, p1z[0]), add(p1o, p1z[1])
+        p3s = add(p3[1], p3a[:1])
+        f2, f2c, f2b, dheads_in, p3s, f1, fo, p2s, p1f = together(f2, f2c, f2b, dheads_in, p3s, f1, fo, p2s, p1f)
+
+        f1a, p3c, p2c, p1y = swap(f1[0], x), swap(p3s, x), swap(p2s, y), far(p1f)
+        f2n, f2f, f2o = split(rank_arg, f2[3], f2b, f2c, turned=True)
+        f2z = near(f2n)
+        dqkv, dx = back(after(dheads_in, f2n))
+        foa = swap(after(fo[0], dqkv), y)
         (fq,) = weight_grad(
             [first_all], [dqkv], [job(0, width, (core, y, x), 0)], (4, 2, 2), 3 * local, 3 * local, flat=True
         )
+        p1d = add(p1o, p1y).reshape(4, width // n_dp, wide // n_seq)
+        f1a, p3c, p2c, foa, p1d, f2z, f2f, dqkv, dx, fq, f1 = together(
+            f1a, p3c, p2c, foa, p1d, f2z, f2f, dqkv, dx, fq, f1
+        )
+
+        f1b, f1c = swap(f1[1], x), swap(add(f1[2], f1a), y)
+        up, low = right(dx[3], 1), left(dx[1], 1)
         fqa = swap(fq[0], core)
-        f2n, f2f, f2o = split(rank_arg, add(f2[3], f2b)[0], f2c[0])
-        p2n, p2f, p2o = split(rank_arg, add(p2[3], p2b)[0], p2c[0])
-        f1a, foa, fob, p3c, p1z, fq, fqa, f2n, p2n, f1, fo = together(
-            f1a, foa, fob, p3c, p1z, fq, fqa, f2n, p2n, f1, fo
+        f2y = far(add(f2f, f2z[0]))
+        p2n, p2f, p2o = split(rank_arg, after(p2[3], fqa), p2b, p2c)
+        p2z = near(p2n)
+        p3n, p3f, p3o = split(rank_arg, after(p3[2], p2n), p3a, p3c, turned=True)
+        fos = add(fo[1], foa[:1])
+        f1b, f1c, up, low, f2y, fqa, p2z, p2f, p3n, fos, p1d = together(
+            f1b, f1c, up, low, f2y, fqa, p2z, p2f, p3n, fos, p1d
         )
 
-        fqs, fqk = add(fq[1], fqa[:2]), add(fq[2], fqa[2:])
-        f1b, f1s, p2z = swap(f1[1], x), add(f1[2], f1a), near(p2n)
-        fqb = swap(fqs, y)
-        fos = add(fo[2], foa)
-        p1y = far(add(p1f, p1z[0]))
-        p1o = add(p1o, p1z[1])
-        p3n, p3f, p3o = split(rank_arg, add(p3[3], p3b)[0], p3c[0])
-        f1b, f1s, p2z, fqb, fos, p1y, p1o, p3n, f2n, fqk, f1 = together(
-            f1b, f1s, p2z, fqb, fos, p1y, p1o, p3n, f2n, fqk, f1
-        )
-
-        f1c, foc, f2z = swap(f1s, y), swap(fos, x), near(f2n)
+        foc, fqb = swap(fos, x), swap(add(fq[1], fqa[:2]), y)
+        up, low = right(add(dx[2], up), 2), left(add(dx[2], low), 2)
+        f1n, f1f, f1o = split(rank_arg, f1[3], f1b, f1c)
+        f1z = near(f1n)
+        fqk = add(fq[2], fqa[2:])
         fqs, fqk = add(fqk[0], fqb[0]), add(fqk[1], fqb[1])
-        fqc = swap(fqs, x)
-        p2y = far(add(p2f, p2z[0]))
-        p2o = add(p2o, p2z[1])
-        g_proj1 = p1o.astype(F32) + p1y.astype(F32)
-        grad_inputs, sums1 = leave(dfirst_in, tokens, dhidden1, mods)
-        f1c, foc, f2z, fqk, fqc, p2y, p2o, p3n, sums1 = together(f1c, foc, f2z, fqk, fqc, p2y, p2o, p3n, sums1)
-
-        f1n, f1f, f1o = split(rank_arg, add(f1[3], f1b)[0], f1c[0])
-        fon, fof, foo = split(rank_arg, add(fo[3], fob)[0], foc[0])
-        f1z, f2y, p3z, foz = near(f1n), far(add(f2f, f2z[0])), near(p3n), near(fon)
-        f2o = add(f2o, f2z[1])
+        p1e = swap(after(p1d[0:2], fqb), y)
+        fqc = swap(after(fqs, foc), x)
+        p2y = far(after(add(p2f, p2z[0]), foc))
+        p3z = near(after(p3n, fqb))
+        foc, fqk, fqc, p1e, up, low, f1z, f1f, p2y, p3z = together(foc, fqk, fqc, p1e, up, low, f1z, f1f, p2y, p3z)
+
+        up, low = right(add(dx[1], up), 3), left(add(dx[3], low), 3)
+        f1y = far(add(f1f, f1z[0]))
+        p1x = swap(add(p1d[2], p1e[0]), x)
         g_heads = add(fqk, fqc)
-        g_proj2 = p2o.astype(F32) + p2y.astype(F32)
-        f1z, f2y, p3z, foz, f1f, fof, f2o, f1o, foo = together(f1z, f2y, p3z, foz, f1f, fof, f2o, f1o, foo)
-
-        f1y, p3y, foy = far(add(f1f, f1z[0])), far(add(p3f, p3z[0])), far(add(fof, foz[0]))
-        g_fc2 = f2o.astype(F32) + f2y.astype(F32)
-        last = lambda own, z, far_got: own.astype(F32) + z[1].astype(F32) + far_got.astype(F32)
-        g_fc1, g_proj3, g_out = last(f1o, f1z, f1y), last(p3o, p3z, p3y), last(foo, foz, foy)
+        fon, fof, foo = split(rank_arg, fo[2], foa, foc)
+        foz = near(after(fon, p1x))
+        p3y = far(after(add(p3f, p3z[0]), p1x))
+        up, low, f1y, p1x, p3y, foz = together(up, low, f1y, p1x, p3y, foz)
+
+        def last(*terms):
+            return sum(v.astype(F32) for v in terms)
+
+        foy = far(add(fof, foz[0]))
+        grad_inputs, sums1 = leave(dx[0], up, low, tokens, dhidden1, mods)
+        g_proj1 = last(p1d[3], p1e[1], p1x)
+        g_proj2, g_fc1, g_fc2 = last(p2o, p2z[1], p2y), last(f1o, f1z[1], f1y), jnp.transpose(last(f2o, f2z[1], f2y))
+        g_proj3, g_out = jnp.transpose(last(p3o, p3z[1], p3y)), last(foo, foz[1], foy)
     else:
         right2, dhidden1, dheads, sums2 = down(dmlp)
-        dqkv, dfirst_parts = back(exchange(dheads))
-        grad_inputs, sums1 = leave(exchange(dfirst_parts), tokens, dhidden1, mods)
+        dqkv, dx = back(exchange(dheads))
+        up, low = None, None
+        for s in range(1, n_seq):
+            up = dx[n_seq - s] if up is None else add(dx[n_seq - s], up)
+            low = dx[s] if low is None else add(dx[s], low)
+            up = lax.ppermute(up, "seq", [(i, i + 1) for i in range(s)])
+            low = lax.ppermute(low, "seq", [(i, i - 1) for i in range(n_seq - s, n_seq)])
+        grad_inputs, sums1 = leave(dx[0], up, low, tokens, dhidden1, mods)
 
         def reduced(a, b):
             share = lax.psum_scatter(matmul(a, b).astype(BF), "dp", scatter_dimension=0, tiled=True)
             return lax.psum_scatter(share, "seq", scatter_dimension=1, tiled=True).astype(F32)
 
-        g_proj3 = reduced(left1[:wide], right1[:, 2 * wide :])
-        g_proj2 = reduced(left1[wide : 2 * wide], right1[:, :wide])
-        g_proj1 = reduced(left1[2 * wide :], right1[:, wide : 2 * wide])
+        g_proj3 = reduced(left1[:wide], right1[:, wide:])
+        g_proj2 = reduced(act1, dr2)
+        g_proj1 = reduced(left1[wide:], right1[:, :wide])
         g_fc2 = reduced(left2[:hidden], dmlp)
         g_fc1 = reduced(left2[hidden : hidden + width], right2[:, :hidden])
         g_out = reduced(left2[hidden + width :], right2[:, hidden:])

time: 494 us -> 448 us (0.907)
  waiting for transfers between devices: 164 us -> 112 us
  starting transfers between devices: 63.2 us -> 78.7 us
  other arithmetic: 53.2 us -> 43.7 us
  local copies, waits for them, and re-layouts: 21.4 us -> 16.4 us
    ppermute x38 -> x37, waiting for transfers between devices: 122 us -> 75.8 us  [flip(): return lax.ppermute(x, axis, [(i, i ^ bit) for i in range(size)])]
    ppermute x0 -> x6, starting transfers between devices: none -> 17.9 us  [the longest x3 13.6 us: right(): return lax.ppermute(v, 'seq', [(i, i + 1) for i in range(step)])]
    squeeze x6 -> x0, other arithmetic: 13 us -> none  [the longest x1 3.09 us: shards(): f1n, f1f, f1o = split(rank_arg, add(f1[3], f1b)[0], f1c[0])]
    pallas_call x7, Pallas kernels: 56.2 us -> 61.9 us  [the longest x1 37.9 us: middle(): pl.pallas_call(middle_kernel, out_shape=(shape((tok, width)), shape((wide...]
    all_to_all x4 -> x3, waiting for transfers between devices: 9.24 us -> 3.58 us  [exchange(): lax.all_to_all(blocks, 'seq', split_axis=0, concat_axis=0, tiled=True)]
    all_to_all x4 -> x3, starting transfers between devices: 14.5 us -> 11.1 us  [exchange(): lax.all_to_all(blocks, 'seq', split_axis=0, concat_axis=0, tiled=True)]
    convert_element_type x15 -> x18, other arithmetic: 26.5 us -> 27.8 us  [add(): return (a.astype(F32) + b.astype(F32)).astype(BF)]
    ppermute x38 -> x37, starting transfers between devices: 36.9 us -> 37.9 us  [flip(): return lax.ppermute(x, axis, [(i, i ^ bit) for i in range(size)])]
  transfers between devices with their start and end apart: 48 -> 52, of which waited for: 21 -> 21; matrix products, arithmetic and copies ran while one was open for 13% -> 11% of each run, Pallas kernels for 20% -> 25%
where the time goes in v4:
time: 448 us; the launch traced here: 441 us
  Pallas kernels  172 us (38%)
  waiting for transfers between devices  112 us (25%)
  starting transfers between devices  78.7 us (18%)
  other arithmetic  43.7 us (10%)
  local copies, waits for them, and re-layouts  16.4 us (4%)
  blocking collectives  15.4 us (3%)
    ppermute x37, waiting for transfers between devices, flip(): return lax.ppermute(x, axis, [(i, i ^ bit) for i in range(size)])  75.8 us
    pallas_call x6, Pallas kernels, weight_grad(): pl.pallas_call(functools.partial(weight_grad_kernel, count, flat, rows, p...  43.5 us
    ppermute x37, starting transfers between devices, flip(): return lax.ppermute(x, axis, [(i, i ^ bit) for i in range(size)])  37.9 us
    pallas_call x1, Pallas kernels, middle(): pl.pallas_call(middle_kernel, out_shape=(shape((tok, width)), shape((wide...  37.9 us
    convert_element_type x18, other arithmetic, add(): return (a.astype(F32) + b.astype(F32)).astype(BF)  27.8 us
    pallas_call x1, Pallas kernels, attend_backward(): pl.pallas_call(functools.partial(attend_backward_kernel, size, heads, til...  21.3 us
    pallas_call x1, Pallas kernels, attend_forward(): pl.pallas_call(functools.partial(attend_forward_kernel, size, heads, tile...  20.9 us
    ppermute x3, waiting for transfers between devices, shards(): lax.ppermute(left[-1], 'seq', [(i, i - 1) for i in range(1, n_seq - s + 1)])  20.6 us
  transfers between devices with their start and end apart: 52, of which 21 were waited for; matrix products, arithmetic and copies ran while one was open for 11% of the time, Pallas kernels for 25%

profile of v4, /device:TPU:0, one launch (start us, length us, event | category | flops | bytes accessed | tf_op | source)
XLA Modules:
  0.0 440.7 jit_solution(11355565375683688562)
XLA Ops:
  2.0 3.1 enter.1
  5.1 5.0 %collective-permute-start.1 = (bf16[1152,256]{1,0:T(8,128)(2,1)}, bf16[1152,256]{1,0:T(8,128)(2,1)S(1)}, u32[]{:S(2)}, u32[]{:S(2)}) collective-permute-start(bf16[1152,256]{1,0:T(8,128)(2,1)} %get-tuple-element.179.refs_0_), channel_id=1, source_target_pairs={{0,1},{1,2},{2,3},{4,5},{5,6},{6,7},{8,9},{9,10},{10,11},{12,13},{... | collective-permute-start | bytes 1769480 | tf_op jit(solution)/shard_map/ppermute | solution.py:746
  11.4 11.5 %collective-permute-done.1.refs_6_ = bf16[1152,256]{1,0:T(8,128)(2,1)S(1)} collective-permute-done((bf16[1152,256]{1,0:T(8,128)(2,1)}, bf16[1152,256]{1,0:T(8,128)(2,1)S(1)}, u32[]{:S(2)}, u32[]{:S(2)}) %collective-permute-start.1) | collective-permute-done | bytes 589856 | tf_op jit(solution)/shard_map/ppermute | solution.py:746
  24.4 2.5 collective-permute-done.refs_1_
  29.8 14.0 %collective-permute-done.4.refs_3_ = bf16[1152,256]{1,0:T(8,128)(2,1)} collective-permute-done((bf16[1152,256]{1,0:T(8,128)(2,1)S(1)}, bf16[1152,256]{1,0:T(8,128)(2,1)}, u32[]{:S(2)}, u32[]{:S(2)}) %collective-permute-start.4) | collective-permute-done | bytes 589856 | tf_op jit(solution)/shard_map/ppermute | solution.py:747
  45.1 3.5 constant_dynamic-slice_fusion.2
  55.3 4.0 collective-permute-done.5.refs_5_
  59.3 20.9 %attend_forward.1 = (bf16[1152,1024]{1,0:T(8,128)(2,1)}, bf16[4,288,256]{2,1,0:T(8,128)(2,1)}, bf16[960,1024]{1,0:T(8,128)(2,1)}, f32[4,1024]{1,0:T(4,128)}) custom-call(s32[1]{0:T(128)S(6)} %convert_element_type.324.one_ref, s32[1]{0:T(128)} %bitcast.rank_ref, bf16[1152,256]{1,0:T(8,128)(2,1)} %get-tuple-element.179.refs_0_, bf16[1152,256]{1,0:T(8,128)(2,1)} %copy-done.18, ...), custom_call_target="tpu_custom_call" | custom-call | tf_op jit(solution)/shard_map/attend_forward/pallas_call | solution.py:163
  80.2 15.4 %all_to_all.25.refs_0_ = bf16[4,288,256]{2,1,0:T(8,128)(2,1)} all-to-all(bf16[4,288,256]{2,1,0:T(8,128)(2,1)} %get-tuple-element.180.refs_2_), channel_id=1, replica_groups=mesh['dp'=8,'seq'=4] {'seq'}, dimensions={0} | all-to-all | bytes 1179648 | tf_op jit(solution)/shard_map/all_to_all | solution.py:722
  95.6 37.9 %middle.1 = (bf16[256,1152]{1,0:T(8,128)(2,1)}, bf16[2048,256]{1,0:T(8,128)(2,1)}, bf16[256,2048]{1,0:T(8,128)(2,1)}, bf16[3200,256]{1,0:T(8,128)(2,1)}, bf16[25...) custom-call(bf16[4,288,256]{2,1,0:T(8,128)(2,1)} %all_to_all.25.refs, ...), custom_call_target="tpu_custom_call" | custom-call | tf_op jit(solution)/shard_map/middle/pallas_call | solution.py:402
  135.2 6.1 %collective-permute-done.6.refs_1_ = bf16[2048,256]{1,0:T(8,128)(2,1)} collective-permute-done((bf16[2048,256]{1,0:T(8,128)(2,1)}, bf16[2048,256]{1,0:T(8,128)(2,1)}, u32[]{:S(2)}, u32[]{:S(2)}) %collective-permute-start.6) | collective-permute-done | bytes 1048608 | tf_op jit(solution)/shard_map/ppermute | solution.py:694
  142.8 7.2 %weight_grad.6 = (bf16[1,256,2048]{2,1,0:T(8,128)(2,1)}, bf16[1,256,2048]{2,1,0:T(8,128)(2,1)}, bf16[1,256,2048]{2,1,0:T(8,128)(2,1)}, bf16[1,256,2048]{2,1,0:T(8,128)(2,1)}) custom-call(s32[4]{0:T(128)} %get-tuple-element.378.rows_ref, bf16[2048,256]{1,0:T(8,128)(2,1)} %get-tuple-element.183.refs_0_, bf16[2048,256]{1,0:T(8,128)(2,1)} %collective-permute-done.6.refs_1_, ...), custom_call_target="tpu_custom_call" | custom-call | tf_op jit(solution)/shard_map/weight_grad/pallas_call | solution.py:562
  152.7 8.7 %weight_grad.7 = (bf16[1,576,1152]{2,1,0:T(8,128)(2,1)}, bf16[1,576,1152]{2,1,0:T(8,128)(2,1)}, bf16[1,576,1152]{2,1,0:T(8,128)(2,1)}, bf16[1,576,1152]{2,1,0:T(8,128)(2,1)}) custom-call(s32[4]{0:T(128)} %get-tuple-element.376.rows_ref, bf16[6912,256]{1,0:T(8,128)(2,1)} %get-tuple-element.235.refs_0_, bf16[6912,256]{1,0:T(8,128)(2,1)} %copy-done, ...), custom_call_target="tpu_custom_call" | custom-call | tf_op jit(solution)/shard_map/weight_grad/pallas_call | solution.py:562
  163.5 7.0 %weight_grad_seq.1 = (bf16[2,576,512]{2,1,0:T(8,128)(2,1)}, bf16[576,512]{1,0:T(8,128)(2,1)}, bf16[576,512]{1,0:T(8,128)(2,1)}) custom-call(s32[8]{0:T(128)} %pad_add_fusion.order_ref, bf16[3200,256]{1,0:T(8,128)(2,1)} %get-tuple-element.206.refs_0_, bf16[3200,256]{1,0:T(8,128)(2,1)} %collective-permute-done.13.refs_1_, ...), custom_call_target="tpu_custom_call" | custom-call | tf_op jit(solution)/shard_map/weight_grad_seq/pallas_call | solution.py:629
  171.1 5.3 %collective-permute-done.10 = bf16[1,256,2048]{2,1,0:T(8,128)(2,1)} collective-permute-done((bf16[1,256,2048]{2,1,0:T(8,128)(2,1)}, bf16[1,256,2048]{2,1,0:T(8,128)(2,1)}, u32[]{:S(2)}, u32[]{:S(2)}) %collective-permute-start.10) | collective-permute-done | bytes 1048608 | tf_op jit(solution)/shard_map/ppermute | solution.py:694
  177.9 5.9 %weight_grad.8 = (bf16[2,256,768]{2,1,0:T(8,128)(2,1)}, bf16[1,256,768]{2,1,0:T(8,128)(2,1)}, bf16[1,256,768]{2,1,0:T(8,128)(2,1)}) custom-call(s32[4]{0:T(128)} %get-tuple-element.375.rows_ref, bf16[3200,256]{1,0:T(8,128)(2,1)} %get-tuple-element.206.refs_0_, bf16[3200,256]{1,0:T(8,128)(2,1)} %collective-permute-done.13.refs_1_, ...), custom_call_target="tpu_custom_call" | custom-call | tf_op jit(solution)/shard_map/weight_grad/pallas_call | solution.py:562
  185.4 16.9 %descend.1 = (bf16[256,5760]{1,0:T(8,128)(2,1)}, f32[256,1152]{1,0:T(8,128)}, bf16[4,288,256]{2,1,0:T(8,128)(2,1)}, f32[8,1152]{1,0:T(8,128)}) custom-call(bf16[256,1152]{1,0:T(8,128)(2,1)} %get-tuple-element.218.refs_2_.refs_0_, bf16[256,4608]{1,0:T(8,128)(2,1)} %get-tuple-element.219.refs_1_, f32[256,1152]{1,0:T(8,128)} %get-tuple-element.220.refs_2_, ...), custom_call_target="tpu_custom_call" | custom-call | tf_op jit(solution)/shard_map/descend/pallas_call | solution.py:469
  202.3 7.3 %collective-permute-done.16.got1_ref = bf16[2,256,768]{2,1,0:T(8,128)(2,1)S(1)} collective-permute-done((bf16[2,256,768]{2,1,0:T(8,128)(2,1)}, bf16[2,256,768]{2,1,0:T(8,128)(2,1)S(1)}, u32[]{:S(2)}, u32[]{:S(2)}) %collective-permute-start.16) | collective-permute-done | bytes 786464 | tf_op jit(solution)/shard_map/ppermute | solution.py:694
  210.9 3.1 add_convert_fusion.1
  216.5 3.5 all-to-all-start.1
  224.2 2.6 add_convert_fusion.2
  228.4 8.6 %weight_grad.9 = (bf16[1,144,4608]{2,1,0:T(8,128)(2,1)}, bf16[1,144,4608]{2,1,0:T(8,128)(2,1)}, bf16[1,144,4608]{2,1,0:T(8,128)(2,1)}, bf16[1,144,4608]{2,1,0:T(8,128)(2,1)}) custom-call(s32[4]{0:T(128)} %get-tuple-element.377.rows_ref, bf16[6912,256]{1,0:T(8,128)(2,1)} %get-tuple-element.235.refs_0_, bf16[6912,256]{1,0:T(8,128)(2,1)} %copy-done, ...), custom_call_target="tpu_custom_call" | custom-call | tf_op jit(solution)/shard_map/weight_grad/pallas_call | solution.py:562
  236.9 5.7 %weight_grad.10 = (bf16[2,144,1152]{2,1,0:T(8,128)(2,1)}, bf16[1,144,1152]{2,1,0:T(8,128)(2,1)}, bf16[1,144,1152]{2,1,0:T(8,128)(2,1)}) custom-call(s32[4]{0:T(128)} %get-tuple-element.373.rows_ref, bf16[6912,256]{1,0:T(8,128)(2,1)} %get-tuple-element.235.refs_0_, bf16[6912,256]{1,0:T(8,128)(2,1)} %copy-done, bf16[256,5760]{1,0:T(8,128)(2,1)} %get-tuple-element.242.refs_2_, ...), custom_call_target="tpu_custom_call" | custom-call | tf_op jit(solution)/shard_map/weight_grad/pallas_call | solution.py:562
  242.7 3.1 collective-permute-done.17.got2_ref
  249.3 4.0 split.5
  253.2 21.3 %attend_backward.1 = (bf16[864,1024]{1,0:T(8,128)(2,1)}, bf16[4,256,1152]{2,1,0:T(8,128)(2,1)}) custom-call(s32[1]{0:T(128)S(6)} %convert_element_type.324.one_ref, s32[1]{0:T(128)} %bitcast.rank_ref, bf16[4,288,256]{2,1,0:T(8,128)(2,1)} %copy-done.3, bf16[960,1024]{1,0:T(8,128)(2,1)} %get-tuple-element.261.refs_1_, ...), custom_call_target="tpu_custom_call" | custom-call | tf_op jit(solution)/shard_map/attend_backward/pallas_call | solution.py:265
  278.3 7.4 %weight_grad.11 = (bf16[4,144,864]{2,1,0:T(8,128)(2,1)}, bf16[2,144,864]{2,1,0:T(8,128)(2,1)}, bf16[2,144,864]{2,1,0:T(8,128)(2,1)}) custom-call(s32[8]{0:T(128)} %xor_multiply_fusion.5.rows_ref, bf16[1152,1024]{1,0:T(8,128)(2,1)} %get-tuple-element.269.refs_0_, bf16[864,1024]{1,0:T(8,128)(2,1)} %get-tuple-element.263.refs_1_), custom_call_target="tpu_custom_call" | custom-call | tf_op jit(solution)/shard_map/weight_grad/pallas_call | solution.py:562
  287.3 3.8 collective-permute-done.25
  292.4 2.9 add_convert_fusion
  299.3 4.6 %collective-permute-start.28 = (bf16[256,1152]{1,0:T(8,128)(2,1)}, bf16[256,1152]{1,0:T(8,128)(2,1)}, u32[]{:S(2)}, u32[]{:S(2)}) collective-permute-start(bf16[256,1152]{1,0:T(8,128)(2,1)} %get-tuple-element.356), channel_id=1, source_target_pairs={{0,1},{4,5},{8,9},{12,13},{16,17},{20,21},{24,25},{28,29}} | collective-permute-start | bytes 1769480 | tf_op jit(solution)/shard_map/ppermute | solution.py:790
  305.4 3.6 split.6
  309.0 7.4 %collective-permute-done.30 = bf16[288,576]{1,0:T(8,128)(2,1)} collective-permute-done((bf16[288,576]{1,0:T(8,128)(2,1)S(1)}, bf16[288,576]{1,0:T(8,128)(2,1)}, u32[]{:S(2)}, u32[]{:S(2)}) %collective-permute-start.30) | collective-permute-done | bytes 331808 | tf_op jit(solution)/shard_map/ppermute | solution.py:694
  320.8 6.3 %collective-permute-done.27.got2_ref = bf16[1,144,4608]{2,1,0:T(8,128)(2,1)} collective-permute-done((bf16[1,144,4608]{2,1,0:T(8,128)(2,1)}, bf16[1,144,4608]{2,1,0:T(8,128)(2,1)}, u32[]{:S(2)}, u32[]{:S(2)}) %collective-permute-start.27) | collective-permute-done | bytes 1327136 | tf_op jit(solution)/shard_map/ppermute | solution.py:694
  334.5 2.5 fusion.1
  337.0 4.9 %collective-permute-start.37 = (bf16[256,1152]{1,0:T(8,128)(2,1)}, bf16[256,1152]{1,0:T(8,128)(2,1)}, u32[]{:S(2)}, u32[]{:S(2)}) collective-permute-start(bf16[256,1152]{1,0:T(8,128)(2,1)} %get-tuple-element.354), channel_id=1, source_target_pairs={{0,1},{1,2},{4,5},{5,6},{8,9},{9,10},{12,13},{13,14},{16,17},{17,1... | collective-permute-start | bytes 1769480 | tf_op jit(solution)/shard_map/ppermute | solution.py:790
  344.1 4.4 %split.8 = (bf16[2,144,1152]{2,1,0:T(8,128)(2,1)}, bf16[144,1152]{1,0:T(8,128)(2,1)}, bf16[144,1152]{1,0:T(8,128)(2,1)}) custom-call(s32[1]{0:T(128)} %bitcast.rank_ref, bf16[1,144,4608]{2,1,0:T(8,128)(2,1)} %get-tuple-element.305.keep_ref, bf16[1,144,4608]{2,1,0:T(8,128)(2,1)} %collective-permute-done.26.got1_ref, ...), custom_call_target="tpu_custom_call" | custom-call | tf_op jit(solution)/shard_map/split/pallas_call | solution.py:683
  355.2 2.5 collective-permute-start.41
  360.7 14.1 %collective-permute-done.40 = bf16[256,512]{1,0:T(8,128)(2,1)S(1)} collective-permute-done((bf16[256,512]{1,0:T(8,128)(2,1)S(1)}, bf16[256,512]{1,0:T(8,128)(2,1)S(1)}, u32[]{:S(2)}, u32[]{:S(2)}) %collective-permute-start.40) | collective-permute-done | bytes 262176 | tf_op jit(solution)/shard_map/ppermute | solution.py:694
  378.9 3.7 collective-permute-start.44
  383.9 3.5 all-to-all-start.3
  387.3 2.5 add_convert_fusion.3
  389.9 4.1 collective-permute-start.42
  395.3 2.6 split.9
  400.4 2.6 collective-permute-start.47
  407.0 14.5 %collective-permute-done.46 = bf16[192,256]{1,0:T(8,128)(2,1)S(1)} collective-permute-done((bf16[192,256]{1,0:T(8,128)(2,1)}, bf16[192,256]{1,0:T(8,128)(2,1)S(1)}, u32[]{:S(2)}, u32[]{:S(2)}) %collective-permute-start.46) | collective-permute-done | bytes 98336 | tf_op jit(solution)/shard_map/ppermute | solution.py:694
  423.7 4.0 leave.1
  429.2 4.2 all-to-all-start.2
  436.0 3.0 all-to-all-done.2
  (236 shorter events, 94.4 us)
Async XLA Ops:
  5.1 17.8 %collective-permute-start.1 = (bf16[1152,256]{1,0:T(8,128)(2,1)}, bf16[1152,256]{1,0:T(8,128)(2,1)S(1)}, u32[]{:S(2)}, u32[]{:S(2)}) collective-permute-start(bf16[1152,256]{1,0:T(8,128)(2,1)} %get-tuple-element.179.refs_0_), channel_id=1, source_target_pairs={{0,1},{1,2},{2,3},{4,5},{5,6},{6,7},{8,9},{9,10},{10,11},{12,13},{... | collective-permute-start | bytes 1769480 | tf_op jit(solution)/shard_map/ppermute | solution.py:746
  10.1 16.9 %collective-permute-start = (bf16[1152,256]{1,0:T(8,128)(2,1)}, bf16[1152,256]{1,0:T(8,128)(2,1)S(1)}, u32[]{:S(2)}, u32[]{:S(2)}) collective-permute-start(bf16[1152,256]{1,0:T(8,128)(2,1)} %get-tuple-element.179.refs_0_), channel_id=1, source_target_pairs={{1,0},{2,1},{3,2},{5,4},{6,5},{7,6},{9,8},{10,9},{11,10},{13,12},{... | collective-permute-start | bytes 1769480 | tf_op jit(solution)/shard_map/ppermute | solution.py:747
  27.0 16.9 %collective-permute-start.4 = (bf16[1152,256]{1,0:T(8,128)(2,1)S(1)}, bf16[1152,256]{1,0:T(8,128)(2,1)}, u32[]{:S(2)}, u32[]{:S(2)}) collective-permute-start(bf16[1152,256]{1,0:T(8,128)(2,1)S(1)} %collective-permute-done.refs_1_), channel_id=1, source_target_pairs={{1,0},{2,1},{5,4},{6,5},{9,8},{10,9},{13,12},{14,13},{17,16},{18,1... | collective-permute-start | bytes 1769480 | tf_op jit(solution)/shard_map/ppermute | solution.py:747
  28.3 27.0 %collective-permute-start.3 = (bf16[1152,256]{1,0:T(8,128)(2,1)}, bf16[1152,256]{1,0:T(8,128)(2,1)}, u32[]{:S(2)}, u32[]{:S(2)}) collective-permute-start(bf16[1152,256]{1,0:T(8,128)(2,1)} %collective-permute-done.2.refs_4_), channel_id=1, source_target_pairs={{2,3},{6,7},{10,11},{14,15},{18,19},{22,23},{26,27},{30,31}} | collective-permute-start | bytes 1769480 | tf_op jit(solution)/shard_map/ppermute | solution.py:746
  43.8 15.5 %collective-permute-start.5 = (bf16[1152,256]{1,0:T(8,128)(2,1)}, bf16[1152,256]{1,0:T(8,128)(2,1)}, u32[]{:S(2)}, u32[]{:S(2)}) collective-permute-start(bf16[1152,256]{1,0:T(8,128)(2,1)} %collective-permute-done.4.refs_3_), channel_id=1, source_target_pairs={{1,0},{5,4},{9,8},{13,12},{17,16},{21,20},{25,24},{29,28}} | collective-permute-start | bytes 1769480 | tf_op jit(solution)/shard_map/ppermute | solution.py:747
  133.5 16.5 %collective-permute-start.8 = (bf16[6912,256]{1,0:T(8,128)(2,1)}, bf16[6912,256]{1,0:T(8,128)(2,1)S(1)}, u32[]{:S(2)}, u32[]{:S(2)}) collective-permute-start(bf16[6912,256]{1,0:T(8,128)(2,1)} %get-tuple-element.235.refs_0_), channel_id=1, source_target_pairs={{0,4},{4,0},{8,12},{12,8},{16,20},{20,16},{24,28},{28,24},{1,5},{5... | collective-permute-start | bytes 10616840 | tf_op jit(solution)/shard_map/ppermute | solution.py:694
  134.2 15.9 %collective-permute-start.9 = (bf16[256,1152]{1,0:T(8,128)(2,1)}, bf16[256,1152]{1,0:T(8,128)(2,1)}, u32[]{:S(2)}, u32[]{:S(2)}) collective-permute-start(bf16[256,1152]{1,0:T(8,128)(2,1)} %get-tuple-element.218.refs_2_.refs_0_), channel_id=1, source_target_pairs={{0,4},{4,0},{8,12},{12,8},{16,20},{20,16},{24,28},{28,24},{1,5},{5... | collective-permute-start | bytes 1769480 | tf_op jit(solution)/shard_map/ppermute | solution.py:694
  150.0 13.5 %collective-permute-start.13 = (bf16[3200,256]{1,0:T(8,128)(2,1)}, bf16[3200,256]{1,0:T(8,128)(2,1)}, u32[]{:S(2)}, u32[]{:S(2)}) collective-permute-start(bf16[3200,256]{1,0:T(8,128)(2,1)} %get-tuple-element.206.refs_0_), channel_id=1, source_target_pairs={{0,4},{4,0},{8,12},{12,8},{16,20},{20,16},{24,28},{28,24},{1,5},{5... | collective-permute-start | bytes 4915208 | tf_op jit(solution)/shard_map/ppermute | solution.py:694
  150.5 13.1 %collective-permute-start.14 = (bf16[256,2816]{1,0:T(8,128)(2,1)}, bf16[256,2816]{1,0:T(8,128)(2,1)}, u32[]{:S(2)}, u32[]{:S(2)}) collective-permute-start(bf16[256,2816]{1,0:T(8,128)(2,1)} %get-tuple-element.213.refs_2_), channel_id=1, source_target_pairs={{0,4},{4,0},{8,12},{12,8},{16,20},{20,16},{24,28},{28,24},{1,5},{5... | collective-permute-start | bytes 4325384 | tf_op jit(solution)/shard_map/ppermute | solution.py:694
  150.6 25.8 %collective-permute-start.10 = (bf16[1,256,2048]{2,1,0:T(8,128)(2,1)}, bf16[1,256,2048]{2,1,0:T(8,128)(2,1)}, u32[]{:S(2)}, u32[]{:S(2)}) collective-permute-start(bf16[1,256,2048]{2,1,0:T(8,128)(2,1)} %get-tuple-element.193), channel_id=1, source_target_pairs={{0,8},{4,12},{8,0},{12,4},{16,24},{20,28},{24,16},{28,20},{1,9},{5... | collective-permute-start | bytes 3145736 | tf_op jit(solution)/shard_map/ppermute | solution.py:694
  161.4 40.9 %collective-permute-start.12 = (bf16[1,576,1152]{2,1,0:T(8,128)(2,1)}, bf16[1,576,1152]{2,1,0:T(8,128)(2,1)S(1)}, u32[]{:S(2)}, u32[]{:S(2)}) collective-permute-start(bf16[1,576,1152]{2,1,0:T(8,128)(2,1)} %get-tuple-element.201), channel_id=1, source_target_pairs={{0,16},{4,20},{8,24},{12,28},{16,0},{20,4},{24,8},{28,12},{1,17},{... | collective-permute-start | bytes 3981320 | tf_op jit(solution)/shard_map/ppermute | solution.py:694
  170.6 39.0 %collective-permute-start.15 = (bf16[2,576,512]{2,1,0:T(8,128)(2,1)}, bf16[2,576,512]{2,1,0:T(8,128)(2,1)S(1)}, u32[]{:S(2)}, u32[]{:S(2)}) collective-permute-start(bf16[2,576,512]{2,1,0:T(8,128)(2,1)} %get-tuple-element.212), channel_id=1, source_target_pairs={{0,1},{1,0},{2,3},{3,2},{4,5},{5,4},{6,7},{7,6},{8,9},{9,8},{10,11... | collective-permute-start | bytes 3538952 | tf_op jit(solution)/shard_map/ppermute | solution.py:694
  176.4 25.9 %collective-permute-start.11 = (bf16[1,256,2048]{2,1,0:T(8,128)(2,1)}, bf16[1,256,2048]{2,1,0:T(8,128)(2,1)}, u32[]{:S(2)}, u32[]{:S(2)}) collective-permute-start(bf16[1,256,2048]{2,1,0:T(8,128)(2,1)} %get-tuple-element.205), channel_id=1, source_target_pairs={{0,8},{4,12},{8,0},{12,4},{16,24},{20,28},{24,16},{28,20},{1,9},{5... | collective-permute-start | bytes 3145736 | tf_op jit(solution)/shard_map/ppermute | solution.py:694
  183.8 25.8 %collective-permute-start.16 = (bf16[2,256,768]{2,1,0:T(8,128)(2,1)}, bf16[2,256,768]{2,1,0:T(8,128)(2,1)S(1)}, u32[]{:S(2)}, u32[]{:S(2)}) collective-permute-start(bf16[2,256,768]{2,1,0:T(8,128)(2,1)} %get-tuple-element.215), channel_id=1, source_target_pairs={{0,16},{4,20},{8,24},{12,28},{16,0},{20,4},{24,8},{28,12},{1,17},{... | collective-permute-start | bytes 2359304 | tf_op jit(solution)/shard_map/ppermute | solution.py:694
  210.9 15.9 %collective-permute-start.19 = (bf16[256,5760]{1,0:T(8,128)(2,1)}, bf16[256,5760]{1,0:T(8,128)(2,1)S(1)}, u32[]{:S(2)}, u32[]{:S(2)}) collective-permute-start(bf16[256,5760]{1,0:T(8,128)(2,1)} %get-tuple-element.242.refs_2_), channel_id=1, source_target_pairs={{0,4},{4,0},{8,12},{12,8},{16,20},{20,16},{24,28},{28,24},{1,5},{5... | collective-permute-start | bytes 8847368 | tf_op jit(solution)/shard_map/ppermute | solution.py:694
  213.9 31.9 %collective-permute-start.17 = (bf16[1,576,1152]{2,1,0:T(8,128)(2,1)}, bf16[1,576,1152]{2,1,0:T(8,128)(2,1)}, u32[]{:S(2)}, u32[]{:S(2)}) collective-permute-start(bf16[1,576,1152]{2,1,0:T(8,128)(2,1)} %add_convert_fusion.1), channel_id=1, source_target_pairs={{0,8},{4,12},{8,0},{12,4},{16,24},{20,28},{24,16},{28,20},{1,9},{5... | collective-permute-start | bytes 3981320 | tf_op jit(solution)/shard_map/ppermute | solution.py:694
  214.9 31.6 %collective-permute-start.18 = (bf16[1,576,1152]{2,1,0:T(8,128)(2,1)}, bf16[1,576,1152]{2,1,0:T(8,128)(2,1)}, u32[]{:S(2)}, u32[]{:S(2)}) collective-permute-start(bf16[1,576,1152]{2,1,0:T(8,128)(2,1)} %get-tuple-element.228), channel_id=1, source_target_pairs={{0,16},{4,20},{8,24},{12,28},{16,0},{20,4},{24,8},{28,12},{1,17},{... | collective-permute-start | bytes 3981320 | tf_op jit(solution)/shard_map/ppermute | solution.py:694
  216.5 26.2 %all-to-all-start.1 = ((bf16[4,288,256]{2,1,0:T(8,128)(2,1)}), bf16[4,288,256]{2,1,0:T(8,128)(2,1)S(1)}, u32[]{:S(2)}, u32[]{:S(2)}) async-start(bf16[4,288,256]{2,1,0:T(8,128)(2,1)} %get-tuple-element.232), calls=%async_computation.1 | async-start | bytes 1179648 | tf_op jit(solution)/shard_map/all_to_all | solution.py:722
  246.5 44.6 %collective-permute-start.20 = (bf16[1,144,4608]{2,1,0:T(8,128)(2,1)}, bf16[1,144,4608]{2,1,0:T(8,128)(2,1)S(1)}, u32[]{:S(2)}, u32[]{:S(2)}) collective-permute-start(bf16[1,144,4608]{2,1,0:T(8,128)(2,1)} %get-tuple-element.251), channel_id=1, source_target_pairs={{0,8},{4,12},{8,0},{12,4},{16,24},{20,28},{24,16},{28,20},{1,9},{5... | collective-permute-start | bytes 3981320 | tf_op jit(solution)/shard_map/ppermute | solution.py:694
  247.6 29.2 %collective-permute-start.24 = (bf16[576,512]{1,0:T(8,128)(2,1)S(1)}, bf16[576,512]{1,0:T(8,128)(2,1)}, u32[]{:S(2)}, u32[]{:S(2)}) collective-permute-start(bf16[576,512]{1,0:T(8,128)(2,1)S(1)} %copy-done.19), channel_id=1, source_target_pairs={{0,2},{1,3},{2,0},{3,1},{4,6},{5,7},{6,4},{7,5},{8,10},{9,11},{10,... | collective-permute-start | bytes 1769480 | tf_op jit(solution)/shard_map/ppermute | solution.py:694
  247.8 43.3 %collective-permute-start.22 = (bf16[1,256,2048]{2,1,0:T(8,128)(2,1)}, bf16[1,256,2048]{2,1,0:T(8,128)(2,1)}, u32[]{:S(2)}, u32[]{:S(2)}) collective-permute-start(bf16[1,256,2048]{2,1,0:T(8,128)(2,1)} %add_convert_fusion.2), channel_id=1, source_target_pairs={{0,16},{4,20},{8,24},{12,28},{16,0},{20,4},{24,8},{28,12},{1,17},{... | collective-permute-start | bytes 3145736 | tf_op jit(solution)/shard_map/ppermute | solution.py:694
  274.6 12.7 %collective-permute-start.23 = (bf16[2,144,1152]{2,1,0:T(8,128)(2,1)}, bf16[2,144,1152]{2,1,0:T(8,128)(2,1)S(1)}, u32[]{:S(2)}, u32[]{:S(2)}) collective-permute-start(bf16[2,144,1152]{2,1,0:T(8,128)(2,1)} %get-tuple-element.264), channel_id=1, source_target_pairs={{0,16},{4,20},{8,24},{12,28},{16,0},{20,4},{24,8},{28,12},{1,17},{... | collective-permute-start | bytes 1990664 | tf_op jit(solution)/shard_map/ppermute | solution.py:694
  275.1 16.0 %collective-permute-start.25 = (bf16[2,288,576]{2,1,0:T(8,128)(2,1)}, bf16[2,288,576]{2,1,0:T(8,128)(2,1)S(1)}, u32[]{:S(2)}, u32[]{:S(2)}) collective-permute-start(bf16[2,288,576]{2,1,0:T(8,128)(2,1)} %get-tuple-element.259), channel_id=1, source_target_pairs={{0,1},{1,0},{2,3},{3,2},{4,5},{5,4},{6,7},{7,6},{8,9},{9,8},{10,11... | collective-permute-start | bytes 1990664 | tf_op jit(solution)/shard_map/ppermute | solution.py:694
  276.7 10.5 %collective-permute-start.21 = (bf16[1,256,768]{2,1,0:T(8,128)(2,1)}, bf16[1,256,768]{2,1,0:T(8,128)(2,1)}, u32[]{:S(2)}, u32[]{:S(2)}) collective-permute-start(bf16[1,256,768]{2,1,0:T(8,128)(2,1)} %add_convert_fusion.8), channel_id=1, source_target_pairs={{0,8},{4,12},{8,0},{12,4},{16,24},{20,28},{24,16},{28,20},{1,9},{5... | collective-permute-start | bytes 1179656 | tf_op jit(solution)/shard_map/ppermute | solution.py:694
  292.4 11.5 %collective-permute-start.31 = (bf16[4,144,864]{2,1,0:T(8,128)(2,1)S(1)}, bf16[4,144,864]{2,1,0:T(8,128)(2,1)}, u32[]{:S(2)}, u32[]{:S(2)}) collective-permute-start(bf16[4,144,864]{2,1,0:T(8,128)(2,1)S(1)} %copy-done.50), channel_id=1, source_target_pairs={{0,4},{4,0},{8,12},{12,8},{16,20},{20,16},{24,28},{28,24},{1,5},{5... | collective-permute-start | bytes 2985992 | tf_op jit(solution)/shard_map/ppermute | solution.py:694
  295.4 31.8 %collective-permute-start.27 = (bf16[1,144,4608]{2,1,0:T(8,128)(2,1)}, bf16[1,144,4608]{2,1,0:T(8,128)(2,1)}, u32[]{:S(2)}, u32[]{:S(2)}) collective-permute-start(bf16[1,144,4608]{2,1,0:T(8,128)(2,1)} %add_convert_fusion), channel_id=1, source_target_pairs={{0,16},{4,20},{8,24},{12,28},{16,0},{20,4},{24,8},{28,12},{1,17},{... | collective-permute-start | bytes 3981320 | tf_op jit(solution)/shard_map/ppermute | solution.py:694
  296.9 31.6 %collective-permute-start.26 = (bf16[1,144,4608]{2,1,0:T(8,128)(2,1)}, bf16[1,144,4608]{2,1,0:T(8,128)(2,1)}, u32[]{:S(2)}, u32[]{:S(2)}) collective-permute-start(bf16[1,144,4608]{2,1,0:T(8,128)(2,1)} %get-tuple-element.277), channel_id=1, source_target_pairs={{0,8},{4,12},{8,0},{12,4},{16,24},{20,28},{24,16},{28,20},{1,9},{5... | collective-permute-start | bytes 3981320 | tf_op jit(solution)/shard_map/ppermute | solution.py:694
  298.0 18.5 %collective-permute-start.30 = (bf16[288,576]{1,0:T(8,128)(2,1)S(1)}, bf16[288,576]{1,0:T(8,128)(2,1)}, u32[]{:S(2)}, u32[]{:S(2)}) collective-permute-start(bf16[288,576]{1,0:T(8,128)(2,1)S(1)} %fusion.6), channel_id=1, source_target_pairs={{0,2},{1,3},{2,0},{3,1},{4,6},{5,7},{6,4},{7,5},{8,10},{9,11},{10,... | collective-permute-start | bytes 995336 | tf_op jit(solution)/shard_map/ppermute | solution.py:694
  299.3 21.6 %collective-permute-start.28 = (bf16[256,1152]{1,0:T(8,128)(2,1)}, bf16[256,1152]{1,0:T(8,128)(2,1)}, u32[]{:S(2)}, u32[]{:S(2)}) collective-permute-start(bf16[256,1152]{1,0:T(8,128)(2,1)} %get-tuple-element.356), channel_id=1, source_target_pairs={{0,1},{4,5},{8,9},{12,13},{16,17},{20,21},{24,25},{28,29}} | collective-permute-start | bytes 1769480 | tf_op jit(solution)/shard_map/ppermute | solution.py:790
  303.9 17.0 %collective-permute-start.29 = (bf16[256,1152]{1,0:T(8,128)(2,1)S(1)}, bf16[256,1152]{1,0:T(8,128)(2,1)}, u32[]{:S(2)}, u32[]{:S(2)}) collective-permute-start(bf16[256,1152]{1,0:T(8,128)(2,1)S(1)} %get-tuple-element.355), channel_id=1, source_target_pairs={{3,2},{7,6},{11,10},{15,14},{19,18},{23,22},{27,26},{31,30}} | collective-permute-start | bytes 1769480 | tf_op jit(solution)/shard_map/ppermute | solution.py:793
  316.4 14.2 %collective-permute-start.32 = (bf16[2,256,512]{2,1,0:T(8,128)(2,1)}, bf16[2,256,512]{2,1,0:T(8,128)(2,1)}, u32[]{:S(2)}, u32[]{:S(2)}) collective-permute-start(bf16[2,256,512]{2,1,0:T(8,128)(2,1)} %get-tuple-element.287), channel_id=1, source_target_pairs={{0,1},{1,0},{2,3},{3,2},{4,5},{5,4},{6,7},{7,6},{8,9},{9,8},{10,11... | collective-permute-start | bytes 1572872 | tf_op jit(solution)/shard_map/ppermute | solution.py:694
  333.0 18.9 %collective-permute-start.34 = (bf16[2,144,864]{2,1,0:T(8,128)(2,1)}, bf16[2,144,864]{2,1,0:T(8,128)(2,1)}, u32[]{:S(2)}, u32[]{:S(2)}) collective-permute-start(bf16[2,144,864]{2,1,0:T(8,128)(2,1)} %get-tuple-element.363), channel_id=1, source_target_pairs={{0,16},{4,20},{8,24},{12,28},{16,0},{20,4},{24,8},{28,12},{1,17},{... | collective-permute-start | bytes 1493000 | tf_op jit(solution)/shard_map/ppermute | solution.py:694
  333.5 16.3 %collective-permute-start.33 = (bf16[1,144,1152]{2,1,0:T(8,128)(2,1)}, bf16[1,144,1152]{2,1,0:T(8,128)(2,1)}, u32[]{:S(2)}, u32[]{:S(2)}) collective-permute-start(bf16[1,144,1152]{2,1,0:T(8,128)(2,1)} %add_convert_fusion.9), channel_id=1, source_target_pairs={{0,8},{4,12},{8,0},{12,4},{16,24},{20,28},{24,16},{28,20},{1,9},{5... | collective-permute-start | bytes 995336 | tf_op jit(solution)/shard_map/ppermute | solution.py:694
  337.0 18.1 %collective-permute-start.37 = (bf16[256,1152]{1,0:T(8,128)(2,1)}, bf16[256,1152]{1,0:T(8,128)(2,1)}, u32[]{:S(2)}, u32[]{:S(2)}) collective-permute-start(bf16[256,1152]{1,0:T(8,128)(2,1)} %get-tuple-element.354), channel_id=1, source_target_pairs={{0,1},{1,2},{4,5},{5,6},{8,9},{9,10},{12,13},{13,14},{16,17},{17,1... | collective-permute-start | bytes 1769480 | tf_op jit(solution)/shard_map/ppermute | solution.py:790
  342.0 15.7 %collective-permute-start.38 = (bf16[256,1152]{1,0:T(8,128)(2,1)}, bf16[256,1152]{1,0:T(8,128)(2,1)}, u32[]{:S(2)}, u32[]{:S(2)}) collective-permute-start(bf16[256,1152]{1,0:T(8,128)(2,1)} %get-tuple-element.353), channel_id=1, source_target_pairs={{2,1},{3,2},{6,5},{7,6},{10,9},{11,10},{14,13},{15,14},{18,17},{19... | collective-permute-start | bytes 1769480 | tf_op jit(solution)/shard_map/ppermute | solution.py:793
  348.5 26.3 %collective-permute-start.39 = (bf16[2,144,1152]{2,1,0:T(8,128)(2,1)}, bf16[2,144,1152]{2,1,0:T(8,128)(2,1)S(1)}, u32[]{:S(2)}, u32[]{:S(2)}) collective-permute-start(bf16[2,144,1152]{2,1,0:T(8,128)(2,1)} %get-tuple-element.308), channel_id=1, source_target_pairs={{0,1},{1,0},{2,3},{3,2},{4,5},{5,4},{6,7},{7,6},{8,9},{9,8},{10,11... | collective-permute-start | bytes 1990664 | tf_op jit(solution)/shard_map/ppermute | solution.py:694
  349.8 25.0 %collective-permute-start.40 = (bf16[256,512]{1,0:T(8,128)(2,1)S(1)}, bf16[256,512]{1,0:T(8,128)(2,1)S(1)}, u32[]{:S(2)}, u32[]{:S(2)}) collective-permute-start(bf16[256,512]{1,0:T(8,128)(2,1)S(1)} %fusion.10), channel_id=1, source_target_pairs={{0,2},{1,3},{2,0},{3,1},{4,6},{5,7},{6,4},{7,5},{8,10},{9,11},{10,... | collective-permute-start | bytes 786440 | tf_op jit(solution)/shard_map/ppermute | solution.py:694
  351.9 25.0 %collective-permute-start.36 = (bf16[2,144,512]{2,1,0:T(8,128)(2,1)S(1)}, bf16[2,144,512]{2,1,0:T(8,128)(2,1)S(1)}, u32[]{:S(2)}, u32[]{:S(2)}) collective-permute-start(bf16[2,144,512]{2,1,0:T(8,128)(2,1)S(1)} %slice.150), channel_id=1, source_target_pairs={{0,16},{4,20},{8,24},{12,28},{16,0},{20,4},{24,8},{28,12},{1,17},{... | collective-permute-start | bytes 884744 | tf_op jit(solution)/shard_map/ppermute | solution.py:694
  355.2 21.7 %collective-permute-start.41 = (bf16[2,192,256]{2,1,0:T(8,128)(2,1)S(1)}, bf16[2,192,256]{2,1,0:T(8,128)(2,1)S(1)}, u32[]{:S(2)}, u32[]{:S(2)}) collective-permute-start(bf16[2,192,256]{2,1,0:T(8,128)(2,1)S(1)} %copy-done.51), channel_id=1, source_target_pairs={{0,1},{1,0},{2,3},{3,2},{4,5},{5,4},{6,7},{7,6},{8,9},{9,8},{10,11... | collective-permute-start | bytes 589832 | tf_op jit(solution)/shard_map/ppermute | solution.py:694
  357.7 19.3 %collective-permute-start.35 = (bf16[144,864]{1,0:T(8,128)(2,1)S(1)}, bf16[144,864]{1,0:T(8,128)(2,1)S(1)}, u32[]{:S(2)}, u32[]{:S(2)}) collective-permute-start(bf16[144,864]{1,0:T(8,128)(2,1)S(1)} %get-tuple-element.300), channel_id=1, source_target_pairs={{0,8},{4,12},{8,0},{12,4},{16,24},{20,28},{24,16},{28,20},{1,9},{5... | collective-permute-start | bytes 746504 | tf_op jit(solution)/shard_map/ppermute | solution.py:694
  377.0 23.4 %collective-permute-start.45 = (bf16[144,512]{1,0:T(8,128)(2,1)S(1)}, bf16[144,512]{1,0:T(8,128)(2,1)}, u32[]{:S(2)}, u32[]{:S(2)}) collective-permute-start(bf16[144,512]{1,0:T(8,128)(2,1)S(1)} %fusion.18), channel_id=1, source_target_pairs={{0,8},{4,12},{8,0},{12,4},{16,24},{20,28},{24,16},{28,20},{1,9},{5... | collective-permute-start | bytes 442376 | tf_op jit(solution)/shard_map/ppermute | solution.py:694
  378.9 42.7 %collective-permute-start.44 = (bf16[144,1152]{1,0:T(8,128)(2,1)}, bf16[144,1152]{1,0:T(8,128)(2,1)}, u32[]{:S(2)}, u32[]{:S(2)}) collective-permute-start(bf16[144,1152]{1,0:T(8,128)(2,1)} %fusion.8), channel_id=1, source_target_pairs={{0,2},{1,3},{2,0},{3,1},{4,6},{5,7},{6,4},{7,5},{8,10},{9,11},{10,... | collective-permute-start | bytes 995336 | tf_op jit(solution)/shard_map/ppermute | solution.py:694
  383.9 22.2 %all-to-all-start.3 = ((bf16[4,144,288]{2,1,0:T(8,128)(2,1)}), bf16[4,144,288]{2,1,0:T(8,128)(2,1)S(1)}, u32[]{:S(2)}, u32[]{:S(2)}) async-start(bf16[4,144,288]{2,1,0:T(8,128)(2,1)} %pad_maximum_fusion.1), calls=%async_computation.3 | async-start | bytes 884736 | tf_op jit(solution)/shard_map/all_to_all | solution.py:722
  389.9 31.7 %collective-permute-start.42 = (bf16[256,1152]{1,0:T(8,128)(2,1)}, bf16[256,1152]{1,0:T(8,128)(2,1)S(1)}, u32[]{:S(2)}, u32[]{:S(2)}) collective-permute-start(bf16[256,1152]{1,0:T(8,128)(2,1)} %get-tuple-element.352), channel_id=1, source_target_pairs={{0,1},{1,2},{2,3},{4,5},{5,6},{6,7},{8,9},{9,10},{10,11},{12,13},{... | collective-permute-start | bytes 1769480 | tf_op jit(solution)/shard_map/ppermute | solution.py:790
  394.0 27.6 %collective-permute-start.43 = (bf16[256,1152]{1,0:T(8,128)(2,1)}, bf16[256,1152]{1,0:T(8,128)(2,1)S(1)}, u32[]{:S(2)}, u32[]{:S(2)}) collective-permute-start(bf16[256,1152]{1,0:T(8,128)(2,1)} %get-tuple-element.351), channel_id=1, source_target_pairs={{1,0},{2,1},{3,2},{5,4},{6,5},{7,6},{9,8},{10,9},{11,10},{13,12},{... | collective-permute-start | bytes 1769480 | tf_op jit(solution)/shard_map/ppermute | solution.py:793
  400.4 21.1 %collective-permute-start.47 = (bf16[2,144,288]{2,1,0:T(8,128)(2,1)}, bf16[2,144,288]{2,1,0:T(8,128)(2,1)S(1)}, u32[]{:S(2)}, u32[]{:S(2)}) collective-permute-start(bf16[2,144,288]{2,1,0:T(8,128)(2,1)} %get-tuple-element.326), channel_id=1, source_target_pairs={{0,1},{1,0},{2,3},{3,2},{4,5},{5,4},{6,7},{7,6},{8,9},{9,8},{10,11... | collective-permute-start | bytes 497672 | tf_op jit(solution)/shard_map/ppermute | solution.py:694
  403.1 18.5 %collective-permute-start.46 = (bf16[192,256]{1,0:T(8,128)(2,1)}, bf16[192,256]{1,0:T(8,128)(2,1)S(1)}, u32[]{:S(2)}, u32[]{:S(2)}) collective-permute-start(bf16[192,256]{1,0:T(8,128)(2,1)} %fusion.17), channel_id=1, source_target_pairs={{0,2},{1,3},{2,0},{3,1},{4,6},{5,7},{6,4},{7,5},{8,10},{9,11},{10,... | collective-permute-start | bytes 294920 | tf_op jit(solution)/shard_map/ppermute | solution.py:694
  423.5 16.3 %collective-permute-start.48 = (bf16[144,288]{1,0:T(8,128)(2,1)S(1)}, bf16[144,288]{1,0:T(8,128)(2,1)S(1)}, u32[]{:S(2)}, u32[]{:S(2)}) collective-permute-start(bf16[144,288]{1,0:T(8,128)(2,1)S(1)} %fusion.13), channel_id=1, source_target_pairs={{0,2},{1,3},{2,0},{3,1},{4,6},{5,7},{6,4},{7,5},{8,10},{9,11},{10,... | collective-permute-start | bytes 248840 | tf_op jit(solution)/shard_map/ppermute | solution.py:694
  (58 other events, 506.9 us)

commit v5 on v4

--- a/solution.py
+++ b/solution.py
@@ -153,7 +153,7 @@
 
     lax.fori_loop(0, heads, head_step, 0)
     for d in range(size):
-        o_ref[lax.rem(rank_ref[0] + d, size)] = o_all_ref[:, d * tok : (d + 1) * tok].astype(BF)
+        o_ref[d] = o_all_ref[:, d * tok : (d + 1) * tok].astype(BF)
 
 
 def attend_forward(one, rank, pieces, w, idk, idq, heads, tile, diagonal):
@@ -188,7 +188,7 @@
         do = dos_ref[owner].astype(F32)
         do_ref[0:local, at] = do
         do_ref[local : local + HP - HD, at] = jnp.zeros((HP - HD, tok), F32)
-        prod = do * o_ref[owner].astype(F32)
+        prod = do * o_ref[d].astype(F32)
         for head in range(heads):
             delta_ref[head : head + 1, at] = col_sum(prod[head * HD : (head + 1) * HD, :])
 
@@ -284,12 +284,13 @@
 STEP = 512
 
 
-def middle_kernel(*refs):
-    (o_refs, tokens_ref, mods_ref, dino_ref, cot_ref, wo_any, w1_any, w2_any, p1_any, p2_any, p3_any) = refs[:11]
+def middle_kernel(size, rank_ref, *refs):
+    o_refs, refs = refs[:size], refs[size:]
+    (tokens_ref, mods_ref, dino_ref, cot_ref, wo_any, w1_any, w2_any, p1_any, p2_any, p3_any) = refs[:10]
     (out_ref, a1_ref, dr2_ref, left1_ref, right1_ref, left2_ref, gp_ref, dmlp_ref, dy_ref, normed_ref, inv_ref, attn_ref,
-     gate_ref) = refs[11:24]
-    (wo_ref, w1_ref, w2_ref, p1_ref, p2_ref, p3_ref, act_ref, w1_sem, sems) = refs[24:]
-    size, local, tok = o_refs.shape
+     gate_ref) = refs[10:23]
+    (wo_ref, w1_ref, w2_ref, p1_ref, p2_ref, p3_ref, act_ref, w1_sem, sems) = refs[23:]
+    local, tok = o_refs[0].shape
     width = size * local
     hidden = w1_any.shape[1]
     wide, narrow = p3_ref.shape
@@ -318,7 +319,8 @@
 
     gate1, shift2, scale2, gate2 = [mods_ref[i : i + 1, :] for i in (2, 3, 4, 5)]
     for d in range(size):
-        o_ref[d * local : (d + 1) * local, :] = o_refs[d]
+        owner = lax.rem(rank_ref[0] + size - d, size)
+        o_ref[pl.ds(pl.multiple_of(owner * local, 16), local), :] = o_refs[d][...]
     wo_copy.wait()
     attn = trans_times(o_ref[...], wo_ref[...])
     attn_ref[...] = attn
@@ -396,17 +398,17 @@
     gate_ref[...] = col_sum(dy * mlp)
 
 
-def middle(os, tokens, mods, dino, cot, wo, w1, w2, p1, p2, p3):
+def middle(rank, os, tokens, mods, dino, cot, wo, w1, w2, p1, p2, p3):
     tok, width = tokens.shape
     hidden, wide, narrow = w1.shape[1], p1.shape[1], p3.shape[1]
     return pl.pallas_call(
-        middle_kernel,
+        functools.partial(middle_kernel, len(os)),
         out_shape=(
             shape((tok, width)), shape((wide, tok)), shape((tok, wide)), shape((wide + width, tok)),
             shape((tok, wide + narrow)), shape((hidden + 2 * width, tok)), shape((tok, hidden)), shape((tok, width)), shape((tok, width), F32),
             shape((tok, width), F32), shape((tok, 1), F32), shape((tok, width), F32), shape((1, width), F32),
         ),
-        in_specs=[VMEM] * 5 + [ANY] * 6,
+        in_specs=[SMEM] + [VMEM] * (len(os) + 4) + [ANY] * 6,
         out_specs=(VMEM,) * 13,
         scratch_shapes=[
             pltpu.VMEM(dims, BF)
@@ -415,7 +417,7 @@
         + [pltpu.SemaphoreType.DMA((4,)), pltpu.SemaphoreType.DMA((5,))],
         compiler_params=params(),
         name="middle",
-    )(os, tokens, mods, dino, cot, wo, w1, w2, p1, p2, p3)
+    )(rank, *os, tokens, mods, dino, cot, wo, w1, w2, p1, p2, p3)
 
 
 def descend_kernel(size, *refs):
@@ -761,9 +763,11 @@
     first_all, heads_out, qkv, lse = attend_forward(
         one, rank_arg, pieces, w_pad, idk, idq, heads, tile, diagonal
     )
-    attended = exchange(heads_out)
+    attended = [heads_out[0]]
+    for d in range(1, n_seq):
+        attended.append(lax.ppermute(heads_out[d], "seq", [(i, (i + d) % n_seq) for i in range(n_seq)]))
     (rounded, act1, dr2, left1, right1, left2, gelu_slope, dmlp, dy, normed2, inv2, attn, sum_gate2) = middle(
-        attended, tokens, mods, dino, cotangent, w_out, w_fc1, w_fc2, w_proj1, w_proj2, w_proj3
+        rank_arg, attended, tokens, mods, dino, cotangent, w_out, w_fc1, w_fc2, w_proj1, w_proj2, w_proj3
     )
 
     fast = all(k % (16 * n_dp) == 0 for k in (width, hidden, wide)) and n_dp == 8 and n_seq == 4
@@ -775,6 +779,20 @@
         return attend_backward(
             one, rank_arg, dos, qkv, heads_out, lse, w_rows, idk, idq, heads, tile, diagonal
         )
+
+    def mods_out(sums1):
+        rows = jnp.concatenate([sums1[0:2], sums2[0:3], sum_gate2], axis=0)
+        return rows.reshape(n_seq, 6 * width // n_seq)
+
+    def units_out(g_heads):
+        units = [g_heads[:, i * local : (i + 1) * local] for i in range(3)]
+        outgoing = []
+        for target in range(n_seq):
+            mine = jnp.zeros_like(units[0])
+            for i in range(3):
+                mine = jnp.where((n_seq * i + rank) // 3 == target, units[i], mine)
+            outgoing.append(mine)
+        return jnp.stack(outgoing)
 
     if fast:
         swap = lambda x, bit: flip(x, "dp", n_dp, bit)
@@ -795,16 +813,28 @@
         def row_starts(base, deep, bits):
             return base + (me ^ jnp.array(masks_of(bits), jnp.int32)) * (deep // n_dp)
 
+        def row_starts(base, deep, bits):
+            return base + (me ^ jnp.array(masks_of(bits), jnp.int32)) * (deep // n_dp)
+
+        def last(*terms):
+            return sum(v.astype(F32) for v in terms)
+
         quarter = (1, 1, 1, 1)
+        lefts2, dmlps = [left2, swap(left2, core)], [dmlp, swap(dmlp, core)]
         act1_other, dr2_other = swap(act1, core), swap(dr2, core)
-        lefts2, dmlps = [left2, swap(left2, core)], [dmlp, swap(dmlp, core)]
+        right2, dhidden1, dheads, sums2 = down(dmlp)
+        act1_other, dr2_other, lefts2, dmlps, left1, right1, right2, dheads = together(
+            act1_other, dr2_other, lefts2, dmlps, left1, right1, right2, dheads
+        )
+
+        dheads_in = exchange(dheads)
         (p2,) = weight_grad([act1, act1_other], [dr2, dr2_other], [job(0, wide, (x, y), 0)], quarter, wide, STEP)
-        p2, lefts2, dmlps, left1, right1 = together(p2, lefts2, dmlps, left1, right1)
+        p2, lefts2, dmlps, left1, right1, right2 = together(p2, lefts2, dmlps, left1, right1, right2)
 
         p2a = swap(p2[0], x)
-        p2b = swap(after(p2[1], p2a), x)
         (f2,) = weight_grad(lefts2, dmlps, [job(0, hidden, (y, x), 0)], quarter, width, 384)
         f2a = swap(f2[0], y)
+        p2b = swap(after(p2[1], p2a), x)
         lefts1, rights1 = [left1, swap(left1, core)], [right1, swap(right1, core)]
         p1n, p1f, p1o = weight_grad_seq(
             lefts1, after(rights1, f2), row_starts(wide, width, (y, x)), width // n_dp,
@@ -812,76 +842,78 @@
         )
         p1z = near(p1n)
         (p3,) = weight_grad(
-            lefts1, after(rights1, p1n), [job(0, wide, (y, x), wide // 256)], (2, 1, 1), narrow, 256
+            lefts1, after(rights1, p1n, dheads_in), [job(0, wide, (y, x), wide // 256)], (2, 1, 1), narrow, 256
         )
         p3a = swap(p3[0], y)
-        right2, dhidden1, dheads, sums2 = down(after(dmlp, p3, p2a))
-        p2, f2, p2a, p2b, f2a, p1f, p1o, p1z, p3, p3a, right2, dhidden1, dheads, sums2, lefts2 = together(
-            p2, f2, p2a, p2b, f2a, p1f, p1o, p1z, p3, p3a, right2, dhidden1, dheads, sums2, lefts2
-        )
-
-        f2c, f2b = swap(add(f2[2], f2a), x), swap(f2[1], y)
-        dheads_in = exchange(dheads)
         rights2 = [right2, swap(right2, core)]
+        dqkv, dx = back(after(dheads_in, p3, p2a))
+        f2s = add(f2[2], after(f2a, dqkv))
+        p2, f2, p2a, p2b, f2s, p1f, p1o, p1z, p3, p3a, rights2, dqkv, dx = together(
+            p2, f2, p2a, p2b, f2s, p1f, p1o, p1z, p3, p3a, rights2, dqkv, dx
+        )
+
+        f2c, f2b = swap(f2s, x), swap(f2[1], y)
+        up, low = right(dx[3], 1), left(dx[1], 1)
         (f1,) = weight_grad(lefts2, rights2, [job(hidden, width, (x, y), 0)], quarter, hidden, 1152)
+        p1y = far(add(p1f, p1z[0]))
+        (fq,) = weight_grad(
+            [first_all], [after(dqkv, f1)], [job(0, width, (core, y, x), 0)], (4, 2, 2), 3 * local, 3 * local,
+            flat=True,
+        )
         (fo,) = weight_grad(
-            lefts2, after(rights2, f1), [job(hidden + width, width, (y, x), hidden // 384)], (2, 1, 1), width, 384
-        )
-        p2s, p1f, p1o = add(p2[2], p2a), add(p1f, p1z[0]), add(p1o, p1z[1])
-        p3s = add(p3[1], p3a[:1])
-        f2, f2c, f2b, dheads_in, p3s, f1, fo, p2s, p1f = together(f2, f2c, f2b, dheads_in, p3s, f1, fo, p2s, p1f)
-
-        f1a, p3c, p2c, p1y = swap(f1[0], x), swap(p3s, x), swap(p2s, y), far(p1f)
-        f2n, f2f, f2o = split(rank_arg, f2[3], f2b, f2c, turned=True)
+            lefts2, after(rights2, fq), [job(hidden + width, width, (y, x), hidden // 384)], (2, 1, 1), width, 384
+        )
+        p2s, p3s, p1o = add(p2[2], p2a), add(p3[1], p3a[:1]), add(p1o, p1z[1])
+        f2, f2c, f2b, up, low, p1y, p3s, f1, fq, fo, p2s, p1o = together(
+            f2, f2c, f2b, up, low, p1y, p3s, f1, fq, fo, p2s, p1o
+        )
+
+        f1a, p2c = swap(f1[0], x), swap(p2s, y)
+        up, low = right(add(dx[2], up), 2), left(add(dx[2], low), 2)
+        fqa = swap(fq[0], core)
+        f2n, f2f, f2o = split(rank_arg, after(f2[3], fqa), f2b, f2c, turned=True)
         f2z = near(f2n)
-        dqkv, dx = back(after(dheads_in, f2n))
-        foa = swap(after(fo[0], dqkv), y)
-        (fq,) = weight_grad(
-            [first_all], [dqkv], [job(0, width, (core, y, x), 0)], (4, 2, 2), 3 * local, 3 * local, flat=True
-        )
+        p3c = swap(after(p3s, f2n), x)
+        foa = swap(after(fo[0], p2c), y)
         p1d = add(p1o, p1y).reshape(4, width // n_dp, wide // n_seq)
-        f1a, p3c, p2c, foa, p1d, f2z, f2f, dqkv, dx, fq, f1 = together(
-            f1a, p3c, p2c, foa, p1d, f2z, f2f, dqkv, dx, fq, f1
-        )
-
-        f1b, f1c = swap(f1[1], x), swap(add(f1[2], f1a), y)
-        up, low = right(dx[3], 1), left(dx[1], 1)
-        fqa = swap(fq[0], core)
+        p2n, p2f, p2o = split(rank_arg, p2[3], p2b, p2c)
+        f1s = add(f1[2], f1a)
+        f1s, p3c, p2n, p2f, foa, p1d, f2z, f2f, up, low, fqa, f1, fo = together(
+            f1s, p3c, p2n, p2f, foa, p1d, f2z, f2f, up, low, fqa, f1, fo
+        )
+
+        f1b, f1c = swap(f1[1], x), swap(f1s, y)
+        up, low = right(add(dx[1], up), 3), left(add(dx[3], low), 3)
         f2y = far(add(f2f, f2z[0]))
-        p2n, p2f, p2o = split(rank_arg, after(p2[3], fqa), p2b, p2c)
         p2z = near(p2n)
-        p3n, p3f, p3o = split(rank_arg, after(p3[2], p2n), p3a, p3c, turned=True)
-        fos = add(fo[1], foa[:1])
-        f1b, f1c, up, low, f2y, fqa, p2z, p2f, p3n, fos, p1d = together(
-            f1b, f1c, up, low, f2y, fqa, p2z, p2f, p3n, fos, p1d
-        )
-
-        foc, fqb = swap(fos, x), swap(add(fq[1], fqa[:2]), y)
-        up, low = right(add(dx[2], up), 2), left(add(dx[2], low), 2)
+        p3n, p3f, p3o = split(rank_arg, p3[2], p3a, p3c, turned=True)
+        fos, fqs, fqk = add(fo[1], foa[:1]), add(fq[1], fqa[:2]), add(fq[2], fqa[2:])
+        f1b, f1c, up, low, f2y, p2z, p2f, p3n, fos, fqs, fqk, p1d = together(
+            f1b, f1c, up, low, f2y, p2z, p2f, p3n, fos, fqs, fqk, p1d
+        )
+
+        foc, fqb = swap(fos, x), swap(fqs, y)
+        p2y = far(add(p2f, p2z[0]))
         f1n, f1f, f1o = split(rank_arg, f1[3], f1b, f1c)
         f1z = near(f1n)
-        fqk = add(fq[2], fqa[2:])
+        p1e = swap(p1d[0:2], y)
+        p3z = near(p3n)
         fqs, fqk = add(fqk[0], fqb[0]), add(fqk[1], fqb[1])
-        p1e = swap(after(p1d[0:2], fqb), y)
         fqc = swap(after(fqs, foc), x)
-        p2y = far(after(add(p2f, p2z[0]), foc))
-        p3z = near(after(p3n, fqb))
-        foc, fqk, fqc, p1e, up, low, f1z, f1f, p2y, p3z = together(foc, fqk, fqc, p1e, up, low, f1z, f1f, p2y, p3z)
-
-        up, low = right(add(dx[1], up), 3), left(add(dx[3], low), 3)
+        grad_inputs, sums1 = leave(after(dx[0], f1n), up, low, tokens, dhidden1, mods)
+        foc, fqk, fqc, p1e, f1z, f1f, p2y, p3z, sums1 = together(foc, fqk, fqc, p1e, f1z, f1f, p2y, p3z, sums1)
+
         f1y = far(add(f1f, f1z[0]))
         p1x = swap(add(p1d[2], p1e[0]), x)
         g_heads = add(fqk, fqc)
         fon, fof, foo = split(rank_arg, fo[2], foa, foc)
-        foz = near(after(fon, p1x))
-        p3y = far(after(add(p3f, p3z[0]), p1x))
-        up, low, f1y, p1x, p3y, foz = together(up, low, f1y, p1x, p3y, foz)
-
-        def last(*terms):
-            return sum(v.astype(F32) for v in terms)
+        foz = near(fon)
+        p3y = far(add(p3f, p3z[0]))
+        incoming = exchange(units_out(g_heads))
+        dmods_in = exchange(mods_out(after(sums1, incoming)))
+        f1y, p1x, p3y, foz, incoming, dmods_in = together(f1y, p1x, p3y, foz, incoming, dmods_in)
 
         foy = far(add(fof, foz[0]))
-        grad_inputs, sums1 = leave(dx[0], up, low, tokens, dhidden1, mods)
         g_proj1 = last(p1d[3], p1e[1], p1x)
         g_proj2, g_fc1, g_fc2 = last(p2o, p2z[1], p2y), last(f1o, f1z[1], f1y), jnp.transpose(last(f2o, f2z[1], f2y))
         g_proj3, g_out = jnp.transpose(last(p3o, p3z[1], p3y)), last(foo, foz[1], foy)
@@ -910,21 +942,13 @@
             times_trans(first_all, dqkv).astype(BF), "dp", scatter_dimension=0, tiled=True
         )
 
-    dmods = jnp.concatenate([sums1[0:2], sums2[0:3], sum_gate2], axis=0)
-    dmods = exchange(dmods.reshape(n_seq, 6 * width // n_seq))
+    if not fast:
+        outgoing = units_out(g_heads)
+        dmods_in, incoming = exchange(mods_out(sums1)), exchange(outgoing)
     slot = jnp.arange(slots, dtype=jnp.int32)[:, None, None]
     whose = image_ids[::tok_dev]
-    grad_mods = jnp.sum(jnp.where(slot == whose[None, :, None], dmods[None], 0.0), axis=1)
-
-    units = [g_heads[:, i * local : (i + 1) * local] for i in range(3)]
-    outgoing = []
-    for target in range(n_seq):
-        mine = jnp.zeros_like(units[0])
-        for i in range(3):
-            mine = jnp.where((n_seq * i + rank) // 3 == target, units[i], mine)
-        outgoing.append(mine)
-    incoming = exchange(jnp.stack(outgoing))
-    columns = [jnp.zeros(units[0].shape, BF) for _ in range(3)]
+    grad_mods = jnp.sum(jnp.where(slot == whose[None, :, None], dmods_in[None], 0.0), axis=1)
+    columns = [jnp.zeros(incoming.shape[1:], BF) for _ in range(3)]
     for source in range(n_seq):
         for i in range(3):
             unit = n_seq * i + source

time: 448 us -> 433 us (0.967)
  blocking collectives: 15.4 us -> 0 us
  Pallas kernels: 172 us -> 160 us
  starting transfers between devices: 78.7 us -> 84.4 us
    ppermute x37, waiting for transfers between devices: 75.8 us -> 55.7 us  [flip(): return lax.ppermute(x, axis, [(i, i ^ bit) for i in range(size)])]
    all_to_all x1 -> x0, blocking collectives: 15.4 us -> none  [exchange(): lax.all_to_all(blocks, 'seq', split_axis=0, concat_axis=0, tiled=True)]
    all_to_all x3, waiting for transfers between devices: 3.58 us -> 18.4 us  [exchange(): lax.all_to_all(blocks, 'seq', split_axis=0, concat_axis=0, tiled=True)]
    ppermute x0 -> x3, waiting for transfers between devices: none -> 9.03 us  [shards(): lax.ppermute(heads_out[d], 'seq', [(i, (i + d) % n_seq) for i in range(n_...]
    pallas_call x1, Pallas kernels: 21.3 us -> 14.4 us  [attend_backward(): pl.pallas_call(functools.partial(attend_backward_kernel, size, heads, til...]
    pallas_call x1, Pallas kernels: 20.9 us -> 15.8 us  [attend_forward(): pl.pallas_call(functools.partial(attend_forward_kernel, size, heads, tile...]
  transfers between devices with their start and end apart: 52 -> 55, of which waited for: 21 -> 19; matrix products, arithmetic and copies ran while one was open for 11% -> 11% of each run, Pallas kernels for 25% -> 22%
where the time goes in v5:
time: 433 us; the launch traced here: 426 us
  Pallas kernels  160 us (37%)
  waiting for transfers between devices  115 us (27%)
  starting transfers between devices  84.4 us (19%)
  other arithmetic  46.6 us (11%)
  local copies, waits for them, and re-layouts  17 us (4%)
    ppermute x37, waiting for transfers between devices, flip(): return lax.ppermute(x, axis, [(i, i ^ bit) for i in range(size)])  55.7 us
    pallas_call x6, Pallas kernels, weight_grad(): pl.pallas_call(functools.partial(weight_grad_kernel, count, flat, rows, p...  44 us
    ppermute x37, starting transfers between devices, flip(): return lax.ppermute(x, axis, [(i, i ^ bit) for i in range(size)])  41.1 us
    pallas_call x1, Pallas kernels, middle(): pl.pallas_call(functools.partial(middle_kernel, len(os)), out_shape=(shap...  38 us
    convert_element_type x18, other arithmetic, add(): return (a.astype(F32) + b.astype(F32)).astype(BF)  29.4 us
    ppermute x3, waiting for transfers between devices, shards(): lax.ppermute(left[-1], 'seq', [(i, i - 1) for i in range(1, n_seq - s + 1)])  20.6 us
    all_to_all x3, waiting for transfers between devices, exchange(): lax.all_to_all(blocks, 'seq', split_axis=0, concat_axis=0, tiled=True)  18.4 us
    pallas_call x5, Pallas kernels, split(): pl.pallas_call(functools.partial(split_kernel, turned), out_shape=(shape(...  17.1 us
  transfers between devices with their start and end apart: 55, of which 19 were waited for; matrix products, arithmetic and copies ran while one was open for 11% of the time, Pallas kernels for 22%

profile of v5, /device:TPU:0, one launch (start us, length us, event | category | flops | bytes accessed | tf_op | source)
XLA Modules:
  0.0 426.4 jit_solution(11680061369660963797)
XLA Ops:
  2.0 3.1 enter.1
  5.1 5.0 %collective-permute-start.1 = (bf16[1152,256]{1,0:T(8,128)(2,1)}, bf16[1152,256]{1,0:T(8,128)(2,1)S(1)}, u32[]{:S(2)}, u32[]{:S(2)}) collective-permute-start(bf16[1152,256]{1,0:T(8,128)(2,1)} %get-tuple-element.191.refs_0_), channel_id=1, source_target_pairs={{0,1},{1,2},{2,3},{4,5},{5,6},{6,7},{8,9},{9,10},{10,11},{12,13},{... | collective-permute-start | bytes 1769480 | tf_op jit(solution)/shard_map/ppermute | solution.py:748
  11.4 11.5 %collective-permute-done.1.refs_6_ = bf16[1152,256]{1,0:T(8,128)(2,1)S(1)} collective-permute-done((bf16[1152,256]{1,0:T(8,128)(2,1)}, bf16[1152,256]{1,0:T(8,128)(2,1)S(1)}, u32[]{:S(2)}, u32[]{:S(2)}) %collective-permute-start.1) | collective-permute-done | bytes 589856 | tf_op jit(solution)/shard_map/ppermute | solution.py:748
  24.4 2.6 collective-permute-done.refs_1_
  29.8 14.0 %collective-permute-done.4.refs_3_ = bf16[1152,256]{1,0:T(8,128)(2,1)} collective-permute-done((bf16[1152,256]{1,0:T(8,128)(2,1)S(1)}, bf16[1152,256]{1,0:T(8,128)(2,1)}, u32[]{:S(2)}, u32[]{:S(2)}) %collective-permute-start.4) | collective-permute-done | bytes 589856 | tf_op jit(solution)/shard_map/ppermute | solution.py:749
  45.1 3.5 constant_dynamic-slice_fusion.2
  55.2 4.0 collective-permute-done.5.refs_5_
  59.2 15.8 %attend_forward.1 = (bf16[1152,1024]{1,0:T(8,128)(2,1)}, bf16[4,288,256]{2,1,0:T(8,128)(2,1)}, bf16[960,1024]{1,0:T(8,128)(2,1)}, f32[4,1024]{1,0:T(4,128)}) custom-call(s32[1]{0:T(128)S(6)} %convert_element_type.324.one_ref, s32[1]{0:T(128)} %bitcast.rank_ref, bf16[1152,256]{1,0:T(8,128)(2,1)} %get-tuple-element.191.refs_0_, bf16[1152,256]{1,0:T(8,128)(2,1)} %copy-done.8, ...), custom_call_target="tpu_custom_call" | custom-call | tf_op jit(solution)/shard_map/attend_forward/pallas_call | solution.py:163
  77.1 3.5 collective-permute-start.8
  80.7 3.6 collective-permute-done.6.refs_1_
  84.3 5.4 %collective-permute-done.7.refs_2_ = bf16[288,256]{1,0:T(8,128)(2,1)S(1)} collective-permute-done((bf16[288,256]{1,0:T(8,128)(2,1)S(1)}, bf16[288,256]{1,0:T(8,128)(2,1)S(1)}, u32[]{:S(2)}, u32[]{:S(2)}) %collective-permute-start.7) | collective-permute-done | bytes 147488 | tf_op jit(solution)/shard_map/ppermute | solution.py:768
  90.4 38.0 %middle.1 = (bf16[256,1152]{1,0:T(8,128)(2,1)}, bf16[2048,256]{1,0:T(8,128)(2,1)}, bf16[256,2048]{1,0:T(8,128)(2,1)}, bf16[3200,256]{1,0:T(8,128)(2,1)}, bf16[25...) custom-call(s32[1]{0:T(128)} %bitcast.rank_ref, ...), custom_call_target="tpu_custom_call" | custom-call | tf_op jit(solution)/shard_map/middle/pallas_call | solution.py:404
  131.6 16.9 %descend.1 = (bf16[256,5760]{1,0:T(8,128)(2,1)}, f32[256,1152]{1,0:T(8,128)}, bf16[4,288,256]{2,1,0:T(8,128)(2,1)}, f32[8,1152]{1,0:T(8,128)}) custom-call(bf16[256,1152]{1,0:T(8,128)(2,1)} %get-tuple-element.227.refs_0_.refs_2_, bf16[256,4608]{1,0:T(8,128)(2,1)} %get-tuple-element.201.refs_1_, f32[256,1152]{1,0:T(8,128)} %get-tuple-element.202.refs_2_, ...), custom_call_target="tpu_custom_call" | custom-call | tf_op jit(solution)/shard_map/descend/pallas_call | solution.py:471
  148.5 7.8 %weight_grad.6 = (bf16[1,256,2048]{2,1,0:T(8,128)(2,1)}, bf16[1,256,2048]{2,1,0:T(8,128)(2,1)}, bf16[1,256,2048]{2,1,0:T(8,128)(2,1)}, bf16[1,256,2048]{2,1,0:T(8,128)(2,1)}) custom-call(s32[4]{0:T(128)} %get-tuple-element.408.rows_ref, bf16[2048,256]{1,0:T(8,128)(2,1)} %get-tuple-element.195.refs_0_, bf16[2048,256]{1,0:T(8,128)(2,1)} %collective-permute-done.9.refs_1_, ...), custom_call_target="tpu_custom_call" | custom-call | tf_op jit(solution)/shard_map/weight_grad/pallas_call | solution.py:564
  157.3 3.0 collective-permute-start.13
  160.9 8.7 %weight_grad.7 = (bf16[1,576,1152]{2,1,0:T(8,128)(2,1)}, bf16[1,576,1152]{2,1,0:T(8,128)(2,1)}, bf16[1,576,1152]{2,1,0:T(8,128)(2,1)}, bf16[1,576,1152]{2,1,0:T(8,128)(2,1)}) custom-call(s32[4]{0:T(128)} %get-tuple-element.406.rows_ref, bf16[6912,256]{1,0:T(8,128)(2,1)} %get-tuple-element.225.refs_0_, bf16[6912,256]{1,0:T(8,128)(2,1)} %copy-done, ...), custom_call_target="tpu_custom_call" | custom-call | tf_op jit(solution)/shard_map/weight_grad/pallas_call | solution.py:564
  169.7 4.6 %all-to-all-start = ((bf16[4,288,256]{2,1,0:T(8,128)(2,1)}), bf16[4,288,256]{2,1,0:T(8,128)(2,1)S(1)}, u32[]{:S(2)}, u32[]{:S(2)}) async-start(bf16[4,288,256]{2,1,0:T(8,128)(2,1)} %get-tuple-element.234), calls=%async_computation | async-start | bytes 1179648 | tf_op jit(solution)/shard_map/all_to_all | solution.py:724
  174.9 7.0 %weight_grad_seq.1 = (bf16[2,576,512]{2,1,0:T(8,128)(2,1)}, bf16[576,512]{1,0:T(8,128)(2,1)}, bf16[576,512]{1,0:T(8,128)(2,1)}) custom-call(s32[8]{0:T(128)} %pad_add_fusion.order_ref, bf16[3200,256]{1,0:T(8,128)(2,1)} %get-tuple-element.235.refs_0_, bf16[3200,256]{1,0:T(8,128)(2,1)} %collective-permute-done.16.refs_1_, ...), custom_call_target="tpu_custom_call" | custom-call | tf_op jit(solution)/shard_map/weight_grad_seq/pallas_call | solution.py:631
  186.2 4.4 %all-to-all-done.refs_0_ = bf16[4,288,256]{2,1,0:T(8,128)(2,1)S(1)} async-done(((bf16[4,288,256]{2,1,0:T(8,128)(2,1)}), bf16[4,288,256]{2,1,0:T(8,128)(2,1)S(1)}, u32[]{:S(2)}, u32[]{:S(2)}) %all-to-all-start) | async-done | bytes 589856 | tf_op jit(solution)/shard_map/all_to_all | solution.py:724
  190.6 5.9 %weight_grad.8 = (bf16[2,256,768]{2,1,0:T(8,128)(2,1)}, bf16[1,256,768]{2,1,0:T(8,128)(2,1)}, bf16[1,256,768]{2,1,0:T(8,128)(2,1)}) custom-call(s32[4]{0:T(128)} %get-tuple-element.404.rows_ref, bf16[3200,256]{1,0:T(8,128)(2,1)} %get-tuple-element.235.refs_0_, bf16[3200,256]{1,0:T(8,128)(2,1)} %collective-permute-done.16.refs_1_, ...), custom_call_target="tpu_custom_call" | custom-call | tf_op jit(solution)/shard_map/weight_grad/pallas_call | solution.py:564
  198.8 14.4 %attend_backward.1 = (bf16[864,1024]{1,0:T(8,128)(2,1)}, bf16[4,256,1152]{2,1,0:T(8,128)(2,1)}) custom-call(s32[1]{0:T(128)S(6)} %convert_element_type.324.one_ref, s32[1]{0:T(128)} %bitcast.rank_ref, bf16[4,288,256]{2,1,0:T(8,128)(2,1)} %copy-done.4, bf16[960,1024]{1,0:T(8,128)(2,1)} %get-tuple-element.246.refs_1_, ...), custom_call_target="tpu_custom_call" | custom-call | tf_op jit(solution)/shard_map/attend_backward/pallas_call | solution.py:265
  213.2 3.2 add_convert_fusion.1
  218.1 3.5 fusion.2
  223.2 3.7 collective-permute-start.21
  228.1 4.8 %collective-permute-start.23 = (bf16[256,1152]{1,0:T(8,128)(2,1)}, bf16[256,1152]{1,0:T(8,128)(2,1)}, u32[]{:S(2)}, u32[]{:S(2)}) collective-permute-start(bf16[256,1152]{1,0:T(8,128)(2,1)} %get-tuple-element.380), channel_id=1, source_target_pairs={{0,1},{4,5},{8,9},{12,13},{16,17},{20,21},{24,25},{28,29}} | collective-permute-start | bytes 1769480 | tf_op jit(solution)/shard_map/ppermute | solution.py:808
  236.3 8.7 %weight_grad.9 = (bf16[1,144,4608]{2,1,0:T(8,128)(2,1)}, bf16[1,144,4608]{2,1,0:T(8,128)(2,1)}, bf16[1,144,4608]{2,1,0:T(8,128)(2,1)}, bf16[1,144,4608]{2,1,0:T(8,128)(2,1)}) custom-call(s32[4]{0:T(128)} %get-tuple-element.407.rows_ref, bf16[6912,256]{1,0:T(8,128)(2,1)} %get-tuple-element.225.refs_0_, bf16[6912,256]{1,0:T(8,128)(2,1)} %copy-done, ...), custom_call_target="tpu_custom_call" | custom-call | tf_op jit(solution)/shard_map/weight_grad/pallas_call | solution.py:564
  245.0 7.2 %weight_grad.10 = (bf16[4,144,864]{2,1,0:T(8,128)(2,1)}, bf16[2,144,864]{2,1,0:T(8,128)(2,1)}, bf16[2,144,864]{2,1,0:T(8,128)(2,1)}) custom-call(s32[8]{0:T(128)} %xor_multiply_fusion.5.rows_ref, bf16[1152,1024]{1,0:T(8,128)(2,1)} %get-tuple-element.268.refs_0_, bf16[864,1024]{1,0:T(8,128)(2,1)} %get-tuple-element.270.refs_1_), custom_call_target="tpu_custom_call" | custom-call | tf_op jit(solution)/shard_map/weight_grad/pallas_call | solution.py:564
  252.2 5.7 %weight_grad.11 = (bf16[2,144,1152]{2,1,0:T(8,128)(2,1)}, bf16[1,144,1152]{2,1,0:T(8,128)(2,1)}, bf16[1,144,1152]{2,1,0:T(8,128)(2,1)}) custom-call(s32[4]{0:T(128)} %get-tuple-element.403.rows_ref, bf16[6912,256]{1,0:T(8,128)(2,1)} %get-tuple-element.225.refs_0_, bf16[6912,256]{1,0:T(8,128)(2,1)} %copy-done, bf16[256,5760]{1,0:T(8,128)(2,1)} %get-tuple-element.274.refs_2_, ...), custom_call_target="tpu_custom_call" | custom-call | tf_op jit(solution)/shard_map/weight_grad/pallas_call | solution.py:564
  257.9 2.7 add_convert_fusion.2
  270.3 4.0 split.5
  274.3 10.9 %collective-permute-done.29.got2_ref = bf16[1,256,2048]{2,1,0:T(8,128)(2,1)} collective-permute-done((bf16[1,256,2048]{2,1,0:T(8,128)(2,1)}, bf16[1,256,2048]{2,1,0:T(8,128)(2,1)}, u32[]{:S(2)}, u32[]{:S(2)}) %collective-permute-start.29) | collective-permute-done | bytes 1048608 | tf_op jit(solution)/shard_map/ppermute | solution.py:696
  285.8 3.7 split.6
  289.5 3.7 collective-permute-done.26
  295.2 3.1 add_convert_fusion
  298.5 5.8 %collective-permute-done.30.got1_ref = bf16[2,144,1152]{2,1,0:T(8,128)(2,1)S(1)} collective-permute-done((bf16[2,144,1152]{2,1,0:T(8,128)(2,1)}, bf16[2,144,1152]{2,1,0:T(8,128)(2,1)S(1)}, u32[]{:S(2)}, u32[]{:S(2)}) %collective-permute-start.30) | collective-permute-done | bytes 663584 | tf_op jit(solution)/shard_map/ppermute | solution.py:696
  305.7 2.5 collective-permute-start.34
  312.3 5.1 %collective-permute-start.36 = (bf16[256,1152]{1,0:T(8,128)(2,1)}, bf16[256,1152]{1,0:T(8,128)(2,1)S(1)}, u32[]{:S(2)}, u32[]{:S(2)}) collective-permute-start(bf16[256,1152]{1,0:T(8,128)(2,1)} %get-tuple-element.376), channel_id=1, source_target_pairs={{0,1},{1,2},{2,3},{4,5},{5,6},{6,7},{8,9},{9,10},{10,11},{12,13},{... | collective-permute-start | bytes 1769480 | tf_op jit(solution)/shard_map/ppermute | solution.py:808
  318.7 3.1 collective-permute-done.38
  328.0 14.7 %collective-permute-done.39 = bf16[2,256,512]{2,1,0:T(8,128)(2,1)S(1)} collective-permute-done((bf16[2,256,512]{2,1,0:T(8,128)(2,1)}, bf16[2,256,512]{2,1,0:T(8,128)(2,1)S(1)}, u32[]{:S(2)}, u32[]{:S(2)}) %collective-permute-start.39) | collective-permute-done | bytes 524320 | tf_op jit(solution)/shard_map/ppermute | solution.py:696
  344.9 4.0 collective-permute-start.40
  349.0 4.5 %split.8 = (bf16[2,144,1152]{2,1,0:T(8,128)(2,1)}, bf16[144,1152]{1,0:T(8,128)(2,1)}, bf16[144,1152]{1,0:T(8,128)(2,1)}) custom-call(s32[1]{0:T(128)} %bitcast.rank_ref, bf16[1,144,4608]{2,1,0:T(8,128)(2,1)} %get-tuple-element.308.keep_ref, bf16[1,144,4608]{2,1,0:T(8,128)(2,1)} %collective-permute-done.34.got1_ref, ...), custom_call_target="tpu_custom_call" | custom-call | tf_op jit(solution)/shard_map/split/pallas_call | solution.py:685
  357.6 3.9 leave.1
  365.8 13.4 %collective-permute-done.46 = bf16[2,192,256]{2,1,0:T(8,128)(2,1)S(1)} collective-permute-done((bf16[2,192,256]{2,1,0:T(8,128)(2,1)}, bf16[2,192,256]{2,1,0:T(8,128)(2,1)S(1)}, u32[]{:S(2)}, u32[]{:S(2)}) %collective-permute-start.46) | collective-permute-done | bytes 196640 | tf_op jit(solution)/shard_map/ppermute | solution.py:696
  381.2 3.6 all-to-all-start.1
  384.9 2.6 split.9
  394.3 5.1 %all-to-all-done.1 = bf16[4,144,288]{2,1,0:T(8,128)(2,1)S(1)} async-done(((bf16[4,144,288]{2,1,0:T(8,128)(2,1)}), bf16[4,144,288]{2,1,0:T(8,128)(2,1)S(1)}, u32[]{:S(2)}, u32[]{:S(2)}) %all-to-all-start.1) | async-done | bytes 331808 | tf_op jit(solution)/shard_map/all_to_all | solution.py:724
  400.8 3.3 all-to-all-start.2
  406.1 8.9 %all-to-all-done.2 = f32[4,1,1728]{2,1,0:T(1,128)S(1)} async-done(((f32[4,1,1728]{2,1,0:T(1,128)}), f32[4,1,1728]{2,1,0:T(1,128)S(1)}, u32[]{:S(2)}, u32[]{:S(2)}) %all-to-all-start.2) | async-done | bytes 27680 | tf_op jit(solution)/shard_map/all_to_all | solution.py:724
  (224 shorter events, 95.5 us)
Async XLA Ops:
  5.1 17.8 %collective-permute-start.1 = (bf16[1152,256]{1,0:T(8,128)(2,1)}, bf16[1152,256]{1,0:T(8,128)(2,1)S(1)}, u32[]{:S(2)}, u32[]{:S(2)}) collective-permute-start(bf16[1152,256]{1,0:T(8,128)(2,1)} %get-tuple-element.191.refs_0_), channel_id=1, source_target_pairs={{0,1},{1,2},{2,3},{4,5},{5,6},{6,7},{8,9},{9,10},{10,11},{12,13},{... | collective-permute-start | bytes 1769480 | tf_op jit(solution)/shard_map/ppermute | solution.py:748
  10.1 16.9 %collective-permute-start = (bf16[1152,256]{1,0:T(8,128)(2,1)}, bf16[1152,256]{1,0:T(8,128)(2,1)S(1)}, u32[]{:S(2)}, u32[]{:S(2)}) collective-permute-start(bf16[1152,256]{1,0:T(8,128)(2,1)} %get-tuple-element.191.refs_0_), channel_id=1, source_target_pairs={{1,0},{2,1},{3,2},{5,4},{6,5},{7,6},{9,8},{10,9},{11,10},{13,12},{... | collective-permute-start | bytes 1769480 | tf_op jit(solution)/shard_map/ppermute | solution.py:749
  27.0 16.8 %collective-permute-start.4 = (bf16[1152,256]{1,0:T(8,128)(2,1)S(1)}, bf16[1152,256]{1,0:T(8,128)(2,1)}, u32[]{:S(2)}, u32[]{:S(2)}) collective-permute-start(bf16[1152,256]{1,0:T(8,128)(2,1)S(1)} %collective-permute-done.refs_1_), channel_id=1, source_target_pairs={{1,0},{2,1},{5,4},{6,5},{9,8},{10,9},{13,12},{14,13},{17,16},{18,1... | collective-permute-start | bytes 1769480 | tf_op jit(solution)/shard_map/ppermute | solution.py:749
  28.3 26.9 %collective-permute-start.3 = (bf16[1152,256]{1,0:T(8,128)(2,1)}, bf16[1152,256]{1,0:T(8,128)(2,1)}, u32[]{:S(2)}, u32[]{:S(2)}) collective-permute-start(bf16[1152,256]{1,0:T(8,128)(2,1)} %collective-permute-done.2.refs_4_), channel_id=1, source_target_pairs={{2,3},{6,7},{10,11},{14,15},{18,19},{22,23},{26,27},{30,31}} | collective-permute-start | bytes 1769480 | tf_op jit(solution)/shard_map/ppermute | solution.py:748
  43.8 15.5 %collective-permute-start.5 = (bf16[1152,256]{1,0:T(8,128)(2,1)}, bf16[1152,256]{1,0:T(8,128)(2,1)}, u32[]{:S(2)}, u32[]{:S(2)}) collective-permute-start(bf16[1152,256]{1,0:T(8,128)(2,1)} %collective-permute-done.4.refs_3_), channel_id=1, source_target_pairs={{1,0},{5,4},{9,8},{13,12},{17,16},{21,20},{25,24},{29,28}} | collective-permute-start | bytes 1769480 | tf_op jit(solution)/shard_map/ppermute | solution.py:749
  128.4 20.1 %collective-permute-start.11 = (bf16[6912,256]{1,0:T(8,128)(2,1)}, bf16[6912,256]{1,0:T(8,128)(2,1)S(1)}, u32[]{:S(2)}, u32[]{:S(2)}) collective-permute-start(bf16[6912,256]{1,0:T(8,128)(2,1)} %get-tuple-element.225.refs_0_), channel_id=1, source_target_pairs={{0,4},{4,0},{8,12},{12,8},{16,20},{20,16},{24,28},{28,24},{1,5},{5... | collective-permute-start | bytes 10616840 | tf_op jit(solution)/shard_map/ppermute | solution.py:696
  130.4 18.1 %collective-permute-start.10 = (bf16[256,2048]{1,0:T(8,128)(2,1)}, bf16[256,2048]{1,0:T(8,128)(2,1)}, u32[]{:S(2)}, u32[]{:S(2)}) collective-permute-start(bf16[256,2048]{1,0:T(8,128)(2,1)} %get-tuple-element.196.refs_2_), channel_id=1, source_target_pairs={{0,4},{4,0},{8,12},{12,8},{16,20},{20,16},{24,28},{28,24},{1,5},{5... | collective-permute-start | bytes 3145736 | tf_op jit(solution)/shard_map/ppermute | solution.py:696
  130.5 18.0 %collective-permute-start.9 = (bf16[2048,256]{1,0:T(8,128)(2,1)}, bf16[2048,256]{1,0:T(8,128)(2,1)}, u32[]{:S(2)}, u32[]{:S(2)}) collective-permute-start(bf16[2048,256]{1,0:T(8,128)(2,1)} %get-tuple-element.195.refs_0_), channel_id=1, source_target_pairs={{0,4},{4,0},{8,12},{12,8},{16,20},{20,16},{24,28},{28,24},{1,5},{5... | collective-permute-start | bytes 3145736 | tf_op jit(solution)/shard_map/ppermute | solution.py:696
  130.9 17.5 %collective-permute-start.12 = (bf16[256,1152]{1,0:T(8,128)(2,1)}, bf16[256,1152]{1,0:T(8,128)(2,1)}, u32[]{:S(2)}, u32[]{:S(2)}) collective-permute-start(bf16[256,1152]{1,0:T(8,128)(2,1)} %get-tuple-element.227.refs_0_.refs_2_), channel_id=1, source_target_pairs={{0,4},{4,0},{8,12},{12,8},{16,20},{20,16},{24,28},{28,24},{1,5},{5... | collective-permute-start | bytes 1769480 | tf_op jit(solution)/shard_map/ppermute | solution.py:696
  156.3 61.8 %collective-permute-start.20 = (bf16[256,5760]{1,0:T(8,128)(2,1)}, bf16[256,5760]{1,0:T(8,128)(2,1)S(1)}, u32[]{:S(2)}, u32[]{:S(2)}) collective-permute-start(bf16[256,5760]{1,0:T(8,128)(2,1)} %get-tuple-element.274.refs_2_), channel_id=1, source_target_pairs={{0,4},{4,0},{8,12},{12,8},{16,20},{20,16},{24,28},{28,24},{1,5},{5... | collective-permute-start | bytes 8847368 | tf_op jit(solution)/shard_map/ppermute | solution.py:696
  156.8 18.1 %collective-permute-start.16 = (bf16[3200,256]{1,0:T(8,128)(2,1)}, bf16[3200,256]{1,0:T(8,128)(2,1)}, u32[]{:S(2)}, u32[]{:S(2)}) collective-permute-start(bf16[3200,256]{1,0:T(8,128)(2,1)} %get-tuple-element.235.refs_0_), channel_id=1, source_target_pairs={{0,4},{4,0},{8,12},{12,8},{16,20},{20,16},{24,28},{28,24},{1,5},{5... | collective-permute-start | bytes 4915208 | tf_op jit(solution)/shard_map/ppermute | solution.py:696
  156.9 18.0 %collective-permute-start.17 = (bf16[256,2816]{1,0:T(8,128)(2,1)}, bf16[256,2816]{1,0:T(8,128)(2,1)}, u32[]{:S(2)}, u32[]{:S(2)}) collective-permute-start(bf16[256,2816]{1,0:T(8,128)(2,1)} %get-tuple-element.240.refs_2_), channel_id=1, source_target_pairs={{0,4},{4,0},{8,12},{12,8},{16,20},{20,16},{24,28},{28,24},{1,5},{5... | collective-permute-start | bytes 4325384 | tf_op jit(solution)/shard_map/ppermute | solution.py:696
  157.3 27.1 %collective-permute-start.13 = (bf16[1,256,2048]{2,1,0:T(8,128)(2,1)}, bf16[1,256,2048]{2,1,0:T(8,128)(2,1)}, u32[]{:S(2)}, u32[]{:S(2)}) collective-permute-start(bf16[1,256,2048]{2,1,0:T(8,128)(2,1)} %get-tuple-element.221), channel_id=1, source_target_pairs={{0,8},{4,12},{8,0},{12,4},{16,24},{20,28},{24,16},{28,20},{1,9},{5... | collective-permute-start | bytes 3145736 | tf_op jit(solution)/shard_map/ppermute | solution.py:696
  169.6 43.6 %collective-permute-start.15 = (bf16[1,576,1152]{2,1,0:T(8,128)(2,1)}, bf16[1,576,1152]{2,1,0:T(8,128)(2,1)}, u32[]{:S(2)}, u32[]{:S(2)}) collective-permute-start(bf16[1,576,1152]{2,1,0:T(8,128)(2,1)} %get-tuple-element.229), channel_id=1, source_target_pairs={{0,16},{4,20},{8,24},{12,28},{16,0},{20,4},{24,8},{28,12},{1,17},{... | collective-permute-start | bytes 3981320 | tf_op jit(solution)/shard_map/ppermute | solution.py:696
  169.7 20.9 %all-to-all-start = ((bf16[4,288,256]{2,1,0:T(8,128)(2,1)}), bf16[4,288,256]{2,1,0:T(8,128)(2,1)S(1)}, u32[]{:S(2)}, u32[]{:S(2)}) async-start(bf16[4,288,256]{2,1,0:T(8,128)(2,1)} %get-tuple-element.234), calls=%async_computation | async-start | bytes 1179648 | tf_op jit(solution)/shard_map/all_to_all | solution.py:724
  181.9 36.1 %collective-permute-start.18 = (bf16[2,576,512]{2,1,0:T(8,128)(2,1)}, bf16[2,576,512]{2,1,0:T(8,128)(2,1)}, u32[]{:S(2)}, u32[]{:S(2)}) collective-permute-start(bf16[2,576,512]{2,1,0:T(8,128)(2,1)} %get-tuple-element.239), channel_id=1, source_target_pairs={{0,1},{1,0},{2,3},{3,2},{4,5},{5,4},{6,7},{7,6},{8,9},{9,8},{10,11... | collective-permute-start | bytes 3538952 | tf_op jit(solution)/shard_map/ppermute | solution.py:696
  184.4 32.0 %collective-permute-start.14 = (bf16[1,256,2048]{2,1,0:T(8,128)(2,1)}, bf16[1,256,2048]{2,1,0:T(8,128)(2,1)}, u32[]{:S(2)}, u32[]{:S(2)}) collective-permute-start(bf16[1,256,2048]{2,1,0:T(8,128)(2,1)} %get-tuple-element.233), channel_id=1, source_target_pairs={{0,8},{4,12},{8,0},{12,4},{16,24},{20,28},{24,16},{28,20},{1,9},{5... | collective-permute-start | bytes 3145736 | tf_op jit(solution)/shard_map/ppermute | solution.py:696
  196.5 21.5 %collective-permute-start.19 = (bf16[2,256,768]{2,1,0:T(8,128)(2,1)}, bf16[2,256,768]{2,1,0:T(8,128)(2,1)}, u32[]{:S(2)}, u32[]{:S(2)}) collective-permute-start(bf16[2,256,768]{2,1,0:T(8,128)(2,1)} %get-tuple-element.242), channel_id=1, source_target_pairs={{0,16},{4,20},{8,24},{12,28},{16,0},{20,4},{24,8},{28,12},{1,17},{... | collective-permute-start | bytes 2359304 | tf_op jit(solution)/shard_map/ppermute | solution.py:696
  221.5 39.1 %collective-permute-start.25 = (bf16[576,512]{1,0:T(8,128)(2,1)}, bf16[576,512]{1,0:T(8,128)(2,1)}, u32[]{:S(2)}, u32[]{:S(2)}) collective-permute-start(bf16[576,512]{1,0:T(8,128)(2,1)} %get-tuple-element.385), channel_id=1, source_target_pairs={{0,2},{1,3},{2,0},{3,1},{4,6},{5,7},{6,4},{7,5},{8,10},{9,11},{10,... | collective-permute-start | bytes 1769480 | tf_op jit(solution)/shard_map/ppermute | solution.py:696
  223.2 37.5 %collective-permute-start.21 = (bf16[1,576,1152]{2,1,0:T(8,128)(2,1)}, bf16[1,576,1152]{2,1,0:T(8,128)(2,1)}, u32[]{:S(2)}, u32[]{:S(2)}) collective-permute-start(bf16[1,576,1152]{2,1,0:T(8,128)(2,1)} %add_convert_fusion.1), channel_id=1, source_target_pairs={{0,8},{4,12},{8,0},{12,4},{16,24},{20,28},{24,16},{28,20},{1,9},{5... | collective-permute-start | bytes 3981320 | tf_op jit(solution)/shard_map/ppermute | solution.py:696
  226.8 33.8 %collective-permute-start.22 = (bf16[1,576,1152]{2,1,0:T(8,128)(2,1)}, bf16[1,576,1152]{2,1,0:T(8,128)(2,1)}, u32[]{:S(2)}, u32[]{:S(2)}) collective-permute-start(bf16[1,576,1152]{2,1,0:T(8,128)(2,1)} %get-tuple-element.255), channel_id=1, source_target_pairs={{0,16},{4,20},{8,24},{12,28},{16,0},{20,4},{24,8},{28,12},{1,17},{... | collective-permute-start | bytes 3981320 | tf_op jit(solution)/shard_map/ppermute | solution.py:696
  228.1 32.6 %collective-permute-start.23 = (bf16[256,1152]{1,0:T(8,128)(2,1)}, bf16[256,1152]{1,0:T(8,128)(2,1)}, u32[]{:S(2)}, u32[]{:S(2)}) collective-permute-start(bf16[256,1152]{1,0:T(8,128)(2,1)} %get-tuple-element.380), channel_id=1, source_target_pairs={{0,1},{4,5},{8,9},{12,13},{16,17},{20,21},{24,25},{28,29}} | collective-permute-start | bytes 1769480 | tf_op jit(solution)/shard_map/ppermute | solution.py:808
  232.9 27.8 %collective-permute-start.24 = (bf16[256,1152]{1,0:T(8,128)(2,1)}, bf16[256,1152]{1,0:T(8,128)(2,1)}, u32[]{:S(2)}, u32[]{:S(2)}) collective-permute-start(bf16[256,1152]{1,0:T(8,128)(2,1)} %get-tuple-element.379), channel_id=1, source_target_pairs={{3,2},{7,6},{11,10},{15,14},{19,18},{23,22},{27,26},{31,30}} | collective-permute-start | bytes 1769480 | tf_op jit(solution)/shard_map/ppermute | solution.py:811
  260.7 32.4 %collective-permute-start.26 = (bf16[1,144,4608]{2,1,0:T(8,128)(2,1)}, bf16[1,144,4608]{2,1,0:T(8,128)(2,1)}, u32[]{:S(2)}, u32[]{:S(2)}) collective-permute-start(bf16[1,144,4608]{2,1,0:T(8,128)(2,1)} %get-tuple-element.283), channel_id=1, source_target_pairs={{0,8},{4,12},{8,0},{12,4},{16,24},{20,28},{24,16},{28,20},{1,9},{5... | collective-permute-start | bytes 3981320 | tf_op jit(solution)/shard_map/ppermute | solution.py:696
  260.8 24.4 %collective-permute-start.29 = (bf16[1,256,2048]{2,1,0:T(8,128)(2,1)}, bf16[1,256,2048]{2,1,0:T(8,128)(2,1)}, u32[]{:S(2)}, u32[]{:S(2)}) collective-permute-start(bf16[1,256,2048]{2,1,0:T(8,128)(2,1)} %add_convert_fusion.2), channel_id=1, source_target_pairs={{0,16},{4,20},{8,24},{12,28},{16,0},{20,4},{24,8},{28,12},{1,17},{... | collective-permute-start | bytes 3145736 | tf_op jit(solution)/shard_map/ppermute | solution.py:696
  265.4 32.9 %collective-permute-start.32 = (bf16[256,1152]{1,0:T(8,128)(2,1)}, bf16[256,1152]{1,0:T(8,128)(2,1)}, u32[]{:S(2)}, u32[]{:S(2)}) collective-permute-start(bf16[256,1152]{1,0:T(8,128)(2,1)} %get-tuple-element.378), channel_id=1, source_target_pairs={{0,1},{1,2},{4,5},{5,6},{8,9},{9,10},{12,13},{13,14},{16,17},{17,1... | collective-permute-start | bytes 1769480 | tf_op jit(solution)/shard_map/ppermute | solution.py:808
  267.5 30.8 %collective-permute-start.33 = (bf16[256,1152]{1,0:T(8,128)(2,1)}, bf16[256,1152]{1,0:T(8,128)(2,1)}, u32[]{:S(2)}, u32[]{:S(2)}) collective-permute-start(bf16[256,1152]{1,0:T(8,128)(2,1)} %get-tuple-element.377), channel_id=1, source_target_pairs={{2,1},{3,2},{6,5},{7,6},{10,9},{11,10},{14,13},{15,14},{18,17},{19... | collective-permute-start | bytes 1769480 | tf_op jit(solution)/shard_map/ppermute | solution.py:811
  274.3 24.2 %collective-permute-start.31 = (bf16[2,288,576]{2,1,0:T(8,128)(2,1)}, bf16[2,288,576]{2,1,0:T(8,128)(2,1)}, u32[]{:S(2)}, u32[]{:S(2)}) collective-permute-start(bf16[2,288,576]{2,1,0:T(8,128)(2,1)} %get-tuple-element.290), channel_id=1, source_target_pairs={{0,1},{1,0},{2,3},{3,2},{4,5},{5,4},{6,7},{7,6},{8,9},{9,8},{10,11... | collective-permute-start | bytes 1990664 | tf_op jit(solution)/shard_map/ppermute | solution.py:696
  285.1 13.3 %collective-permute-start.28 = (bf16[1,256,768]{2,1,0:T(8,128)(2,1)S(1)}, bf16[1,256,768]{2,1,0:T(8,128)(2,1)}, u32[]{:S(2)}, u32[]{:S(2)}) collective-permute-start(bf16[1,256,768]{2,1,0:T(8,128)(2,1)S(1)} %copy-done.17), channel_id=1, source_target_pairs={{0,8},{4,12},{8,0},{12,4},{16,24},{20,28},{24,16},{28,20},{1,9},{5... | collective-permute-start | bytes 1179656 | tf_op jit(solution)/shard_map/ppermute | solution.py:696
  305.6 16.1 %collective-permute-start.38 = (bf16[288,576]{1,0:T(8,128)(2,1)S(1)}, bf16[288,576]{1,0:T(8,128)(2,1)S(1)}, u32[]{:S(2)}, u32[]{:S(2)}) collective-permute-start(bf16[288,576]{1,0:T(8,128)(2,1)S(1)} %fusion.6), channel_id=1, source_target_pairs={{0,2},{1,3},{2,0},{3,1},{4,6},{5,7},{6,4},{7,5},{8,10},{9,11},{10,... | collective-permute-start | bytes 995336 | tf_op jit(solution)/shard_map/ppermute | solution.py:696
  305.7 37.9 %collective-permute-start.34 = (bf16[1,144,4608]{2,1,0:T(8,128)(2,1)}, bf16[1,144,4608]{2,1,0:T(8,128)(2,1)}, u32[]{:S(2)}, u32[]{:S(2)}) collective-permute-start(bf16[1,144,4608]{2,1,0:T(8,128)(2,1)} %get-tuple-element.309), channel_id=1, source_target_pairs={{0,8},{4,12},{8,0},{12,4},{16,24},{20,28},{24,16},{28,20},{1,9},{5... | collective-permute-start | bytes 3981320 | tf_op jit(solution)/shard_map/ppermute | solution.py:696
  308.3 35.3 %collective-permute-start.35 = (bf16[1,144,4608]{2,1,0:T(8,128)(2,1)}, bf16[1,144,4608]{2,1,0:T(8,128)(2,1)}, u32[]{:S(2)}, u32[]{:S(2)}) collective-permute-start(bf16[1,144,4608]{2,1,0:T(8,128)(2,1)} %add_convert_fusion), channel_id=1, source_target_pairs={{0,16},{4,20},{8,24},{12,28},{16,0},{20,4},{24,8},{28,12},{1,17},{... | collective-permute-start | bytes 3981320 | tf_op jit(solution)/shard_map/ppermute | solution.py:696
  312.3 30.5 %collective-permute-start.36 = (bf16[256,1152]{1,0:T(8,128)(2,1)}, bf16[256,1152]{1,0:T(8,128)(2,1)S(1)}, u32[]{:S(2)}, u32[]{:S(2)}) collective-permute-start(bf16[256,1152]{1,0:T(8,128)(2,1)} %get-tuple-element.376), channel_id=1, source_target_pairs={{0,1},{1,2},{2,3},{4,5},{5,6},{6,7},{8,9},{9,10},{10,11},{12,13},{... | collective-permute-start | bytes 1769480 | tf_op jit(solution)/shard_map/ppermute | solution.py:808
  317.4 25.4 %collective-permute-start.37 = (bf16[256,1152]{1,0:T(8,128)(2,1)}, bf16[256,1152]{1,0:T(8,128)(2,1)S(1)}, u32[]{:S(2)}, u32[]{:S(2)}) collective-permute-start(bf16[256,1152]{1,0:T(8,128)(2,1)} %get-tuple-element.375), channel_id=1, source_target_pairs={{1,0},{2,1},{3,2},{5,4},{6,5},{7,6},{9,8},{10,9},{11,10},{13,12},{... | collective-permute-start | bytes 1769480 | tf_op jit(solution)/shard_map/ppermute | solution.py:811
  322.5 20.3 %collective-permute-start.39 = (bf16[2,256,512]{2,1,0:T(8,128)(2,1)}, bf16[2,256,512]{2,1,0:T(8,128)(2,1)S(1)}, u32[]{:S(2)}, u32[]{:S(2)}) collective-permute-start(bf16[2,256,512]{2,1,0:T(8,128)(2,1)} %get-tuple-element.315), channel_id=1, source_target_pairs={{0,1},{1,0},{2,3},{3,2},{4,5},{5,4},{6,7},{7,6},{8,9},{9,8},{10,11... | collective-permute-start | bytes 1572872 | tf_op jit(solution)/shard_map/ppermute | solution.py:696
  343.6 17.9 %collective-permute-start.41 = (bf16[2,144,864]{2,1,0:T(8,128)(2,1)}, bf16[2,144,864]{2,1,0:T(8,128)(2,1)S(1)}, u32[]{:S(2)}, u32[]{:S(2)}) collective-permute-start(bf16[2,144,864]{2,1,0:T(8,128)(2,1)} %get-tuple-element.336), channel_id=1, source_target_pairs={{0,16},{4,20},{8,24},{12,28},{16,0},{20,4},{24,8},{28,12},{1,17},{... | collective-permute-start | bytes 1493000 | tf_op jit(solution)/shard_map/ppermute | solution.py:696
  344.9 18.7 %collective-permute-start.40 = (bf16[1,144,1152]{2,1,0:T(8,128)(2,1)}, bf16[1,144,1152]{2,1,0:T(8,128)(2,1)S(1)}, u32[]{:S(2)}, u32[]{:S(2)}) collective-permute-start(bf16[1,144,1152]{2,1,0:T(8,128)(2,1)} %add_convert_fusion.9), channel_id=1, source_target_pairs={{0,8},{4,12},{8,0},{12,4},{16,24},{20,28},{24,16},{28,20},{1,9},{5... | collective-permute-start | bytes 995336 | tf_op jit(solution)/shard_map/ppermute | solution.py:696
  353.5 25.8 %collective-permute-start.44 = (bf16[2,144,1152]{2,1,0:T(8,128)(2,1)}, bf16[2,144,1152]{2,1,0:T(8,128)(2,1)S(1)}, u32[]{:S(2)}, u32[]{:S(2)}) collective-permute-start(bf16[2,144,1152]{2,1,0:T(8,128)(2,1)} %get-tuple-element.328), channel_id=1, source_target_pairs={{0,1},{1,0},{2,3},{3,2},{4,5},{5,4},{6,7},{7,6},{8,9},{9,8},{10,11... | collective-permute-start | bytes 1990664 | tf_op jit(solution)/shard_map/ppermute | solution.py:696
  355.2 24.0 %collective-permute-start.45 = (bf16[256,512]{1,0:T(8,128)(2,1)}, bf16[256,512]{1,0:T(8,128)(2,1)}, u32[]{:S(2)}, u32[]{:S(2)}) collective-permute-start(bf16[256,512]{1,0:T(8,128)(2,1)} %fusion.10), channel_id=1, source_target_pairs={{0,2},{1,3},{2,0},{3,1},{4,6},{5,7},{6,4},{7,5},{8,10},{9,11},{10,... | collective-permute-start | bytes 786440 | tf_op jit(solution)/shard_map/ppermute | solution.py:696
  356.0 23.3 %collective-permute-start.43 = (bf16[2,144,512]{2,1,0:T(8,128)(2,1)}, bf16[2,144,512]{2,1,0:T(8,128)(2,1)S(1)}, u32[]{:S(2)}, u32[]{:S(2)}) collective-permute-start(bf16[2,144,512]{2,1,0:T(8,128)(2,1)} %slice.168), channel_id=1, source_target_pairs={{0,16},{4,20},{8,24},{12,28},{16,0},{20,4},{24,8},{28,12},{1,17},{... | collective-permute-start | bytes 884744 | tf_op jit(solution)/shard_map/ppermute | solution.py:696
  361.5 17.8 %collective-permute-start.46 = (bf16[2,192,256]{2,1,0:T(8,128)(2,1)}, bf16[2,192,256]{2,1,0:T(8,128)(2,1)S(1)}, u32[]{:S(2)}, u32[]{:S(2)}) collective-permute-start(bf16[2,192,256]{2,1,0:T(8,128)(2,1)} %get-tuple-element.342), channel_id=1, source_target_pairs={{0,1},{1,0},{2,3},{3,2},{4,5},{5,4},{6,7},{7,6},{8,9},{9,8},{10,11... | collective-permute-start | bytes 589832 | tf_op jit(solution)/shard_map/ppermute | solution.py:696
  363.7 15.6 %collective-permute-start.42 = (bf16[144,864]{1,0:T(8,128)(2,1)S(1)}, bf16[144,864]{1,0:T(8,128)(2,1)S(1)}, u32[]{:S(2)}, u32[]{:S(2)}) collective-permute-start(bf16[144,864]{1,0:T(8,128)(2,1)S(1)} %get-tuple-element.337), channel_id=1, source_target_pairs={{0,8},{4,12},{8,0},{12,4},{16,24},{20,28},{24,16},{28,20},{1,9},{5... | collective-permute-start | bytes 746504 | tf_op jit(solution)/shard_map/ppermute | solution.py:696
  381.2 18.1 %all-to-all-start.1 = ((bf16[4,144,288]{2,1,0:T(8,128)(2,1)}), bf16[4,144,288]{2,1,0:T(8,128)(2,1)S(1)}, u32[]{:S(2)}, u32[]{:S(2)}) async-start(bf16[4,144,288]{2,1,0:T(8,128)(2,1)} %pad_maximum_fusion.1), calls=%async_computation.1 | async-start | bytes 884736 | tf_op jit(solution)/shard_map/all_to_all | solution.py:724
  387.5 27.6 %collective-permute-start.50 = (bf16[2,144,288]{2,1,0:T(8,128)(2,1)}, bf16[2,144,288]{2,1,0:T(8,128)(2,1)}, u32[]{:S(2)}, u32[]{:S(2)}) collective-permute-start(bf16[2,144,288]{2,1,0:T(8,128)(2,1)} %get-tuple-element.351), channel_id=1, source_target_pairs={{0,1},{1,0},{2,3},{3,2},{4,5},{5,4},{6,7},{7,6},{8,9},{9,8},{10,11... | collective-permute-start | bytes 497672 | tf_op jit(solution)/shard_map/ppermute | solution.py:696
  390.1 24.9 %collective-permute-start.49 = (bf16[192,256]{1,0:T(8,128)(2,1)}, bf16[192,256]{1,0:T(8,128)(2,1)}, u32[]{:S(2)}, u32[]{:S(2)}) collective-permute-start(bf16[192,256]{1,0:T(8,128)(2,1)} %fusion.17), channel_id=1, source_target_pairs={{0,2},{1,3},{2,0},{3,1},{4,6},{5,7},{6,4},{7,5},{8,10},{9,11},{10,... | collective-permute-start | bytes 294920 | tf_op jit(solution)/shard_map/ppermute | solution.py:696
  393.2 21.9 %collective-permute-start.48 = (bf16[144,512]{1,0:T(8,128)(2,1)}, bf16[144,512]{1,0:T(8,128)(2,1)}, u32[]{:S(2)}, u32[]{:S(2)}) collective-permute-start(bf16[144,512]{1,0:T(8,128)(2,1)} %fusion.18), channel_id=1, source_target_pairs={{0,8},{4,12},{8,0},{12,4},{16,24},{20,28},{24,16},{28,20},{1,9},{5... | collective-permute-start | bytes 442376 | tf_op jit(solution)/shard_map/ppermute | solution.py:696
  393.6 21.4 %collective-permute-start.47 = (bf16[144,1152]{1,0:T(8,128)(2,1)S(1)}, bf16[144,1152]{1,0:T(8,128)(2,1)S(1)}, u32[]{:S(2)}, u32[]{:S(2)}) collective-permute-start(bf16[144,1152]{1,0:T(8,128)(2,1)S(1)} %fusion.8), channel_id=1, source_target_pairs={{0,2},{1,3},{2,0},{3,1},{4,6},{5,7},{6,4},{7,5},{8,10},{9,11},{10,... | collective-permute-start | bytes 995336 | tf_op jit(solution)/shard_map/ppermute | solution.py:696
  400.8 14.2 %all-to-all-start.2 = ((f32[4,1,1728]{2,1,0:T(1,128)}), f32[4,1,1728]{2,1,0:T(1,128)S(1)}, u32[]{:S(2)}, u32[]{:S(2)}) async-start(f32[4,1,1728]{2,1,0:T(1,128)} %all_to_all.19), calls=%async_computation.2 | async-start | bytes 57344 | tf_op jit(solution)/shard_map/all_to_all | solution.py:724
  (52 other events, 485.9 us)
